TPU v7x, 32 devices: a whole 2x2x4 slice. The times are simulated.
32 devices in a mesh: dp: 16 (over z, y, x), tensor: 2 (over core).
Axes of the slice: x: 2, y: 2, z: 4, core: 2. Of those that a mesh axis runs over, the one named last changes fastest.
Arguments:
- images: bfloat16 [64, 256, 768], P(('dp', 'tensor')), may hold values from -6 to 6
- valid_count: int32 [64], P('dp'), may hold values from 16 to 256, as said below
- ln_gain: float32 [2, 2, 768], replicated, may hold values from 0.25 to 1.75
- ln_bias: float32 [2, 2, 768], replicated, may hold values from -1.5 to 1.5
- w_qkv: bfloat16 [2, 768, 3, 768], P(None, None, None, 'tensor'), may hold values from -0.21875 to 0.21875
- qv_bias: float32 [2, 2, 768], P(None, None, 'tensor'), may hold values from -2.5 to 2.5
- w_out: bfloat16 [2, 768, 768], P(None, 'tensor'), may hold values from -0.875 to 0.875
- out_bias: float32 [2, 2, 768], replicated, may hold values from -1.5 to 1.5
- w_up: bfloat16 [2, 768, 3072], P(None, None, 'tensor'), may hold values from -0.21875 to 0.21875
- up_bias: float32 [2, 3072], P(None, 'tensor'), may hold values from -1.5 to 1.5
- w_down: bfloat16 [2, 3072, 768], P(None, 'tensor'), may hold values from -0.109375 to 0.109375
- cotangent: bfloat16 [64, 256, 768], P(('dp', 'tensor')), may hold values from -6 to 6
Outputs:
- layer_out: float32 [64, 256, 768], P(('dp', 'tensor'))
- pooled: float32 [64, 768], P(('dp', 'tensor'))
- input_grad: float32 [64, 256, 768], P(('dp', 'tensor'))
- ln_gain_grad: float32 [2, 2, 768], replicated
- ln_bias_grad: float32 [2, 2, 768], replicated
- qkv_grad: float32 [2, 768, 3, 768], P(None, 'dp', None, 'tensor')
- qv_bias_grad: float32 [2, 2, 768], P(None, None, 'tensor')
- out_grad: float32 [2, 768, 768], P(None, 'tensor', 'dp')
- out_bias_grad: float32 [2, 2, 768], replicated
- up_grad: float32 [2, 768, 3072], P(None, 'dp', 'tensor')
- up_bias_grad: float32 [2, 3072], P(None, 'tensor')
- down_grad: float32 [2, 3072, 768], P(None, 'tensor', 'dp')
Inputs may be any that keep to these rules, and one draw needn't show every extreme that they name: `valid_count`: some image has exactly 256 valid patches and some other exactly 16; an image's valid patches are its first slots.
All inputs are finite; a program needn't handle non-finite values.
Results may differ from a plain program's by a relative error of at most 0.024.
Values may be sent and summed in bfloat16 or wider, within the bound.
No kernel may reach another device: no remote copies, remote signals or barrier semaphores. Data moves between devices by JAX's collectives and lax.ppermute only.
A program may use at most 192 MiB of HBM per device.

v0:
```python
import functools
import math

import jax
import jax.numpy as jnp
from jax import lax
from jax.experimental import pallas as pl
from jax.experimental.pallas import tpu as pltpu
from jax.sharding import PartitionSpec as P

HEAD_DIM = 64
LAYERS = 2
EPSILON = 1e-06
NEGATIVE = -1e30
BF16 = jnp.bfloat16
F32 = jnp.float32
CHUNK = 16


def dot(left, right):
    return lax.dot_general(left, right, (((1,), (0,)), ((), ())), preferred_element_type=F32)


def dot_nt(left, right):
    return lax.dot_general(left, right, (((1,), (1,)), ((), ())), preferred_element_type=F32)


def fixed(shape, *lead):
    where = tuple(lead) + (0,) * (len(shape) - len(lead))
    return pl.BlockSpec(shape, lambda *_: where)


def out(shape, dtype):
    return jax.ShapeDtypeStruct(shape, dtype)


def in_hbm(values):
    return pltpu.with_memory_space_constraint(values, pltpu.HBM)


def cost(flops, *arrays):
    total = sum(math.prod(a.shape) * a.dtype.itemsize for a in arrays)
    return pl.CostEstimate(flops=int(flops) // 64, bytes_accessed=int(total) // 64, transcendentals=0)


MIB = 1 << 20


def call(body, name, grid, ins, in_specs, outs, out_specs, scratch=(), flops=0, limit=24):
    return pl.pallas_call(
        body,
        name=name,
        grid=grid,
        in_specs=in_specs,
        out_specs=out_specs,
        out_shape=outs,
        scratch_shapes=list(scratch),
        compiler_params=pltpu.CompilerParams(vmem_limit_bytes=limit * MIB),
        cost_estimate=cost(flops, *ins, *outs),
    )(*ins)


def whole():
    return pl.BlockSpec(memory_space=pltpu.VMEM)


def by_blocks(target, left, right, product, rows=256, add=False):
    def block(index, carry):
        here = pl.ds(pl.multiple_of(index * rows, rows), rows)
        value = product(left[here, :], right())
        if add:
            value = target[here, :] + value
        target[here, :] = value.astype(target.dtype)
        return carry

    lax.fori_loop(0, left.shape[0] // rows, block, 0)


def hbm():
    return pl.BlockSpec(memory_space=pltpu.HBM)


def by_rows(rows, body, unroll=1):
    def step(index, carry):
        for part in range(unroll):
            body(pl.multiple_of((index * unroll + part) * CHUNK, CHUNK))
        return carry

    lax.fori_loop(0, rows // (CHUNK * unroll), step, 0)


def moments(values):
    average = jnp.mean(values, axis=-1, keepdims=True)
    centred = values - average
    variance = jnp.mean(centred * centred, axis=-1, keepdims=True)
    return centred, lax.rsqrt(variance + EPSILON)


def normalized(values, gain, bias):
    centred, scale = moments(values)
    return centred * scale * gain + bias


def norm_backward(values, grad_normed, gain):
    centred, scale = moments(values)
    unit = centred * scale
    grad_unit = grad_normed * gain
    first = jnp.mean(grad_unit, axis=-1, keepdims=True)
    second = jnp.mean(grad_unit * unit, axis=-1, keepdims=True)
    return scale * (grad_unit - first - unit * second), grad_normed * unit


def fold_rows(values):
    total = values[0:8]
    for start in range(8, values.shape[0], 8):
        total = total + values[start : start + 8]
    return total


def prep_kernel(images, cotangent, gain, bias, order, normed, normed_t, cotangent_t, wide_cotangent):
    def rows(start):
        here = pl.ds(start, CHUNK)
        values = images[here, :].astype(F32)
        normed[here, :] = normalized(values, gain[0, 0:1, :], bias[0, 0:1, :]).astype(BF16)
        wide_cotangent[here, :] = cotangent[here, :].astype(F32)

    by_rows(images.shape[0], rows, 4)
    by_blocks(normed_t, order, lambda: normed[...], dot_nt)
    by_blocks(cotangent_t, order, lambda: cotangent[...], dot_nt)


def head_masks(slots):
    lane = lax.broadcasted_iota(jnp.int32, (slots, 2 * HEAD_DIM), 1)
    return lane < HEAD_DIM, lane >= HEAD_DIM


def own_count(counts, image, images):
    return counts[lax.axis_index("tensor") * images + image]


def attend_kernel(
    slots,
    which,
    counts,
    normed,
    weight_own,
    weight_far,
    bias_own,
    bias_far,
    joint_own,
    joint_far,
    att_own,
    att_far,
    lse_own,
    lse_far,
    held,
    sem,
):
    width = att_own.shape[1]
    pairs = width // (2 * HEAD_DIM)
    scale = HEAD_DIM ** (-0.5)
    layer = which[0]
    weights = (weight_own, weight_far)
    for side in range(2):
        for member in range(3):
            fetch(weights[side].at[layer, member], held.at[side, member], sem.at[side, member])
    for side, (joint, bias) in enumerate(((joint_own, bias_own), (joint_far, bias_far))):

        def project(member, carry):
            pltpu.make_async_copy(
                weights[side].at[layer, member], held.at[side, member], sem.at[side, member]
            ).wait()
            shift = bias[layer, pl.ds(member // 2, 1), :]
            shift = jnp.where(member == 1, jnp.zeros_like(shift), shift)
            joint[member] = (dot(normed[...], held[side, member]) + shift).astype(BF16)
            return carry

        lax.fori_loop(0, 3, project, 0)
    masks = head_masks(slots)
    key_index = lax.broadcasted_iota(jnp.int32, (slots, slots), 0)

    def step(index, carry):
        image = index // pairs
        pair = index % pairs
        rows = pl.ds(pl.multiple_of(image * slots, slots), slots)
        lanes = pl.ds(pl.multiple_of(pair * 2 * HEAD_DIM, 2 * HEAD_DIM), 2 * HEAD_DIM)
        valid = key_index < own_count(counts, image, normed.shape[0] // slots)
        for joint, attended, lse in (
            (joint_own, att_own, lse_own),
            (joint_far, att_far, lse_far),
        ):
            queries = joint[0, rows, lanes]
            keys_in = joint[1, rows, lanes] * jnp.asarray(scale, BF16)
            values_t = joint[2, rows, lanes].T
            parts = []
            for side in range(2):
                keys_side = jnp.where(masks[side], keys_in, jnp.zeros_like(keys_in))
                scores = jnp.where(valid, dot_nt(keys_side, queries), NEGATIVE)
                largest = jnp.max(scores, axis=0, keepdims=True)
                exponent = jnp.exp(scores - largest)
                total = jnp.sum(exponent, axis=0, keepdims=True)
                probs = (exponent * (1.0 / total)).astype(BF16)
                parts.append(dot(values_t[side * HEAD_DIM : (side + 1) * HEAD_DIM], probs))
                lse[2 * index + side] = largest + jnp.log(total)
            attended[rows, lanes] = jnp.concatenate(parts, axis=0).T.astype(BF16)
        return carry

    lax.fori_loop(0, (normed.shape[0] // slots) * pairs, step, 0)


def fetch(source, target, sem):
    copy = pltpu.make_async_copy(source, target, sem)
    copy.start()
    return copy


def feed_kernel(
    layer,
    slots,
    last_layer,
    counts,
    stream,
    att_own,
    att_far,
    out_own,
    out_far,
    out_bias,
    gain,
    bias,
    order,
    up_own,
    up_far,
    up_bias_own,
    up_bias_far,
    down_own,
    down_far,
    mid,
    normed_t,
    hid_own,
    hid_far,
    slope_own,
    slope_far,
    stream_out,
    *rest,
):
    if last_layer:
        pooled = rest[0]
    else:
        next_normed, next_t = rest[:2]
    normed, total, pre, w_out, w_up, w_down, hid, slope, in_sem, out_sem = rest[1 if last_layer else 2 :]
    tokens = stream.shape[0]
    half = w_out.shape[0] // 2
    units = w_up.shape[0]
    tile = w_up.shape[2]
    tiles = units // 2
    out_in = [
        fetch(ref.at[layer], w_out.at[pl.ds(side * half, half)], in_sem.at[side])
        for side, ref in enumerate((out_own, out_far))
    ]
    up_in, down_in = [], []
    for unit in range(units):
        side, part = unit // tiles, unit % tiles
        columns = pl.ds(part * tile, tile)
        up_ref, down_ref = ((up_own, down_own), (up_far, down_far))[side]
        up_in.append(fetch(up_ref.at[layer, :, columns], w_up.at[unit], in_sem.at[2 + unit]))
        down_in.append(
            fetch(down_ref.at[layer, columns, :], w_down.at[unit], in_sem.at[2 + units + unit])
        )
    for copy in out_in:
        copy.wait()
    total[...] = dot(jnp.concatenate([att_own[...], att_far[...]], axis=1), w_out[...])

    def enter(start):
        here = pl.ds(start, CHUNK)
        value = stream[here, :].astype(F32) + (total[here, :] + out_bias[layer, 0:1, :])
        mid[here, :] = value
        normed[here, :] = normalized(value, gain[layer, 1:2, :], bias[layer, 1:2, :]).astype(BF16)

    by_rows(tokens, enter, 4)
    up_in[0].wait()
    by_blocks(pre.at[0], normed, lambda: w_up[0], dot)
    by_blocks(normed_t, order, lambda: normed[...], dot_nt)
    rows = 128
    out_copies = []
    for unit in range(units):
        side, part = unit // tiles, unit % tiles
        shift = (up_bias_own, up_bias_far)[side][layer : layer + 1, part * tile : (part + 1) * tile]
        if unit + 1 < units:
            up_in[unit + 1].wait()
        if unit > 0:
            down_in[unit - 1].wait()

        def chunk(index, carry):
            block = pl.ds(pl.multiple_of(index * rows, rows), rows)
            if unit + 1 < units:
                pre[(unit + 1) % 2, block, :] = dot(normed[block, :], w_up[unit + 1])
            if unit == 1:
                total[block, :] = dot(hid[unit - 1, block, :], w_down[unit - 1])
            elif unit > 1:
                total[block, :] += dot(hid[unit - 1, block, :], w_down[unit - 1])
            for sub in range(0, rows, CHUNK):
                here = pl.ds(pl.multiple_of(index * rows + sub, CHUNK), CHUNK)
                value = pre[unit % 2, here, :] + shift
                cdf = 0.5 + 0.5 * lax.erf(value * (0.5**0.5))
                hid[unit, here, :] = (value * cdf).astype(BF16)
                density = jnp.exp(-0.5 * value * value) * ((2.0 * math.pi) ** -0.5)
                slope[unit, here, :] = (cdf + value * density).astype(BF16)
            return carry

        lax.fori_loop(0, tokens // rows, chunk, 0)
        hid_ref, slope_ref = ((hid_own, slope_own), (hid_far, slope_far))[side]
        columns = pl.ds(part * tile, tile)
        out_copies.append(fetch(hid.at[unit], hid_ref.at[:, columns], out_sem.at[unit]))
        out_copies.append(fetch(slope.at[unit], slope_ref.at[:, columns], out_sem.at[units + unit]))
    down_in[units - 1].wait()
    by_blocks(total, hid.at[units - 1], lambda: w_down[units - 1], dot, add=True)

    def leave(start):
        here = pl.ds(start, CHUNK)
        value = mid[here, :] + (total[here, :] + out_bias[layer, 1:2, :])
        stream_out[here, :] = value
        if not last_layer:
            next_normed[here, :] = normalized(
                value, gain[layer + 1, 0:1, :], bias[layer + 1, 0:1, :]
            ).astype(BF16)

    by_rows(tokens, leave, 4)
    if last_layer:
        index = lax.broadcasted_iota(jnp.int32, (slots, 1), 0)
        for image in range(tokens // slots):
            block = stream_out[image * slots : (image + 1) * slots, :]
            count = own_count(counts, image, tokens // slots)
            summed = jnp.sum(jnp.where(index < count, block, 0.0), axis=0, keepdims=True)
            pooled[image : image + 1, :] = summed / count.astype(F32)
    else:
        by_blocks(next_t, order, lambda: next_normed[...], dot_nt)
    for copy in out_copies:
        copy.wait()


def feed_back_kernel(
    which,
    grad_in,
    mid,
    gain,
    order,
    down_own,
    down_far,
    up_own,
    up_far,
    slope_own,
    slope_far,
    out_own,
    out_far,
    pre_own,
    pre_far,
    bias_own,
    bias_far,
    grad_mid,
    mid_t,
    att_own,
    att_far,
    sums,
    low,
    total,
    hidden,
    partial,
    w_down,
    w_up,
    slope,
    pre,
    w_out,
    in_sem,
    out_sem,
):
    layer = which[0]
    tokens = grad_in.shape[0]
    units = w_up.shape[0]
    tile = w_up.shape[2]
    tiles = units // 2
    down_in, up_in, slope_in = [], [], []
    for unit in range(units):
        columns = pl.ds(unit % tiles * tile, tile)
        down_ref, up_ref, slope_ref = ((down_far, up_far, slope_far), (down_own, up_own, slope_own))[
            unit // tiles
        ]
        down_in.append(fetch(down_ref.at[layer, columns, :], w_down.at[unit], in_sem.at[0, unit]))
        slope_in.append(fetch(slope_ref.at[:, columns], slope.at[unit], in_sem.at[1, unit]))
        up_in.append(fetch(up_ref.at[layer, :, columns], w_up.at[unit], in_sem.at[2, unit]))
    out_in = [
        fetch(ref.at[layer], w_out.at[side], in_sem.at[3, side])
        for side, ref in enumerate((out_far, out_own))
    ]
    partial[...] = jnp.zeros_like(partial)

    def enter(start):
        here = pl.ds(start, CHUNK)
        value = grad_in[here, :].astype(F32)
        low[here, :] = value.astype(BF16)
        partial[0] += fold_rows(value)

    by_rows(tokens, enter)
    down_in[0].wait()
    by_blocks(hidden.at[0], low, lambda: w_down[0], dot_nt)
    rows = 256
    total[...] = jnp.zeros_like(total)
    pre[units - 1] = jnp.zeros_like(pre[units - 1])
    pre_refs = (pre_far, pre_own)

    def result(unit, side):
        columns = pl.ds(pl.multiple_of(unit % tiles * tile, tile), tile)
        return pltpu.make_async_copy(pre.at[unit], pre_refs[side].at[:, columns], out_sem.at[unit])

    def turn(unit, carry):
        after = jnp.minimum(unit + 1, units - 1)
        before = jnp.maximum(unit - 1, 0)

        @pl.when(unit + 1 < units)
        def _():
            pltpu.make_async_copy(
                down_own.at[layer, pl.ds(0, tile), :], w_down.at[after], in_sem.at[0, after]
            ).wait()

        @pl.when(unit != 1)
        def _():
            pltpu.make_async_copy(
                up_own.at[layer, :, pl.ds(0, tile)], w_up.at[before], in_sem.at[2, before]
            ).wait()

        pltpu.make_async_copy(
            slope_own.at[:, pl.ds(0, tile)], slope.at[unit], in_sem.at[1, unit]
        ).wait()
        idle = (unit + units - 1) % units

        def chunk(index, carry):
            block = pl.ds(pl.multiple_of(index * rows, rows), rows)
            hidden[(unit + 1) % 2, block, :] = dot_nt(low[block, :], w_down[after])
            total[block, :] += dot_nt(pre[idle, block, :], w_up[before])
            for sub in range(0, rows, CHUNK):
                here = pl.ds(pl.multiple_of(index * rows + sub, CHUNK), CHUNK)
                value = hidden[unit % 2, here, :] * slope[unit, here, :].astype(F32)
                pre[unit, here, :] = value.astype(BF16)
                carry = carry + fold_rows(value)
            return carry

        summed = lax.fori_loop(0, tokens // rows, chunk, jnp.zeros((8, tile), F32))
        row = jnp.sum(summed, axis=0, keepdims=True)
        for side, bias in enumerate((bias_far, bias_own)):

            @pl.when(unit // tiles == side)
            def _():
                bias[pl.ds(unit % tiles, 1), :] = row
                result(unit, side).start()

        return carry

    lax.fori_loop(0, units, turn, 0)
    up_in[units - 1].wait()
    by_blocks(total, pre.at[units - 1], lambda: w_up[units - 1], dot_nt, add=True)

    def leave(start):
        here = pl.ds(start, CHUNK)
        normed_grad = total[here, :]
        through, gain_term = norm_backward(mid[here, :], normed_grad, gain[layer, 1:2, :])
        value = grad_in[here, :].astype(F32) + through
        grad_mid[here, :] = value
        low[here, :] = value.astype(BF16)
        partial[1] += fold_rows(value)
        partial[2] += fold_rows(gain_term)
        partial[3] += fold_rows(normed_grad)

    by_rows(tokens, leave, 2)
    sums[...] = jnp.sum(partial[...], axis=1)
    by_blocks(mid_t, order, lambda: low[...], dot_nt)
    for copy in out_in:
        copy.wait()
    by_blocks(att_far, low, lambda: w_out[0], dot_nt)
    by_blocks(att_own, low, lambda: w_out[1], dot_nt)
    for unit in range(units):
        result(unit, unit // tiles).wait()


def attend_back_kernel(slots, counts, joint, lse, grad_att, grad_joint, bias_sums):
    width = grad_att.shape[1]
    pairs = width // (2 * HEAD_DIM)
    scale = HEAD_DIM ** (-0.5)
    masks = head_masks(slots)
    key_index = lax.broadcasted_iota(jnp.int32, (slots, slots), 0)
    bias_sums[...] = jnp.zeros_like(bias_sums)

    def step(index, carry):
        image = index // pairs
        pair = index % pairs
        rows = pl.ds(pl.multiple_of(image * slots, slots), slots)
        lanes = pl.ds(pl.multiple_of(pair * 2 * HEAD_DIM, 2 * HEAD_DIM), 2 * HEAD_DIM)
        queries = joint[0, rows, lanes]
        keys_in = joint[1, rows, lanes]
        values_in = joint[2, rows, lanes]
        grads = grad_att[rows, lanes]
        keys_t = keys_in.T
        keys_scaled = keys_in * jnp.asarray(scale, BF16)
        valid = key_index < own_count(counts, image, grad_att.shape[0] // slots)
        zeros = jnp.zeros_like(keys_in)
        query_parts, key_parts, value_parts = [], [], []
        for side in range(2):
            keys_side = jnp.where(masks[side], keys_scaled, zeros)
            values_side = jnp.where(masks[side], values_in, zeros)
            scores = jnp.where(valid, dot_nt(keys_side, queries), NEGATIVE)
            probs = jnp.exp(scores - lse[2 * index + side])
            grad_probs = dot_nt(values_side, grads)
            inner = jnp.sum(grad_probs * probs, axis=0, keepdims=True)
            grad_scores = (probs * (grad_probs - inner)).astype(BF16)
            value_parts.append(dot(probs.astype(BF16), grads))
            key_parts.append(dot(grad_scores, queries))
            query_parts.append(dot(keys_t[side * HEAD_DIM : (side + 1) * HEAD_DIM], grad_scores))
        grad_queries = jnp.concatenate(query_parts, axis=0).T * scale
        grad_keys = jnp.where(masks[0], key_parts[0], key_parts[1]) * scale
        grad_values = jnp.where(masks[0], value_parts[0], value_parts[1])
        bias_sums[0:1, lanes] += jnp.sum(grad_queries, axis=0, keepdims=True)
        value_lanes = pl.ds(
            pl.multiple_of(width + pair * 2 * HEAD_DIM, 2 * HEAD_DIM), 2 * HEAD_DIM
        )
        bias_sums[0:1, value_lanes] += jnp.sum(grad_values, axis=0, keepdims=True)
        grad_joint[0, rows, lanes] = grad_queries.astype(BF16)
        grad_joint[1, rows, lanes] = grad_keys.astype(BF16)
        grad_joint[2, rows, lanes] = grad_values.astype(BF16)
        return carry

    lax.fori_loop(0, (grad_att.shape[0] // slots) * pairs, step, 0)


def entry_back_kernel(
    layer, with_low, joint_own, joint_far, weight_own, weight_far, stream, gain, grad_mid, order, *rest
):
    if with_low:
        grad_out, sums, low_t, total, partial, low = rest
    else:
        grad_out, sums, total, partial = rest
    member = pl.program_id(0)

    @pl.when(member == 0)
    def _():
        total[...] = jnp.zeros_like(total)
        partial[...] = jnp.zeros_like(partial)

    left = jnp.concatenate([joint_own[member], joint_far[member]], axis=1)
    right = jnp.concatenate([weight_own[0, 0], weight_far[0, 0]], axis=1)
    total[...] += dot_nt(left, right)

    def rows(start):
        here = pl.ds(start, CHUNK)
        normed_grad = total[here, :]
        through, gain_term = norm_backward(
            stream[here, :].astype(F32), normed_grad, gain[layer, 0:1, :]
        )
        value = grad_mid[here, :] + through
        grad_out[here, :] = value
        if with_low:
            low[here, :] = value.astype(BF16)
        partial[0] += fold_rows(gain_term)
        partial[1] += fold_rows(normed_grad)

    @pl.when(member == 2)
    def _():
        by_rows(stream.shape[0], rows, 2)
        sums[...] = jnp.sum(partial[...], axis=1)
        if with_low:
            by_blocks(low_t, order, lambda: low[...], dot_nt)


def pack_kernel(layers, *refs):
    ins, (own_out, far_out) = refs[:-2], refs[-2:]
    for layer in range(layers):
        sums_mid, sums_in, qv_own, qv_far, upb_own, upb_far = ins[6 * layer : 6 * layer + 6]
        tiles = upb_own.shape[0]
        for ref, qv, upb in ((own_out, qv_own, upb_own), (far_out, qv_far, upb_far)):
            for row, value in (
                (2 * layer, sums_in[0:1, :]),
                (2 * layer + 1, sums_mid[2:3, :]),
                (2 * (layers + layer), sums_in[1:2, :]),
                (2 * (layers + layer) + 1, sums_mid[3:4, :]),
                (2 * (2 * layers + layer), sums_mid[1:2, :]),
                (2 * (2 * layers + layer) + 1, sums_mid[0:1, :]),
                (6 * layers + layer, qv[...]),
            ):
                ref[row : row + 1, :] = value
            start = 7 * layers + tiles * layer
            ref[start : start + tiles, :] = upb[...]


def unpack_kernel(layers, mine, got, gain, bias, out_bias, qv, upb):
    total = mine[...] + got[...]
    half = qv.shape[2]
    tiles = upb.shape[1] // mine.shape[1]
    width = mine.shape[1]
    for layer in range(layers):
        for norm in range(2):
            row = 2 * layer + norm
            gain[layer, norm : norm + 1, :] = total[row : row + 1]
            row += 2 * layers
            bias[layer, norm : norm + 1, :] = total[row : row + 1]
            row += 2 * layers
            out_bias[layer, norm : norm + 1, :] = total[row : row + 1]
        row = 6 * layers + layer
        for kind in range(2):
            qv[layer, kind : kind + 1, :] = total[row : row + 1, kind * half : (kind + 1) * half]
        row = 7 * layers + tiles * layer
        for part in range(tiles):
            upb[layer : layer + 1, part * width : (part + 1) * width] = total[
                row + part : row + part + 1
            ]


def chunk_sources(order):
    first = list(order[:4])
    sources = []
    for target in range(16):
        source = 0
        for place, bit in enumerate(first):
            if (target >> (3 - place)) & 1:
                source |= 1 << (3 - bit)
        sources.append(source)
    return sources


def weight_kernel(sources, tiles, has_extra, *refs):
    if has_extra:
        left_own, left_far, right_own, right_far, lx_own, lx_far, rx_own, rx_far, keep, send = refs
    else:
        left_own, left_far, right_own, right_far, keep, send = refs

    def product(a_own, a_far, b_own, b_far):
        left = jnp.concatenate([a_own[...], a_far[...]], axis=1)
        right = jnp.concatenate([b_own[...].reshape(b_own.shape[-2:]), b_far[...].reshape(b_far.shape[-2:])], axis=0)
        size = left.shape[0] // 16
        low = dot(left, right).astype(BF16)
        for target, source in enumerate(sources):
            ref = keep if target < 8 else send
            ref[(target % 8) * size : (target % 8 + 1) * size, :] = low[
                source * size : (source + 1) * size, :
            ]

    if has_extra:

        @pl.when(pl.program_id(0) < tiles)
        def _():
            product(left_own, left_far, right_own, right_far)

        @pl.when(pl.program_id(0) == tiles)
        def _():
            product(lx_own, lx_far, rx_own, rx_far)

    else:
        product(left_own, left_far, right_own, right_far)


def weight_grad(name, order, left, right, extra=None, tiles=None, first=0):
    left_own, left_far = left
    right_own, right_far = right
    width, tokens = left_own.shape
    if right_own.ndim == 3:
        tile = right_own.shape[2]
        right_spec = pl.BlockSpec(
            (1, tokens, tile), lambda j: (jnp.minimum(j, tiles - 1) + first, 0, 0)
        )
    else:
        tile = 768 if tiles else 512
        tiles = tiles or right_own.shape[1] // tile
        right_spec = pl.BlockSpec((tokens, tile), lambda j: (0, j + first))
    steps = tiles + (1 if extra is not None else 0)
    ins = [left_own, left_far, right_own, right_far]
    specs = [fixed((width, tokens))] * 2 + [right_spec] * 2
    if extra is not None:
        ins += list(extra)
        specs += [fixed((width, tokens))] * 2 + [fixed((tokens, tile))] * 2
    half = out((width // 2, steps * tile), BF16)
    half_spec = pl.BlockSpec((width // 2, tile), lambda j: (0, j))
    return call(
        functools.partial(weight_kernel, chunk_sources(order), tiles, extra is not None),
        name,
        (steps,),
        ins,
        specs,
        [half, half],
        [half_spec, half_spec],
        flops=4 * width * tokens * steps * tile,
    )


def flip(bit):
    size = lax.axis_size("dp")
    return [(index, index ^ (1 << bit)) for index in range(size)]


class DpSum:
    def __init__(self, order, halves=None, units=()):
        self.order = list(order)
        self.incoming = None
        if halves is not None:
            keep, self.outgoing = halves
            self.members = [[keep]]
        else:
            self.members = [parts for unit in units for parts in unit.members]
            self.halve()

    def halve(self):
        rows = self.members[0][0].shape[0] // 2
        sends = [
            sum(part[rows:].astype(F32) for part in parts).astype(BF16) for parts in self.members
        ]
        self.outgoing = sends[0] if len(sends) == 1 else jnp.concatenate(sends, axis=1)
        self.members = [[part[:rows] for part in parts] for parts in self.members]

    def start(self):
        self.incoming = lax.ppermute(self.outgoing, "dp", flip(self.order.pop(0)))

    def turn(self):
        column = 0
        for parts in self.members:
            width = parts[0].shape[1]
            parts.append(self.incoming[:, column : column + width])
            column += width
        self.incoming = None
        if self.order:
            self.halve()
            self.start()

    def results(self):
        return [sum(part.astype(F32) for part in parts) for parts in self.members]


class Everywhere:
    def __init__(self, mine, far, bits):
        self.mine = mine
        self.incoming = swap(far)
        self.bits = list(range(bits))

    def turn(self):
        self.mine = self.mine + self.incoming
        self.incoming = lax.ppermute(self.mine, "dp", flip(self.bits.pop(0)))


def gate(value, starts=(), turns=(), after=()):
    held = [unit.outgoing for unit in starts] + [unit.incoming for unit in turns]
    value, *held = lax.optimization_barrier((value, *held, *after))
    for unit, array in zip(starts, held):
        unit.outgoing = array
        unit.start()
    for unit, array in zip(turns, held[len(starts) :]):
        unit.incoming = array
        unit.turn()
    return value


def swap(values):
    return lax.ppermute(values, "tensor", [(0, 1), (1, 0)])


def shards(
    images,
    valid_count,
    ln_gain,
    ln_bias,
    w_qkv,
    qv_bias,
    w_out,
    out_bias,
    w_up,
    up_bias,
    w_down,
    cotangent,
):
    local_rows, slots, width = images.shape
    tokens = local_rows * slots
    half = w_qkv.shape[3]
    ff_half = w_up.shape[2]
    tile = 768
    steps = ff_half // tile
    heads = half // HEAD_DIM
    dp = lax.axis_size("dp")
    bits = dp.bit_length() - 1
    assert dp == 1 << bits and bits >= 4 and lax.axis_size("tensor") == 2
    tail = tuple(range(4, bits))
    order_a = (0, 1, 2, 3) + tail
    order_b = (1, 0, 2, 3) + tail
    order_c = (2, 3, 0, 1) + tail
    order_d = (0, 2, 3, 1) + tail

    me = lax.axis_index("dp")
    counts = valid_count

    block = width // dp
    row = jnp.arange(width, dtype=jnp.int32)
    index = row // block
    mirrored = jnp.zeros_like(index)
    for bit in range(bits):
        mirrored = mirrored | (((index >> (bits - 1 - bit)) & 1) << bit)
    source = (mirrored ^ me) * block + row % block
    order = (source[:, None] == row[None, :]).astype(BF16)

    w_qkv = jnp.transpose(w_qkv, (0, 2, 1, 3))
    qkv = (w_qkv, swap(w_qkv))
    qv = (qv_bias, swap(qv_bias))

    images_2d = images.reshape(tokens, width)
    cotangent_2d = cotangent.reshape(tokens, width)
    smem = pl.BlockSpec(memory_space=pltpu.SMEM)
    wide = (tokens, width)
    flops_wide = 2 * width * width * tokens

    normed, normed_t, cotangent_t, wide_cotangent = call(
        prep_kernel,
        "prep",
        (),
        [images_2d, cotangent_2d, ln_gain, ln_bias, order],
        [whole()] * 5,
        [out(wide, BF16), out((width, tokens), BF16), out((width, tokens), BF16), out(wide, F32)],
        [whole()] * 4,
        flops=2 * flops_wide,
    )

    wout, wup, wdown = [
        (weight, swap(lax.optimization_barrier((weight, normed, qkv[1], qv[1]))[0]))
        for weight in (w_out, w_up, w_down)
    ]

    def attend(layer, normed, counts):
        lse_shape = (local_rows * heads, 1, slots)
        joint_out = out((3, tokens, half), BF16)
        att_out = out((tokens, half), BF16)
        lse_out = out(lse_shape, F32)
        results = call(
            functools.partial(attend_kernel, slots),
            "attend",
            (),
            [jnp.full((1,), layer, jnp.int32), counts, normed, in_hbm(qkv[0]), in_hbm(qkv[1]), qv[0], qv[1]],
            [smem, smem, whole(), hbm(), hbm(), whole(), whole()],
            [joint_out, joint_out, att_out, att_out, lse_out, lse_out],
            [whole()] * 6,
            [pltpu.VMEM((2, 3, width, half), BF16), pltpu.SemaphoreType.DMA((2, 3))],
            flops=12 * tokens * width * half + 8 * tokens * slots * half,
            limit=44,
        )
        return results[0::2], results[1::2]

    stream = images_2d
    saved = []
    got_cotangent_t = swap(cotangent_t)
    pooled = None
    for layer in range(LAYERS):
        last = layer == LAYERS - 1
        own, far = attend(layer, normed, counts)
        if layer == 0:
            upb = (up_bias, swap(up_bias))
        gain_in = ln_gain
        if layer > 0:
            before = saved[layer - 1]
            names = ("got_normed_t", "got_att", "got_mid_normed_t", "got_hid")
            gain_in, got_cotangent_t, *got = lax.optimization_barrier(
                (ln_gain, got_cotangent_t, *[before[name] for name in names])
            )
            before.update(zip(names, got))
        ff = pltpu.HBM((tokens, ff_half), BF16)
        extra = (
            [out((local_rows, width), F32)]
            if last
            else [out(wide, BF16), out((width, tokens), BF16)]
        )
        results = call(
            functools.partial(feed_kernel, layer, slots, last),
            "feed",
            (),
            [
                counts,
                stream,
                own[1],
                far[1],
                in_hbm(wout[0]),
                in_hbm(wout[1]),
                out_bias,
                gain_in,
                ln_bias,
                order,
                in_hbm(wup[0]),
                in_hbm(wup[1]),
                upb[0],
                upb[1],
                in_hbm(wdown[0]),
                in_hbm(wdown[1]),
            ],
            [smem]
            + [whole()] * 3
            + [hbm()] * 2
            + [whole()] * 4
            + [hbm()] * 2
            + [whole()] * 2
            + [hbm()] * 2,
            [out(wide, F32), out((width, tokens), BF16), ff, ff, ff, ff, out(wide, F32)] + extra,
            [whole()] * 2 + [hbm()] * 4 + [whole()] * (1 + len(extra)),
            [
                pltpu.VMEM(wide, BF16),
                pltpu.VMEM(wide, F32),
                pltpu.VMEM((2, tokens, tile), F32),
                pltpu.VMEM((2 * half, width), BF16),
                pltpu.VMEM((2 * steps, width, tile), BF16),
                pltpu.VMEM((2 * steps, tile, width), BF16),
                pltpu.VMEM((2 * steps, tokens, tile), BF16),
                pltpu.VMEM((2 * steps, tokens, tile), BF16),
                pltpu.SemaphoreType.DMA((2 + 4 * steps,)),
                pltpu.SemaphoreType.DMA((4 * steps,)),
            ],
            flops=8 * tokens * width * ff_half + 2 * flops_wide,
            limit=32,
        )
        mid, mid_normed_t, hid_own, hid_far, slope_own, slope_far, stream_next = results[:7]
        saved.append(
            dict(
                stream=stream,
                own=own,
                far=far,
                mid=mid,
                slope=(slope_own, slope_far),
                hid=hid_own,
                attended=own[1],
                normed_t=normed_t,
                mid_normed_t=mid_normed_t,
                got_hid=swap(hid_far),
                got_att=swap(far[1]),
                got_normed_t=swap(normed_t),
                got_mid_normed_t=swap(mid_normed_t),
            )
        )
        stream = stream_next
        if last:
            pooled = results[7]
        else:
            normed, normed_t = results[7:9]

    def feed_back(layer, grad, gain_in):
        kept = saved[layer]
        ff = pltpu.HBM((tokens, ff_half), BF16)
        bias_shape = out((steps, tile), F32)
        att_shape = out((tokens, half), BF16)
        return call(
            feed_back_kernel,
            "feed_back",
            (),
            [
                jnp.full((1,), layer, jnp.int32),
                grad,
                kept["mid"],
                gain_in,
                order,
                in_hbm(wdown[0]),
                in_hbm(wdown[1]),
                in_hbm(wup[0]),
                in_hbm(wup[1]),
                kept["slope"][0],
                kept["slope"][1],
                in_hbm(wout[0]),
                in_hbm(wout[1]),
            ],
            [smem] + [whole()] * 4 + [hbm()] * 8,
            [
                ff,
                ff,
                bias_shape,
                bias_shape,
                out(wide, F32),
                out((width, tokens), BF16),
                att_shape,
                att_shape,
                out((4, width), F32),
            ],
            [hbm()] * 2 + [whole()] * 7,
            [
                pltpu.VMEM(wide, BF16),
                pltpu.VMEM(wide, F32),
                pltpu.VMEM((2, tokens, tile), F32),
                pltpu.VMEM((4, 8, width), F32),
                pltpu.VMEM((2 * steps, tile, width), BF16),
                pltpu.VMEM((2 * steps, width, tile), BF16),
                pltpu.VMEM((2 * steps, tokens, tile), BF16),
                pltpu.VMEM((2 * steps, tokens, tile), BF16),
                pltpu.VMEM((2, half, width), BF16),
                pltpu.SemaphoreType.DMA((4, 2 * steps)),
                pltpu.SemaphoreType.DMA((2 * steps,)),
            ],
            flops=8 * tokens * width * ff_half + 2 * flops_wide,
            limit=32,
        )

    def attend_back(forward, grad_att, counts_in):
        joint, _, lse = forward
        return call(
            functools.partial(attend_back_kernel, slots),
            "attend_back",
            (),
            [counts_in, joint, lse, grad_att],
            [smem, whole(), whole(), whole()],
            [out(joint.shape, BF16), out((1, 2 * half), F32)],
            [whole()] * 2,
            flops=10 * tokens * slots * half,
        )

    def entry_back(layer, joint_own, joint_far, grad_mid, gain_in):
        with_low = layer > 0
        return call(
            functools.partial(entry_back_kernel, layer, with_low),
            "entry_back",
            (3,),
            [
                joint_own,
                joint_far,
                in_hbm(qkv[0]),
                in_hbm(qkv[1]),
                saved[layer]["stream"],
                gain_in,
                grad_mid,
                order,
            ],
            [whole()] * 2
            + [pl.BlockSpec((1, 1, width, half), lambda c: (layer, c, 0, 0))] * 2
            + [whole()] * 4,
            [out(wide, F32), out((2, width), F32)]
            + ([out((width, tokens), BF16)] if with_low else []),
            [whole()] * (3 if with_low else 2),
            [pltpu.VMEM(wide, F32), pltpu.VMEM((2, 8, width), F32)]
            + ([pltpu.VMEM(wide, BF16)] if with_low else []),
            flops=12 * tokens * width * half,
        )

    def down_halves(layer, order_of, grad_t, got_grad_t):
        kept = saved[layer]
        return weight_grad(
            "down_grad", order_of, (grad_t, got_grad_t), (in_hbm(kept["hid"]), kept["got_hid"])
        )

    def up_halves(layer, order_of, pre_own, got_pre, tiles=None, first=0):
        kept = saved[layer]
        return weight_grad(
            "up_grad",
            order_of,
            (kept["mid_normed_t"], kept["got_mid_normed_t"]),
            (pre_own, got_pre),
            tiles=tiles,
            first=first,
        )

    def lefts(layer):
        return saved[layer]["normed_t"], saved[layer]["got_normed_t"]

    def extras(layer, mid_t, got_mid_t):
        return mid_t, got_mid_t, saved[layer]["attended"], saved[layer]["got_att"]

    small = [None] * LAYERS
    down_1 = DpSum(order_a, down_halves(1, order_a, cotangent_t, got_cotangent_t))
    gain_in = gate(ln_gain, [down_1])
    pre_own, pre_far, upb_own, upb_far, grad_mid, mid_t, att_own, att_far, sums_mid = feed_back(
        1, wide_cotangent, gain_in
    )
    got_pre, got_mid_t = swap(pre_far), swap(mid_t)
    joint_far, qv_far = attend_back(saved[1]["far"], att_far, counts)
    got_joint = swap(joint_far)
    counts_in = gate(counts, [], [down_1], [qv_far])
    joint_own, qv_own = attend_back(saved[1]["own"], att_own, counts_in)
    pre_own = gate(pre_own, after=[qv_own])
    up_1 = DpSum(order_a, up_halves(1, order_a, pre_own, got_pre))
    gain_in = gate(gain_in, [up_1], [down_1])
    grad, sums_in, grad_t = entry_back(1, joint_own, joint_far, grad_mid, gain_in)
    got_grad_t = swap(grad_t)
    small[1] = (sums_mid, sums_in, qv_own, qv_far, upb_own, upb_far)
    joint_own = gate(joint_own, [], [down_1], [sums_in])
    rest_1 = DpSum(
        order_c,
        weight_grad(
            "qkv_out_grad",
            order_c,
            lefts(1),
            (joint_own, got_joint),
            extras(1, mid_t, got_mid_t),
            tiles=3,
        ),
    )
    grad_t = gate(grad_t, [rest_1])
    down_0 = DpSum(order_a, down_halves(0, order_a, grad_t, got_grad_t))

    gain_in = gate(gain_in, [down_0], [up_1, down_1])
    pre_own, pre_far, upb_own, upb_far, grad_mid, mid_t, att_own, att_far, sums_mid = feed_back(
        0, grad, gain_in
    )
    got_pre, got_mid_t = swap(pre_far), swap(mid_t)
    counts_in = gate(counts_in, [], [up_1, rest_1], [sums_mid])
    joint_far, qv_far = attend_back(saved[0]["far"], att_far, counts_in)
    got_joint = swap(joint_far)
    pre_own = gate(pre_own, [], [down_0, up_1], [qv_far])
    up_0 = DpSum(order_d, up_halves(0, order_d, pre_own, got_pre))
    counts_in = gate(counts_in, [up_0], [], [got_mid_t, got_joint])
    joint_own, qv_own = attend_back(saved[0]["own"], att_own, counts_in)
    rest_0 = DpSum(
        order_b,
        weight_grad(
            "qkv_out_grad",
            order_b,
            lefts(0),
            (joint_own, got_joint),
            extras(0, mid_t, got_mid_t),
            tiles=3,
        ),
    )
    gain_in = gate(gain_in, [rest_0], [down_0], [qv_own])
    grad, sums_in = entry_back(0, joint_own, joint_far, grad_mid, gain_in)
    last = gate(sums_in, [], [up_0, down_0, rest_1, up_1])
    small[0] = (sums_mid, last, qv_own, qv_far, upb_own, upb_far)
    ins = [array for arrays in small for array in arrays]
    vector_shape = out(((7 + steps) * LAYERS, width), F32)
    mine, far = call(
        functools.partial(pack_kernel, LAYERS),
        "pack_small",
        (),
        ins,
        [whole()] * len(ins),
        [vector_shape] * 2,
        [whole()] * 2,
    )
    vector = Everywhere(mine, far, bits)
    last = gate(last, [], [rest_0, up_0, down_0, rest_1, vector])
    last = gate(last, [], [rest_0, up_0, rest_1, vector])
    last = gate(last, [], [rest_0, up_0, vector])
    last = gate(last, [], [rest_0, vector])
    running = [down_1, up_1, rest_1, down_0, up_0, rest_0]
    while any(unit.incoming is not None for unit in running):
        last = gate(last, [], [unit for unit in running if unit.incoming is not None][:4])

    (down_1_sum,), (up_1_sum,) = down_1.results(), up_1.results()
    (down_0_sum,), (up_0_sum,) = down_0.results(), up_0.results()
    (both,), (first_both,) = rest_1.results(), rest_0.results()
    summed = [
        (
            first_both[:, : 3 * half].reshape(block, 3, half),
            first_both[:, 3 * half :].T,
            up_0_sum,
            down_0_sum.T,
        ),
        (
            both[:, : 3 * half].reshape(block, 3, half),
            both[:, 3 * half :].T,
            up_1_sum,
            down_1_sum.T,
        ),
    ]

    while vector.bits:
        vector.turn()
    mine, got = vector.mine, vector.incoming
    gain_grads, shift_grads, outb_grads, qv_grads, upb_grads = call(
        functools.partial(unpack_kernel, LAYERS),
        "unpack_small",
        (),
        [mine, got],
        [whole()] * 2,
        [
            out(ln_gain.shape, F32),
            out(ln_bias.shape, F32),
            out(out_bias.shape, F32),
            out(qv_bias.shape, F32),
            out(up_bias.shape, F32),
        ],
        [whole()] * 5,
    )
    stacked = [jnp.stack([summed[layer][member] for layer in range(LAYERS)]) for member in range(4)]
    return (
        stream.reshape(images.shape),
        pooled,
        grad.reshape(images.shape),
        gain_grads,
        shift_grads,
        stacked[0],
        qv_grads,
        stacked[1],
        outb_grads,
        stacked[2],
        upb_grads,
        stacked[3],
    )


def solution(mesh):
    placed = (
        P(("dp", "tensor"), None, None),
        P("dp"),
        P(),
        P(),
        P(None, None, None, "tensor"),
        P(None, None, "tensor"),
        P(None, "tensor", None),
        P(),
        P(None, None, "tensor"),
        P(None, "tensor"),
        P(None, "tensor", None),
        P(("dp", "tensor"), None, None),
    )
    return jax.shard_map(
        shards,
        mesh=mesh,
        in_specs=placed,
        out_specs=(
            P(("dp", "tensor"), None, None),
            P(("dp", "tensor"), None),
            P(("dp", "tensor"), None, None),
            P(),
            P(),
            P(None, "dp", None, "tensor"),
            P(None, None, "tensor"),
            P(None, "tensor", "dp"),
            P(),
            P(None, "dp", "tensor"),
            P(None, "tensor"),
            P(None, "tensor", "dp"),
        ),
        check_vma=False,
    )
```

profile of v0, /device:TPU:0, one launch (start us, length us, event | category | flops | bytes accessed | tf_op | source)
XLA Modules:
  0.0 293.1 jit_solution(16402466127817234718)
XLA Ops:
  2.9 4.0 %prep.1 = (bf16[512,768]{1,0:T(8,128)(2,1)S(1)}, bf16[768,512]{1,0:T(8,128)(2,1)S(1)}, bf16[768,512]{1,0:T(8,128)(2,1)S(1)}, f32[512,768]{1,0:T(8,128)S(1)}) custom-call(bf16[512,768]{1,0:T(8,128)(2,1)S(1)} %bitcast.25, bf16[512,768]{1,0:T(8,128)(2,1)S(1)} %bitcast.28, f32[2,2,768]{2,1,0:T(2,128)S(1)} %copy-done.18, f32[2,2,768]{2,1,0:T(2,128)S(1)} %copy-done.19, ...), custom_call_target="tpu_custom_call" | custom-call | flops 18874368 | bytes 104832 | tf_op jit(solution)/shard_map/prep/pallas_call | solution.py:50
  8.4 14.4 %attend.2 = (bf16[3,512,384]{2,1,0:T(8,128)(2,1)S(1)}, bf16[3,512,384]{2,1,0:T(8,128)(2,1)S(1)}, bf16[512,384]{1,0:T(8,128)(2,1)S(1)}, bf16[512,384]{1,0:T(8,128...) custom-call(s32[1]{0:T(128)} %constant.14.clone.1.which, s32[4]{0:T(128)S(1)} %copy-done.23, ...), custom_call_target="tpu_custom_call" | custom-call | flops 34603008 | bytes 172608 | tf_op jit(solution)/shard_map/attend/pallas_call | solution.py:50
  22.9 1.2 collective-permute-done.5.down_far
  24.1 18.3 %feed.2 = (f32[512,768]{1,0:T(8,128)S(1)}, bf16[768,512]{1,0:T(8,128)(2,1)S(1)}, bf16[512,1536]{1,0:T(8,128)(2,1)}, bf16[512,1536]{1,0:T(8,128)(2,1)}, bf16[512,...) custom-call(s32[4]{0:T(128)S(1)} %copy-done.23, ...), custom_call_target="tpu_custom_call" | custom-call | flops 94371840 | bytes 560064 | tf_op jit(solution)/shard_map/feed/pallas_call | solution.py:50
  44.8 14.4 %attend.3 = (bf16[3,512,384]{2,1,0:T(8,128)(2,1)S(1)}, bf16[3,512,384]{2,1,0:T(8,128)(2,1)S(1)}, bf16[512,384]{1,0:T(8,128)(2,1)S(1)}, bf16[512,384]{1,0:T(8,128...) custom-call(s32[1]{0:T(128)} %constant.36.clone.1.which, s32[4]{0:T(128)S(1)} %copy-done.23, ...), custom_call_target="tpu_custom_call" | custom-call | flops 34603008 | bytes 172608 | tf_op jit(solution)/shard_map/attend/pallas_call | solution.py:50
  59.2 17.4 %feed.3 = (f32[512,768]{1,0:T(8,128)S(1)}, bf16[768,512]{1,0:T(8,128)(2,1)S(1)}, bf16[512,1536]{1,0:T(8,128)(2,1)}, bf16[512,1536]{1,0:T(8,128)(2,1)}, bf16[512,...) custom-call(s32[4]{0:T(128)S(1)} %copy-done.23, ...), custom_call_target="tpu_custom_call" | custom-call | flops 94371840 | bytes 547872 | tf_op jit(solution)/shard_map/feed/pallas_call | solution.py:50
  76.9 3.5 %collective-permute-done.11.refs_3_ = bf16[512,1536]{1,0:T(8,128)(2,1)S(1)} collective-permute-done((bf16[512,1536]{1,0:T(8,128)(2,1)}, bf16[512,1536]{1,0:T(8,128)(2,1)S(1)}, u32[]{:S(2)}, u32[]{:S(2)}) %collective-permute-start.11) | collective-permute-done | bytes 1572896 | tf_op jit(solution)/shard_map/ppermute | solution.py:756
  81.5 4.3 %down_grad.2 = (bf16[384,1536]{1,0:T(8,128)(2,1)S(1)}, bf16[384,1536]{1,0:T(8,128)(2,1)S(1)}) custom-call(bf16[768,512]{1,0:T(8,128)(2,1)S(1)} %copy-done.14, bf16[768,512]{1,0:T(8,128)(2,1)S(1)} %copy-done.16, bf16[512,1536]{1,0:T(8,128)(2,1)} %get-tuple-element.168.refs_2_, bf16[512,1536]{1,0:T(8,128)(2,1)S(1)} %collective-permute-done.11.refs_3_), custom_call_target="tpu_custom_call" | custom-call | flops 37748736 | bytes 110592 | tf_op jit(solution)/shard_map/down_grad/pallas_call | solution.py:50
  85.8 2.7 collective-permute-start.12
  88.5 17.9 %feed_back.2 = (bf16[512,1536]{1,0:T(8,128)(2,1)}, bf16[512,1536]{1,0:T(8,128)(2,1)}, f32[2,768]{1,0:T(2,128)S(1)}, f32[2,768]{1,0:T(2,128)S(1)}, f32[512,768]{1...) custom-call(s32[1]{0:T(128)} %constant.36.clone.1.which, ...), custom_call_target="tpu_custom_call" | custom-call | flops 94371840 | bytes 547392 | tf_op jit(solution)/shard_map/feed_back/pallas_call | solution.py:50
  107.0 5.6 %attend_back.4 = (bf16[3,512,384]{2,1,0:T(8,128)(2,1)S(1)}, f32[1,768]{1,0:T(1,128)S(1)}) custom-call(s32[4]{0:T(128)S(1)} %copy-done.23, bf16[3,512,384]{2,1,0:T(8,128)(2,1)S(1)} %get-tuple-element.172.joint, f32[12,1,256]{2,1,0:T(1,128)S(1)} %get-tuple-element.173.lse, bf16[512,384]{1,0:T(8,128)(2,1)S(1)} %get-tuple-element.179.grad_att), custom_call_target="tpu_custom_call" | custom-call | flops 7864320 | bytes 43248 | tf_op jit(solution)/shard_map/attend_back/pallas_call | solution.py:50
  112.6 2.4 collective-permute-done.12
  115.2 1.8 collective-permute-start.15
  117.5 5.6 %attend_back.5 = (bf16[3,512,384]{2,1,0:T(8,128)(2,1)S(1)}, f32[1,768]{1,0:T(1,128)S(1)}) custom-call(s32[4]{0:T(128)S(1)} %copy-done.23, bf16[3,512,384]{2,1,0:T(8,128)(2,1)S(1)} %get-tuple-element.184.joint, f32[12,1,256]{2,1,0:T(1,128)S(1)} %get-tuple-element.185.lse, bf16[512,384]{1,0:T(8,128)(2,1)S(1)} %get-tuple-element.186.grad_att), custom_call_target="tpu_custom_call" | custom-call | flops 7864320 | bytes 43248 | tf_op jit(solution)/shard_map/attend_back/pallas_call | solution.py:50
  123.1 3.3 %up_grad.2 = (bf16[384,1536]{1,0:T(8,128)(2,1)S(1)}, bf16[384,1536]{1,0:T(8,128)(2,1)S(1)}) custom-call(bf16[768,512]{1,0:T(8,128)(2,1)S(1)} %get-tuple-element.182.refs_0_, bf16[768,512]{1,0:T(8,128)(2,1)S(1)} %collective-permute-done.13.refs_1_, bf16[512,1536]{1,0:T(8,128)(2,1)S(1)} %copy-done.6, bf16[512,1536]{1,0:T(8,128)(2,1)S(1)} %collective-permute-done.14.refs_3_), custom_call_target="tpu_custom_call" | custom-call | flops 37748736 | bytes 110592 | tf_op jit(solution)/shard_map/up_grad/pallas_call | solution.py:50
  126.4 3.8 %collective-permute-done.15 = bf16[192,1536]{1,0:T(8,128)(2,1)S(1)} collective-permute-done((bf16[192,1536]{1,0:T(8,128)(2,1)S(1)}, bf16[192,1536]{1,0:T(8,128)(2,1)S(1)}, u32[]{:S(2)}, u32[]{:S(2)}) %collective-permute-start.15) | collective-permute-done | bytes 589856 | tf_op jit(solution)/shard_map/ppermute | solution.py:715
  130.3 1.5 collective-permute-start.22
  131.9 1.7 collective-permute-start.17
  134.1 9.9 %entry_back.2 = (f32[512,768]{1,0:T(8,128)S(1)}, f32[2,768]{1,0:T(2,128)S(1)}, bf16[768,512]{1,0:T(8,128)(2,1)S(1)}) custom-call(bf16[3,512,384]{2,1,0:T(8,128)(2,1)S(1)} %get-tuple-element.202.joint_own.refs_2_, bf16[3,512,384]{2,1,0:T(8,128)(2,1)S(1)} %get-tuple-element.196.joint_far, bf16[2,3,768,384]{3,2,1,0:T(8,128)(2,1)} %bitcast.32, ...), custom_call_target="tpu_custom_call" | custom-call | flops 28311552 | bytes 252192 | tf_op jit(solution)/shard_map/entry_back/pallas_call | solution.py:50
  144.2 2.7 collective-permute-start.23
  146.9 4.2 %qkv_out_grad.2 = (bf16[384,1536]{1,0:T(8,128)(2,1)S(1)}, bf16[384,1536]{1,0:T(8,128)(2,1)S(1)}) custom-call(bf16[768,512]{1,0:T(8,128)(2,1)S(1)} %copy-done.12, bf16[768,512]{1,0:T(8,128)(2,1)S(1)} %collective-permute-done.16.refs_1_, bf16[3,512,384]{2,1,0:T(8,128)(2,1)S(1)} %get-tuple-element.202.joint_own.refs_2_, ...), custom_call_target="tpu_custom_call" | custom-call | flops 37748736 | bytes 135168 | tf_op jit(solution)/shard_map/qkv_out_grad/pallas_call | solution.py:50
  151.6 4.3 %down_grad.3 = (bf16[384,1536]{1,0:T(8,128)(2,1)S(1)}, bf16[384,1536]{1,0:T(8,128)(2,1)S(1)}) custom-call(bf16[768,512]{1,0:T(8,128)(2,1)S(1)} %get-tuple-element.205.refs_0_, bf16[768,512]{1,0:T(8,128)(2,1)S(1)} %collective-permute-done.21.refs_1_, bf16[512,1536]{1,0:T(8,128)(2,1)} %get-tuple-element.206.refs_2_, ...), custom_call_target="tpu_custom_call" | custom-call | flops 37748736 | bytes 110592 | tf_op jit(solution)/shard_map/down_grad/pallas_call | solution.py:50
  157.2 1.3 collective-permute-start.24
  158.6 1.5 collective-permute-start.26
  160.0 18.1 %feed_back.3 = (bf16[512,1536]{1,0:T(8,128)(2,1)}, bf16[512,1536]{1,0:T(8,128)(2,1)}, f32[2,768]{1,0:T(2,128)S(1)}, f32[2,768]{1,0:T(2,128)S(1)}, f32[512,768]{1...) custom-call(s32[1]{0:T(128)} %constant.14.clone.1.which, ...), custom_call_target="tpu_custom_call" | custom-call | flops 94371840 | bytes 547392 | tf_op jit(solution)/shard_map/feed_back/pallas_call | solution.py:50
  178.3 1.4 collective-permute-done.25
  181.0 5.6 %attend_back.6 = (bf16[3,512,384]{2,1,0:T(8,128)(2,1)S(1)}, f32[1,768]{1,0:T(1,128)S(1)}) custom-call(s32[4]{0:T(128)S(1)} %copy-done.23, bf16[3,512,384]{2,1,0:T(8,128)(2,1)S(1)} %get-tuple-element.224.joint, f32[12,1,256]{2,1,0:T(1,128)S(1)} %get-tuple-element.225.lse, bf16[512,384]{1,0:T(8,128)(2,1)S(1)} %get-tuple-element.226.grad_att), custom_call_target="tpu_custom_call" | custom-call | flops 7864320 | bytes 43248 | tf_op jit(solution)/shard_map/attend_back/pallas_call | solution.py:50
  187.2 2.4 collective-permute-done.27
  189.7 1.6 collective-permute-start.31
  192.5 3.3 %up_grad.3 = (bf16[384,1536]{1,0:T(8,128)(2,1)S(1)}, bf16[384,1536]{1,0:T(8,128)(2,1)S(1)}) custom-call(bf16[768,512]{1,0:T(8,128)(2,1)S(1)} %get-tuple-element.162.refs_0_, bf16[768,512]{1,0:T(8,128)(2,1)S(1)} %collective-permute-done.9.refs_1_, bf16[512,1536]{1,0:T(8,128)(2,1)S(1)} %copy-done.5, bf16[512,1536]{1,0:T(8,128)(2,1)S(1)} %collective-permute-done.28.refs_3_), custom_call_target="tpu_custom_call" | custom-call | flops 37748736 | bytes 110592 | tf_op jit(solution)/shard_map/up_grad/pallas_call | solution.py:50
  197.4 2.1 collective-permute-start.35
  199.5 5.6 %attend_back.7 = (bf16[3,512,384]{2,1,0:T(8,128)(2,1)S(1)}, f32[1,768]{1,0:T(1,128)S(1)}) custom-call(s32[4]{0:T(128)S(1)} %copy-done.23, bf16[3,512,384]{2,1,0:T(8,128)(2,1)S(1)} %get-tuple-element.234.joint, f32[12,1,256]{2,1,0:T(1,128)S(1)} %get-tuple-element.235.lse, bf16[512,384]{1,0:T(8,128)(2,1)S(1)} %get-tuple-element.236.grad_att), custom_call_target="tpu_custom_call" | custom-call | flops 7864320 | bytes 43248 | tf_op jit(solution)/shard_map/attend_back/pallas_call | solution.py:50
  205.1 4.2 %qkv_out_grad.3 = (bf16[384,1536]{1,0:T(8,128)(2,1)S(1)}, bf16[384,1536]{1,0:T(8,128)(2,1)S(1)}) custom-call(bf16[768,512]{1,0:T(8,128)(2,1)S(1)} %copy-done.8, bf16[768,512]{1,0:T(8,128)(2,1)S(1)} %copy-done.10, bf16[3,512,384]{2,1,0:T(8,128)(2,1)S(1)} %get-tuple-element.237.refs_2_.joint_own, bf16[3,512,384]{2,1,0:T(8,128)(2,1)S(1)} %collective-permute-done.30.refs_3_, ...), custom_call_target="tpu_custom_call" | custom-call | flops 37748736 | bytes 135168 | tf_op jit(solution)/shard_map/qkv_out_grad/pallas_call | solution.py:50
  212.0 9.8 %entry_back.3 = (f32[512,768]{1,0:T(8,128)}, f32[2,768]{1,0:T(2,128)S(1)}) custom-call(bf16[3,512,384]{2,1,0:T(8,128)(2,1)S(1)} %get-tuple-element.237.refs_2_.joint_own, bf16[3,512,384]{2,1,0:T(8,128)(2,1)S(1)} %get-tuple-element.232.joint_far, bf16[2,3,768,384]{3,2,1,0:T(8,128)(2,1)} %bitcast.33, bf16[2,3,768,384]{3,2,1,0:T(8,128)(2,1)} %collective-permute-done.weight_far, ...), custom_call_target="tpu_custom_call" | custom-call | flops 28311552 | bytes 227616 | tf_op jit(solution)/shard_map/entry_back/pallas_call | solution.py:50
  222.7 2.6 collective-permute-done.35
  225.3 6.2 %collective-permute-done.33 = bf16[96,1536]{1,0:T(8,128)(2,1)S(1)} collective-permute-done((bf16[96,1536]{1,0:T(8,128)(2,1)S(1)}, bf16[96,1536]{1,0:T(8,128)(2,1)S(1)}, u32[]{:S(2)}, u32[]{:S(2)}) %collective-permute-start.33) | collective-permute-done | bytes 294944 | tf_op jit(solution)/shard_map/ppermute | solution.py:715
  231.9 3.5 %collective-permute-start.38 = (bf16[48,1536]{1,0:T(8,128)(2,1)S(1)}, bf16[48,1536]{1,0:T(8,128)(2,1)S(1)}, u32[]{:S(2)}, u32[]{:S(2)}) collective-permute-start(bf16[48,1536]{1,0:T(8,128)(2,1)S(1)} %add_convert_fusion.15), channel_id=1, source_target_pairs={{0,16},{2,18},{4,20},{6,22},{8,24},{10,26},{12,28},{14,30},{16,0},... | collective-permute-start | bytes 442376 | tf_op jit(solution)/shard_map/ppermute | solution.py:715
  237.9 10.1 %collective-permute-done.38 = bf16[48,1536]{1,0:T(8,128)(2,1)S(1)} collective-permute-done((bf16[48,1536]{1,0:T(8,128)(2,1)S(1)}, bf16[48,1536]{1,0:T(8,128)(2,1)S(1)}, u32[]{:S(2)}, u32[]{:S(2)}) %collective-permute-start.38) | collective-permute-done | bytes 147488 | tf_op jit(solution)/shard_map/ppermute | solution.py:715
  248.0 2.2 collective-permute-done.37
  251.1 1.3 collective-permute-start.42
  253.4 1.6 collective-permute-start.44
  256.0 10.4 %collective-permute-done.44 = f32[18,768]{1,0:T(8,128)S(1)} collective-permute-done((f32[18,768]{1,0:T(8,128)S(1)}, f32[18,768]{1,0:T(8,128)S(1)}, u32[]{:S(2)}, u32[]{:S(2)}) %collective-permute-start.44) | collective-permute-done | bytes 55328 | tf_op jit(solution)/shard_map/ppermute | solution.py:740
  267.4 2.1 collective-permute-start.45
  274.1 2.3 collective-permute-done.47
  277.5 1.9 collective-permute-start.48
  280.6 1.2 add_bitcast_fusion.3
  283.8 1.4 collective-permute-done.48
  288.5 4.0 %collective-permute-done.50.got = f32[18,768]{1,0:T(8,128)S(1)} collective-permute-done((f32[18,768]{1,0:T(8,128)S(1)}, f32[18,768]{1,0:T(8,128)S(1)}, u32[]{:S(2)}, u32[]{:S(2)}) %collective-permute-start.50) | collective-permute-done | bytes 55328 | tf_op jit(solution)/shard_map/ppermute | solution.py:740
  (191 shorter events, 39.2 us)
Async XLA Ops:
  0.7 6.7 %collective-permute-start = (bf16[2,3,768,384]{3,2,1,0:T(8,128)(2,1)}, bf16[2,3,768,384]{3,2,1,0:T(8,128)(2,1)}, u32[]{:S(2)}, u32[]{:S(2)}) collective-permute-start(bf16[2,3,768,384]{3,2,1,0:T(8,128)(2,1)} %bitcast.29), channel_id=1, source_target_pairs={{0,1},{1,0},{2,3},{3,2},{4,5},{5,4},{6,7},{7,6},{8,9},{9,8},{10,11... | collective-permute-start | bytes 10616840 | tf_op jit(solution)/shard_map/ppermute | solution.py:756
  1.2 5.8 %collective-permute-start.1 = (f32[2,2,384]{2,1,0:T(2,128)}, f32[2,2,384]{2,1,0:T(2,128)S(1)}, u32[]{:S(2)}, u32[]{:S(2)}) collective-permute-start(f32[2,2,384]{2,1,0:T(2,128)} %bias_own.3), channel_id=1, source_target_pairs={{0,1},{1,0},{2,3},{3,2},{4,5},{5,4},{6,7},{7,6},{8,9},{9,8},{10,11... | collective-permute-start | bytes 18440 | tf_op jit(solution)/shard_map/ppermute | solution.py:756
  7.4 15.4 %collective-permute-start.3 = (bf16[2,768,1536]{2,1,0:T(8,128)(2,1)}, bf16[2,768,1536]{2,1,0:T(8,128)(2,1)}, u32[]{:S(2)}, u32[]{:S(2)}) collective-permute-start(bf16[2,768,1536]{2,1,0:T(8,128)(2,1)} %up_own.7), channel_id=1, source_target_pairs={{0,1},{1,0},{2,3},{3,2},{4,5},{5,4},{6,7},{7,6},{8,9},{9,8},{10,11... | collective-permute-start | bytes 14155784 | tf_op jit(solution)/shard_map/ppermute | solution.py:756
  7.8 16.3 %collective-permute-start.5 = (bf16[2,1536,768]{2,1,0:T(8,128)(2,1)}, bf16[2,1536,768]{2,1,0:T(8,128)(2,1)}, u32[]{:S(2)}, u32[]{:S(2)}) collective-permute-start(bf16[2,1536,768]{2,1,0:T(8,128)(2,1)} %down_own.7), channel_id=1, source_target_pairs={{0,1},{1,0},{2,3},{3,2},{4,5},{5,4},{6,7},{7,6},{8,9},{9,8},{10,11... | collective-permute-start | bytes 14155784 | tf_op jit(solution)/shard_map/ppermute | solution.py:756
  7.9 14.9 %collective-permute-start.2 = (bf16[2,384,768]{2,1,0:T(8,128)(2,1)S(1)}, bf16[2,384,768]{2,1,0:T(8,128)(2,1)S(1)}, u32[]{:S(2)}, u32[]{:S(2)}) collective-permute-start(bf16[2,384,768]{2,1,0:T(8,128)(2,1)S(1)} %copy-done.27), channel_id=1, source_target_pairs={{0,1},{1,0},{2,3},{3,2},{4,5},{5,4},{6,7},{7,6},{8,9},{9,8},{10,11... | collective-permute-start | bytes 3538952 | tf_op jit(solution)/shard_map/ppermute | solution.py:756
  8.3 14.5 %collective-permute-start.4 = (f32[2,1536]{1,0:T(2,128)S(1)}, f32[2,1536]{1,0:T(2,128)S(1)}, u32[]{:S(2)}, u32[]{:S(2)}) collective-permute-start(f32[2,1536]{1,0:T(2,128)S(1)} %copy-done.22), channel_id=1, source_target_pairs={{0,1},{1,0},{2,3},{3,2},{4,5},{5,4},{6,7},{7,6},{8,9},{9,8},{10,11... | collective-permute-start | bytes 36872 | tf_op jit(solution)/shard_map/ppermute | solution.py:756
  43.4 15.8 %collective-permute-start.10 = (bf16[512,1536]{1,0:T(8,128)(2,1)}, bf16[512,1536]{1,0:T(8,128)(2,1)S(1)}, u32[]{:S(2)}, u32[]{:S(2)}) collective-permute-start(bf16[512,1536]{1,0:T(8,128)(2,1)} %get-tuple-element.163), channel_id=1, source_target_pairs={{0,1},{1,0},{2,3},{3,2},{4,5},{5,4},{6,7},{7,6},{8,9},{9,8},{10,11... | collective-permute-start | bytes 4718600 | tf_op jit(solution)/shard_map/ppermute | solution.py:756
  43.8 15.4 %collective-permute-start.6 = (bf16[768,512]{1,0:T(8,128)(2,1)S(1)}, bf16[768,512]{1,0:T(8,128)(2,1)S(1)}, u32[]{:S(2)}, u32[]{:S(2)}) collective-permute-start(bf16[768,512]{1,0:T(8,128)(2,1)S(1)} %get-tuple-element.160.refs_0_), channel_id=1, source_target_pairs={{0,1},{1,0},{2,3},{3,2},{4,5},{5,4},{6,7},{7,6},{8,9},{9,8},{10,11... | collective-permute-start | bytes 2359304 | tf_op jit(solution)/shard_map/ppermute | solution.py:756
  43.9 15.3 %collective-permute-start.7 = (bf16[768,512]{1,0:T(8,128)(2,1)S(1)}, bf16[768,512]{1,0:T(8,128)(2,1)S(1)}, u32[]{:S(2)}, u32[]{:S(2)}) collective-permute-start(bf16[768,512]{1,0:T(8,128)(2,1)S(1)} %get-tuple-element.161.refs_0_), channel_id=1, source_target_pairs={{0,1},{1,0},{2,3},{3,2},{4,5},{5,4},{6,7},{7,6},{8,9},{9,8},{10,11... | collective-permute-start | bytes 2359304 | tf_op jit(solution)/shard_map/ppermute | solution.py:756
  44.3 14.9 %collective-permute-start.9 = (bf16[768,512]{1,0:T(8,128)(2,1)S(1)}, bf16[768,512]{1,0:T(8,128)(2,1)S(1)}, u32[]{:S(2)}, u32[]{:S(2)}) collective-permute-start(bf16[768,512]{1,0:T(8,128)(2,1)S(1)} %get-tuple-element.162.refs_0_), channel_id=1, source_target_pairs={{0,1},{1,0},{2,3},{3,2},{4,5},{5,4},{6,7},{7,6},{8,9},{9,8},{10,11... | collective-permute-start | bytes 2359304 | tf_op jit(solution)/shard_map/ppermute | solution.py:756
  44.4 14.8 %collective-permute-start.8 = (bf16[512,384]{1,0:T(8,128)(2,1)S(1)}, bf16[512,384]{1,0:T(8,128)(2,1)S(1)}, u32[]{:S(2)}, u32[]{:S(2)}) collective-permute-start(bf16[512,384]{1,0:T(8,128)(2,1)S(1)} %get-tuple-element.152.att_far), channel_id=1, source_target_pairs={{0,1},{1,0},{2,3},{3,2},{4,5},{5,4},{6,7},{7,6},{8,9},{9,8},{10,11... | collective-permute-start | bytes 1179656 | tf_op jit(solution)/shard_map/ppermute | solution.py:756
  85.8 29.2 %collective-permute-start.12 = (bf16[384,1536]{1,0:T(8,128)(2,1)S(1)}, bf16[384,1536]{1,0:T(8,128)(2,1)S(1)}, u32[]{:S(2)}, u32[]{:S(2)}) collective-permute-start(bf16[384,1536]{1,0:T(8,128)(2,1)S(1)} %get-tuple-element.171), channel_id=1, source_target_pairs={{0,2},{2,0},{4,6},{6,4},{8,10},{10,8},{12,14},{14,12},{16,18},{18,... | collective-permute-start | bytes 3538952 | tf_op jit(solution)/shard_map/ppermute | solution.py:715
  106.5 16.6 %collective-permute-start.14 = (bf16[512,1536]{1,0:T(8,128)(2,1)}, bf16[512,1536]{1,0:T(8,128)(2,1)S(1)}, u32[]{:S(2)}, u32[]{:S(2)}) collective-permute-start(bf16[512,1536]{1,0:T(8,128)(2,1)} %get-tuple-element.189), channel_id=1, source_target_pairs={{0,1},{1,0},{2,3},{3,2},{4,5},{5,4},{6,7},{7,6},{8,9},{9,8},{10,11... | collective-permute-start | bytes 4718600 | tf_op jit(solution)/shard_map/ppermute | solution.py:756
  106.6 16.5 %collective-permute-start.13 = (bf16[768,512]{1,0:T(8,128)(2,1)S(1)}, bf16[768,512]{1,0:T(8,128)(2,1)S(1)}, u32[]{:S(2)}, u32[]{:S(2)}) collective-permute-start(bf16[768,512]{1,0:T(8,128)(2,1)S(1)} %get-tuple-element.182.refs_0_), channel_id=1, source_target_pairs={{0,1},{1,0},{2,3},{3,2},{4,5},{5,4},{6,7},{7,6},{8,9},{9,8},{10,11... | collective-permute-start | bytes 2359304 | tf_op jit(solution)/shard_map/ppermute | solution.py:756
  115.2 15.1 %collective-permute-start.15 = (bf16[192,1536]{1,0:T(8,128)(2,1)S(1)}, bf16[192,1536]{1,0:T(8,128)(2,1)S(1)}, u32[]{:S(2)}, u32[]{:S(2)}) collective-permute-start(bf16[192,1536]{1,0:T(8,128)(2,1)S(1)} %add_convert_fusion.5), channel_id=1, source_target_pairs={{0,4},{2,6},{4,0},{6,2},{8,12},{10,14},{12,8},{14,10},{16,20},{18,... | collective-permute-start | bytes 1769480 | tf_op jit(solution)/shard_map/ppermute | solution.py:715
  117.0 16.5 %collective-permute-start.20 = (bf16[512,384]{1,0:T(8,128)(2,1)S(1)}, bf16[512,384]{1,0:T(8,128)(2,1)S(1)}, u32[]{:S(2)}, u32[]{:S(2)}) collective-permute-start(bf16[512,384]{1,0:T(8,128)(2,1)S(1)} %get-tuple-element.159.att_far), channel_id=1, source_target_pairs={{0,1},{1,0},{2,3},{3,2},{4,5},{5,4},{6,7},{7,6},{8,9},{9,8},{10,11... | collective-permute-start | bytes 1179656 | tf_op jit(solution)/shard_map/ppermute | solution.py:756
  117.0 29.8 %collective-permute-start.18 = (bf16[3,512,384]{2,1,0:T(8,128)(2,1)S(1)}, bf16[3,512,384]{2,1,0:T(8,128)(2,1)S(1)}, u32[]{:S(2)}, u32[]{:S(2)}) collective-permute-start(bf16[3,512,384]{2,1,0:T(8,128)(2,1)S(1)} %get-tuple-element.196.joint_far), channel_id=1, source_target_pairs={{0,1},{1,0},{2,3},{3,2},{4,5},{5,4},{6,7},{7,6},{8,9},{9,8},{10,11... | collective-permute-start | bytes 3538952 | tf_op jit(solution)/shard_map/ppermute | solution.py:756
  130.3 26.8 %collective-permute-start.22 = (bf16[384,1536]{1,0:T(8,128)(2,1)S(1)}, bf16[384,1536]{1,0:T(8,128)(2,1)S(1)}, u32[]{:S(2)}, u32[]{:S(2)}) collective-permute-start(bf16[384,1536]{1,0:T(8,128)(2,1)S(1)} %get-tuple-element.209), channel_id=1, source_target_pairs={{0,2},{2,0},{4,6},{6,4},{8,10},{10,8},{12,14},{14,12},{16,18},{18,... | collective-permute-start | bytes 3538952 | tf_op jit(solution)/shard_map/ppermute | solution.py:715
  131.9 12.1 %collective-permute-start.17 = (bf16[96,1536]{1,0:T(8,128)(2,1)S(1)}, bf16[96,1536]{1,0:T(8,128)(2,1)S(1)}, u32[]{:S(2)}, u32[]{:S(2)}) collective-permute-start(bf16[96,1536]{1,0:T(8,128)(2,1)S(1)} %add_convert_fusion.11), channel_id=1, source_target_pairs={{0,8},{2,10},{4,12},{6,14},{8,0},{10,2},{12,4},{14,6},{16,24},{18,... | collective-permute-start | bytes 884744 | tf_op jit(solution)/shard_map/ppermute | solution.py:715
  133.5 10.6 %collective-permute-start.16 = (bf16[768,512]{1,0:T(8,128)(2,1)S(1)}, bf16[768,512]{1,0:T(8,128)(2,1)S(1)}, u32[]{:S(2)}, u32[]{:S(2)}) collective-permute-start(bf16[768,512]{1,0:T(8,128)(2,1)S(1)} %copy-done.12), channel_id=1, source_target_pairs={{0,1},{1,0},{2,3},{3,2},{4,5},{5,4},{6,7},{7,6},{8,9},{9,8},{10,11... | collective-permute-start | bytes 2359304 | tf_op jit(solution)/shard_map/ppermute | solution.py:756
  133.6 13.3 %collective-permute-start.19 = (bf16[768,512]{1,0:T(8,128)(2,1)S(1)}, bf16[768,512]{1,0:T(8,128)(2,1)S(1)}, u32[]{:S(2)}, u32[]{:S(2)}) collective-permute-start(bf16[768,512]{1,0:T(8,128)(2,1)S(1)} %get-tuple-element.203.refs_4_), channel_id=1, source_target_pairs={{0,1},{1,0},{2,3},{3,2},{4,5},{5,4},{6,7},{7,6},{8,9},{9,8},{10,11... | collective-permute-start | bytes 2359304 | tf_op jit(solution)/shard_map/ppermute | solution.py:756
  144.0 7.6 %collective-permute-start.21 = (bf16[768,512]{1,0:T(8,128)(2,1)S(1)}, bf16[768,512]{1,0:T(8,128)(2,1)S(1)}, u32[]{:S(2)}, u32[]{:S(2)}) collective-permute-start(bf16[768,512]{1,0:T(8,128)(2,1)S(1)} %get-tuple-element.205.refs_0_), channel_id=1, source_target_pairs={{0,1},{1,0},{2,3},{3,2},{4,5},{5,4},{6,7},{7,6},{8,9},{9,8},{10,11... | collective-permute-start | bytes 2359304 | tf_op jit(solution)/shard_map/ppermute | solution.py:756
  144.2 11.7 %collective-permute-start.23 = (bf16[48,1536]{1,0:T(8,128)(2,1)S(1)}, bf16[48,1536]{1,0:T(8,128)(2,1)S(1)}, u32[]{:S(2)}, u32[]{:S(2)}) collective-permute-start(bf16[48,1536]{1,0:T(8,128)(2,1)S(1)} %add_convert_fusion.17), channel_id=1, source_target_pairs={{0,16},{2,18},{4,20},{6,22},{8,24},{10,26},{12,28},{14,30},{16,0},... | collective-permute-start | bytes 442376 | tf_op jit(solution)/shard_map/ppermute | solution.py:715
  151.1 28.6 %collective-permute-start.25 = (bf16[384,1536]{1,0:T(8,128)(2,1)S(1)}, bf16[384,1536]{1,0:T(8,128)(2,1)S(1)}, u32[]{:S(2)}, u32[]{:S(2)}) collective-permute-start(bf16[384,1536]{1,0:T(8,128)(2,1)S(1)} %get-tuple-element.212), channel_id=1, source_target_pairs={{0,8},{2,10},{4,12},{6,14},{8,0},{10,2},{12,4},{14,6},{16,24},{18,... | collective-permute-start | bytes 3538952 | tf_op jit(solution)/shard_map/ppermute | solution.py:715
  157.2 22.5 %collective-permute-start.24 = (bf16[192,1536]{1,0:T(8,128)(2,1)S(1)}, bf16[192,1536]{1,0:T(8,128)(2,1)S(1)}, u32[]{:S(2)}, u32[]{:S(2)}) collective-permute-start(bf16[192,1536]{1,0:T(8,128)(2,1)S(1)} %add_convert_fusion.4), channel_id=1, source_target_pairs={{0,4},{2,6},{4,0},{6,2},{8,12},{10,14},{12,8},{14,10},{16,20},{18,... | collective-permute-start | bytes 1769480 | tf_op jit(solution)/shard_map/ppermute | solution.py:715
  158.6 31.0 %collective-permute-start.26 = (bf16[384,1536]{1,0:T(8,128)(2,1)S(1)}, bf16[384,1536]{1,0:T(8,128)(2,1)S(1)}, u32[]{:S(2)}, u32[]{:S(2)}) collective-permute-start(bf16[384,1536]{1,0:T(8,128)(2,1)S(1)} %get-tuple-element.222), channel_id=1, source_target_pairs={{0,2},{2,0},{4,6},{6,4},{8,10},{10,8},{12,14},{14,12},{16,18},{18,... | collective-permute-start | bytes 3538952 | tf_op jit(solution)/shard_map/ppermute | solution.py:715
  178.2 14.3 %collective-permute-start.28 = (bf16[512,1536]{1,0:T(8,128)(2,1)}, bf16[512,1536]{1,0:T(8,128)(2,1)S(1)}, u32[]{:S(2)}, u32[]{:S(2)}) collective-permute-start(bf16[512,1536]{1,0:T(8,128)(2,1)} %get-tuple-element.229), channel_id=1, source_target_pairs={{0,1},{1,0},{2,3},{3,2},{4,5},{5,4},{6,7},{7,6},{8,9},{9,8},{10,11... | collective-permute-start | bytes 4718600 | tf_op jit(solution)/shard_map/ppermute | solution.py:756
  180.8 8.8 %collective-permute-start.27 = (bf16[96,1536]{1,0:T(8,128)(2,1)S(1)}, bf16[96,1536]{1,0:T(8,128)(2,1)S(1)}, u32[]{:S(2)}, u32[]{:S(2)}) collective-permute-start(bf16[96,1536]{1,0:T(8,128)(2,1)S(1)} %add_convert_fusion.10), channel_id=1, source_target_pairs={{0,8},{2,10},{4,12},{6,14},{8,0},{10,2},{12,4},{14,6},{16,24},{18,... | collective-permute-start | bytes 884744 | tf_op jit(solution)/shard_map/ppermute | solution.py:715
  186.6 9.2 %collective-permute-start.30 = (bf16[3,512,384]{2,1,0:T(8,128)(2,1)S(1)}, bf16[3,512,384]{2,1,0:T(8,128)(2,1)S(1)}, u32[]{:S(2)}, u32[]{:S(2)}) collective-permute-start(bf16[3,512,384]{2,1,0:T(8,128)(2,1)S(1)} %get-tuple-element.232.joint_far), channel_id=1, source_target_pairs={{0,1},{1,0},{2,3},{3,2},{4,5},{5,4},{6,7},{7,6},{8,9},{9,8},{10,11... | collective-permute-start | bytes 3538952 | tf_op jit(solution)/shard_map/ppermute | solution.py:756
  186.9 8.9 %collective-permute-start.29 = (bf16[768,512]{1,0:T(8,128)(2,1)S(1)}, bf16[768,512]{1,0:T(8,128)(2,1)S(1)}, u32[]{:S(2)}, u32[]{:S(2)}) collective-permute-start(bf16[768,512]{1,0:T(8,128)(2,1)S(1)} %get-tuple-element.231.refs_4_), channel_id=1, source_target_pairs={{0,1},{1,0},{2,3},{3,2},{4,5},{5,4},{6,7},{7,6},{8,9},{9,8},{10,11... | collective-permute-start | bytes 2359304 | tf_op jit(solution)/shard_map/ppermute | solution.py:756
  189.7 19.6 %collective-permute-start.31 = (bf16[192,1536]{1,0:T(8,128)(2,1)S(1)}, bf16[192,1536]{1,0:T(8,128)(2,1)S(1)}, u32[]{:S(2)}, u32[]{:S(2)}) collective-permute-start(bf16[192,1536]{1,0:T(8,128)(2,1)S(1)} %add_convert_fusion.3), channel_id=1, source_target_pairs={{0,4},{2,6},{4,0},{6,2},{8,12},{10,14},{12,8},{14,10},{16,20},{18,... | collective-permute-start | bytes 1769480 | tf_op jit(solution)/shard_map/ppermute | solution.py:715
  191.4 31.3 %collective-permute-start.34 = (bf16[192,1536]{1,0:T(8,128)(2,1)S(1)}, bf16[192,1536]{1,0:T(8,128)(2,1)S(1)}, u32[]{:S(2)}, u32[]{:S(2)}) collective-permute-start(bf16[192,1536]{1,0:T(8,128)(2,1)S(1)} %add_convert_fusion.2), channel_id=1, source_target_pairs={{0,16},{2,18},{4,20},{6,22},{8,24},{10,26},{12,28},{14,30},{16,0},... | collective-permute-start | bytes 1769480 | tf_op jit(solution)/shard_map/ppermute | solution.py:715
  195.8 35.7 %collective-permute-start.32 = (bf16[384,1536]{1,0:T(8,128)(2,1)S(1)}, bf16[384,1536]{1,0:T(8,128)(2,1)S(1)}, u32[]{:S(2)}, u32[]{:S(2)}) collective-permute-start(bf16[384,1536]{1,0:T(8,128)(2,1)S(1)} %get-tuple-element.248), channel_id=1, source_target_pairs={{0,2},{2,0},{4,6},{6,4},{8,10},{10,8},{12,14},{14,12},{16,18},{18,... | collective-permute-start | bytes 3538952 | tf_op jit(solution)/shard_map/ppermute | solution.py:715
  197.4 27.9 %collective-permute-start.35 = (bf16[48,1536]{1,0:T(8,128)(2,1)S(1)}, bf16[48,1536]{1,0:T(8,128)(2,1)S(1)}, u32[]{:S(2)}, u32[]{:S(2)}) collective-permute-start(bf16[48,1536]{1,0:T(8,128)(2,1)S(1)} %add_convert_fusion.16), channel_id=1, source_target_pairs={{0,16},{2,18},{4,20},{6,22},{8,24},{10,26},{12,28},{14,30},{16,0},... | collective-permute-start | bytes 442376 | tf_op jit(solution)/shard_map/ppermute | solution.py:715
  209.5 22.0 %collective-permute-start.33 = (bf16[96,1536]{1,0:T(8,128)(2,1)S(1)}, bf16[96,1536]{1,0:T(8,128)(2,1)S(1)}, u32[]{:S(2)}, u32[]{:S(2)}) collective-permute-start(bf16[96,1536]{1,0:T(8,128)(2,1)S(1)} %add_convert_fusion.9), channel_id=1, source_target_pairs={{0,8},{2,10},{4,12},{6,14},{8,0},{10,2},{12,4},{14,6},{16,24},{18,... | collective-permute-start | bytes 884744 | tf_op jit(solution)/shard_map/ppermute | solution.py:715
  211.0 26.9 %collective-permute-start.36 = (bf16[384,1536]{1,0:T(8,128)(2,1)S(1)}, bf16[384,1536]{1,0:T(8,128)(2,1)S(1)}, u32[]{:S(2)}, u32[]{:S(2)}) collective-permute-start(bf16[384,1536]{1,0:T(8,128)(2,1)S(1)} %get-tuple-element.260), channel_id=1, source_target_pairs={{0,4},{2,6},{4,0},{6,2},{8,12},{10,14},{12,8},{14,10},{16,20},{18,... | collective-permute-start | bytes 3538952 | tf_op jit(solution)/shard_map/ppermute | solution.py:715
  231.7 18.5 %collective-permute-start.37 = (bf16[192,1536]{1,0:T(8,128)(2,1)S(1)}, bf16[192,1536]{1,0:T(8,128)(2,1)S(1)}, u32[]{:S(2)}, u32[]{:S(2)}) collective-permute-start(bf16[192,1536]{1,0:T(8,128)(2,1)S(1)} %add_convert_fusion.1), channel_id=1, source_target_pairs={{0,8},{2,10},{4,12},{6,14},{8,0},{10,2},{12,4},{14,6},{16,24},{18,... | collective-permute-start | bytes 1769480 | tf_op jit(solution)/shard_map/ppermute | solution.py:715
  231.9 16.1 %collective-permute-start.38 = (bf16[48,1536]{1,0:T(8,128)(2,1)S(1)}, bf16[48,1536]{1,0:T(8,128)(2,1)S(1)}, u32[]{:S(2)}, u32[]{:S(2)}) collective-permute-start(bf16[48,1536]{1,0:T(8,128)(2,1)S(1)} %add_convert_fusion.15), channel_id=1, source_target_pairs={{0,16},{2,18},{4,20},{6,22},{8,24},{10,26},{12,28},{14,30},{16,0},... | collective-permute-start | bytes 442376 | tf_op jit(solution)/shard_map/ppermute | solution.py:715
  235.5 12.5 %collective-permute-start.39 = (bf16[96,1536]{1,0:T(8,128)(2,1)S(1)}, bf16[96,1536]{1,0:T(8,128)(2,1)S(1)}, u32[]{:S(2)}, u32[]{:S(2)}) collective-permute-start(bf16[96,1536]{1,0:T(8,128)(2,1)S(1)} %add_convert_fusion.8), channel_id=1, source_target_pairs={{0,2},{2,0},{4,6},{6,4},{8,10},{10,8},{12,14},{14,12},{16,18},{18,... | collective-permute-start | bytes 884744 | tf_op jit(solution)/shard_map/ppermute | solution.py:715
  250.3 16.1 %collective-permute-start.41 = (bf16[192,1536]{1,0:T(8,128)(2,1)S(1)}, bf16[192,1536]{1,0:T(8,128)(2,1)S(1)}, u32[]{:S(2)}, u32[]{:S(2)}) collective-permute-start(bf16[192,1536]{1,0:T(8,128)(2,1)S(1)} %add_convert_fusion), channel_id=1, source_target_pairs={{0,2},{2,0},{4,6},{6,4},{8,10},{10,8},{12,14},{14,12},{16,18},{18,... | collective-permute-start | bytes 1769480 | tf_op jit(solution)/shard_map/ppermute | solution.py:715
  251.1 15.3 %collective-permute-start.42 = (bf16[96,1536]{1,0:T(8,128)(2,1)S(1)}, bf16[96,1536]{1,0:T(8,128)(2,1)S(1)}, u32[]{:S(2)}, u32[]{:S(2)}) collective-permute-start(bf16[96,1536]{1,0:T(8,128)(2,1)S(1)} %add_convert_fusion.7), channel_id=1, source_target_pairs={{0,16},{2,18},{4,20},{6,22},{8,24},{10,26},{12,28},{14,30},{16,0},... | collective-permute-start | bytes 884744 | tf_op jit(solution)/shard_map/ppermute | solution.py:715
  252.4 13.9 %collective-permute-start.43 = (bf16[48,1536]{1,0:T(8,128)(2,1)S(1)}, bf16[48,1536]{1,0:T(8,128)(2,1)S(1)}, u32[]{:S(2)}, u32[]{:S(2)}) collective-permute-start(bf16[48,1536]{1,0:T(8,128)(2,1)S(1)} %add_convert_fusion.14), channel_id=1, source_target_pairs={{0,4},{2,6},{4,0},{6,2},{8,12},{10,14},{12,8},{14,10},{16,20},{18,... | collective-permute-start | bytes 442376 | tf_op jit(solution)/shard_map/ppermute | solution.py:715
  253.4 12.9 %collective-permute-start.44 = (f32[18,768]{1,0:T(8,128)S(1)}, f32[18,768]{1,0:T(8,128)S(1)}, u32[]{:S(2)}, u32[]{:S(2)}) collective-permute-start(f32[18,768]{1,0:T(8,128)S(1)} %add.238), channel_id=1, source_target_pairs={{0,2},{2,0},{4,6},{6,4},{8,10},{10,8},{12,14},{14,12},{16,18},{18,... | collective-permute-start | bytes 165896 | tf_op jit(solution)/shard_map/ppermute | solution.py:740
  267.4 9.0 %collective-permute-start.45 = (bf16[96,1536]{1,0:T(8,128)(2,1)}, bf16[96,1536]{1,0:T(8,128)(2,1)}, u32[]{:S(2)}, u32[]{:S(2)}) collective-permute-start(bf16[96,1536]{1,0:T(8,128)(2,1)} %add_convert_fusion.6), channel_id=1, source_target_pairs={{0,8},{2,10},{4,12},{6,14},{8,0},{10,2},{12,4},{14,6},{16,24},{18,... | collective-permute-start | bytes 884744 | tf_op jit(solution)/shard_map/ppermute | solution.py:715
  270.2 6.1 %collective-permute-start.46 = (bf16[48,1536]{1,0:T(8,128)(2,1)}, bf16[48,1536]{1,0:T(8,128)(2,1)}, u32[]{:S(2)}, u32[]{:S(2)}) collective-permute-start(bf16[48,1536]{1,0:T(8,128)(2,1)} %add_convert_fusion.13), channel_id=1, source_target_pairs={{0,4},{2,6},{4,0},{6,2},{8,12},{10,14},{12,8},{14,10},{16,20},{18,... | collective-permute-start | bytes 442376 | tf_op jit(solution)/shard_map/ppermute | solution.py:715
  271.4 5.0 %collective-permute-start.47 = (f32[18,768]{1,0:T(8,128)S(1)}, f32[18,768]{1,0:T(8,128)S(1)}, u32[]{:S(2)}, u32[]{:S(2)}) collective-permute-start(f32[18,768]{1,0:T(8,128)S(1)} %add.245), channel_id=1, source_target_pairs={{0,4},{2,6},{4,0},{6,2},{8,12},{10,14},{12,8},{14,10},{16,20},{18,... | collective-permute-start | bytes 165896 | tf_op jit(solution)/shard_map/ppermute | solution.py:740
  277.5 7.7 %collective-permute-start.48 = (bf16[48,1536]{1,0:T(8,128)(2,1)S(1)}, bf16[48,1536]{1,0:T(8,128)(2,1)S(1)}, u32[]{:S(2)}, u32[]{:S(2)}) collective-permute-start(bf16[48,1536]{1,0:T(8,128)(2,1)S(1)} %add_convert_fusion.12), channel_id=1, source_target_pairs={{0,16},{2,18},{4,20},{6,22},{8,24},{10,26},{12,28},{14,30},{16,0},... | collective-permute-start | bytes 442376 | tf_op jit(solution)/shard_map/ppermute | solution.py:715
  286.4 6.1 %collective-permute-start.50 = (f32[18,768]{1,0:T(8,128)S(1)}, f32[18,768]{1,0:T(8,128)S(1)}, u32[]{:S(2)}, u32[]{:S(2)}) collective-permute-start(f32[18,768]{1,0:T(8,128)S(1)} %add.255.mine), channel_id=1, source_target_pairs={{0,16},{2,18},{4,20},{6,22},{8,24},{10,26},{12,28},{14,30},{16,0},... | collective-permute-start | bytes 165896 | tf_op jit(solution)/shard_map/ppermute | solution.py:740
  (41 other events, 420.0 us)
where the time goes:
time: 294 us; the launch traced here: 293 us
  Pallas kernels  171 us (58%)
  waiting for transfers between devices  58.1 us (20%)
  starting transfers between devices  42.7 us (15%)
  other arithmetic  13.9 us (5%)
  local copies, waits for them, and re-layouts  6.16 us (2%)
    pallas_call x21, Pallas kernels, call(): pl.pallas_call(body, name=name, grid=grid, in_specs=in_specs, out_specs=o...  171 us
    ppermute x24, waiting for transfers between devices, start(): self.incoming = lax.ppermute(self.outgoing, 'dp', flip(self.order.pop(0)))  35.3 us
    ppermute x24, starting transfers between devices, start(): self.incoming = lax.ppermute(self.outgoing, 'dp', flip(self.order.pop(0)))  33 us
    ppermute x4, waiting for transfers between devices, turn(): self.incoming = lax.ppermute(self.mine, 'dp', flip(self.bits.pop(0)))  17.7 us
    convert_element_type x18, other arithmetic, halve(): sum((part[rows:].astype(F32) for part in parts)).astype(BF16)  6.46 us
  transfers between devices with their start and end apart: 51, of which 19 were waited for; matrix products, arithmetic and copies ran while one was open for 4% of the time, Pallas kernels for 44%

commit v1 on v0

--- a/solution.py
+++ b/solution.py
@@ -588,8 +588,8 @@
             ref[start : start + tiles, :] = upb[...]
 
 
-def unpack_kernel(layers, mine, got, gain, bias, out_bias, qv, upb):
-    total = mine[...] + got[...]
+def unpack_kernel(layers, mine, gain, bias, out_bias, qv, upb):
+    total = mine[...]
     half = qv.shape[2]
     tiles = upb.shape[1] // mine.shape[1]
     width = mine.shape[1]
@@ -609,6 +609,21 @@
             upb[layer : layer + 1, part * width : (part + 1) * width] = total[
                 row + part : row + part + 1
             ]
+
+
+def finish_kernel(parts, *refs):
+    layers = len(refs) // parts
+    outs = refs[layers * parts :]
+    for layer in range(layers):
+        total = refs[layer * parts][...].astype(F32)
+        for ref in refs[layer * parts + 1 : (layer + 1) * parts]:
+            total = total + ref[...].astype(F32)
+        column = 0
+        for ref in outs:
+            size = ref.shape[3]
+            for member in range(ref.shape[1]):
+                ref[layer, member] = total[:, column : column + size]
+                column += size
 
 
 def chunk_sources(order):
@@ -714,7 +729,7 @@
     def start(self):
         self.incoming = lax.ppermute(self.outgoing, "dp", flip(self.order.pop(0)))
 
-    def turn(self):
+    def turn(self, go=True):
         column = 0
         for parts in self.members:
             width = parts[0].shape[1]
@@ -723,32 +738,60 @@
         self.incoming = None
         if self.order:
             self.halve()
-            self.start()
-
-    def results(self):
-        return [sum(part.astype(F32) for part in parts) for parts in self.members]
+            if go:
+                self.start()
+
+    def flying(self):
+        return [self.incoming]
+
+    def land(self, arrays):
+        (self.incoming,) = arrays
 
 
 class Everywhere:
-    def __init__(self, mine, far, bits):
+    def __init__(self, mine, far, groups):
         self.mine = mine
-        self.incoming = swap(far)
-        self.bits = list(range(bits))
+        self.incoming = [swap(far)]
+        self.groups = list(groups)
+
+    def flying(self):
+        return self.incoming
+
+    def land(self, arrays):
+        self.incoming = arrays
 
     def turn(self):
-        self.mine = self.mine + self.incoming
-        self.incoming = lax.ppermute(self.mine, "dp", flip(self.bits.pop(0)))
-
-
-def gate(value, starts=(), turns=(), after=()):
-    held = [unit.outgoing for unit in starts] + [unit.incoming for unit in turns]
+        if len(self.incoming) == 1:
+            self.mine = self.mine + self.incoming[0]
+        else:
+            near, far, across = self.incoming
+            self.mine = (self.mine + near) + (far + across)
+        self.incoming = []
+        if self.groups:
+            group = self.groups.pop(0)
+            masks = [1 << bit for bit in group]
+            if len(masks) == 2:
+                masks.append(masks[0] | masks[1])
+            size = lax.axis_size("dp")
+            self.incoming = [
+                lax.ppermute(self.mine, "dp", [(index, index ^ mask) for index in range(size)])
+                for mask in masks
+            ]
+
+
+def gate(value, starts=(), turns=(), after=(), holds=()):
+    ends = [*turns, *holds]
+    held = [unit.outgoing for unit in starts] + [array for unit in ends for array in unit.flying()]
     value, *held = lax.optimization_barrier((value, *held, *after))
-    for unit, array in zip(starts, held):
-        unit.outgoing = array
+    for unit in starts:
+        unit.outgoing = held.pop(0)
         unit.start()
-    for unit, array in zip(turns, held[len(starts) :]):
-        unit.incoming = array
+    for unit in ends:
+        unit.land([held.pop(0) for _ in unit.flying()])
+    for unit in turns:
         unit.turn()
+    for unit in holds:
+        unit.turn(go=False)
     return value
 
 
@@ -783,7 +826,7 @@
     tail = tuple(range(4, bits))
     order_a = (0, 1, 2, 3) + tail
     order_b = (1, 0, 2, 3) + tail
-    order_c = (2, 3, 0, 1) + tail
+    order_e = (2, 0, 1, 3) + tail
     order_d = (0, 2, 3, 1) + tail
 
     me = lax.axis_index("dp")
@@ -1066,16 +1109,16 @@
     joint_own, qv_own = attend_back(saved[1]["own"], att_own, counts_in)
     pre_own = gate(pre_own, after=[qv_own])
     up_1 = DpSum(order_a, up_halves(1, order_a, pre_own, got_pre))
-    gain_in = gate(gain_in, [up_1], [down_1])
+    gain_in = gate(gain_in, [up_1])
     grad, sums_in, grad_t = entry_back(1, joint_own, joint_far, grad_mid, gain_in)
     got_grad_t = swap(grad_t)
     small[1] = (sums_mid, sums_in, qv_own, qv_far, upb_own, upb_far)
     joint_own = gate(joint_own, [], [down_1], [sums_in])
     rest_1 = DpSum(
-        order_c,
+        order_e,
         weight_grad(
             "qkv_out_grad",
-            order_c,
+            order_e,
             lefts(1),
             (joint_own, got_joint),
             extras(1, mid_t, got_mid_t),
@@ -1085,15 +1128,15 @@
     grad_t = gate(grad_t, [rest_1])
     down_0 = DpSum(order_a, down_halves(0, order_a, grad_t, got_grad_t))
 
-    gain_in = gate(gain_in, [down_0], [up_1, down_1])
+    gain_in = gate(gain_in, [down_0], [up_1], holds=[down_1])
     pre_own, pre_far, upb_own, upb_far, grad_mid, mid_t, att_own, att_far, sums_mid = feed_back(
         0, grad, gain_in
     )
     got_pre, got_mid_t = swap(pre_far), swap(mid_t)
-    counts_in = gate(counts_in, [], [up_1, rest_1], [sums_mid])
+    counts_in = gate(counts_in, [], [], [sums_mid], [up_1, rest_1])
     joint_far, qv_far = attend_back(saved[0]["far"], att_far, counts_in)
     got_joint = swap(joint_far)
-    pre_own = gate(pre_own, [], [down_0, up_1], [qv_far])
+    pre_own = gate(pre_own, [down_1, up_1], [down_0], [qv_far])
     up_0 = DpSum(order_d, up_halves(0, order_d, pre_own, got_pre))
     counts_in = gate(counts_in, [up_0], [], [got_mid_t, got_joint])
     joint_own, qv_own = attend_back(saved[0]["own"], att_own, counts_in)
@@ -1108,9 +1151,9 @@
             tiles=3,
         ),
     )
-    gain_in = gate(gain_in, [rest_0], [down_0], [qv_own])
+    gain_in = gate(gain_in, [rest_0], [down_0, up_1, down_1], [qv_own])
     grad, sums_in = entry_back(0, joint_own, joint_far, grad_mid, gain_in)
-    last = gate(sums_in, [], [up_0, down_0, rest_1, up_1])
+    last = gate(sums_in, [rest_1], [up_0, down_0, up_1])
     small[0] = (sums_mid, last, qv_own, qv_far, upb_own, upb_far)
     ins = [array for arrays in small for array in arrays]
     vector_shape = out(((7 + steps) * LAYERS, width), F32)
@@ -1123,42 +1166,38 @@
         [vector_shape] * 2,
         [whole()] * 2,
     )
-    vector = Everywhere(mine, far, bits)
+    vector = Everywhere(mine, far, [(1,), (0,), (2, 3), *[(bit,) for bit in tail]])
     last = gate(last, [], [rest_0, up_0, down_0, rest_1, vector])
     last = gate(last, [], [rest_0, up_0, rest_1, vector])
-    last = gate(last, [], [rest_0, up_0, vector])
+    last = gate(last, [], [rest_0, up_0, rest_1, vector])
     last = gate(last, [], [rest_0, vector])
+    while vector.flying():
+        vector.turn()
     running = [down_1, up_1, rest_1, down_0, up_0, rest_0]
     while any(unit.incoming is not None for unit in running):
         last = gate(last, [], [unit for unit in running if unit.incoming is not None][:4])
 
-    (down_1_sum,), (up_1_sum,) = down_1.results(), up_1.results()
-    (down_0_sum,), (up_0_sum,) = down_0.results(), up_0.results()
-    (both,), (first_both,) = rest_1.results(), rest_0.results()
-    summed = [
-        (
-            first_both[:, : 3 * half].reshape(block, 3, half),
-            first_both[:, 3 * half :].T,
-            up_0_sum,
-            down_0_sum.T,
-        ),
-        (
-            both[:, : 3 * half].reshape(block, 3, half),
-            both[:, 3 * half :].T,
-            up_1_sum,
-            down_1_sum.T,
-        ),
-    ]
-
-    while vector.bits:
-        vector.turn()
-    mine, got = vector.mine, vector.incoming
+    def finish(first, second, shapes):
+        ins = [*first.members[0], *second.members[0]]
+        return call(
+            functools.partial(finish_kernel, len(first.members[0])),
+            "finish",
+            (),
+            ins,
+            [whole()] * len(ins),
+            [out((LAYERS,) + shape, F32) for shape in shapes],
+            [whole()] * len(shapes),
+        )
+
+    (down_grad,) = finish(down_0, down_1, [(1, block, ff_half)])
+    (up_grad,) = finish(up_0, up_1, [(1, block, ff_half)])
+    qkv_grad, out_grad = finish(rest_0, rest_1, [(3, block, half), (1, block, half)])
     gain_grads, shift_grads, outb_grads, qv_grads, upb_grads = call(
         functools.partial(unpack_kernel, LAYERS),
         "unpack_small",
         (),
-        [mine, got],
-        [whole()] * 2,
+        [vector.mine],
+        [whole()],
         [
             out(ln_gain.shape, F32),
             out(ln_bias.shape, F32),
@@ -1168,20 +1207,19 @@
         ],
         [whole()] * 5,
     )
-    stacked = [jnp.stack([summed[layer][member] for layer in range(LAYERS)]) for member in range(4)]
     return (
         stream.reshape(images.shape),
         pooled,
         grad.reshape(images.shape),
         gain_grads,
         shift_grads,
-        stacked[0],
+        jnp.transpose(qkv_grad, (0, 2, 1, 3)),
         qv_grads,
-        stacked[1],
+        jnp.transpose(out_grad[:, 0], (0, 2, 1)),
         outb_grads,
-        stacked[2],
+        up_grad[:, 0],
         upb_grads,
-        stacked[3],
+        jnp.transpose(down_grad[:, 0], (0, 2, 1)),
     )
 
 

time: 294 us -> 286 us (0.973)
  other arithmetic: 13.9 us -> 2.41 us
  waiting for transfers between devices: 58.1 us -> 62.5 us
  Pallas kernels: 171 us -> 174 us
    ppermute x24, waiting for transfers between devices: 35.3 us -> 43.5 us  [start(): self.incoming = lax.ppermute(self.outgoing, 'dp', flip(self.order.pop(0)))]
    another operation x8 -> x0, other arithmetic: 5.87 us -> none  [shards(): jnp.stack([summed[layer][member] for layer in range(LAYERS)])]
    ppermute x24, starting transfers between devices: 33 us -> 27.5 us  [start(): self.incoming = lax.ppermute(self.outgoing, 'dp', flip(self.order.pop(0)))]
    ppermute x4 -> x5, waiting for transfers between devices: 17.7 us -> 12.5 us  [turn(): lax.ppermute(self.mine, 'dp', [(index, index ^ mask) for index in range(s...]
    convert_element_type x18, other arithmetic: 6.46 us -> 2.09 us  [halve(): sum((part[rows:].astype(F32) for part in parts)).astype(BF16)]
    ppermute x4 -> x5, starting transfers between devices: 4.04 us -> 8.31 us  [turn(): lax.ppermute(self.mine, 'dp', [(index, index ^ mask) for index in range(s...]
    pallas_call x21 -> x24, Pallas kernels: 171 us -> 174 us  [call(): pl.pallas_call(body, name=name, grid=grid, in_specs=in_specs, out_specs=o...]
  transfers between devices with their start and end apart: 51 -> 52, of which waited for: 19 -> 16; matrix products, arithmetic and copies ran while one was open for 4% -> 1% of each run, Pallas kernels for 44% -> 46%
where the time goes in v1:
time: 286 us
  Pallas kernels  174 us (61%)
  waiting for transfers between devices  62.5 us (22%)
  starting transfers between devices  41.6 us (15%)
  local copies, waits for them, and re-layouts  3.74 us (1%)
    pallas_call x24, Pallas kernels, call(): pl.pallas_call(body, name=name, grid=grid, in_specs=in_specs, out_specs=o...  174 us
    ppermute x24, waiting for transfers between devices, start(): self.incoming = lax.ppermute(self.outgoing, 'dp', flip(self.order.pop(0)))  43.5 us
    ppermute x24, starting transfers between devices, start(): self.incoming = lax.ppermute(self.outgoing, 'dp', flip(self.order.pop(0)))  27.5 us
    ppermute x5, waiting for transfers between devices, turn(): lax.ppermute(self.mine, 'dp', [(index, index ^ mask) for index in range(s...  12.5 us
    ppermute x5, starting transfers between devices, turn(): lax.ppermute(self.mine, 'dp', [(index, index ^ mask) for index in range(s...  8.31 us
    ppermute x23, waiting for transfers between devices, swap(): return lax.ppermute(values, 'tensor', [(0, 1), (1, 0)])  6.45 us
    ppermute x23, starting transfers between devices, swap(): return lax.ppermute(values, 'tensor', [(0, 1), (1, 0)])  5.75 us
  transfers between devices with their start and end apart: 52, of which 16 were waited for; matrix products, arithmetic and copies ran while one was open for 1% of the time, Pallas kernels for 46%

profile of v1, /device:TPU:0, one launch (start us, length us, event | category | flops | bytes accessed | tf_op | source)
XLA Modules:
  0.0 285.7 jit_solution(6717674279426901414)
XLA Ops:
  2.9 4.0 %prep.1 = (bf16[512,768]{1,0:T(8,128)(2,1)S(1)}, bf16[768,512]{1,0:T(8,128)(2,1)S(1)}, bf16[768,512]{1,0:T(8,128)(2,1)S(1)}, f32[512,768]{1,0:T(8,128)S(1)}) custom-call(bf16[512,768]{1,0:T(8,128)(2,1)S(1)} %bitcast.13, bf16[512,768]{1,0:T(8,128)(2,1)S(1)} %bitcast.16, f32[2,2,768]{2,1,0:T(2,128)S(1)} %copy-done.22, f32[2,2,768]{2,1,0:T(2,128)S(1)} %copy-done.23, ...), custom_call_target="tpu_custom_call" | custom-call | flops 18874368 | bytes 104832 | tf_op jit(solution)/shard_map/prep/pallas_call | solution.py:50
  8.4 14.3 %attend.2 = (bf16[3,512,384]{2,1,0:T(8,128)(2,1)S(1)}, bf16[3,512,384]{2,1,0:T(8,128)(2,1)S(1)}, bf16[512,384]{1,0:T(8,128)(2,1)S(1)}, bf16[512,384]{1,0:T(8,128...) custom-call(s32[1]{0:T(128)} %constant.14.clone.1.which, s32[4]{0:T(128)S(1)} %copy-done.26, ...), custom_call_target="tpu_custom_call" | custom-call | flops 34603008 | bytes 172608 | tf_op jit(solution)/shard_map/attend/pallas_call | solution.py:50
  22.8 1.3 collective-permute-done.5.down_far
  24.1 18.3 %feed.2 = (f32[512,768]{1,0:T(8,128)S(1)}, bf16[768,512]{1,0:T(8,128)(2,1)S(1)}, bf16[512,1536]{1,0:T(8,128)(2,1)}, bf16[512,1536]{1,0:T(8,128)(2,1)}, bf16[512,...) custom-call(s32[4]{0:T(128)S(1)} %copy-done.26, ...), custom_call_target="tpu_custom_call" | custom-call | flops 94371840 | bytes 560064 | tf_op jit(solution)/shard_map/feed/pallas_call | solution.py:50
  44.7 14.3 %attend.3 = (bf16[3,512,384]{2,1,0:T(8,128)(2,1)S(1)}, bf16[3,512,384]{2,1,0:T(8,128)(2,1)S(1)}, bf16[512,384]{1,0:T(8,128)(2,1)S(1)}, bf16[512,384]{1,0:T(8,128...) custom-call(s32[1]{0:T(128)} %constant.36.clone.1.which, s32[4]{0:T(128)S(1)} %copy-done.26, ...), custom_call_target="tpu_custom_call" | custom-call | flops 34603008 | bytes 172608 | tf_op jit(solution)/shard_map/attend/pallas_call | solution.py:50
  59.2 17.7 %feed.3 = (f32[512,768]{1,0:T(8,128)S(1)}, bf16[768,512]{1,0:T(8,128)(2,1)S(1)}, bf16[512,1536]{1,0:T(8,128)(2,1)}, bf16[512,1536]{1,0:T(8,128)(2,1)}, bf16[512,...) custom-call(s32[4]{0:T(128)S(1)} %copy-done.26, ...), custom_call_target="tpu_custom_call" | custom-call | flops 94371840 | bytes 547872 | tf_op jit(solution)/shard_map/feed/pallas_call | solution.py:50
  77.2 3.5 %collective-permute-done.11.refs_3_ = bf16[512,1536]{1,0:T(8,128)(2,1)S(1)} collective-permute-done((bf16[512,1536]{1,0:T(8,128)(2,1)}, bf16[512,1536]{1,0:T(8,128)(2,1)S(1)}, u32[]{:S(2)}, u32[]{:S(2)}) %collective-permute-start.11) | collective-permute-done | bytes 1572896 | tf_op jit(solution)/shard_map/ppermute | solution.py:799
  81.8 4.3 %down_grad.2 = (bf16[384,1536]{1,0:T(8,128)(2,1)S(1)}, bf16[384,1536]{1,0:T(8,128)(2,1)S(1)}) custom-call(bf16[768,512]{1,0:T(8,128)(2,1)S(1)} %copy-done.18, bf16[768,512]{1,0:T(8,128)(2,1)S(1)} %copy-done.20, bf16[512,1536]{1,0:T(8,128)(2,1)} %get-tuple-element.175.refs_2_, bf16[512,1536]{1,0:T(8,128)(2,1)S(1)} %collective-permute-done.11.refs_3_), custom_call_target="tpu_custom_call" | custom-call | flops 37748736 | bytes 110592 | tf_op jit(solution)/shard_map/down_grad/pallas_call | solution.py:50
  86.1 2.7 collective-permute-start.12
  88.8 17.9 %feed_back.2 = (bf16[512,1536]{1,0:T(8,128)(2,1)}, bf16[512,1536]{1,0:T(8,128)(2,1)}, f32[2,768]{1,0:T(2,128)S(1)}, f32[2,768]{1,0:T(2,128)S(1)}, f32[512,768]{1...) custom-call(s32[1]{0:T(128)} %constant.36.clone.1.which, ...), custom_call_target="tpu_custom_call" | custom-call | flops 94371840 | bytes 547392 | tf_op jit(solution)/shard_map/feed_back/pallas_call | solution.py:50
  107.3 5.6 %attend_back.4 = (bf16[3,512,384]{2,1,0:T(8,128)(2,1)S(1)}, f32[1,768]{1,0:T(1,128)S(1)}) custom-call(s32[4]{0:T(128)S(1)} %copy-done.26, bf16[3,512,384]{2,1,0:T(8,128)(2,1)S(1)} %get-tuple-element.179.joint, f32[12,1,256]{2,1,0:T(1,128)S(1)} %get-tuple-element.180.lse, bf16[512,384]{1,0:T(8,128)(2,1)S(1)} %get-tuple-element.186.grad_att), custom_call_target="tpu_custom_call" | custom-call | flops 7864320 | bytes 43248 | tf_op jit(solution)/shard_map/attend_back/pallas_call | solution.py:50
  112.9 2.4 collective-permute-done.12
  115.5 1.8 collective-permute-start.16
  117.8 5.6 %attend_back.5 = (bf16[3,512,384]{2,1,0:T(8,128)(2,1)S(1)}, f32[1,768]{1,0:T(1,128)S(1)}) custom-call(s32[4]{0:T(128)S(1)} %copy-done.26, bf16[3,512,384]{2,1,0:T(8,128)(2,1)S(1)} %get-tuple-element.191.joint, f32[12,1,256]{2,1,0:T(1,128)S(1)} %get-tuple-element.192.lse, bf16[512,384]{1,0:T(8,128)(2,1)S(1)} %get-tuple-element.193.grad_att), custom_call_target="tpu_custom_call" | custom-call | flops 7864320 | bytes 43248 | tf_op jit(solution)/shard_map/attend_back/pallas_call | solution.py:50
  123.4 3.3 %up_grad.2 = (bf16[384,1536]{1,0:T(8,128)(2,1)S(1)}, bf16[384,1536]{1,0:T(8,128)(2,1)S(1)}) custom-call(bf16[768,512]{1,0:T(8,128)(2,1)S(1)} %get-tuple-element.189.refs_0_, bf16[768,512]{1,0:T(8,128)(2,1)S(1)} %collective-permute-done.13.refs_1_, bf16[512,1536]{1,0:T(8,128)(2,1)S(1)} %copy-done.6, bf16[512,1536]{1,0:T(8,128)(2,1)S(1)} %collective-permute-done.14.refs_3_), custom_call_target="tpu_custom_call" | custom-call | flops 37748736 | bytes 110592 | tf_op jit(solution)/shard_map/up_grad/pallas_call | solution.py:50
  126.7 1.6 collective-permute-start.21
  128.8 9.9 %entry_back.2 = (f32[512,768]{1,0:T(8,128)S(1)}, f32[2,768]{1,0:T(2,128)S(1)}, bf16[768,512]{1,0:T(8,128)(2,1)S(1)}) custom-call(bf16[3,512,384]{2,1,0:T(8,128)(2,1)S(1)} %get-tuple-element.208.joint_own.refs_2_, bf16[3,512,384]{2,1,0:T(8,128)(2,1)S(1)} %get-tuple-element.201.joint_far, bf16[2,3,768,384]{3,2,1,0:T(8,128)(2,1)} %bitcast.20, ...), custom_call_target="tpu_custom_call" | custom-call | flops 28311552 | bytes 252192 | tf_op jit(solution)/shard_map/entry_back/pallas_call | solution.py:50
  139.0 1.6 collective-permute-start.22
  140.6 4.2 %qkv_out_grad.2 = (bf16[384,1536]{1,0:T(8,128)(2,1)S(1)}, bf16[384,1536]{1,0:T(8,128)(2,1)S(1)}) custom-call(bf16[768,512]{1,0:T(8,128)(2,1)S(1)} %copy-done.16, bf16[768,512]{1,0:T(8,128)(2,1)S(1)} %collective-permute-done.15.refs_1_, bf16[3,512,384]{2,1,0:T(8,128)(2,1)S(1)} %get-tuple-element.208.joint_own.refs_2_, ...), custom_call_target="tpu_custom_call" | custom-call | flops 37748736 | bytes 135168 | tf_op jit(solution)/shard_map/qkv_out_grad/pallas_call | solution.py:50
  145.4 4.3 %down_grad.3 = (bf16[384,1536]{1,0:T(8,128)(2,1)S(1)}, bf16[384,1536]{1,0:T(8,128)(2,1)S(1)}) custom-call(bf16[768,512]{1,0:T(8,128)(2,1)S(1)} %get-tuple-element.211.refs_0_, bf16[768,512]{1,0:T(8,128)(2,1)S(1)} %collective-permute-done.20.refs_1_, bf16[512,1536]{1,0:T(8,128)(2,1)} %get-tuple-element.212.refs_2_, ...), custom_call_target="tpu_custom_call" | custom-call | flops 37748736 | bytes 110592 | tf_op jit(solution)/shard_map/down_grad/pallas_call | solution.py:50
  149.7 5.0 %collective-permute-done.21 = bf16[384,1536]{1,0:T(8,128)(2,1)S(1)} collective-permute-done((bf16[384,1536]{1,0:T(8,128)(2,1)S(1)}, bf16[384,1536]{1,0:T(8,128)(2,1)S(1)}, u32[]{:S(2)}, u32[]{:S(2)}) %collective-permute-start.21) | collective-permute-done | bytes 1179680 | tf_op jit(solution)/shard_map/ppermute | solution.py:730
  154.7 1.5 collective-permute-start.25
  156.9 18.1 %feed_back.3 = (bf16[512,1536]{1,0:T(8,128)(2,1)}, bf16[512,1536]{1,0:T(8,128)(2,1)}, f32[2,768]{1,0:T(2,128)S(1)}, f32[2,768]{1,0:T(2,128)S(1)}, f32[512,768]{1...) custom-call(s32[1]{0:T(128)} %constant.14.clone.1.which, ...), custom_call_target="tpu_custom_call" | custom-call | flops 94371840 | bytes 547392 | tf_op jit(solution)/shard_map/feed_back/pallas_call | solution.py:50
  175.7 5.6 %attend_back.6 = (bf16[3,512,384]{2,1,0:T(8,128)(2,1)S(1)}, f32[1,768]{1,0:T(1,128)S(1)}) custom-call(s32[4]{0:T(128)S(1)} %copy-done.26, bf16[3,512,384]{2,1,0:T(8,128)(2,1)S(1)} %get-tuple-element.231.joint, f32[12,1,256]{2,1,0:T(1,128)S(1)} %get-tuple-element.232.lse, bf16[512,384]{1,0:T(8,128)(2,1)S(1)} %get-tuple-element.233.grad_att), custom_call_target="tpu_custom_call" | custom-call | flops 7864320 | bytes 43248 | tf_op jit(solution)/shard_map/attend_back/pallas_call | solution.py:50
  181.9 1.5 collective-permute-start.29
  183.3 1.6 collective-permute-start.30
  184.9 2.6 collective-permute-start.31
  187.5 3.3 %up_grad.3 = (bf16[384,1536]{1,0:T(8,128)(2,1)S(1)}, bf16[384,1536]{1,0:T(8,128)(2,1)S(1)}) custom-call(bf16[768,512]{1,0:T(8,128)(2,1)S(1)} %copy-done.12, bf16[768,512]{1,0:T(8,128)(2,1)S(1)} %copy-done.14, bf16[512,1536]{1,0:T(8,128)(2,1)S(1)} %copy-done.5, bf16[512,1536]{1,0:T(8,128)(2,1)S(1)} %collective-permute-done.26.refs_3_), custom_call_target="tpu_custom_call" | custom-call | flops 37748736 | bytes 110592 | tf_op jit(solution)/shard_map/up_grad/pallas_call | solution.py:50
  190.9 5.6 %attend_back.7 = (bf16[3,512,384]{2,1,0:T(8,128)(2,1)S(1)}, f32[1,768]{1,0:T(1,128)S(1)}) custom-call(s32[4]{0:T(128)S(1)} %copy-done.26, bf16[3,512,384]{2,1,0:T(8,128)(2,1)S(1)} %get-tuple-element.241.joint, f32[12,1,256]{2,1,0:T(1,128)S(1)} %get-tuple-element.242.lse, bf16[512,384]{1,0:T(8,128)(2,1)S(1)} %get-tuple-element.243.grad_att), custom_call_target="tpu_custom_call" | custom-call | flops 7864320 | bytes 43248 | tf_op jit(solution)/shard_map/attend_back/pallas_call | solution.py:50
  196.5 4.3 %qkv_out_grad.3 = (bf16[384,1536]{1,0:T(8,128)(2,1)S(1)}, bf16[384,1536]{1,0:T(8,128)(2,1)S(1)}) custom-call(bf16[768,512]{1,0:T(8,128)(2,1)S(1)} %copy-done.8, bf16[768,512]{1,0:T(8,128)(2,1)S(1)} %copy-done.10, bf16[3,512,384]{2,1,0:T(8,128)(2,1)S(1)} %get-tuple-element.244.refs_2_.joint_own, bf16[3,512,384]{2,1,0:T(8,128)(2,1)S(1)} %collective-permute-done.28.refs_3_, ...), custom_call_target="tpu_custom_call" | custom-call | flops 37748736 | bytes 135168 | tf_op jit(solution)/shard_map/qkv_out_grad/pallas_call | solution.py:50
  202.6 1.5 collective-permute-start.35
  204.3 9.8 %entry_back.3 = (f32[512,768]{1,0:T(8,128)}, f32[2,768]{1,0:T(2,128)S(1)}) custom-call(bf16[3,512,384]{2,1,0:T(8,128)(2,1)S(1)} %get-tuple-element.244.refs_2_.joint_own, bf16[3,512,384]{2,1,0:T(8,128)(2,1)S(1)} %get-tuple-element.239.joint_far, bf16[2,3,768,384]{3,2,1,0:T(8,128)(2,1)} %bitcast.21, bf16[2,3,768,384]{3,2,1,0:T(8,128)(2,1)} %collective-permute-done.weight_far, ...), custom_call_target="tpu_custom_call" | custom-call | flops 28311552 | bytes 227616 | tf_op jit(solution)/shard_map/entry_back/pallas_call | solution.py:50
  214.1 14.3 %collective-permute-done.32 = bf16[384,1536]{1,0:T(8,128)(2,1)S(1)} collective-permute-done((bf16[384,1536]{1,0:T(8,128)(2,1)S(1)}, bf16[384,1536]{1,0:T(8,128)(2,1)S(1)}, u32[]{:S(2)}, u32[]{:S(2)}) %collective-permute-start.32) | collective-permute-done | bytes 1179680 | tf_op jit(solution)/shard_map/ppermute | solution.py:730
  230.2 1.2 collective-permute-done.39
  231.4 12.2 %collective-permute-done.37.refs_4_ = bf16[48,1536]{1,0:T(8,128)(2,1)S(1)} collective-permute-done((bf16[48,1536]{1,0:T(8,128)(2,1)S(1)}, bf16[48,1536]{1,0:T(8,128)(2,1)S(1)}, u32[]{:S(2)}, u32[]{:S(2)}) %collective-permute-start.37) | collective-permute-done | bytes 147488 | tf_op jit(solution)/shard_map/ppermute | solution.py:730
  243.6 2.0 collective-permute-done.36
  246.5 1.4 collective-permute-start.41
  248.2 2.1 collective-permute-start.43
  250.2 5.4 %collective-permute-done.43 = f32[18,768]{1,0:T(8,128)S(1)} collective-permute-done((f32[18,768]{1,0:T(8,128)S(1)}, f32[18,768]{1,0:T(8,128)S(1)}, u32[]{:S(2)}, u32[]{:S(2)}) %collective-permute-start.43) | collective-permute-done | bytes 55328 | tf_op jit(solution)/shard_map/ppermute | solution.py:777
  255.6 4.1 %collective-permute-done.41 = bf16[96,1536]{1,0:T(8,128)(2,1)S(1)} collective-permute-done((bf16[96,1536]{1,0:T(8,128)(2,1)S(1)}, bf16[96,1536]{1,0:T(8,128)(2,1)S(1)}, u32[]{:S(2)}, u32[]{:S(2)}) %collective-permute-start.41) | collective-permute-done | bytes 294944 | tf_op jit(solution)/shard_map/ppermute | solution.py:730
  260.7 2.8 collective-permute-start.46
  263.6 1.8 collective-permute-start.47
  265.3 2.6 collective-permute-done.47
  269.1 2.2 collective-permute-done.44
  271.4 1.4 collective-permute-start.48
  272.8 1.7 collective-permute-start.50
  274.5 2.7 collective-permute-start.51
  279.7 4.4 %collective-permute-done.50 = f32[18,768]{1,0:T(8,128)S(1)} collective-permute-done((f32[18,768]{1,0:T(8,128)S(1)}, f32[18,768]{1,0:T(8,128)S(1)}, u32[]{:S(2)}, u32[]{:S(2)}) %collective-permute-start.50) | collective-permute-done | bytes 55328 | tf_op jit(solution)/shard_map/ppermute | solution.py:777
  (188 shorter events, 22.9 us)
Async XLA Ops:
  0.7 6.7 %collective-permute-start = (bf16[2,3,768,384]{3,2,1,0:T(8,128)(2,1)}, bf16[2,3,768,384]{3,2,1,0:T(8,128)(2,1)}, u32[]{:S(2)}, u32[]{:S(2)}) collective-permute-start(bf16[2,3,768,384]{3,2,1,0:T(8,128)(2,1)} %bitcast.17), channel_id=1, source_target_pairs={{0,1},{1,0},{2,3},{3,2},{4,5},{5,4},{6,7},{7,6},{8,9},{9,8},{10,11... | collective-permute-start | bytes 10616840 | tf_op jit(solution)/shard_map/ppermute | solution.py:799
  7.4 15.4 %collective-permute-start.3 = (bf16[2,768,1536]{2,1,0:T(8,128)(2,1)}, bf16[2,768,1536]{2,1,0:T(8,128)(2,1)}, u32[]{:S(2)}, u32[]{:S(2)}) collective-permute-start(bf16[2,768,1536]{2,1,0:T(8,128)(2,1)} %up_own.7), channel_id=1, source_target_pairs={{0,1},{1,0},{2,3},{3,2},{4,5},{5,4},{6,7},{7,6},{8,9},{9,8},{10,11... | collective-permute-start | bytes 14155784 | tf_op jit(solution)/shard_map/ppermute | solution.py:799
  7.8 16.3 %collective-permute-start.5 = (bf16[2,1536,768]{2,1,0:T(8,128)(2,1)}, bf16[2,1536,768]{2,1,0:T(8,128)(2,1)}, u32[]{:S(2)}, u32[]{:S(2)}) collective-permute-start(bf16[2,1536,768]{2,1,0:T(8,128)(2,1)} %down_own.7), channel_id=1, source_target_pairs={{0,1},{1,0},{2,3},{3,2},{4,5},{5,4},{6,7},{7,6},{8,9},{9,8},{10,11... | collective-permute-start | bytes 14155784 | tf_op jit(solution)/shard_map/ppermute | solution.py:799
  7.9 14.9 %collective-permute-start.2 = (bf16[2,384,768]{2,1,0:T(8,128)(2,1)S(1)}, bf16[2,384,768]{2,1,0:T(8,128)(2,1)S(1)}, u32[]{:S(2)}, u32[]{:S(2)}) collective-permute-start(bf16[2,384,768]{2,1,0:T(8,128)(2,1)S(1)} %copy-done.28), channel_id=1, source_target_pairs={{0,1},{1,0},{2,3},{3,2},{4,5},{5,4},{6,7},{7,6},{8,9},{9,8},{10,11... | collective-permute-start | bytes 3538952 | tf_op jit(solution)/shard_map/ppermute | solution.py:799
  8.3 14.5 %collective-permute-start.4 = (f32[2,1536]{1,0:T(2,128)S(1)}, f32[2,1536]{1,0:T(2,128)S(1)}, u32[]{:S(2)}, u32[]{:S(2)}) collective-permute-start(f32[2,1536]{1,0:T(2,128)S(1)} %copy-done.25), channel_id=1, source_target_pairs={{0,1},{1,0},{2,3},{3,2},{4,5},{5,4},{6,7},{7,6},{8,9},{9,8},{10,11... | collective-permute-start | bytes 36872 | tf_op jit(solution)/shard_map/ppermute | solution.py:799
  43.3 15.8 %collective-permute-start.10 = (bf16[512,1536]{1,0:T(8,128)(2,1)}, bf16[512,1536]{1,0:T(8,128)(2,1)S(1)}, u32[]{:S(2)}, u32[]{:S(2)}) collective-permute-start(bf16[512,1536]{1,0:T(8,128)(2,1)} %get-tuple-element.170), channel_id=1, source_target_pairs={{0,1},{1,0},{2,3},{3,2},{4,5},{5,4},{6,7},{7,6},{8,9},{9,8},{10,11... | collective-permute-start | bytes 4718600 | tf_op jit(solution)/shard_map/ppermute | solution.py:799
  43.7 15.4 %collective-permute-start.6 = (bf16[768,512]{1,0:T(8,128)(2,1)S(1)}, bf16[768,512]{1,0:T(8,128)(2,1)S(1)}, u32[]{:S(2)}, u32[]{:S(2)}) collective-permute-start(bf16[768,512]{1,0:T(8,128)(2,1)S(1)} %get-tuple-element.167.refs_0_), channel_id=1, source_target_pairs={{0,1},{1,0},{2,3},{3,2},{4,5},{5,4},{6,7},{7,6},{8,9},{9,8},{10,11... | collective-permute-start | bytes 2359304 | tf_op jit(solution)/shard_map/ppermute | solution.py:799
  43.8 15.3 %collective-permute-start.7 = (bf16[768,512]{1,0:T(8,128)(2,1)S(1)}, bf16[768,512]{1,0:T(8,128)(2,1)S(1)}, u32[]{:S(2)}, u32[]{:S(2)}) collective-permute-start(bf16[768,512]{1,0:T(8,128)(2,1)S(1)} %get-tuple-element.168.refs_0_), channel_id=1, source_target_pairs={{0,1},{1,0},{2,3},{3,2},{4,5},{5,4},{6,7},{7,6},{8,9},{9,8},{10,11... | collective-permute-start | bytes 2359304 | tf_op jit(solution)/shard_map/ppermute | solution.py:799
  44.2 14.9 %collective-permute-start.9 = (bf16[768,512]{1,0:T(8,128)(2,1)S(1)}, bf16[768,512]{1,0:T(8,128)(2,1)S(1)}, u32[]{:S(2)}, u32[]{:S(2)}) collective-permute-start(bf16[768,512]{1,0:T(8,128)(2,1)S(1)} %get-tuple-element.169.refs_0_), channel_id=1, source_target_pairs={{0,1},{1,0},{2,3},{3,2},{4,5},{5,4},{6,7},{7,6},{8,9},{9,8},{10,11... | collective-permute-start | bytes 2359304 | tf_op jit(solution)/shard_map/ppermute | solution.py:799
  44.3 14.8 %collective-permute-start.8 = (bf16[512,384]{1,0:T(8,128)(2,1)S(1)}, bf16[512,384]{1,0:T(8,128)(2,1)S(1)}, u32[]{:S(2)}, u32[]{:S(2)}) collective-permute-start(bf16[512,384]{1,0:T(8,128)(2,1)S(1)} %get-tuple-element.159.att_far), channel_id=1, source_target_pairs={{0,1},{1,0},{2,3},{3,2},{4,5},{5,4},{6,7},{7,6},{8,9},{9,8},{10,11... | collective-permute-start | bytes 1179656 | tf_op jit(solution)/shard_map/ppermute | solution.py:799
  86.1 29.2 %collective-permute-start.12 = (bf16[384,1536]{1,0:T(8,128)(2,1)S(1)}, bf16[384,1536]{1,0:T(8,128)(2,1)S(1)}, u32[]{:S(2)}, u32[]{:S(2)}) collective-permute-start(bf16[384,1536]{1,0:T(8,128)(2,1)S(1)} %get-tuple-element.178), channel_id=1, source_target_pairs={{0,2},{2,0},{4,6},{6,4},{8,10},{10,8},{12,14},{14,12},{16,18},{18,... | collective-permute-start | bytes 3538952 | tf_op jit(solution)/shard_map/ppermute | solution.py:730
  106.7 16.7 %collective-permute-start.14 = (bf16[512,1536]{1,0:T(8,128)(2,1)}, bf16[512,1536]{1,0:T(8,128)(2,1)S(1)}, u32[]{:S(2)}, u32[]{:S(2)}) collective-permute-start(bf16[512,1536]{1,0:T(8,128)(2,1)} %get-tuple-element.196), channel_id=1, source_target_pairs={{0,1},{1,0},{2,3},{3,2},{4,5},{5,4},{6,7},{7,6},{8,9},{9,8},{10,11... | collective-permute-start | bytes 4718600 | tf_op jit(solution)/shard_map/ppermute | solution.py:799
  106.9 16.5 %collective-permute-start.13 = (bf16[768,512]{1,0:T(8,128)(2,1)S(1)}, bf16[768,512]{1,0:T(8,128)(2,1)S(1)}, u32[]{:S(2)}, u32[]{:S(2)}) collective-permute-start(bf16[768,512]{1,0:T(8,128)(2,1)S(1)} %get-tuple-element.189.refs_0_), channel_id=1, source_target_pairs={{0,1},{1,0},{2,3},{3,2},{4,5},{5,4},{6,7},{7,6},{8,9},{9,8},{10,11... | collective-permute-start | bytes 2359304 | tf_op jit(solution)/shard_map/ppermute | solution.py:799
  115.5 23.2 %collective-permute-start.16 = (bf16[192,1536]{1,0:T(8,128)(2,1)S(1)}, bf16[192,1536]{1,0:T(8,128)(2,1)S(1)}, u32[]{:S(2)}, u32[]{:S(2)}) collective-permute-start(bf16[192,1536]{1,0:T(8,128)(2,1)S(1)} %add_convert_fusion.5), channel_id=1, source_target_pairs={{0,4},{2,6},{4,0},{6,2},{8,12},{10,14},{12,8},{14,10},{16,20},{18,... | collective-permute-start | bytes 1769480 | tf_op jit(solution)/shard_map/ppermute | solution.py:730
  117.3 11.0 %collective-permute-start.19 = (bf16[512,384]{1,0:T(8,128)(2,1)S(1)}, bf16[512,384]{1,0:T(8,128)(2,1)S(1)}, u32[]{:S(2)}, u32[]{:S(2)}) collective-permute-start(bf16[512,384]{1,0:T(8,128)(2,1)S(1)} %get-tuple-element.166.att_far), channel_id=1, source_target_pairs={{0,1},{1,0},{2,3},{3,2},{4,5},{5,4},{6,7},{7,6},{8,9},{9,8},{10,11... | collective-permute-start | bytes 1179656 | tf_op jit(solution)/shard_map/ppermute | solution.py:799
  117.3 23.3 %collective-permute-start.17 = (bf16[3,512,384]{2,1,0:T(8,128)(2,1)S(1)}, bf16[3,512,384]{2,1,0:T(8,128)(2,1)S(1)}, u32[]{:S(2)}, u32[]{:S(2)}) collective-permute-start(bf16[3,512,384]{2,1,0:T(8,128)(2,1)S(1)} %get-tuple-element.201.joint_far), channel_id=1, source_target_pairs={{0,1},{1,0},{2,3},{3,2},{4,5},{5,4},{6,7},{7,6},{8,9},{9,8},{10,11... | collective-permute-start | bytes 3538952 | tf_op jit(solution)/shard_map/ppermute | solution.py:799
  126.7 27.9 %collective-permute-start.21 = (bf16[384,1536]{1,0:T(8,128)(2,1)S(1)}, bf16[384,1536]{1,0:T(8,128)(2,1)S(1)}, u32[]{:S(2)}, u32[]{:S(2)}) collective-permute-start(bf16[384,1536]{1,0:T(8,128)(2,1)S(1)} %get-tuple-element.215), channel_id=1, source_target_pairs={{0,2},{2,0},{4,6},{6,4},{8,10},{10,8},{12,14},{14,12},{16,18},{18,... | collective-permute-start | bytes 3538952 | tf_op jit(solution)/shard_map/ppermute | solution.py:730
  128.3 10.7 %collective-permute-start.15 = (bf16[768,512]{1,0:T(8,128)(2,1)S(1)}, bf16[768,512]{1,0:T(8,128)(2,1)S(1)}, u32[]{:S(2)}, u32[]{:S(2)}) collective-permute-start(bf16[768,512]{1,0:T(8,128)(2,1)S(1)} %copy-done.16), channel_id=1, source_target_pairs={{0,1},{1,0},{2,3},{3,2},{4,5},{5,4},{6,7},{7,6},{8,9},{9,8},{10,11... | collective-permute-start | bytes 2359304 | tf_op jit(solution)/shard_map/ppermute | solution.py:799
  128.3 12.3 %collective-permute-start.18 = (bf16[768,512]{1,0:T(8,128)(2,1)S(1)}, bf16[768,512]{1,0:T(8,128)(2,1)S(1)}, u32[]{:S(2)}, u32[]{:S(2)}) collective-permute-start(bf16[768,512]{1,0:T(8,128)(2,1)S(1)} %get-tuple-element.209.refs_4_), channel_id=1, source_target_pairs={{0,1},{1,0},{2,3},{3,2},{4,5},{5,4},{6,7},{7,6},{8,9},{9,8},{10,11... | collective-permute-start | bytes 2359304 | tf_op jit(solution)/shard_map/ppermute | solution.py:799
  138.7 6.7 %collective-permute-start.20 = (bf16[768,512]{1,0:T(8,128)(2,1)S(1)}, bf16[768,512]{1,0:T(8,128)(2,1)S(1)}, u32[]{:S(2)}, u32[]{:S(2)}) collective-permute-start(bf16[768,512]{1,0:T(8,128)(2,1)S(1)} %get-tuple-element.211.refs_0_), channel_id=1, source_target_pairs={{0,1},{1,0},{2,3},{3,2},{4,5},{5,4},{6,7},{7,6},{8,9},{9,8},{10,11... | collective-permute-start | bytes 2359304 | tf_op jit(solution)/shard_map/ppermute | solution.py:799
  139.0 10.7 %collective-permute-start.22 = (bf16[96,1536]{1,0:T(8,128)(2,1)S(1)}, bf16[96,1536]{1,0:T(8,128)(2,1)S(1)}, u32[]{:S(2)}, u32[]{:S(2)}) collective-permute-start(bf16[96,1536]{1,0:T(8,128)(2,1)S(1)} %add_convert_fusion.11), channel_id=1, source_target_pairs={{0,8},{2,10},{4,12},{6,14},{8,0},{10,2},{12,4},{14,6},{16,24},{18,... | collective-permute-start | bytes 884744 | tf_op jit(solution)/shard_map/ppermute | solution.py:730
  144.8 30.9 %collective-permute-start.24 = (bf16[384,1536]{1,0:T(8,128)(2,1)S(1)}, bf16[384,1536]{1,0:T(8,128)(2,1)S(1)}, u32[]{:S(2)}, u32[]{:S(2)}) collective-permute-start(bf16[384,1536]{1,0:T(8,128)(2,1)S(1)} %get-tuple-element.218), channel_id=1, source_target_pairs={{0,8},{2,10},{4,12},{6,14},{8,0},{10,2},{12,4},{14,6},{16,24},{18,... | collective-permute-start | bytes 3538952 | tf_op jit(solution)/shard_map/ppermute | solution.py:730
  154.7 27.0 %collective-permute-start.25 = (bf16[384,1536]{1,0:T(8,128)(2,1)S(1)}, bf16[384,1536]{1,0:T(8,128)(2,1)S(1)}, u32[]{:S(2)}, u32[]{:S(2)}) collective-permute-start(bf16[384,1536]{1,0:T(8,128)(2,1)S(1)} %get-tuple-element.230), channel_id=1, source_target_pairs={{0,2},{2,0},{4,6},{6,4},{8,10},{10,8},{12,14},{14,12},{16,18},{18,... | collective-permute-start | bytes 3538952 | tf_op jit(solution)/shard_map/ppermute | solution.py:730
  156.3 19.4 %collective-permute-start.23 = (bf16[192,1536]{1,0:T(8,128)(2,1)S(1)}, bf16[192,1536]{1,0:T(8,128)(2,1)S(1)}, u32[]{:S(2)}, u32[]{:S(2)}) collective-permute-start(bf16[192,1536]{1,0:T(8,128)(2,1)S(1)} %add_convert_fusion.4), channel_id=1, source_target_pairs={{0,4},{2,6},{4,0},{6,2},{8,12},{10,14},{12,8},{14,10},{16,20},{18,... | collective-permute-start | bytes 1769480 | tf_op jit(solution)/shard_map/ppermute | solution.py:730
  175.0 9.9 %collective-permute-start.26 = (bf16[512,1536]{1,0:T(8,128)(2,1)}, bf16[512,1536]{1,0:T(8,128)(2,1)S(1)}, u32[]{:S(2)}, u32[]{:S(2)}) collective-permute-start(bf16[512,1536]{1,0:T(8,128)(2,1)} %get-tuple-element.236), channel_id=1, source_target_pairs={{0,1},{1,0},{2,3},{3,2},{4,5},{5,4},{6,7},{7,6},{8,9},{9,8},{10,11... | collective-permute-start | bytes 4718600 | tf_op jit(solution)/shard_map/ppermute | solution.py:799
  175.2 15.7 %collective-permute-start.27 = (bf16[768,512]{1,0:T(8,128)(2,1)S(1)}, bf16[768,512]{1,0:T(8,128)(2,1)S(1)}, u32[]{:S(2)}, u32[]{:S(2)}) collective-permute-start(bf16[768,512]{1,0:T(8,128)(2,1)S(1)} %get-tuple-element.238.refs_4_), channel_id=1, source_target_pairs={{0,1},{1,0},{2,3},{3,2},{4,5},{5,4},{6,7},{7,6},{8,9},{9,8},{10,11... | collective-permute-start | bytes 2359304 | tf_op jit(solution)/shard_map/ppermute | solution.py:799
  181.3 9.6 %collective-permute-start.28 = (bf16[3,512,384]{2,1,0:T(8,128)(2,1)S(1)}, bf16[3,512,384]{2,1,0:T(8,128)(2,1)S(1)}, u32[]{:S(2)}, u32[]{:S(2)}) collective-permute-start(bf16[3,512,384]{2,1,0:T(8,128)(2,1)S(1)} %get-tuple-element.239.joint_far), channel_id=1, source_target_pairs={{0,1},{1,0},{2,3},{3,2},{4,5},{5,4},{6,7},{7,6},{8,9},{9,8},{10,11... | collective-permute-start | bytes 3538952 | tf_op jit(solution)/shard_map/ppermute | solution.py:799
  181.9 18.9 %collective-permute-start.29 = (bf16[192,1536]{1,0:T(8,128)(2,1)S(1)}, bf16[192,1536]{1,0:T(8,128)(2,1)S(1)}, u32[]{:S(2)}, u32[]{:S(2)}) collective-permute-start(bf16[192,1536]{1,0:T(8,128)(2,1)S(1)} %add_convert_fusion.3), channel_id=1, source_target_pairs={{0,4},{2,6},{4,0},{6,2},{8,12},{10,14},{12,8},{14,10},{16,20},{18,... | collective-permute-start | bytes 1769480 | tf_op jit(solution)/shard_map/ppermute | solution.py:730
  183.3 17.4 %collective-permute-start.30 = (bf16[96,1536]{1,0:T(8,128)(2,1)S(1)}, bf16[96,1536]{1,0:T(8,128)(2,1)S(1)}, u32[]{:S(2)}, u32[]{:S(2)}) collective-permute-start(bf16[96,1536]{1,0:T(8,128)(2,1)S(1)} %add_convert_fusion.10), channel_id=1, source_target_pairs={{0,8},{2,10},{4,12},{6,14},{8,0},{10,2},{12,4},{14,6},{16,24},{18,... | collective-permute-start | bytes 884744 | tf_op jit(solution)/shard_map/ppermute | solution.py:730
  184.9 15.8 %collective-permute-start.31 = (bf16[48,1536]{1,0:T(8,128)(2,1)S(1)}, bf16[48,1536]{1,0:T(8,128)(2,1)S(1)}, u32[]{:S(2)}, u32[]{:S(2)}) collective-permute-start(bf16[48,1536]{1,0:T(8,128)(2,1)S(1)} %add_convert_fusion.17), channel_id=1, source_target_pairs={{0,16},{2,18},{4,20},{6,22},{8,24},{10,26},{12,28},{14,30},{16,0},... | collective-permute-start | bytes 442376 | tf_op jit(solution)/shard_map/ppermute | solution.py:730
  200.8 27.6 %collective-permute-start.32 = (bf16[384,1536]{1,0:T(8,128)(2,1)S(1)}, bf16[384,1536]{1,0:T(8,128)(2,1)S(1)}, u32[]{:S(2)}, u32[]{:S(2)}) collective-permute-start(bf16[384,1536]{1,0:T(8,128)(2,1)S(1)} %get-tuple-element.259), channel_id=1, source_target_pairs={{0,2},{2,0},{4,6},{6,4},{8,10},{10,8},{12,14},{14,12},{16,18},{18,... | collective-permute-start | bytes 3538952 | tf_op jit(solution)/shard_map/ppermute | solution.py:730
  201.6 12.5 %collective-permute-start.33 = (bf16[96,1536]{1,0:T(8,128)(2,1)S(1)}, bf16[96,1536]{1,0:T(8,128)(2,1)S(1)}, u32[]{:S(2)}, u32[]{:S(2)}) collective-permute-start(bf16[96,1536]{1,0:T(8,128)(2,1)S(1)} %add_convert_fusion.9), channel_id=1, source_target_pairs={{0,8},{2,10},{4,12},{6,14},{8,0},{10,2},{12,4},{14,6},{16,24},{18,... | collective-permute-start | bytes 884744 | tf_op jit(solution)/shard_map/ppermute | solution.py:730
  202.2 11.9 %collective-permute-start.34 = (bf16[48,1536]{1,0:T(8,128)(2,1)S(1)}, bf16[48,1536]{1,0:T(8,128)(2,1)S(1)}, u32[]{:S(2)}, u32[]{:S(2)}) collective-permute-start(bf16[48,1536]{1,0:T(8,128)(2,1)S(1)} %add_convert_fusion.16), channel_id=1, source_target_pairs={{0,16},{2,18},{4,20},{6,22},{8,24},{10,26},{12,28},{14,30},{16,0},... | collective-permute-start | bytes 442376 | tf_op jit(solution)/shard_map/ppermute | solution.py:730
  202.6 27.6 %collective-permute-start.35 = (bf16[384,1536]{1,0:T(8,128)(2,1)S(1)}, bf16[384,1536]{1,0:T(8,128)(2,1)S(1)}, u32[]{:S(2)}, u32[]{:S(2)}) collective-permute-start(bf16[384,1536]{1,0:T(8,128)(2,1)S(1)} %get-tuple-element.269), channel_id=1, source_target_pairs={{0,4},{2,6},{4,0},{6,2},{8,12},{10,14},{12,8},{14,10},{16,20},{18,... | collective-permute-start | bytes 3538952 | tf_op jit(solution)/shard_map/ppermute | solution.py:730
  228.5 17.2 %collective-permute-start.36 = (bf16[192,1536]{1,0:T(8,128)(2,1)S(1)}, bf16[192,1536]{1,0:T(8,128)(2,1)S(1)}, u32[]{:S(2)}, u32[]{:S(2)}) collective-permute-start(bf16[192,1536]{1,0:T(8,128)(2,1)S(1)} %add_convert_fusion.1), channel_id=1, source_target_pairs={{0,8},{2,10},{4,12},{6,14},{8,0},{10,2},{12,4},{14,6},{16,24},{18,... | collective-permute-start | bytes 1769480 | tf_op jit(solution)/shard_map/ppermute | solution.py:730
  229.0 16.7 %collective-permute-start.38 = (bf16[192,1536]{1,0:T(8,128)(2,1)S(1)}, bf16[192,1536]{1,0:T(8,128)(2,1)S(1)}, u32[]{:S(2)}, u32[]{:S(2)}) collective-permute-start(bf16[192,1536]{1,0:T(8,128)(2,1)S(1)} %add_convert_fusion.2), channel_id=1, source_target_pairs={{0,2},{2,0},{4,6},{6,4},{8,10},{10,8},{12,14},{14,12},{16,18},{18,... | collective-permute-start | bytes 1769480 | tf_op jit(solution)/shard_map/ppermute | solution.py:730
  229.7 14.0 %collective-permute-start.37 = (bf16[48,1536]{1,0:T(8,128)(2,1)S(1)}, bf16[48,1536]{1,0:T(8,128)(2,1)S(1)}, u32[]{:S(2)}, u32[]{:S(2)}) collective-permute-start(bf16[48,1536]{1,0:T(8,128)(2,1)S(1)} %add_convert_fusion.15), channel_id=1, source_target_pairs={{0,16},{2,18},{4,20},{6,22},{8,24},{10,26},{12,28},{14,30},{16,0},... | collective-permute-start | bytes 442376 | tf_op jit(solution)/shard_map/ppermute | solution.py:730
  245.8 13.9 %collective-permute-start.40 = (bf16[192,1536]{1,0:T(8,128)(2,1)S(1)}, bf16[192,1536]{1,0:T(8,128)(2,1)S(1)}, u32[]{:S(2)}, u32[]{:S(2)}) collective-permute-start(bf16[192,1536]{1,0:T(8,128)(2,1)S(1)} %add_convert_fusion), channel_id=1, source_target_pairs={{0,2},{2,0},{4,6},{6,4},{8,10},{10,8},{12,14},{14,12},{16,18},{18,... | collective-permute-start | bytes 1769480 | tf_op jit(solution)/shard_map/ppermute | solution.py:730
  246.5 13.2 %collective-permute-start.41 = (bf16[96,1536]{1,0:T(8,128)(2,1)S(1)}, bf16[96,1536]{1,0:T(8,128)(2,1)S(1)}, u32[]{:S(2)}, u32[]{:S(2)}) collective-permute-start(bf16[96,1536]{1,0:T(8,128)(2,1)S(1)} %add_convert_fusion.8), channel_id=1, source_target_pairs={{0,16},{2,18},{4,20},{6,22},{8,24},{10,26},{12,28},{14,30},{16,0},... | collective-permute-start | bytes 884744 | tf_op jit(solution)/shard_map/ppermute | solution.py:730
  248.1 11.7 %collective-permute-start.42 = (bf16[96,1536]{1,0:T(8,128)(2,1)S(1)}, bf16[96,1536]{1,0:T(8,128)(2,1)S(1)}, u32[]{:S(2)}, u32[]{:S(2)}) collective-permute-start(bf16[96,1536]{1,0:T(8,128)(2,1)S(1)} %add_convert_fusion.7), channel_id=1, source_target_pairs={{0,4},{2,6},{4,0},{6,2},{8,12},{10,14},{12,8},{14,10},{16,20},{18,... | collective-permute-start | bytes 884744 | tf_op jit(solution)/shard_map/ppermute | solution.py:730
  248.2 7.5 %collective-permute-start.43 = (f32[18,768]{1,0:T(8,128)S(1)}, f32[18,768]{1,0:T(8,128)S(1)}, u32[]{:S(2)}, u32[]{:S(2)}) collective-permute-start(f32[18,768]{1,0:T(8,128)S(1)} %add.170), channel_id=1, source_target_pairs={{0,4},{2,6},{4,0},{6,2},{8,12},{10,14},{12,8},{14,10},{16,20},{18,... | collective-permute-start | bytes 165896 | tf_op jit(solution)/shard_map/ppermute | solution.py:777
  259.8 11.5 %collective-permute-start.44 = (bf16[96,1536]{1,0:T(8,128)(2,1)S(1)}, bf16[96,1536]{1,0:T(8,128)(2,1)S(1)}, u32[]{:S(2)}, u32[]{:S(2)}) collective-permute-start(bf16[96,1536]{1,0:T(8,128)(2,1)S(1)} %add_convert_fusion.6), channel_id=1, source_target_pairs={{0,8},{2,10},{4,12},{6,14},{8,0},{10,2},{12,4},{14,6},{16,24},{18,... | collective-permute-start | bytes 884744 | tf_op jit(solution)/shard_map/ppermute | solution.py:730
  260.0 8.0 %collective-permute-start.45 = (bf16[48,1536]{1,0:T(8,128)(2,1)S(1)}, bf16[48,1536]{1,0:T(8,128)(2,1)S(1)}, u32[]{:S(2)}, u32[]{:S(2)}) collective-permute-start(bf16[48,1536]{1,0:T(8,128)(2,1)S(1)} %add_convert_fusion.14), channel_id=1, source_target_pairs={{0,4},{2,6},{4,0},{6,2},{8,12},{10,14},{12,8},{14,10},{16,20},{18,... | collective-permute-start | bytes 442376 | tf_op jit(solution)/shard_map/ppermute | solution.py:730
  260.7 8.4 %collective-permute-start.46 = (bf16[48,1536]{1,0:T(8,128)(2,1)S(1)}, bf16[48,1536]{1,0:T(8,128)(2,1)S(1)}, u32[]{:S(2)}, u32[]{:S(2)}) collective-permute-start(bf16[48,1536]{1,0:T(8,128)(2,1)S(1)} %add_convert_fusion.13), channel_id=1, source_target_pairs={{0,16},{2,18},{4,20},{6,22},{8,24},{10,26},{12,28},{14,30},{16,0},... | collective-permute-start | bytes 442376 | tf_op jit(solution)/shard_map/ppermute | solution.py:730
  271.4 12.7 %collective-permute-start.48 = (bf16[48,1536]{1,0:T(8,128)(2,1)S(1)}, bf16[48,1536]{1,0:T(8,128)(2,1)S(1)}, u32[]{:S(2)}, u32[]{:S(2)}) collective-permute-start(bf16[48,1536]{1,0:T(8,128)(2,1)S(1)} %add_convert_fusion.12), channel_id=1, source_target_pairs={{0,16},{2,18},{4,20},{6,22},{8,24},{10,26},{12,28},{14,30},{16,0},... | collective-permute-start | bytes 442376 | tf_op jit(solution)/shard_map/ppermute | solution.py:730
  272.8 6.9 %collective-permute-start.49 = (f32[18,768]{1,0:T(8,128)S(1)}, f32[18,768]{1,0:T(8,128)S(1)}, u32[]{:S(2)}, u32[]{:S(2)}) collective-permute-start(f32[18,768]{1,0:T(8,128)S(1)} %add.185), channel_id=1, source_target_pairs={{0,8},{2,10},{4,12},{6,14},{8,0},{10,2},{12,4},{14,6},{16,24},{18,... | collective-permute-start | bytes 165896 | tf_op jit(solution)/shard_map/ppermute | solution.py:777
  272.8 11.3 %collective-permute-start.50 = (f32[18,768]{1,0:T(8,128)S(1)}, f32[18,768]{1,0:T(8,128)S(1)}, u32[]{:S(2)}, u32[]{:S(2)}) collective-permute-start(f32[18,768]{1,0:T(8,128)S(1)} %add.185), channel_id=1, source_target_pairs={{0,16},{2,18},{4,20},{6,22},{8,24},{10,26},{12,28},{14,30},{16,0},... | collective-permute-start | bytes 165896 | tf_op jit(solution)/shard_map/ppermute | solution.py:777
  274.5 9.6 %collective-permute-start.51 = (f32[18,768]{1,0:T(8,128)S(1)}, f32[18,768]{1,0:T(8,128)S(1)}, u32[]{:S(2)}, u32[]{:S(2)}) collective-permute-start(f32[18,768]{1,0:T(8,128)S(1)} %add.185), channel_id=1, source_target_pairs={{0,24},{2,26},{4,28},{6,30},{8,16},{10,18},{12,20},{14,22},{16,8},... | collective-permute-start | bytes 165896 | tf_op jit(solution)/shard_map/ppermute | solution.py:777
  (34 other events, 306.2 us)

commit v2 on v1

--- a/solution.py
+++ b/solution.py
@@ -1105,11 +1105,12 @@
     got_pre, got_mid_t = swap(pre_far), swap(mid_t)
     joint_far, qv_far = attend_back(saved[1]["far"], att_far, counts)
     got_joint = swap(joint_far)
-    counts_in = gate(counts, [], [down_1], [qv_far])
+    pre_own = gate(pre_own, [], [], [qv_far], [down_1])
+    pre_own = gate(pre_own, [down_1])
+    up_1 = DpSum(order_a, up_halves(1, order_a, pre_own, got_pre))
+    counts_in = gate(counts, [up_1])
     joint_own, qv_own = attend_back(saved[1]["own"], att_own, counts_in)
-    pre_own = gate(pre_own, after=[qv_own])
-    up_1 = DpSum(order_a, up_halves(1, order_a, pre_own, got_pre))
-    gain_in = gate(gain_in, [up_1])
+    gain_in = gate(gain_in, after=[qv_own])
     grad, sums_in, grad_t = entry_back(1, joint_own, joint_far, grad_mid, gain_in)
     got_grad_t = swap(grad_t)
     small[1] = (sums_mid, sums_in, qv_own, qv_far, upb_own, upb_far)
@@ -1133,10 +1134,11 @@
         0, grad, gain_in
     )
     got_pre, got_mid_t = swap(pre_far), swap(mid_t)
-    counts_in = gate(counts_in, [], [], [sums_mid], [up_1, rest_1])
+    counts_in = gate(counts_in, [], [up_1], [sums_mid], [rest_1])
     joint_far, qv_far = attend_back(saved[0]["far"], att_far, counts_in)
     got_joint = swap(joint_far)
-    pre_own = gate(pre_own, [down_1, up_1], [down_0], [qv_far])
+    pre_own = gate(pre_own, [], [], [qv_far], [down_0, up_1])
+    pre_own = gate(pre_own, [down_0, up_1, down_1])
     up_0 = DpSum(order_d, up_halves(0, order_d, pre_own, got_pre))
     counts_in = gate(counts_in, [up_0], [], [got_mid_t, got_joint])
     joint_own, qv_own = attend_back(saved[0]["own"], att_own, counts_in)
@@ -1153,7 +1155,7 @@
     )
     gain_in = gate(gain_in, [rest_0], [down_0, up_1, down_1], [qv_own])
     grad, sums_in = entry_back(0, joint_own, joint_far, grad_mid, gain_in)
-    last = gate(sums_in, [rest_1], [up_0, down_0, up_1])
+    last = gate(sums_in, [rest_1], [up_0])
     small[0] = (sums_mid, last, qv_own, qv_far, upb_own, upb_far)
     ins = [array for arrays in small for array in arrays]
     vector_shape = out(((7 + steps) * LAYERS, width), F32)
@@ -1166,11 +1168,13 @@
         [vector_shape] * 2,
         [whole()] * 2,
     )
-    vector = Everywhere(mine, far, [(1,), (0,), (2, 3), *[(bit,) for bit in tail]])
+    vector = Everywhere(mine, far, [(0, 1), (2,), (3,), *[(bit,) for bit in tail]])
+    last = gate(last, holds=[down_0])
+    last = gate(last, [], [rest_0, up_0, vector], [down_0.outgoing], [rest_1])
+    last = gate(last, [down_0, rest_1], [rest_0, up_0, vector])
     last = gate(last, [], [rest_0, up_0, down_0, rest_1, vector])
-    last = gate(last, [], [rest_0, up_0, rest_1, vector])
-    last = gate(last, [], [rest_0, up_0, rest_1, vector])
-    last = gate(last, [], [rest_0, vector])
+    last = gate(last, [], [rest_0, rest_1])
+    last = gate(last, [], [vector])
     while vector.flying():
         vector.turn()
     running = [down_1, up_1, rest_1, down_0, up_0, rest_0]
@@ -1192,11 +1196,12 @@
     (down_grad,) = finish(down_0, down_1, [(1, block, ff_half)])
     (up_grad,) = finish(up_0, up_1, [(1, block, ff_half)])
     qkv_grad, out_grad = finish(rest_0, rest_1, [(3, block, half), (1, block, half)])
+    total, qkv_grad = lax.optimization_barrier((vector.mine, qkv_grad))
     gain_grads, shift_grads, outb_grads, qv_grads, upb_grads = call(
         functools.partial(unpack_kernel, LAYERS),
         "unpack_small",
         (),
-        [vector.mine],
+        [total],
         [whole()],
         [
             out(ln_gain.shape, F32),

time: 286 us -> 284 us (level)
  waiting for transfers between devices: 62.5 us -> 53.8 us
  other arithmetic: 2.41 us -> 5.38 us
    ppermute x24, waiting for transfers between devices: 43.5 us -> 30.4 us  [start(): self.incoming = lax.ppermute(self.outgoing, 'dp', flip(self.order.pop(0)))]
    ppermute x5, waiting for transfers between devices: 12.5 us -> 18.2 us  [turn(): lax.ppermute(self.mine, 'dp', [(index, index ^ mask) for index in range(s...]
    ppermute x24, starting transfers between devices: 27.5 us -> 32.5 us  [start(): self.incoming = lax.ppermute(self.outgoing, 'dp', flip(self.order.pop(0)))]
    ppermute x5, starting transfers between devices: 8.31 us -> 4.74 us  [turn(): lax.ppermute(self.mine, 'dp', [(index, index ^ mask) for index in range(s...]
    convert_element_type x18, other arithmetic: 2.09 us -> 5.06 us  [halve(): sum((part[rows:].astype(F32) for part in parts)).astype(BF16)]
  transfers between devices with their start and end apart: 52 -> 52, of which waited for: 16 -> 13; matrix products, arithmetic and copies ran while one was open for 1% -> 2% of each run, Pallas kernels for 46% -> 47%
where the time goes in v2:
time: 284 us; the launch traced here: 283 us
  Pallas kernels  174 us (61%)
  waiting for transfers between devices  53.8 us (19%)
  starting transfers between devices  42.9 us (15%)
  local copies, waits for them, and re-layouts  5.87 us (2%)
  other arithmetic  5.38 us (2%)
    pallas_call x24, Pallas kernels, call(): pl.pallas_call(body, name=name, grid=grid, in_specs=in_specs, out_specs=o...  174 us
    ppermute x24, starting transfers between devices, start(): self.incoming = lax.ppermute(self.outgoing, 'dp', flip(self.order.pop(0)))  32.5 us
    ppermute x24, waiting for transfers between devices, start(): self.incoming = lax.ppermute(self.outgoing, 'dp', flip(self.order.pop(0)))  30.4 us
    ppermute x5, waiting for transfers between devices, turn(): lax.ppermute(self.mine, 'dp', [(index, index ^ mask) for index in range(s...  18.2 us
    ppermute x23, starting transfers between devices, swap(): return lax.ppermute(values, 'tensor', [(0, 1), (1, 0)])  5.72 us
  transfers between devices with their start and end apart: 52, of which 13 were waited for; matrix products, arithmetic and copies ran while one was open for 2% of the time, Pallas kernels for 47%

profile of v2, /device:TPU:0, one launch (start us, length us, event | category | flops | bytes accessed | tf_op | source)
XLA Modules:
  0.0 283.0 jit_solution(12605768143542113975)
XLA Ops:
  1.8 1.1 copy-done.15
  2.9 4.0 %prep.1 = (bf16[512,768]{1,0:T(8,128)(2,1)S(1)}, bf16[768,512]{1,0:T(8,128)(2,1)S(1)}, bf16[768,512]{1,0:T(8,128)(2,1)S(1)}, f32[512,768]{1,0:T(8,128)S(1)}) custom-call(bf16[512,768]{1,0:T(8,128)(2,1)S(1)} %bitcast.13, bf16[512,768]{1,0:T(8,128)(2,1)S(1)} %bitcast.16, f32[2,2,768]{2,1,0:T(2,128)S(1)} %copy-done.16, f32[2,2,768]{2,1,0:T(2,128)S(1)} %copy-done.17, ...), custom_call_target="tpu_custom_call" | custom-call | flops 18874368 | bytes 104832 | tf_op jit(solution)/shard_map/prep/pallas_call | solution.py:50
  8.4 14.3 %attend.2 = (bf16[3,512,384]{2,1,0:T(8,128)(2,1)S(1)}, bf16[3,512,384]{2,1,0:T(8,128)(2,1)S(1)}, bf16[512,384]{1,0:T(8,128)(2,1)S(1)}, bf16[512,384]{1,0:T(8,128...) custom-call(s32[1]{0:T(128)} %constant.14.clone.1.which, s32[4]{0:T(128)S(1)} %copy-done.21, ...), custom_call_target="tpu_custom_call" | custom-call | flops 34603008 | bytes 172608 | tf_op jit(solution)/shard_map/attend/pallas_call | solution.py:50
  22.8 1.3 collective-permute-done.5.down_far
  24.1 18.3 %feed.2 = (f32[512,768]{1,0:T(8,128)S(1)}, bf16[768,512]{1,0:T(8,128)(2,1)S(1)}, bf16[512,1536]{1,0:T(8,128)(2,1)}, bf16[512,1536]{1,0:T(8,128)(2,1)}, bf16[512,...) custom-call(s32[4]{0:T(128)S(1)} %copy-done.21, ...), custom_call_target="tpu_custom_call" | custom-call | flops 94371840 | bytes 560064 | tf_op jit(solution)/shard_map/feed/pallas_call | solution.py:50
  44.8 14.3 %attend.3 = (bf16[3,512,384]{2,1,0:T(8,128)(2,1)S(1)}, bf16[3,512,384]{2,1,0:T(8,128)(2,1)S(1)}, bf16[512,384]{1,0:T(8,128)(2,1)S(1)}, bf16[512,384]{1,0:T(8,128...) custom-call(s32[1]{0:T(128)} %constant.36.clone.1.which, s32[4]{0:T(128)S(1)} %copy-done.21, ...), custom_call_target="tpu_custom_call" | custom-call | flops 34603008 | bytes 172608 | tf_op jit(solution)/shard_map/attend/pallas_call | solution.py:50
  59.2 17.3 %feed.3 = (f32[512,768]{1,0:T(8,128)S(1)}, bf16[768,512]{1,0:T(8,128)(2,1)S(1)}, bf16[512,1536]{1,0:T(8,128)(2,1)}, bf16[512,1536]{1,0:T(8,128)(2,1)}, bf16[512,...) custom-call(s32[4]{0:T(128)S(1)} %copy-done.21, ...), custom_call_target="tpu_custom_call" | custom-call | flops 94371840 | bytes 547872 | tf_op jit(solution)/shard_map/feed/pallas_call | solution.py:50
  76.8 3.5 %collective-permute-done.12.refs_3_ = bf16[512,1536]{1,0:T(8,128)(2,1)S(1)} collective-permute-done((bf16[512,1536]{1,0:T(8,128)(2,1)}, bf16[512,1536]{1,0:T(8,128)(2,1)S(1)}, u32[]{:S(2)}, u32[]{:S(2)}) %collective-permute-start.12) | collective-permute-done | bytes 1572896 | tf_op jit(solution)/shard_map/ppermute | solution.py:799
  80.2 1.1 copy-done.14
  81.4 4.3 %down_grad.2 = (bf16[384,1536]{1,0:T(8,128)(2,1)S(1)}, bf16[384,1536]{1,0:T(8,128)(2,1)S(1)}) custom-call(bf16[768,512]{1,0:T(8,128)(2,1)S(1)} %copy-done.10, bf16[768,512]{1,0:T(8,128)(2,1)S(1)} %copy-done.14, bf16[512,1536]{1,0:T(8,128)(2,1)} %get-tuple-element.185.refs_2_, bf16[512,1536]{1,0:T(8,128)(2,1)S(1)} %collective-permute-done.12.refs_3_), custom_call_target="tpu_custom_call" | custom-call | flops 37748736 | bytes 110592 | tf_op jit(solution)/shard_map/down_grad/pallas_call | solution.py:50
  85.7 2.7 collective-permute-start.13
  88.4 17.9 %feed_back.2 = (bf16[512,1536]{1,0:T(8,128)(2,1)}, bf16[512,1536]{1,0:T(8,128)(2,1)}, f32[2,768]{1,0:T(2,128)S(1)}, f32[2,768]{1,0:T(2,128)S(1)}, f32[512,768]{1...) custom-call(s32[1]{0:T(128)} %constant.36.clone.1.which, ...), custom_call_target="tpu_custom_call" | custom-call | flops 94371840 | bytes 547392 | tf_op jit(solution)/shard_map/feed_back/pallas_call | solution.py:50
  106.9 5.6 %attend_back.4 = (bf16[3,512,384]{2,1,0:T(8,128)(2,1)S(1)}, f32[1,768]{1,0:T(1,128)S(1)}) custom-call(s32[4]{0:T(128)S(1)} %copy-done.21, bf16[3,512,384]{2,1,0:T(8,128)(2,1)S(1)} %get-tuple-element.193.joint, f32[12,1,256]{2,1,0:T(1,128)S(1)} %get-tuple-element.194.lse, bf16[512,384]{1,0:T(8,128)(2,1)S(1)} %get-tuple-element.195.grad_att), custom_call_target="tpu_custom_call" | custom-call | flops 7864320 | bytes 43248 | tf_op jit(solution)/shard_map/attend_back/pallas_call | solution.py:50
  112.5 2.4 collective-permute-done.13
  115.0 1.8 collective-permute-start.16
  117.4 3.3 %up_grad.2 = (bf16[384,1536]{1,0:T(8,128)(2,1)S(1)}, bf16[384,1536]{1,0:T(8,128)(2,1)S(1)}) custom-call(bf16[768,512]{1,0:T(8,128)(2,1)S(1)} %copy-done.12, bf16[768,512]{1,0:T(8,128)(2,1)S(1)} %collective-permute-done.11.refs_1_, bf16[512,1536]{1,0:T(8,128)(2,1)S(1)} %copy-done.6, bf16[512,1536]{1,0:T(8,128)(2,1)S(1)} %collective-permute-done.14.refs_3_), custom_call_target="tpu_custom_call" | custom-call | flops 37748736 | bytes 110592 | tf_op jit(solution)/shard_map/up_grad/pallas_call | solution.py:50
  120.7 1.6 collective-permute-start.21
  122.8 5.6 %attend_back.5 = (bf16[3,512,384]{2,1,0:T(8,128)(2,1)S(1)}, f32[1,768]{1,0:T(1,128)S(1)}) custom-call(s32[4]{0:T(128)S(1)} %copy-done.21, bf16[3,512,384]{2,1,0:T(8,128)(2,1)S(1)} %get-tuple-element.205.joint, f32[12,1,256]{2,1,0:T(1,128)S(1)} %get-tuple-element.206.lse, bf16[512,384]{1,0:T(8,128)(2,1)S(1)} %get-tuple-element.207.grad_att), custom_call_target="tpu_custom_call" | custom-call | flops 7864320 | bytes 43248 | tf_op jit(solution)/shard_map/attend_back/pallas_call | solution.py:50
  128.4 9.9 %entry_back.2 = (f32[512,768]{1,0:T(8,128)S(1)}, f32[2,768]{1,0:T(2,128)S(1)}, bf16[768,512]{1,0:T(8,128)(2,1)S(1)}) custom-call(bf16[3,512,384]{2,1,0:T(8,128)(2,1)S(1)} %get-tuple-element.217.joint_own.refs_2_, bf16[3,512,384]{2,1,0:T(8,128)(2,1)S(1)} %get-tuple-element.211.joint_far, bf16[2,3,768,384]{3,2,1,0:T(8,128)(2,1)} %bitcast.20, ...), custom_call_target="tpu_custom_call" | custom-call | flops 28311552 | bytes 252192 | tf_op jit(solution)/shard_map/entry_back/pallas_call | solution.py:50
  138.6 1.6 collective-permute-start.22
  140.2 4.2 %qkv_out_grad.2 = (bf16[384,1536]{1,0:T(8,128)(2,1)S(1)}, bf16[384,1536]{1,0:T(8,128)(2,1)S(1)}) custom-call(bf16[768,512]{1,0:T(8,128)(2,1)S(1)} %copy-done.8, bf16[768,512]{1,0:T(8,128)(2,1)S(1)} %collective-permute-done.15.refs_1_, bf16[3,512,384]{2,1,0:T(8,128)(2,1)S(1)} %get-tuple-element.217.joint_own.refs_2_, ...), custom_call_target="tpu_custom_call" | custom-call | flops 37748736 | bytes 135168 | tf_op jit(solution)/shard_map/qkv_out_grad/pallas_call | solution.py:50
  145.0 4.3 %down_grad.3 = (bf16[384,1536]{1,0:T(8,128)(2,1)S(1)}, bf16[384,1536]{1,0:T(8,128)(2,1)S(1)}) custom-call(bf16[768,512]{1,0:T(8,128)(2,1)S(1)} %get-tuple-element.220.refs_0_, bf16[768,512]{1,0:T(8,128)(2,1)S(1)} %collective-permute-done.20.refs_1_, bf16[512,1536]{1,0:T(8,128)(2,1)} %get-tuple-element.221.refs_2_, ...), custom_call_target="tpu_custom_call" | custom-call | flops 37748736 | bytes 110592 | tf_op jit(solution)/shard_map/down_grad/pallas_call | solution.py:50
  150.9 18.1 %feed_back.3 = (bf16[512,1536]{1,0:T(8,128)(2,1)}, bf16[512,1536]{1,0:T(8,128)(2,1)}, f32[2,768]{1,0:T(2,128)S(1)}, f32[2,768]{1,0:T(2,128)S(1)}, f32[512,768]{1...) custom-call(s32[1]{0:T(128)} %constant.14.clone.1.which, ...), custom_call_target="tpu_custom_call" | custom-call | flops 94371840 | bytes 547392 | tf_op jit(solution)/shard_map/feed_back/pallas_call | solution.py:50
  169.1 4.2 %collective-permute-done.24 = bf16[384,1536]{1,0:T(8,128)(2,1)} collective-permute-done((bf16[384,1536]{1,0:T(8,128)(2,1)S(1)}, bf16[384,1536]{1,0:T(8,128)(2,1)}, u32[]{:S(2)}, u32[]{:S(2)}) %collective-permute-start.24) | collective-permute-done | bytes 1179680 | tf_op jit(solution)/shard_map/ppermute | solution.py:730
  173.5 1.6 collective-permute-start.26
  175.2 5.6 %attend_back.6 = (bf16[3,512,384]{2,1,0:T(8,128)(2,1)S(1)}, f32[1,768]{1,0:T(1,128)S(1)}) custom-call(s32[4]{0:T(128)S(1)} %copy-done.21, bf16[3,512,384]{2,1,0:T(8,128)(2,1)S(1)} %get-tuple-element.239.joint, f32[12,1,256]{2,1,0:T(1,128)S(1)} %get-tuple-element.240.lse, bf16[512,384]{1,0:T(8,128)(2,1)S(1)} %get-tuple-element.241.grad_att), custom_call_target="tpu_custom_call" | custom-call | flops 7864320 | bytes 43248 | tf_op jit(solution)/shard_map/attend_back/pallas_call | solution.py:50
  182.4 1.2 copy-done.5
  183.6 3.3 %up_grad.3 = (bf16[384,1536]{1,0:T(8,128)(2,1)S(1)}, bf16[384,1536]{1,0:T(8,128)(2,1)S(1)}) custom-call(bf16[768,512]{1,0:T(8,128)(2,1)S(1)} %get-tuple-element.176.refs_0_, bf16[768,512]{1,0:T(8,128)(2,1)S(1)} %collective-permute-done.9.refs_1_, bf16[512,1536]{1,0:T(8,128)(2,1)S(1)} %copy-done.5, bf16[512,1536]{1,0:T(8,128)(2,1)S(1)} %collective-permute-done.27.refs_3_), custom_call_target="tpu_custom_call" | custom-call | flops 37748736 | bytes 110592 | tf_op jit(solution)/shard_map/up_grad/pallas_call | solution.py:50
  187.9 2.7 collective-permute-start.31
  190.8 1.2 add_convert_fusion.2
  192.0 5.6 %attend_back.7 = (bf16[3,512,384]{2,1,0:T(8,128)(2,1)S(1)}, f32[1,768]{1,0:T(1,128)S(1)}) custom-call(s32[4]{0:T(128)S(1)} %copy-done.21, bf16[3,512,384]{2,1,0:T(8,128)(2,1)S(1)} %get-tuple-element.254.joint, f32[12,1,256]{2,1,0:T(1,128)S(1)} %get-tuple-element.255.lse, bf16[512,384]{1,0:T(8,128)(2,1)S(1)} %get-tuple-element.256.grad_att), custom_call_target="tpu_custom_call" | custom-call | flops 7864320 | bytes 43248 | tf_op jit(solution)/shard_map/attend_back/pallas_call | solution.py:50
  197.6 4.2 %qkv_out_grad.3 = (bf16[384,1536]{1,0:T(8,128)(2,1)S(1)}, bf16[384,1536]{1,0:T(8,128)(2,1)S(1)}) custom-call(bf16[768,512]{1,0:T(8,128)(2,1)S(1)} %get-tuple-element.175.refs_0_, bf16[768,512]{1,0:T(8,128)(2,1)S(1)} %collective-permute-done.7.refs_1_, bf16[3,512,384]{2,1,0:T(8,128)(2,1)S(1)} %get-tuple-element.257.refs_2_.joint_own, ...), custom_call_target="tpu_custom_call" | custom-call | flops 37748736 | bytes 135168 | tf_op jit(solution)/shard_map/qkv_out_grad/pallas_call | solution.py:50
  202.9 1.5 collective-permute-start.34
  205.3 9.8 %entry_back.3 = (f32[512,768]{1,0:T(8,128)}, f32[2,768]{1,0:T(2,128)S(1)}) custom-call(bf16[3,512,384]{2,1,0:T(8,128)(2,1)S(1)} %get-tuple-element.257.refs_2_.joint_own, bf16[3,512,384]{2,1,0:T(8,128)(2,1)S(1)} %get-tuple-element.252.joint_far, bf16[2,3,768,384]{3,2,1,0:T(8,128)(2,1)} %bitcast.21, bf16[2,3,768,384]{3,2,1,0:T(8,128)(2,1)} %collective-permute-done.weight_far, ...), custom_call_target="tpu_custom_call" | custom-call | flops 28311552 | bytes 227616 | tf_op jit(solution)/shard_map/entry_back/pallas_call | solution.py:50
  215.3 1.4 collective-permute-start.35
  216.6 1.5 collective-permute-start.37
  218.3 11.9 %collective-permute-done.34 = bf16[384,1536]{1,0:T(8,128)(2,1)S(1)} collective-permute-done((bf16[384,1536]{1,0:T(8,128)(2,1)S(1)}, bf16[384,1536]{1,0:T(8,128)(2,1)S(1)}, u32[]{:S(2)}, u32[]{:S(2)}) %collective-permute-start.34) | collective-permute-done | bytes 1179680 | tf_op jit(solution)/shard_map/ppermute | solution.py:730
  230.5 1.6 collective-permute-start.41
  232.0 1.3 collective-permute-start.42
  234.2 1.6 collective-permute-start.39
  235.9 2.1 collective-permute-start.40
  238.0 1.1 add_convert_fusion.8
  239.4 9.8 %collective-permute-done.40 = bf16[96,1536]{1,0:T(8,128)(2,1)S(1)} collective-permute-done((bf16[96,1536]{1,0:T(8,128)(2,1)S(1)}, bf16[96,1536]{1,0:T(8,128)(2,1)S(1)}, u32[]{:S(2)}, u32[]{:S(2)}) %collective-permute-start.40) | collective-permute-done | bytes 294944 | tf_op jit(solution)/shard_map/ppermute | solution.py:730
  249.4 1.5 collective-permute-start.47
  251.7 3.1 %collective-permute-start.46 = (bf16[48,1536]{1,0:T(8,128)(2,1)S(1)}, bf16[48,1536]{1,0:T(8,128)(2,1)S(1)}, u32[]{:S(2)}, u32[]{:S(2)}) collective-permute-start(bf16[48,1536]{1,0:T(8,128)(2,1)S(1)} %add_convert_fusion.15), channel_id=1, source_target_pairs={{0,16},{2,18},{4,20},{6,22},{8,24},{10,26},{12,28},{14,30},{16,0},... | collective-permute-start | bytes 442376 | tf_op jit(solution)/shard_map/ppermute | solution.py:730
  255.0 7.5 %collective-permute-done.48 = f32[18,768]{1,0:T(8,128)S(1)} collective-permute-done((f32[18,768]{1,0:T(8,128)S(1)}, f32[18,768]{1,0:T(8,128)S(1)}, u32[]{:S(2)}, u32[]{:S(2)}) %collective-permute-start.48) | collective-permute-done | bytes 55328 | tf_op jit(solution)/shard_map/ppermute | solution.py:777
  264.6 2.0 collective-permute-start.50
  271.0 10.3 %collective-permute-done.49 = f32[18,768]{1,0:T(8,128)S(1)} collective-permute-done((f32[18,768]{1,0:T(8,128)S(1)}, f32[18,768]{1,0:T(8,128)S(1)}, u32[]{:S(2)}, u32[]{:S(2)}) %collective-permute-start.49) | collective-permute-done | bytes 55328 | tf_op jit(solution)/shard_map/ppermute | solution.py:777
  (186 shorter events, 25.3 us)
Async XLA Ops:
  0.7 6.7 %collective-permute-start = (bf16[2,3,768,384]{3,2,1,0:T(8,128)(2,1)}, bf16[2,3,768,384]{3,2,1,0:T(8,128)(2,1)}, u32[]{:S(2)}, u32[]{:S(2)}) collective-permute-start(bf16[2,3,768,384]{3,2,1,0:T(8,128)(2,1)} %bitcast.17), channel_id=1, source_target_pairs={{0,1},{1,0},{2,3},{3,2},{4,5},{5,4},{6,7},{7,6},{8,9},{9,8},{10,11... | collective-permute-start | bytes 10616840 | tf_op jit(solution)/shard_map/ppermute | solution.py:799
  7.4 15.4 %collective-permute-start.3 = (bf16[2,768,1536]{2,1,0:T(8,128)(2,1)}, bf16[2,768,1536]{2,1,0:T(8,128)(2,1)}, u32[]{:S(2)}, u32[]{:S(2)}) collective-permute-start(bf16[2,768,1536]{2,1,0:T(8,128)(2,1)} %up_own.7), channel_id=1, source_target_pairs={{0,1},{1,0},{2,3},{3,2},{4,5},{5,4},{6,7},{7,6},{8,9},{9,8},{10,11... | collective-permute-start | bytes 14155784 | tf_op jit(solution)/shard_map/ppermute | solution.py:799
  7.8 16.3 %collective-permute-start.5 = (bf16[2,1536,768]{2,1,0:T(8,128)(2,1)}, bf16[2,1536,768]{2,1,0:T(8,128)(2,1)}, u32[]{:S(2)}, u32[]{:S(2)}) collective-permute-start(bf16[2,1536,768]{2,1,0:T(8,128)(2,1)} %down_own.7), channel_id=1, source_target_pairs={{0,1},{1,0},{2,3},{3,2},{4,5},{5,4},{6,7},{7,6},{8,9},{9,8},{10,11... | collective-permute-start | bytes 14155784 | tf_op jit(solution)/shard_map/ppermute | solution.py:799
  7.9 14.9 %collective-permute-start.2 = (bf16[2,384,768]{2,1,0:T(8,128)(2,1)S(1)}, bf16[2,384,768]{2,1,0:T(8,128)(2,1)S(1)}, u32[]{:S(2)}, u32[]{:S(2)}) collective-permute-start(bf16[2,384,768]{2,1,0:T(8,128)(2,1)S(1)} %copy-done.25), channel_id=1, source_target_pairs={{0,1},{1,0},{2,3},{3,2},{4,5},{5,4},{6,7},{7,6},{8,9},{9,8},{10,11... | collective-permute-start | bytes 3538952 | tf_op jit(solution)/shard_map/ppermute | solution.py:799
  8.3 14.5 %collective-permute-start.4 = (f32[2,1536]{1,0:T(2,128)S(1)}, f32[2,1536]{1,0:T(2,128)S(1)}, u32[]{:S(2)}, u32[]{:S(2)}) collective-permute-start(f32[2,1536]{1,0:T(2,128)S(1)} %copy-done.20), channel_id=1, source_target_pairs={{0,1},{1,0},{2,3},{3,2},{4,5},{5,4},{6,7},{7,6},{8,9},{9,8},{10,11... | collective-permute-start | bytes 36872 | tf_op jit(solution)/shard_map/ppermute | solution.py:799
  43.4 15.8 %collective-permute-start.10 = (bf16[512,1536]{1,0:T(8,128)(2,1)}, bf16[512,1536]{1,0:T(8,128)(2,1)S(1)}, u32[]{:S(2)}, u32[]{:S(2)}) collective-permute-start(bf16[512,1536]{1,0:T(8,128)(2,1)} %get-tuple-element.177), channel_id=1, source_target_pairs={{0,1},{1,0},{2,3},{3,2},{4,5},{5,4},{6,7},{7,6},{8,9},{9,8},{10,11... | collective-permute-start | bytes 4718600 | tf_op jit(solution)/shard_map/ppermute | solution.py:799
  43.8 15.4 %collective-permute-start.6 = (bf16[768,512]{1,0:T(8,128)(2,1)S(1)}, bf16[768,512]{1,0:T(8,128)(2,1)S(1)}, u32[]{:S(2)}, u32[]{:S(2)}) collective-permute-start(bf16[768,512]{1,0:T(8,128)(2,1)S(1)} %get-tuple-element.174.refs_0_), channel_id=1, source_target_pairs={{0,1},{1,0},{2,3},{3,2},{4,5},{5,4},{6,7},{7,6},{8,9},{9,8},{10,11... | collective-permute-start | bytes 2359304 | tf_op jit(solution)/shard_map/ppermute | solution.py:799
  43.9 15.3 %collective-permute-start.7 = (bf16[768,512]{1,0:T(8,128)(2,1)S(1)}, bf16[768,512]{1,0:T(8,128)(2,1)S(1)}, u32[]{:S(2)}, u32[]{:S(2)}) collective-permute-start(bf16[768,512]{1,0:T(8,128)(2,1)S(1)} %get-tuple-element.175.refs_0_), channel_id=1, source_target_pairs={{0,1},{1,0},{2,3},{3,2},{4,5},{5,4},{6,7},{7,6},{8,9},{9,8},{10,11... | collective-permute-start | bytes 2359304 | tf_op jit(solution)/shard_map/ppermute | solution.py:799
  44.3 14.9 %collective-permute-start.9 = (bf16[768,512]{1,0:T(8,128)(2,1)S(1)}, bf16[768,512]{1,0:T(8,128)(2,1)S(1)}, u32[]{:S(2)}, u32[]{:S(2)}) collective-permute-start(bf16[768,512]{1,0:T(8,128)(2,1)S(1)} %get-tuple-element.176.refs_0_), channel_id=1, source_target_pairs={{0,1},{1,0},{2,3},{3,2},{4,5},{5,4},{6,7},{7,6},{8,9},{9,8},{10,11... | collective-permute-start | bytes 2359304 | tf_op jit(solution)/shard_map/ppermute | solution.py:799
  44.4 14.8 %collective-permute-start.8 = (bf16[512,384]{1,0:T(8,128)(2,1)S(1)}, bf16[512,384]{1,0:T(8,128)(2,1)S(1)}, u32[]{:S(2)}, u32[]{:S(2)}) collective-permute-start(bf16[512,384]{1,0:T(8,128)(2,1)S(1)} %get-tuple-element.166.att_far), channel_id=1, source_target_pairs={{0,1},{1,0},{2,3},{3,2},{4,5},{5,4},{6,7},{7,6},{8,9},{9,8},{10,11... | collective-permute-start | bytes 1179656 | tf_op jit(solution)/shard_map/ppermute | solution.py:799
  85.7 29.2 %collective-permute-start.13 = (bf16[384,1536]{1,0:T(8,128)(2,1)S(1)}, bf16[384,1536]{1,0:T(8,128)(2,1)S(1)}, u32[]{:S(2)}, u32[]{:S(2)}) collective-permute-start(bf16[384,1536]{1,0:T(8,128)(2,1)S(1)} %get-tuple-element.192), channel_id=1, source_target_pairs={{0,2},{2,0},{4,6},{6,4},{8,10},{10,8},{12,14},{14,12},{16,18},{18,... | collective-permute-start | bytes 3538952 | tf_op jit(solution)/shard_map/ppermute | solution.py:730
  106.3 11.1 %collective-permute-start.14 = (bf16[512,1536]{1,0:T(8,128)(2,1)}, bf16[512,1536]{1,0:T(8,128)(2,1)S(1)}, u32[]{:S(2)}, u32[]{:S(2)}) collective-permute-start(bf16[512,1536]{1,0:T(8,128)(2,1)} %get-tuple-element.201), channel_id=1, source_target_pairs={{0,1},{1,0},{2,3},{3,2},{4,5},{5,4},{6,7},{7,6},{8,9},{9,8},{10,11... | collective-permute-start | bytes 4718600 | tf_op jit(solution)/shard_map/ppermute | solution.py:799
  106.5 10.9 %collective-permute-start.11 = (bf16[768,512]{1,0:T(8,128)(2,1)S(1)}, bf16[768,512]{1,0:T(8,128)(2,1)S(1)}, u32[]{:S(2)}, u32[]{:S(2)}) collective-permute-start(bf16[768,512]{1,0:T(8,128)(2,1)S(1)} %get-tuple-element.181.refs_0_), channel_id=1, source_target_pairs={{0,1},{1,0},{2,3},{3,2},{4,5},{5,4},{6,7},{7,6},{8,9},{9,8},{10,11... | collective-permute-start | bytes 2359304 | tf_op jit(solution)/shard_map/ppermute | solution.py:799
  115.0 23.2 %collective-permute-start.16 = (bf16[192,1536]{1,0:T(8,128)(2,1)S(1)}, bf16[192,1536]{1,0:T(8,128)(2,1)S(1)}, u32[]{:S(2)}, u32[]{:S(2)}) collective-permute-start(bf16[192,1536]{1,0:T(8,128)(2,1)S(1)} %add_convert_fusion.5), channel_id=1, source_target_pairs={{0,4},{2,6},{4,0},{6,2},{8,12},{10,14},{12,8},{14,10},{16,20},{18,... | collective-permute-start | bytes 1769480 | tf_op jit(solution)/shard_map/ppermute | solution.py:730
  116.9 23.3 %collective-permute-start.17 = (bf16[3,512,384]{2,1,0:T(8,128)(2,1)S(1)}, bf16[3,512,384]{2,1,0:T(8,128)(2,1)S(1)}, u32[]{:S(2)}, u32[]{:S(2)}) collective-permute-start(bf16[3,512,384]{2,1,0:T(8,128)(2,1)S(1)} %get-tuple-element.211.joint_far), channel_id=1, source_target_pairs={{0,1},{1,0},{2,3},{3,2},{4,5},{5,4},{6,7},{7,6},{8,9},{9,8},{10,11... | collective-permute-start | bytes 3538952 | tf_op jit(solution)/shard_map/ppermute | solution.py:799
  120.7 28.6 %collective-permute-start.21 = (bf16[384,1536]{1,0:T(8,128)(2,1)S(1)}, bf16[384,1536]{1,0:T(8,128)(2,1)S(1)}, u32[]{:S(2)}, u32[]{:S(2)}) collective-permute-start(bf16[384,1536]{1,0:T(8,128)(2,1)S(1)} %get-tuple-element.224), channel_id=1, source_target_pairs={{0,2},{2,0},{4,6},{6,4},{8,10},{10,8},{12,14},{14,12},{16,18},{18,... | collective-permute-start | bytes 3538952 | tf_op jit(solution)/shard_map/ppermute | solution.py:730
  122.3 16.3 %collective-permute-start.15 = (bf16[768,512]{1,0:T(8,128)(2,1)S(1)}, bf16[768,512]{1,0:T(8,128)(2,1)S(1)}, u32[]{:S(2)}, u32[]{:S(2)}) collective-permute-start(bf16[768,512]{1,0:T(8,128)(2,1)S(1)} %copy-done.8), channel_id=1, source_target_pairs={{0,1},{1,0},{2,3},{3,2},{4,5},{5,4},{6,7},{7,6},{8,9},{9,8},{10,11... | collective-permute-start | bytes 2359304 | tf_op jit(solution)/shard_map/ppermute | solution.py:799
  122.3 17.9 %collective-permute-start.18 = (bf16[768,512]{1,0:T(8,128)(2,1)S(1)}, bf16[768,512]{1,0:T(8,128)(2,1)S(1)}, u32[]{:S(2)}, u32[]{:S(2)}) collective-permute-start(bf16[768,512]{1,0:T(8,128)(2,1)S(1)} %get-tuple-element.218.refs_4_), channel_id=1, source_target_pairs={{0,1},{1,0},{2,3},{3,2},{4,5},{5,4},{6,7},{7,6},{8,9},{9,8},{10,11... | collective-permute-start | bytes 2359304 | tf_op jit(solution)/shard_map/ppermute | solution.py:799
  138.3 6.7 %collective-permute-start.20 = (bf16[768,512]{1,0:T(8,128)(2,1)S(1)}, bf16[768,512]{1,0:T(8,128)(2,1)S(1)}, u32[]{:S(2)}, u32[]{:S(2)}) collective-permute-start(bf16[768,512]{1,0:T(8,128)(2,1)S(1)} %get-tuple-element.220.refs_0_), channel_id=1, source_target_pairs={{0,1},{1,0},{2,3},{3,2},{4,5},{5,4},{6,7},{7,6},{8,9},{9,8},{10,11... | collective-permute-start | bytes 2359304 | tf_op jit(solution)/shard_map/ppermute | solution.py:799
  138.6 10.7 %collective-permute-start.22 = (bf16[96,1536]{1,0:T(8,128)(2,1)S(1)}, bf16[96,1536]{1,0:T(8,128)(2,1)S(1)}, u32[]{:S(2)}, u32[]{:S(2)}) collective-permute-start(bf16[96,1536]{1,0:T(8,128)(2,1)S(1)} %add_convert_fusion.11), channel_id=1, source_target_pairs={{0,8},{2,10},{4,12},{6,14},{8,0},{10,2},{12,4},{14,6},{16,24},{18,... | collective-permute-start | bytes 884744 | tf_op jit(solution)/shard_map/ppermute | solution.py:730
  144.5 28.9 %collective-permute-start.24 = (bf16[384,1536]{1,0:T(8,128)(2,1)S(1)}, bf16[384,1536]{1,0:T(8,128)(2,1)}, u32[]{:S(2)}, u32[]{:S(2)}) collective-permute-start(bf16[384,1536]{1,0:T(8,128)(2,1)S(1)} %get-tuple-element.227), channel_id=1, source_target_pairs={{0,8},{2,10},{4,12},{6,14},{8,0},{10,2},{12,4},{14,6},{16,24},{18,... | collective-permute-start | bytes 3538952 | tf_op jit(solution)/shard_map/ppermute | solution.py:730
  149.5 23.9 %collective-permute-start.23 = (bf16[192,1536]{1,0:T(8,128)(2,1)S(1)}, bf16[192,1536]{1,0:T(8,128)(2,1)S(1)}, u32[]{:S(2)}, u32[]{:S(2)}) collective-permute-start(bf16[192,1536]{1,0:T(8,128)(2,1)S(1)} %add_convert_fusion.4), channel_id=1, source_target_pairs={{0,4},{2,6},{4,0},{6,2},{8,12},{10,14},{12,8},{14,10},{16,20},{18,... | collective-permute-start | bytes 1769480 | tf_op jit(solution)/shard_map/ppermute | solution.py:730
  150.1 32.1 %collective-permute-start.25 = (bf16[384,1536]{1,0:T(8,128)(2,1)S(1)}, bf16[384,1536]{1,0:T(8,128)(2,1)S(1)}, u32[]{:S(2)}, u32[]{:S(2)}) collective-permute-start(bf16[384,1536]{1,0:T(8,128)(2,1)S(1)} %get-tuple-element.237), channel_id=1, source_target_pairs={{0,2},{2,0},{4,6},{6,4},{8,10},{10,8},{12,14},{14,12},{16,18},{18,... | collective-permute-start | bytes 3538952 | tf_op jit(solution)/shard_map/ppermute | solution.py:730
  169.1 13.3 %collective-permute-start.27 = (bf16[512,1536]{1,0:T(8,128)(2,1)}, bf16[512,1536]{1,0:T(8,128)(2,1)S(1)}, u32[]{:S(2)}, u32[]{:S(2)}) collective-permute-start(bf16[512,1536]{1,0:T(8,128)(2,1)} %get-tuple-element.249), channel_id=1, source_target_pairs={{0,1},{1,0},{2,3},{3,2},{4,5},{5,4},{6,7},{7,6},{8,9},{9,8},{10,11... | collective-permute-start | bytes 4718600 | tf_op jit(solution)/shard_map/ppermute | solution.py:799
  173.5 8.6 %collective-permute-start.26 = (bf16[96,1536]{1,0:T(8,128)(2,1)S(1)}, bf16[96,1536]{1,0:T(8,128)(2,1)S(1)}, u32[]{:S(2)}, u32[]{:S(2)}) collective-permute-start(bf16[96,1536]{1,0:T(8,128)(2,1)S(1)} %add_convert_fusion.10), channel_id=1, source_target_pairs={{0,8},{2,10},{4,12},{6,14},{8,0},{10,2},{12,4},{14,6},{16,24},{18,... | collective-permute-start | bytes 884744 | tf_op jit(solution)/shard_map/ppermute | solution.py:730
  180.7 6.2 %collective-permute-start.29 = (bf16[3,512,384]{2,1,0:T(8,128)(2,1)S(1)}, bf16[3,512,384]{2,1,0:T(8,128)(2,1)S(1)}, u32[]{:S(2)}, u32[]{:S(2)}) collective-permute-start(bf16[3,512,384]{2,1,0:T(8,128)(2,1)S(1)} %get-tuple-element.252.joint_far), channel_id=1, source_target_pairs={{0,1},{1,0},{2,3},{3,2},{4,5},{5,4},{6,7},{7,6},{8,9},{9,8},{10,11... | collective-permute-start | bytes 3538952 | tf_op jit(solution)/shard_map/ppermute | solution.py:799
  186.9 28.2 %collective-permute-start.33 = (bf16[384,1536]{1,0:T(8,128)(2,1)S(1)}, bf16[384,1536]{1,0:T(8,128)(2,1)S(1)}, u32[]{:S(2)}, u32[]{:S(2)}) collective-permute-start(bf16[384,1536]{1,0:T(8,128)(2,1)S(1)} %get-tuple-element.271), channel_id=1, source_target_pairs={{0,2},{2,0},{4,6},{6,4},{8,10},{10,8},{12,14},{14,12},{16,18},{18,... | collective-permute-start | bytes 3538952 | tf_op jit(solution)/shard_map/ppermute | solution.py:730
  187.5 15.4 %collective-permute-start.30 = (bf16[192,1536]{1,0:T(8,128)(2,1)S(1)}, bf16[192,1536]{1,0:T(8,128)(2,1)S(1)}, u32[]{:S(2)}, u32[]{:S(2)}) collective-permute-start(bf16[192,1536]{1,0:T(8,128)(2,1)S(1)} %add_convert_fusion.3), channel_id=1, source_target_pairs={{0,4},{2,6},{4,0},{6,2},{8,12},{10,14},{12,8},{14,10},{16,20},{18,... | collective-permute-start | bytes 1769480 | tf_op jit(solution)/shard_map/ppermute | solution.py:730
  187.9 14.0 %collective-permute-start.31 = (bf16[48,1536]{1,0:T(8,128)(2,1)S(1)}, bf16[48,1536]{1,0:T(8,128)(2,1)S(1)}, u32[]{:S(2)}, u32[]{:S(2)}) collective-permute-start(bf16[48,1536]{1,0:T(8,128)(2,1)S(1)} %add_convert_fusion.17), channel_id=1, source_target_pairs={{0,16},{2,18},{4,20},{6,22},{8,24},{10,26},{12,28},{14,30},{16,0},... | collective-permute-start | bytes 442376 | tf_op jit(solution)/shard_map/ppermute | solution.py:730
  190.6 12.3 %collective-permute-start.32 = (bf16[48,1536]{1,0:T(8,128)(2,1)S(1)}, bf16[48,1536]{1,0:T(8,128)(2,1)S(1)}, u32[]{:S(2)}, u32[]{:S(2)}) collective-permute-start(bf16[48,1536]{1,0:T(8,128)(2,1)S(1)} %add_convert_fusion.16), channel_id=1, source_target_pairs={{0,16},{2,18},{4,20},{6,22},{8,24},{10,26},{12,28},{14,30},{16,0},... | collective-permute-start | bytes 442376 | tf_op jit(solution)/shard_map/ppermute | solution.py:730
  202.9 27.4 %collective-permute-start.34 = (bf16[384,1536]{1,0:T(8,128)(2,1)S(1)}, bf16[384,1536]{1,0:T(8,128)(2,1)S(1)}, u32[]{:S(2)}, u32[]{:S(2)}) collective-permute-start(bf16[384,1536]{1,0:T(8,128)(2,1)S(1)} %get-tuple-element.279), channel_id=1, source_target_pairs={{0,4},{2,6},{4,0},{6,2},{8,12},{10,14},{12,8},{14,10},{16,20},{18,... | collective-permute-start | bytes 3538952 | tf_op jit(solution)/shard_map/ppermute | solution.py:730
  204.5 13.7 %collective-permute-start.38 = (bf16[96,1536]{1,0:T(8,128)(2,1)S(1)}, bf16[96,1536]{1,0:T(8,128)(2,1)S(1)}, u32[]{:S(2)}, u32[]{:S(2)}) collective-permute-start(bf16[96,1536]{1,0:T(8,128)(2,1)S(1)} %add_convert_fusion.9), channel_id=1, source_target_pairs={{0,8},{2,10},{4,12},{6,14},{8,0},{10,2},{12,4},{14,6},{16,24},{18,... | collective-permute-start | bytes 884744 | tf_op jit(solution)/shard_map/ppermute | solution.py:730
  215.3 15.0 %collective-permute-start.35 = (bf16[192,1536]{1,0:T(8,128)(2,1)S(1)}, bf16[192,1536]{1,0:T(8,128)(2,1)S(1)}, u32[]{:S(2)}, u32[]{:S(2)}) collective-permute-start(bf16[192,1536]{1,0:T(8,128)(2,1)S(1)} %add_convert_fusion.1), channel_id=1, source_target_pairs={{0,8},{2,10},{4,12},{6,14},{8,0},{10,2},{12,4},{14,6},{16,24},{18,... | collective-permute-start | bytes 1769480 | tf_op jit(solution)/shard_map/ppermute | solution.py:730
  216.6 13.8 %collective-permute-start.37 = (bf16[192,1536]{1,0:T(8,128)(2,1)S(1)}, bf16[192,1536]{1,0:T(8,128)(2,1)S(1)}, u32[]{:S(2)}, u32[]{:S(2)}) collective-permute-start(bf16[192,1536]{1,0:T(8,128)(2,1)S(1)} %add_convert_fusion.2), channel_id=1, source_target_pairs={{0,2},{2,0},{4,6},{6,4},{8,10},{10,8},{12,14},{14,12},{16,18},{18,... | collective-permute-start | bytes 1769480 | tf_op jit(solution)/shard_map/ppermute | solution.py:730
  218.2 12.1 %collective-permute-start.36 = (f32[18,768]{1,0:T(8,128)S(1)}, f32[18,768]{1,0:T(8,128)S(1)}, u32[]{:S(2)}, u32[]{:S(2)}) collective-permute-start(f32[18,768]{1,0:T(8,128)S(1)} %get-tuple-element.282), channel_id=1, source_target_pairs={{0,1},{1,0},{2,3},{3,2},{4,5},{5,4},{6,7},{7,6},{8,9},{9,8},{10,11... | collective-permute-start | bytes 165896 | tf_op jit(solution)/shard_map/ppermute | solution.py:799
  230.5 8.6 %collective-permute-start.41 = (f32[18,768]{1,0:T(8,128)S(1)}, f32[18,768]{1,0:T(8,128)S(1)}, u32[]{:S(2)}, u32[]{:S(2)}) collective-permute-start(f32[18,768]{1,0:T(8,128)S(1)} %add.170), channel_id=1, source_target_pairs={{0,2},{2,0},{4,6},{6,4},{8,10},{10,8},{12,14},{14,12},{16,18},{18,... | collective-permute-start | bytes 165896 | tf_op jit(solution)/shard_map/ppermute | solution.py:777
  232.0 7.0 %collective-permute-start.42 = (f32[18,768]{1,0:T(8,128)S(1)}, f32[18,768]{1,0:T(8,128)S(1)}, u32[]{:S(2)}, u32[]{:S(2)}) collective-permute-start(f32[18,768]{1,0:T(8,128)S(1)} %add.170), channel_id=1, source_target_pairs={{0,4},{2,6},{4,0},{6,2},{8,12},{10,14},{12,8},{14,10},{16,20},{18,... | collective-permute-start | bytes 165896 | tf_op jit(solution)/shard_map/ppermute | solution.py:777
  233.3 6.1 %collective-permute-start.43 = (f32[18,768]{1,0:T(8,128)S(1)}, f32[18,768]{1,0:T(8,128)S(1)}, u32[]{:S(2)}, u32[]{:S(2)}) collective-permute-start(f32[18,768]{1,0:T(8,128)S(1)} %add.170), channel_id=1, source_target_pairs={{0,6},{2,4},{4,2},{6,0},{8,14},{10,12},{12,10},{14,8},{16,22},{18,... | collective-permute-start | bytes 165896 | tf_op jit(solution)/shard_map/ppermute | solution.py:777
  234.2 15.1 %collective-permute-start.39 = (bf16[192,1536]{1,0:T(8,128)(2,1)S(1)}, bf16[192,1536]{1,0:T(8,128)(2,1)S(1)}, u32[]{:S(2)}, u32[]{:S(2)}) collective-permute-start(bf16[192,1536]{1,0:T(8,128)(2,1)S(1)} %add_convert_fusion), channel_id=1, source_target_pairs={{0,2},{2,0},{4,6},{6,4},{8,10},{10,8},{12,14},{14,12},{16,18},{18,... | collective-permute-start | bytes 1769480 | tf_op jit(solution)/shard_map/ppermute | solution.py:730
  235.9 13.4 %collective-permute-start.40 = (bf16[96,1536]{1,0:T(8,128)(2,1)S(1)}, bf16[96,1536]{1,0:T(8,128)(2,1)S(1)}, u32[]{:S(2)}, u32[]{:S(2)}) collective-permute-start(bf16[96,1536]{1,0:T(8,128)(2,1)S(1)} %add_convert_fusion.7), channel_id=1, source_target_pairs={{0,16},{2,18},{4,20},{6,22},{8,24},{10,26},{12,28},{14,30},{16,0},... | collective-permute-start | bytes 884744 | tf_op jit(solution)/shard_map/ppermute | solution.py:730
  249.3 13.1 %collective-permute-start.44 = (bf16[96,1536]{1,0:T(8,128)(2,1)S(1)}, bf16[96,1536]{1,0:T(8,128)(2,1)S(1)}, u32[]{:S(2)}, u32[]{:S(2)}) collective-permute-start(bf16[96,1536]{1,0:T(8,128)(2,1)S(1)} %add_convert_fusion.6), channel_id=1, source_target_pairs={{0,8},{2,10},{4,12},{6,14},{8,0},{10,2},{12,4},{14,6},{16,24},{18,... | collective-permute-start | bytes 884744 | tf_op jit(solution)/shard_map/ppermute | solution.py:730
  249.4 13.1 %collective-permute-start.47 = (bf16[96,1536]{1,0:T(8,128)(2,1)S(1)}, bf16[96,1536]{1,0:T(8,128)(2,1)S(1)}, u32[]{:S(2)}, u32[]{:S(2)}) collective-permute-start(bf16[96,1536]{1,0:T(8,128)(2,1)S(1)} %add_convert_fusion.8), channel_id=1, source_target_pairs={{0,4},{2,6},{4,0},{6,2},{8,12},{10,14},{12,8},{14,10},{16,20},{18,... | collective-permute-start | bytes 884744 | tf_op jit(solution)/shard_map/ppermute | solution.py:730
  251.0 11.4 %collective-permute-start.45 = (bf16[48,1536]{1,0:T(8,128)(2,1)S(1)}, bf16[48,1536]{1,0:T(8,128)(2,1)S(1)}, u32[]{:S(2)}, u32[]{:S(2)}) collective-permute-start(bf16[48,1536]{1,0:T(8,128)(2,1)S(1)} %add_convert_fusion.14), channel_id=1, source_target_pairs={{0,4},{2,6},{4,0},{6,2},{8,12},{10,14},{12,8},{14,10},{16,20},{18,... | collective-permute-start | bytes 442376 | tf_op jit(solution)/shard_map/ppermute | solution.py:730
  251.7 10.8 %collective-permute-start.46 = (bf16[48,1536]{1,0:T(8,128)(2,1)S(1)}, bf16[48,1536]{1,0:T(8,128)(2,1)S(1)}, u32[]{:S(2)}, u32[]{:S(2)}) collective-permute-start(bf16[48,1536]{1,0:T(8,128)(2,1)S(1)} %add_convert_fusion.15), channel_id=1, source_target_pairs={{0,16},{2,18},{4,20},{6,22},{8,24},{10,26},{12,28},{14,30},{16,0},... | collective-permute-start | bytes 442376 | tf_op jit(solution)/shard_map/ppermute | solution.py:730
  254.8 7.7 %collective-permute-start.48 = (f32[18,768]{1,0:T(8,128)S(1)}, f32[18,768]{1,0:T(8,128)S(1)}, u32[]{:S(2)}, u32[]{:S(2)}) collective-permute-start(f32[18,768]{1,0:T(8,128)S(1)} %add_add_fusion), channel_id=1, source_target_pairs={{0,8},{2,10},{4,12},{6,14},{8,0},{10,2},{12,4},{14,6},{16,24},{18,... | collective-permute-start | bytes 165896 | tf_op jit(solution)/shard_map/ppermute | solution.py:777
  263.5 17.9 %collective-permute-start.51 = (bf16[48,1536]{1,0:T(8,128)(2,1)S(1)}, bf16[48,1536]{1,0:T(8,128)(2,1)S(1)}, u32[]{:S(2)}, u32[]{:S(2)}) collective-permute-start(bf16[48,1536]{1,0:T(8,128)(2,1)S(1)} %add_convert_fusion.12), channel_id=1, source_target_pairs={{0,16},{2,18},{4,20},{6,22},{8,24},{10,26},{12,28},{14,30},{16,0},... | collective-permute-start | bytes 442376 | tf_op jit(solution)/shard_map/ppermute | solution.py:730
  264.6 16.8 %collective-permute-start.50 = (bf16[48,1536]{1,0:T(8,128)(2,1)S(1)}, bf16[48,1536]{1,0:T(8,128)(2,1)S(1)}, u32[]{:S(2)}, u32[]{:S(2)}) collective-permute-start(bf16[48,1536]{1,0:T(8,128)(2,1)S(1)} %add_convert_fusion.13), channel_id=1, source_target_pairs={{0,16},{2,18},{4,20},{6,22},{8,24},{10,26},{12,28},{14,30},{16,0},... | collective-permute-start | bytes 442376 | tf_op jit(solution)/shard_map/ppermute | solution.py:730
  266.7 14.7 %collective-permute-start.49 = (f32[18,768]{1,0:T(8,128)S(1)}, f32[18,768]{1,0:T(8,128)S(1)}, u32[]{:S(2)}, u32[]{:S(2)}) collective-permute-start(f32[18,768]{1,0:T(8,128)S(1)} %add.184), channel_id=1, source_target_pairs={{0,16},{2,18},{4,20},{6,22},{8,24},{10,26},{12,28},{14,30},{16,0},... | collective-permute-start | bytes 165896 | tf_op jit(solution)/shard_map/ppermute | solution.py:777
  (33 other events, 280.3 us)

commit v3 on v2

--- a/solution.py
+++ b/solution.py
@@ -185,23 +185,28 @@
         rows = pl.ds(pl.multiple_of(image * slots, slots), slots)
         lanes = pl.ds(pl.multiple_of(pair * 2 * HEAD_DIM, 2 * HEAD_DIM), 2 * HEAD_DIM)
         valid = key_index < own_count(counts, image, normed.shape[0] // slots)
-        for joint, attended, lse in (
-            (joint_own, att_own, lse_own),
-            (joint_far, att_far, lse_far),
-        ):
+        sets = ((joint_own, att_own, lse_own), (joint_far, att_far, lse_far))
+        heads = []
+        for joint, _, _ in sets:
             queries = joint[0, rows, lanes]
             keys_in = joint[1, rows, lanes] * jnp.asarray(scale, BF16)
-            values_t = joint[2, rows, lanes].T
+            for side in range(2):
+                keys_side = jnp.where(masks[side], keys_in, jnp.zeros_like(keys_in))
+                heads.append(dot_nt(keys_side, queries))
+        values_t = [joint[2, rows, lanes].T for joint, _, _ in sets]
+        heads = [jnp.where(valid, scores, NEGATIVE) for scores in heads]
+        largest = [jnp.max(scores, axis=0, keepdims=True) for scores in heads]
+        heads = [jnp.exp(scores - top) for scores, top in zip(heads, largest)]
+        totals = [jnp.sum(exponent, axis=0, keepdims=True) for exponent in heads]
+        heads = [(exponent * (1.0 / total)).astype(BF16) for exponent, total in zip(heads, totals)]
+        for which_set, (_, attended, lse) in enumerate(sets):
             parts = []
             for side in range(2):
-                keys_side = jnp.where(masks[side], keys_in, jnp.zeros_like(keys_in))
-                scores = jnp.where(valid, dot_nt(keys_side, queries), NEGATIVE)
-                largest = jnp.max(scores, axis=0, keepdims=True)
-                exponent = jnp.exp(scores - largest)
-                total = jnp.sum(exponent, axis=0, keepdims=True)
-                probs = (exponent * (1.0 / total)).astype(BF16)
-                parts.append(dot(values_t[side * HEAD_DIM : (side + 1) * HEAD_DIM], probs))
-                lse[2 * index + side] = largest + jnp.log(total)
+                head = 2 * which_set + side
+                lse[2 * index + side] = largest[head] + jnp.log(totals[head])
+                parts.append(
+                    dot(values_t[which_set][side * HEAD_DIM : (side + 1) * HEAD_DIM], heads[head])
+                )
             attended[rows, lanes] = jnp.concatenate(parts, axis=0).T.astype(BF16)
         return carry
 
@@ -280,7 +285,7 @@
     up_in[0].wait()
     by_blocks(pre.at[0], normed, lambda: w_up[0], dot)
     by_blocks(normed_t, order, lambda: normed[...], dot_nt)
-    rows = 128
+    rows = 256
     out_copies = []
     for unit in range(units):
         side, part = unit // tiles, unit % tiles
@@ -501,18 +506,27 @@
         keys_scaled = keys_in * jnp.asarray(scale, BF16)
         valid = key_index < own_count(counts, image, grad_att.shape[0] // slots)
         zeros = jnp.zeros_like(keys_in)
-        query_parts, key_parts, value_parts = [], [], []
-        for side in range(2):
-            keys_side = jnp.where(masks[side], keys_scaled, zeros)
-            values_side = jnp.where(masks[side], values_in, zeros)
-            scores = jnp.where(valid, dot_nt(keys_side, queries), NEGATIVE)
-            probs = jnp.exp(scores - lse[2 * index + side])
-            grad_probs = dot_nt(values_side, grads)
-            inner = jnp.sum(grad_probs * probs, axis=0, keepdims=True)
-            grad_scores = (probs * (grad_probs - inner)).astype(BF16)
-            value_parts.append(dot(probs.astype(BF16), grads))
-            key_parts.append(dot(grad_scores, queries))
-            query_parts.append(dot(keys_t[side * HEAD_DIM : (side + 1) * HEAD_DIM], grad_scores))
+        scores = [
+            dot_nt(jnp.where(masks[side], keys_scaled, zeros), queries) for side in range(2)
+        ]
+        grad_probs = [dot_nt(jnp.where(masks[side], values_in, zeros), grads) for side in range(2)]
+        probs = [
+            jnp.exp(jnp.where(valid, scores[side], NEGATIVE) - lse[2 * index + side])
+            for side in range(2)
+        ]
+        value_parts = [dot(weights.astype(BF16), grads) for weights in probs]
+        inner = [
+            jnp.sum(back * weights, axis=0, keepdims=True) for back, weights in zip(grad_probs, probs)
+        ]
+        grad_scores = [
+            (weights * (back - total)).astype(BF16)
+            for weights, back, total in zip(probs, grad_probs, inner)
+        ]
+        key_parts = [dot(back, queries) for back in grad_scores]
+        query_parts = [
+            dot(keys_t[side * HEAD_DIM : (side + 1) * HEAD_DIM], grad_scores[side])
+            for side in range(2)
+        ]
         grad_queries = jnp.concatenate(query_parts, axis=0).T * scale
         grad_keys = jnp.where(masks[0], key_parts[0], key_parts[1]) * scale
         grad_values = jnp.where(masks[0], value_parts[0], value_parts[1])
@@ -725,6 +739,12 @@
         ]
         self.outgoing = sends[0] if len(sends) == 1 else jnp.concatenate(sends, axis=1)
         self.members = [[part[:rows] for part in parts] for parts in self.members]
+
+    @classmethod
+    def joined(cls, units):
+        whole_unit = cls(units[0].order, (None, jnp.concatenate([u.outgoing for u in units], axis=1)))
+        whole_unit.members = [parts for unit in units for parts in unit.members]
+        return whole_unit
 
     def start(self):
         self.incoming = lax.ppermute(self.outgoing, "dp", flip(self.order.pop(0)))
@@ -1076,7 +1096,7 @@
     def down_halves(layer, order_of, grad_t, got_grad_t):
         kept = saved[layer]
         return weight_grad(
-            "down_grad", order_of, (grad_t, got_grad_t), (in_hbm(kept["hid"]), kept["got_hid"])
+            "down_grad", order_of, (grad_t, got_grad_t), (in_hbm(kept["hid"]) if layer else kept["hid"], kept["got_hid"])
         )
 
     def up_halves(layer, order_of, pre_own, got_pre, tiles=None, first=0):
@@ -1138,7 +1158,8 @@
     joint_far, qv_far = attend_back(saved[0]["far"], att_far, counts_in)
     got_joint = swap(joint_far)
     pre_own = gate(pre_own, [], [], [qv_far], [down_0, up_1])
-    pre_own = gate(pre_own, [down_0, up_1, down_1])
+    late_1 = DpSum.joined([up_1, down_1])
+    pre_own = gate(pre_own, [down_0, late_1])
     up_0 = DpSum(order_d, up_halves(0, order_d, pre_own, got_pre))
     counts_in = gate(counts_in, [up_0], [], [got_mid_t, got_joint])
     joint_own, qv_own = attend_back(saved[0]["own"], att_own, counts_in)
@@ -1153,7 +1174,7 @@
             tiles=3,
         ),
     )
-    gain_in = gate(gain_in, [rest_0], [down_0, up_1, down_1], [qv_own])
+    gain_in = gate(gain_in, [rest_0], [down_0, late_1], [qv_own])
     grad, sums_in = entry_back(0, joint_own, joint_far, grad_mid, gain_in)
     last = gate(sums_in, [rest_1], [up_0])
     small[0] = (sums_mid, last, qv_own, qv_far, upb_own, upb_far)
@@ -1171,20 +1192,21 @@
     vector = Everywhere(mine, far, [(0, 1), (2,), (3,), *[(bit,) for bit in tail]])
     last = gate(last, holds=[down_0])
     last = gate(last, [], [rest_0, up_0, vector], [down_0.outgoing], [rest_1])
-    last = gate(last, [down_0, rest_1], [rest_0, up_0, vector])
+    last = gate(last, holds=[rest_0, up_0])
+    last = gate(last, [rest_0, up_0, down_0, rest_1], [vector])
     last = gate(last, [], [rest_0, up_0, down_0, rest_1, vector])
     last = gate(last, [], [rest_0, rest_1])
     last = gate(last, [], [vector])
     while vector.flying():
         vector.turn()
-    running = [down_1, up_1, rest_1, down_0, up_0, rest_0]
+    running = [late_1, rest_1, down_0, up_0, rest_0]
     while any(unit.incoming is not None for unit in running):
         last = gate(last, [], [unit for unit in running if unit.incoming is not None][:4])
 
     def finish(first, second, shapes):
-        ins = [*first.members[0], *second.members[0]]
+        ins = [*first, *second]
         return call(
-            functools.partial(finish_kernel, len(first.members[0])),
+            functools.partial(finish_kernel, len(first)),
             "finish",
             (),
             ins,
@@ -1193,9 +1215,9 @@
             [whole()] * len(shapes),
         )
 
-    (down_grad,) = finish(down_0, down_1, [(1, block, ff_half)])
-    (up_grad,) = finish(up_0, up_1, [(1, block, ff_half)])
-    qkv_grad, out_grad = finish(rest_0, rest_1, [(3, block, half), (1, block, half)])
+    (down_grad,) = finish(down_0.members[0], late_1.members[1], [(1, block, ff_half)])
+    (up_grad,) = finish(up_0.members[0], late_1.members[0], [(1, block, ff_half)])
+    qkv_grad, out_grad = finish(rest_0.members[0], rest_1.members[0], [(3, block, half), (1, block, half)])
     total, qkv_grad = lax.optimization_barrier((vector.mine, qkv_grad))
     gain_grads, shift_grads, outb_grads, qv_grads, upb_grads = call(
         functools.partial(unpack_kernel, LAYERS),

time: 284 us -> 278 us (0.979)
  Pallas kernels: 174 us -> 159 us
  starting transfers between devices: 42.9 us -> 47.3 us
  other arithmetic: 5.38 us -> 8.34 us
    pallas_call x24, Pallas kernels: 174 us -> 159 us  [call(): pl.pallas_call(body, name=name, grid=grid, in_specs=in_specs, out_specs=o...]
    ppermute x5, waiting for transfers between devices: 18.2 us -> 13.4 us  [turn(): lax.ppermute(self.mine, 'dp', [(index, index ^ mask) for index in range(s...]
    ppermute x23, waiting for transfers between devices: 5.21 us -> 9.91 us  [swap(): return lax.ppermute(values, 'tensor', [(0, 1), (1, 0)])]
    convert_element_type x18, other arithmetic: 5.06 us -> 7.99 us  [halve(): sum((part[rows:].astype(F32) for part in parts)).astype(BF16)]
    ppermute x24 -> x23, starting transfers between devices: 32.5 us -> 35 us  [start(): self.incoming = lax.ppermute(self.outgoing, 'dp', flip(self.order.pop(0)))]
    ppermute x24 -> x23, waiting for transfers between devices: 30.4 us -> 31.4 us  [start(): self.incoming = lax.ppermute(self.outgoing, 'dp', flip(self.order.pop(0)))]
  transfers between devices with their start and end apart: 52 -> 51, of which waited for: 13 -> 15; matrix products, arithmetic and copies ran while one was open for 2% -> 4% of each run, Pallas kernels for 47% -> 43%
where the time goes in v3:
time: 278 us
  Pallas kernels  159 us (57%)
  waiting for transfers between devices  54.7 us (20%)
  starting transfers between devices  47.3 us (17%)
  other arithmetic  8.34 us (3%)
  local copies, waits for them, and re-layouts  6.78 us (2%)
    pallas_call x24, Pallas kernels, call(): pl.pallas_call(body, name=name, grid=grid, in_specs=in_specs, out_specs=o...  159 us
    ppermute x23, starting transfers between devices, start(): self.incoming = lax.ppermute(self.outgoing, 'dp', flip(self.order.pop(0)))  35 us
    ppermute x23, waiting for transfers between devices, start(): self.incoming = lax.ppermute(self.outgoing, 'dp', flip(self.order.pop(0)))  31.4 us
    ppermute x5, waiting for transfers between devices, turn(): lax.ppermute(self.mine, 'dp', [(index, index ^ mask) for index in range(s...  13.4 us
    ppermute x23, waiting for transfers between devices, swap(): return lax.ppermute(values, 'tensor', [(0, 1), (1, 0)])  9.91 us
    convert_element_type x18, other arithmetic, halve(): sum((part[rows:].astype(F32) for part in parts)).astype(BF16)  7.99 us
    ppermute x5, starting transfers between devices, turn(): lax.ppermute(self.mine, 'dp', [(index, index ^ mask) for index in range(s...  6.67 us
    ppermute x23, starting transfers between devices, swap(): return lax.ppermute(values, 'tensor', [(0, 1), (1, 0)])  5.63 us
  transfers between devices with their start and end apart: 51, of which 15 were waited for; matrix products, arithmetic and copies ran while one was open for 4% of the time, Pallas kernels for 43%

profile of v3, /device:TPU:0, one launch (start us, length us, event | category | flops | bytes accessed | tf_op | source)
XLA Modules:
  0.0 277.6 jit_solution(4048947925944504324)
XLA Ops:
  2.9 4.0 %prep.1 = (bf16[512,768]{1,0:T(8,128)(2,1)S(1)}, bf16[768,512]{1,0:T(8,128)(2,1)S(1)}, bf16[768,512]{1,0:T(8,128)(2,1)S(1)}, f32[512,768]{1,0:T(8,128)S(1)}) custom-call(bf16[512,768]{1,0:T(8,128)(2,1)S(1)} %bitcast.13, bf16[512,768]{1,0:T(8,128)(2,1)S(1)} %bitcast.16, f32[2,2,768]{2,1,0:T(2,128)S(1)} %copy-done.17, f32[2,2,768]{2,1,0:T(2,128)S(1)} %copy-done.18, ...), custom_call_target="tpu_custom_call" | custom-call | flops 18874368 | bytes 104832 | tf_op jit(solution)/shard_map/prep/pallas_call | solution.py:50
  8.4 9.7 %attend.2 = (bf16[3,512,384]{2,1,0:T(8,128)(2,1)S(1)}, bf16[3,512,384]{2,1,0:T(8,128)(2,1)S(1)}, bf16[512,384]{1,0:T(8,128)(2,1)S(1)}, bf16[512,384]{1,0:T(8,128...) custom-call(s32[1]{0:T(128)} %constant.14.clone.1.which, s32[4]{0:T(128)S(1)} %copy-done.22, ...), custom_call_target="tpu_custom_call" | custom-call | flops 34603008 | bytes 172608 | tf_op jit(solution)/shard_map/attend/pallas_call | solution.py:50
  18.1 6.0 %collective-permute-done.5.down_far = bf16[2,1536,768]{2,1,0:T(8,128)(2,1)} collective-permute-done((bf16[2,1536,768]{2,1,0:T(8,128)(2,1)}, bf16[2,1536,768]{2,1,0:T(8,128)(2,1)}, u32[]{:S(2)}, u32[]{:S(2)}) %collective-permute-start.5) | collective-permute-done | bytes 4718624 | tf_op jit(solution)/shard_map/ppermute | solution.py:819
  24.1 17.7 %feed.2 = (f32[512,768]{1,0:T(8,128)S(1)}, bf16[768,512]{1,0:T(8,128)(2,1)S(1)}, bf16[512,1536]{1,0:T(8,128)(2,1)}, bf16[512,1536]{1,0:T(8,128)(2,1)}, bf16[512,...) custom-call(s32[4]{0:T(128)S(1)} %copy-done.22, ...), custom_call_target="tpu_custom_call" | custom-call | flops 94371840 | bytes 560064 | tf_op jit(solution)/shard_map/feed/pallas_call | solution.py:50
  44.2 9.7 %attend.3 = (bf16[3,512,384]{2,1,0:T(8,128)(2,1)S(1)}, bf16[3,512,384]{2,1,0:T(8,128)(2,1)S(1)}, bf16[512,384]{1,0:T(8,128)(2,1)S(1)}, bf16[512,384]{1,0:T(8,128...) custom-call(s32[1]{0:T(128)} %constant.36.clone.1.which, s32[4]{0:T(128)S(1)} %copy-done.22, ...), custom_call_target="tpu_custom_call" | custom-call | flops 34603008 | bytes 172608 | tf_op jit(solution)/shard_map/attend/pallas_call | solution.py:50
  54.0 16.6 %feed.3 = (f32[512,768]{1,0:T(8,128)S(1)}, bf16[768,512]{1,0:T(8,128)(2,1)S(1)}, bf16[512,1536]{1,0:T(8,128)(2,1)}, bf16[512,1536]{1,0:T(8,128)(2,1)}, bf16[512,...) custom-call(s32[4]{0:T(128)S(1)} %copy-done.22, ...), custom_call_target="tpu_custom_call" | custom-call | flops 94371840 | bytes 547872 | tf_op jit(solution)/shard_map/feed/pallas_call | solution.py:50
  70.8 3.5 %collective-permute-done.12.refs_3_ = bf16[512,1536]{1,0:T(8,128)(2,1)S(1)} collective-permute-done((bf16[512,1536]{1,0:T(8,128)(2,1)}, bf16[512,1536]{1,0:T(8,128)(2,1)S(1)}, u32[]{:S(2)}, u32[]{:S(2)}) %collective-permute-start.12) | collective-permute-done | bytes 1572896 | tf_op jit(solution)/shard_map/ppermute | solution.py:819
  75.5 4.3 %down_grad.2 = (bf16[384,1536]{1,0:T(8,128)(2,1)S(1)}, bf16[384,1536]{1,0:T(8,128)(2,1)S(1)}) custom-call(bf16[768,512]{1,0:T(8,128)(2,1)S(1)} %copy-done.11, bf16[768,512]{1,0:T(8,128)(2,1)S(1)} %copy-done.15, bf16[512,1536]{1,0:T(8,128)(2,1)} %get-tuple-element.185.refs_2_, bf16[512,1536]{1,0:T(8,128)(2,1)S(1)} %collective-permute-done.12.refs_3_), custom_call_target="tpu_custom_call" | custom-call | flops 37748736 | bytes 110592 | tf_op jit(solution)/shard_map/down_grad/pallas_call | solution.py:50
  79.8 2.7 collective-permute-start.13
  82.5 17.9 %feed_back.2 = (bf16[512,1536]{1,0:T(8,128)(2,1)}, bf16[512,1536]{1,0:T(8,128)(2,1)}, f32[2,768]{1,0:T(2,128)S(1)}, f32[2,768]{1,0:T(2,128)S(1)}, f32[512,768]{1...) custom-call(s32[1]{0:T(128)} %constant.36.clone.1.which, ...), custom_call_target="tpu_custom_call" | custom-call | flops 94371840 | bytes 547392 | tf_op jit(solution)/shard_map/feed_back/pallas_call | solution.py:50
  101.0 4.8 %attend_back.4 = (bf16[3,512,384]{2,1,0:T(8,128)(2,1)S(1)}, f32[1,768]{1,0:T(1,128)S(1)}) custom-call(s32[4]{0:T(128)S(1)} %copy-done.22, bf16[3,512,384]{2,1,0:T(8,128)(2,1)S(1)} %get-tuple-element.193.joint, f32[12,1,256]{2,1,0:T(1,128)S(1)} %get-tuple-element.194.lse, bf16[512,384]{1,0:T(8,128)(2,1)S(1)} %get-tuple-element.195.grad_att), custom_call_target="tpu_custom_call" | custom-call | flops 7864320 | bytes 43248 | tf_op jit(solution)/shard_map/attend_back/pallas_call | solution.py:50
  105.8 3.2 %collective-permute-done.13 = bf16[384,1536]{1,0:T(8,128)(2,1)S(1)} collective-permute-done((bf16[384,1536]{1,0:T(8,128)(2,1)S(1)}, bf16[384,1536]{1,0:T(8,128)(2,1)S(1)}, u32[]{:S(2)}, u32[]{:S(2)}) %collective-permute-start.13) | collective-permute-done | bytes 1179680 | tf_op jit(solution)/shard_map/ppermute | solution.py:750
  109.1 1.8 collective-permute-start.16
  111.5 3.3 %up_grad.2 = (bf16[384,1536]{1,0:T(8,128)(2,1)S(1)}, bf16[384,1536]{1,0:T(8,128)(2,1)S(1)}) custom-call(bf16[768,512]{1,0:T(8,128)(2,1)S(1)} %copy-done.13, bf16[768,512]{1,0:T(8,128)(2,1)S(1)} %collective-permute-done.11.refs_1_, bf16[512,1536]{1,0:T(8,128)(2,1)S(1)} %copy-done.7, bf16[512,1536]{1,0:T(8,128)(2,1)S(1)} %collective-permute-done.14.refs_3_), custom_call_target="tpu_custom_call" | custom-call | flops 37748736 | bytes 110592 | tf_op jit(solution)/shard_map/up_grad/pallas_call | solution.py:50
  114.8 1.6 collective-permute-start.21
  116.9 4.8 %attend_back.5 = (bf16[3,512,384]{2,1,0:T(8,128)(2,1)S(1)}, f32[1,768]{1,0:T(1,128)S(1)}) custom-call(s32[4]{0:T(128)S(1)} %copy-done.22, bf16[3,512,384]{2,1,0:T(8,128)(2,1)S(1)} %get-tuple-element.205.joint, f32[12,1,256]{2,1,0:T(1,128)S(1)} %get-tuple-element.206.lse, bf16[512,384]{1,0:T(8,128)(2,1)S(1)} %get-tuple-element.207.grad_att), custom_call_target="tpu_custom_call" | custom-call | flops 7864320 | bytes 43248 | tf_op jit(solution)/shard_map/attend_back/pallas_call | solution.py:50
  121.6 9.9 %entry_back.2 = (f32[512,768]{1,0:T(8,128)S(1)}, f32[2,768]{1,0:T(2,128)S(1)}, bf16[768,512]{1,0:T(8,128)(2,1)S(1)}) custom-call(bf16[3,512,384]{2,1,0:T(8,128)(2,1)S(1)} %get-tuple-element.217.joint_own.refs_2_, bf16[3,512,384]{2,1,0:T(8,128)(2,1)S(1)} %get-tuple-element.211.joint_far, bf16[2,3,768,384]{3,2,1,0:T(8,128)(2,1)} %bitcast.20, ...), custom_call_target="tpu_custom_call" | custom-call | flops 28311552 | bytes 252192 | tf_op jit(solution)/shard_map/entry_back/pallas_call | solution.py:50
  131.8 1.6 collective-permute-start.22
  133.5 4.2 %qkv_out_grad.2 = (bf16[384,1536]{1,0:T(8,128)(2,1)S(1)}, bf16[384,1536]{1,0:T(8,128)(2,1)S(1)}) custom-call(bf16[768,512]{1,0:T(8,128)(2,1)S(1)} %copy-done.9, bf16[768,512]{1,0:T(8,128)(2,1)S(1)} %collective-permute-done.15.refs_1_, bf16[3,512,384]{2,1,0:T(8,128)(2,1)S(1)} %get-tuple-element.217.joint_own.refs_2_, ...), custom_call_target="tpu_custom_call" | custom-call | flops 37748736 | bytes 135168 | tf_op jit(solution)/shard_map/qkv_out_grad/pallas_call | solution.py:50
  138.3 3.3 %down_grad.3 = (bf16[384,1536]{1,0:T(8,128)(2,1)S(1)}, bf16[384,1536]{1,0:T(8,128)(2,1)S(1)}) custom-call(bf16[768,512]{1,0:T(8,128)(2,1)S(1)} %get-tuple-element.220.refs_0_, bf16[768,512]{1,0:T(8,128)(2,1)S(1)} %collective-permute-done.20.refs_1_, bf16[512,1536]{1,0:T(8,128)(2,1)S(1)} %copy-done.5, bf16[512,1536]{1,0:T(8,128)(2,1)S(1)} %collective-permute-done.10.refs_3_), custom_call_target="tpu_custom_call" | custom-call | flops 37748736 | bytes 110592 | tf_op jit(solution)/shard_map/down_grad/pallas_call | solution.py:50
  143.2 1.7 collective-permute-start.25
  144.9 18.2 %feed_back.3 = (bf16[512,1536]{1,0:T(8,128)(2,1)}, bf16[512,1536]{1,0:T(8,128)(2,1)}, f32[2,768]{1,0:T(2,128)S(1)}, f32[2,768]{1,0:T(2,128)S(1)}, f32[512,768]{1...) custom-call(s32[1]{0:T(128)} %constant.14.clone.1.which, ...), custom_call_target="tpu_custom_call" | custom-call | flops 94371840 | bytes 547392 | tf_op jit(solution)/shard_map/feed_back/pallas_call | solution.py:50
  163.8 2.9 %collective-permute-done.24 = bf16[384,1536]{1,0:T(8,128)(2,1)} collective-permute-done((bf16[384,1536]{1,0:T(8,128)(2,1)S(1)}, bf16[384,1536]{1,0:T(8,128)(2,1)}, u32[]{:S(2)}, u32[]{:S(2)}) %collective-permute-start.24) | collective-permute-done | bytes 1179680 | tf_op jit(solution)/shard_map/ppermute | solution.py:750
  166.8 1.6 collective-permute-start.26
  168.5 4.8 %attend_back.6 = (bf16[3,512,384]{2,1,0:T(8,128)(2,1)S(1)}, f32[1,768]{1,0:T(1,128)S(1)}) custom-call(s32[4]{0:T(128)S(1)} %copy-done.22, bf16[3,512,384]{2,1,0:T(8,128)(2,1)S(1)} %get-tuple-element.239.joint, f32[12,1,256]{2,1,0:T(1,128)S(1)} %get-tuple-element.240.lse, bf16[512,384]{1,0:T(8,128)(2,1)S(1)} %get-tuple-element.241.grad_att), custom_call_target="tpu_custom_call" | custom-call | flops 7864320 | bytes 43248 | tf_op jit(solution)/shard_map/attend_back/pallas_call | solution.py:50
  173.4 2.1 collective-permute-done.26
  175.6 1.3 add_convert_fusion.3
  177.1 3.3 %up_grad.3 = (bf16[384,1536]{1,0:T(8,128)(2,1)S(1)}, bf16[384,1536]{1,0:T(8,128)(2,1)S(1)}) custom-call(bf16[768,512]{1,0:T(8,128)(2,1)S(1)} %get-tuple-element.176.refs_0_, bf16[768,512]{1,0:T(8,128)(2,1)S(1)} %collective-permute-done.9.refs_1_, bf16[512,1536]{1,0:T(8,128)(2,1)S(1)} %copy-done.6, bf16[512,1536]{1,0:T(8,128)(2,1)S(1)} %collective-permute-done.27.refs_3_), custom_call_target="tpu_custom_call" | custom-call | flops 37748736 | bytes 110592 | tf_op jit(solution)/shard_map/up_grad/pallas_call | solution.py:50
  181.4 2.7 collective-permute-start.31
  185.3 4.8 %attend_back.7 = (bf16[3,512,384]{2,1,0:T(8,128)(2,1)S(1)}, f32[1,768]{1,0:T(1,128)S(1)}) custom-call(s32[4]{0:T(128)S(1)} %copy-done.22, bf16[3,512,384]{2,1,0:T(8,128)(2,1)S(1)} %get-tuple-element.254.joint, f32[12,1,256]{2,1,0:T(1,128)S(1)} %get-tuple-element.255.lse, bf16[512,384]{1,0:T(8,128)(2,1)S(1)} %get-tuple-element.256.grad_att), custom_call_target="tpu_custom_call" | custom-call | flops 7864320 | bytes 43248 | tf_op jit(solution)/shard_map/attend_back/pallas_call | solution.py:50
  190.1 4.2 %qkv_out_grad.3 = (bf16[384,1536]{1,0:T(8,128)(2,1)S(1)}, bf16[384,1536]{1,0:T(8,128)(2,1)S(1)}) custom-call(bf16[768,512]{1,0:T(8,128)(2,1)S(1)} %get-tuple-element.175.refs_0_, bf16[768,512]{1,0:T(8,128)(2,1)S(1)} %collective-permute-done.7.refs_1_, bf16[3,512,384]{2,1,0:T(8,128)(2,1)S(1)} %get-tuple-element.257.refs_2_.joint_own, ...), custom_call_target="tpu_custom_call" | custom-call | flops 37748736 | bytes 135168 | tf_op jit(solution)/shard_map/qkv_out_grad/pallas_call | solution.py:50
  194.4 1.5 collective-permute-done.31
  195.9 1.5 collective-permute-start.33
  199.2 9.8 %entry_back.3 = (f32[512,768]{1,0:T(8,128)}, f32[2,768]{1,0:T(2,128)S(1)}) custom-call(bf16[3,512,384]{2,1,0:T(8,128)(2,1)S(1)} %get-tuple-element.257.refs_2_.joint_own, bf16[3,512,384]{2,1,0:T(8,128)(2,1)S(1)} %get-tuple-element.252.joint_far, bf16[2,3,768,384]{3,2,1,0:T(8,128)(2,1)} %bitcast.21, bf16[2,3,768,384]{3,2,1,0:T(8,128)(2,1)} %collective-permute-done.weight_far, ...), custom_call_target="tpu_custom_call" | custom-call | flops 28311552 | bytes 227616 | tf_op jit(solution)/shard_map/entry_back/pallas_call | solution.py:50
  209.1 1.4 collective-permute-start.34
  210.6 1.5 collective-permute-start.36
  213.2 9.5 %collective-permute-done.33 = bf16[384,1536]{1,0:T(8,128)(2,1)S(1)} collective-permute-done((bf16[384,1536]{1,0:T(8,128)(2,1)S(1)}, bf16[384,1536]{1,0:T(8,128)(2,1)S(1)}, u32[]{:S(2)}, u32[]{:S(2)}) %collective-permute-start.33) | collective-permute-done | bytes 1179680 | tf_op jit(solution)/shard_map/ppermute | solution.py:750
  224.0 1.6 collective-permute-start.40
  226.0 1.5 collective-permute-start.42
  227.7 1.6 collective-permute-start.38
  229.4 3.4 %collective-permute-start.39 = (bf16[96,1536]{1,0:T(8,128)(2,1)S(1)}, bf16[96,1536]{1,0:T(8,128)(2,1)S(1)}, u32[]{:S(2)}, u32[]{:S(2)}) collective-permute-start(bf16[96,1536]{1,0:T(8,128)(2,1)S(1)} %add_convert_fusion.8), channel_id=1, source_target_pairs={{0,16},{2,18},{4,20},{6,22},{8,24},{10,26},{12,28},{14,30},{16,0},... | collective-permute-start | bytes 884744 | tf_op jit(solution)/shard_map/ppermute | solution.py:750
  233.9 9.8 %collective-permute-done.39 = bf16[96,1536]{1,0:T(8,128)(2,1)S(1)} collective-permute-done((bf16[96,1536]{1,0:T(8,128)(2,1)S(1)}, bf16[96,1536]{1,0:T(8,128)(2,1)S(1)}, u32[]{:S(2)}, u32[]{:S(2)}) %collective-permute-start.39) | collective-permute-done | bytes 294944 | tf_op jit(solution)/shard_map/ppermute | solution.py:750
  245.2 1.5 collective-permute-start.44
  246.7 3.4 %collective-permute-start.45 = (bf16[48,1536]{1,0:T(8,128)(2,1)S(1)}, bf16[48,1536]{1,0:T(8,128)(2,1)S(1)}, u32[]{:S(2)}, u32[]{:S(2)}) collective-permute-start(bf16[48,1536]{1,0:T(8,128)(2,1)S(1)} %add_convert_fusion.15), channel_id=1, source_target_pairs={{0,16},{2,18},{4,20},{6,22},{8,24},{10,26},{12,28},{14,30},{16,0},... | collective-permute-start | bytes 442376 | tf_op jit(solution)/shard_map/ppermute | solution.py:750
  253.4 3.4 %collective-permute-done.47 = f32[18,768]{1,0:T(8,128)S(1)} collective-permute-done((f32[18,768]{1,0:T(8,128)S(1)}, f32[18,768]{1,0:T(8,128)S(1)}, u32[]{:S(2)}, u32[]{:S(2)}) %collective-permute-start.47) | collective-permute-done | bytes 55328 | tf_op jit(solution)/shard_map/ppermute | solution.py:797
  257.8 2.8 %collective-permute-start.50 = (bf16[48,1536]{1,0:T(8,128)(2,1)S(1)}, bf16[48,1536]{1,0:T(8,128)(2,1)S(1)}, u32[]{:S(2)}, u32[]{:S(2)}) collective-permute-start(bf16[48,1536]{1,0:T(8,128)(2,1)S(1)} %add_convert_fusion.12), channel_id=1, source_target_pairs={{0,16},{2,18},{4,20},{6,22},{8,24},{10,26},{12,28},{14,30},{16,0},... | collective-permute-start | bytes 442376 | tf_op jit(solution)/shard_map/ppermute | solution.py:750
  261.0 2.8 %collective-permute-start.48 = (f32[18,768]{1,0:T(8,128)S(1)}, f32[18,768]{1,0:T(8,128)S(1)}, u32[]{:S(2)}, u32[]{:S(2)}) collective-permute-start(f32[18,768]{1,0:T(8,128)S(1)} %add.184), channel_id=1, source_target_pairs={{0,16},{2,18},{4,20},{6,22},{8,24},{10,26},{12,28},{14,30},{16,0},... | collective-permute-start | bytes 165896 | tf_op jit(solution)/shard_map/ppermute | solution.py:797
  266.0 10.0 %collective-permute-done.48 = f32[18,768]{1,0:T(8,128)S(1)} collective-permute-done((f32[18,768]{1,0:T(8,128)S(1)}, f32[18,768]{1,0:T(8,128)S(1)}, u32[]{:S(2)}, u32[]{:S(2)}) %collective-permute-start.48) | collective-permute-done | bytes 55328 | tf_op jit(solution)/shard_map/ppermute | solution.py:797
  (190 shorter events, 30.8 us)
Async XLA Ops:
  0.7 6.7 %collective-permute-start = (bf16[2,3,768,384]{3,2,1,0:T(8,128)(2,1)}, bf16[2,3,768,384]{3,2,1,0:T(8,128)(2,1)}, u32[]{:S(2)}, u32[]{:S(2)}) collective-permute-start(bf16[2,3,768,384]{3,2,1,0:T(8,128)(2,1)} %bitcast.17), channel_id=1, source_target_pairs={{0,1},{1,0},{2,3},{3,2},{4,5},{5,4},{6,7},{7,6},{8,9},{9,8},{10,11... | collective-permute-start | bytes 10616840 | tf_op jit(solution)/shard_map/ppermute | solution.py:819
  7.4 10.7 %collective-permute-start.3 = (bf16[2,768,1536]{2,1,0:T(8,128)(2,1)}, bf16[2,768,1536]{2,1,0:T(8,128)(2,1)}, u32[]{:S(2)}, u32[]{:S(2)}) collective-permute-start(bf16[2,768,1536]{2,1,0:T(8,128)(2,1)} %up_own.7), channel_id=1, source_target_pairs={{0,1},{1,0},{2,3},{3,2},{4,5},{5,4},{6,7},{7,6},{8,9},{9,8},{10,11... | collective-permute-start | bytes 14155784 | tf_op jit(solution)/shard_map/ppermute | solution.py:819
  7.8 16.3 %collective-permute-start.5 = (bf16[2,1536,768]{2,1,0:T(8,128)(2,1)}, bf16[2,1536,768]{2,1,0:T(8,128)(2,1)}, u32[]{:S(2)}, u32[]{:S(2)}) collective-permute-start(bf16[2,1536,768]{2,1,0:T(8,128)(2,1)} %down_own.7), channel_id=1, source_target_pairs={{0,1},{1,0},{2,3},{3,2},{4,5},{5,4},{6,7},{7,6},{8,9},{9,8},{10,11... | collective-permute-start | bytes 14155784 | tf_op jit(solution)/shard_map/ppermute | solution.py:819
  7.9 10.2 %collective-permute-start.2 = (bf16[2,384,768]{2,1,0:T(8,128)(2,1)S(1)}, bf16[2,384,768]{2,1,0:T(8,128)(2,1)S(1)}, u32[]{:S(2)}, u32[]{:S(2)}) collective-permute-start(bf16[2,384,768]{2,1,0:T(8,128)(2,1)S(1)} %copy-done.26), channel_id=1, source_target_pairs={{0,1},{1,0},{2,3},{3,2},{4,5},{5,4},{6,7},{7,6},{8,9},{9,8},{10,11... | collective-permute-start | bytes 3538952 | tf_op jit(solution)/shard_map/ppermute | solution.py:819
  8.3 9.8 %collective-permute-start.4 = (f32[2,1536]{1,0:T(2,128)S(1)}, f32[2,1536]{1,0:T(2,128)S(1)}, u32[]{:S(2)}, u32[]{:S(2)}) collective-permute-start(f32[2,1536]{1,0:T(2,128)S(1)} %copy-done.21), channel_id=1, source_target_pairs={{0,1},{1,0},{2,3},{3,2},{4,5},{5,4},{6,7},{7,6},{8,9},{9,8},{10,11... | collective-permute-start | bytes 36872 | tf_op jit(solution)/shard_map/ppermute | solution.py:819
  42.8 11.1 %collective-permute-start.10 = (bf16[512,1536]{1,0:T(8,128)(2,1)}, bf16[512,1536]{1,0:T(8,128)(2,1)S(1)}, u32[]{:S(2)}, u32[]{:S(2)}) collective-permute-start(bf16[512,1536]{1,0:T(8,128)(2,1)} %get-tuple-element.177), channel_id=1, source_target_pairs={{0,1},{1,0},{2,3},{3,2},{4,5},{5,4},{6,7},{7,6},{8,9},{9,8},{10,11... | collective-permute-start | bytes 4718600 | tf_op jit(solution)/shard_map/ppermute | solution.py:819
  43.2 10.7 %collective-permute-start.6 = (bf16[768,512]{1,0:T(8,128)(2,1)S(1)}, bf16[768,512]{1,0:T(8,128)(2,1)S(1)}, u32[]{:S(2)}, u32[]{:S(2)}) collective-permute-start(bf16[768,512]{1,0:T(8,128)(2,1)S(1)} %get-tuple-element.174.refs_0_), channel_id=1, source_target_pairs={{0,1},{1,0},{2,3},{3,2},{4,5},{5,4},{6,7},{7,6},{8,9},{9,8},{10,11... | collective-permute-start | bytes 2359304 | tf_op jit(solution)/shard_map/ppermute | solution.py:819
  43.3 10.6 %collective-permute-start.7 = (bf16[768,512]{1,0:T(8,128)(2,1)S(1)}, bf16[768,512]{1,0:T(8,128)(2,1)S(1)}, u32[]{:S(2)}, u32[]{:S(2)}) collective-permute-start(bf16[768,512]{1,0:T(8,128)(2,1)S(1)} %get-tuple-element.175.refs_0_), channel_id=1, source_target_pairs={{0,1},{1,0},{2,3},{3,2},{4,5},{5,4},{6,7},{7,6},{8,9},{9,8},{10,11... | collective-permute-start | bytes 2359304 | tf_op jit(solution)/shard_map/ppermute | solution.py:819
  43.7 10.2 %collective-permute-start.9 = (bf16[768,512]{1,0:T(8,128)(2,1)S(1)}, bf16[768,512]{1,0:T(8,128)(2,1)S(1)}, u32[]{:S(2)}, u32[]{:S(2)}) collective-permute-start(bf16[768,512]{1,0:T(8,128)(2,1)S(1)} %get-tuple-element.176.refs_0_), channel_id=1, source_target_pairs={{0,1},{1,0},{2,3},{3,2},{4,5},{5,4},{6,7},{7,6},{8,9},{9,8},{10,11... | collective-permute-start | bytes 2359304 | tf_op jit(solution)/shard_map/ppermute | solution.py:819
  43.8 10.1 %collective-permute-start.8 = (bf16[512,384]{1,0:T(8,128)(2,1)S(1)}, bf16[512,384]{1,0:T(8,128)(2,1)S(1)}, u32[]{:S(2)}, u32[]{:S(2)}) collective-permute-start(bf16[512,384]{1,0:T(8,128)(2,1)S(1)} %get-tuple-element.166.att_far), channel_id=1, source_target_pairs={{0,1},{1,0},{2,3},{3,2},{4,5},{5,4},{6,7},{7,6},{8,9},{9,8},{10,11... | collective-permute-start | bytes 1179656 | tf_op jit(solution)/shard_map/ppermute | solution.py:819
  79.8 29.2 %collective-permute-start.13 = (bf16[384,1536]{1,0:T(8,128)(2,1)S(1)}, bf16[384,1536]{1,0:T(8,128)(2,1)S(1)}, u32[]{:S(2)}, u32[]{:S(2)}) collective-permute-start(bf16[384,1536]{1,0:T(8,128)(2,1)S(1)} %get-tuple-element.192), channel_id=1, source_target_pairs={{0,2},{2,0},{4,6},{6,4},{8,10},{10,8},{12,14},{14,12},{16,18},{18,... | collective-permute-start | bytes 3538952 | tf_op jit(solution)/shard_map/ppermute | solution.py:750
  100.4 11.1 %collective-permute-start.14 = (bf16[512,1536]{1,0:T(8,128)(2,1)}, bf16[512,1536]{1,0:T(8,128)(2,1)S(1)}, u32[]{:S(2)}, u32[]{:S(2)}) collective-permute-start(bf16[512,1536]{1,0:T(8,128)(2,1)} %get-tuple-element.201), channel_id=1, source_target_pairs={{0,1},{1,0},{2,3},{3,2},{4,5},{5,4},{6,7},{7,6},{8,9},{9,8},{10,11... | collective-permute-start | bytes 4718600 | tf_op jit(solution)/shard_map/ppermute | solution.py:819
  100.5 10.9 %collective-permute-start.11 = (bf16[768,512]{1,0:T(8,128)(2,1)S(1)}, bf16[768,512]{1,0:T(8,128)(2,1)S(1)}, u32[]{:S(2)}, u32[]{:S(2)}) collective-permute-start(bf16[768,512]{1,0:T(8,128)(2,1)S(1)} %get-tuple-element.181.refs_0_), channel_id=1, source_target_pairs={{0,1},{1,0},{2,3},{3,2},{4,5},{5,4},{6,7},{7,6},{8,9},{9,8},{10,11... | collective-permute-start | bytes 2359304 | tf_op jit(solution)/shard_map/ppermute | solution.py:819
  109.1 22.5 %collective-permute-start.16 = (bf16[192,1536]{1,0:T(8,128)(2,1)S(1)}, bf16[192,1536]{1,0:T(8,128)(2,1)S(1)}, u32[]{:S(2)}, u32[]{:S(2)}) collective-permute-start(bf16[192,1536]{1,0:T(8,128)(2,1)S(1)} %add_convert_fusion.5), channel_id=1, source_target_pairs={{0,4},{2,6},{4,0},{6,2},{8,12},{10,14},{12,8},{14,10},{16,20},{18,... | collective-permute-start | bytes 1769480 | tf_op jit(solution)/shard_map/ppermute | solution.py:750
  110.9 22.5 %collective-permute-start.17 = (bf16[3,512,384]{2,1,0:T(8,128)(2,1)S(1)}, bf16[3,512,384]{2,1,0:T(8,128)(2,1)S(1)}, u32[]{:S(2)}, u32[]{:S(2)}) collective-permute-start(bf16[3,512,384]{2,1,0:T(8,128)(2,1)S(1)} %get-tuple-element.211.joint_far), channel_id=1, source_target_pairs={{0,1},{1,0},{2,3},{3,2},{4,5},{5,4},{6,7},{7,6},{8,9},{9,8},{10,11... | collective-permute-start | bytes 3538952 | tf_op jit(solution)/shard_map/ppermute | solution.py:819
  114.8 28.0 %collective-permute-start.21 = (bf16[384,1536]{1,0:T(8,128)(2,1)S(1)}, bf16[384,1536]{1,0:T(8,128)(2,1)S(1)}, u32[]{:S(2)}, u32[]{:S(2)}) collective-permute-start(bf16[384,1536]{1,0:T(8,128)(2,1)S(1)} %get-tuple-element.224), channel_id=1, source_target_pairs={{0,2},{2,0},{4,6},{6,4},{8,10},{10,8},{12,14},{14,12},{16,18},{18,... | collective-permute-start | bytes 3538952 | tf_op jit(solution)/shard_map/ppermute | solution.py:750
  116.3 15.5 %collective-permute-start.15 = (bf16[768,512]{1,0:T(8,128)(2,1)S(1)}, bf16[768,512]{1,0:T(8,128)(2,1)S(1)}, u32[]{:S(2)}, u32[]{:S(2)}) collective-permute-start(bf16[768,512]{1,0:T(8,128)(2,1)S(1)} %copy-done.9), channel_id=1, source_target_pairs={{0,1},{1,0},{2,3},{3,2},{4,5},{5,4},{6,7},{7,6},{8,9},{9,8},{10,11... | collective-permute-start | bytes 2359304 | tf_op jit(solution)/shard_map/ppermute | solution.py:819
  116.3 17.1 %collective-permute-start.18 = (bf16[768,512]{1,0:T(8,128)(2,1)S(1)}, bf16[768,512]{1,0:T(8,128)(2,1)S(1)}, u32[]{:S(2)}, u32[]{:S(2)}) collective-permute-start(bf16[768,512]{1,0:T(8,128)(2,1)S(1)} %get-tuple-element.218.refs_4_), channel_id=1, source_target_pairs={{0,1},{1,0},{2,3},{3,2},{4,5},{5,4},{6,7},{7,6},{8,9},{9,8},{10,11... | collective-permute-start | bytes 2359304 | tf_op jit(solution)/shard_map/ppermute | solution.py:819
  131.6 6.7 %collective-permute-start.20 = (bf16[768,512]{1,0:T(8,128)(2,1)S(1)}, bf16[768,512]{1,0:T(8,128)(2,1)S(1)}, u32[]{:S(2)}, u32[]{:S(2)}) collective-permute-start(bf16[768,512]{1,0:T(8,128)(2,1)S(1)} %get-tuple-element.220.refs_0_), channel_id=1, source_target_pairs={{0,1},{1,0},{2,3},{3,2},{4,5},{5,4},{6,7},{7,6},{8,9},{9,8},{10,11... | collective-permute-start | bytes 2359304 | tf_op jit(solution)/shard_map/ppermute | solution.py:819
  131.8 9.9 %collective-permute-start.22 = (bf16[96,1536]{1,0:T(8,128)(2,1)S(1)}, bf16[96,1536]{1,0:T(8,128)(2,1)S(1)}, u32[]{:S(2)}, u32[]{:S(2)}) collective-permute-start(bf16[96,1536]{1,0:T(8,128)(2,1)S(1)} %add_convert_fusion.11), channel_id=1, source_target_pairs={{0,8},{2,10},{4,12},{6,14},{8,0},{10,2},{12,4},{14,6},{16,24},{18,... | collective-permute-start | bytes 884744 | tf_op jit(solution)/shard_map/ppermute | solution.py:750
  137.7 28.9 %collective-permute-start.24 = (bf16[384,1536]{1,0:T(8,128)(2,1)S(1)}, bf16[384,1536]{1,0:T(8,128)(2,1)}, u32[]{:S(2)}, u32[]{:S(2)}) collective-permute-start(bf16[384,1536]{1,0:T(8,128)(2,1)S(1)} %get-tuple-element.227), channel_id=1, source_target_pairs={{0,8},{2,10},{4,12},{6,14},{8,0},{10,2},{12,4},{14,6},{16,24},{18,... | collective-permute-start | bytes 3538952 | tf_op jit(solution)/shard_map/ppermute | solution.py:750
  142.9 23.8 %collective-permute-start.23 = (bf16[192,1536]{1,0:T(8,128)(2,1)S(1)}, bf16[192,1536]{1,0:T(8,128)(2,1)S(1)}, u32[]{:S(2)}, u32[]{:S(2)}) collective-permute-start(bf16[192,1536]{1,0:T(8,128)(2,1)S(1)} %add_convert_fusion.4), channel_id=1, source_target_pairs={{0,4},{2,6},{4,0},{6,2},{8,12},{10,14},{12,8},{14,10},{16,20},{18,... | collective-permute-start | bytes 1769480 | tf_op jit(solution)/shard_map/ppermute | solution.py:750
  143.2 32.2 %collective-permute-start.25 = (bf16[384,1536]{1,0:T(8,128)(2,1)S(1)}, bf16[384,1536]{1,0:T(8,128)(2,1)}, u32[]{:S(2)}, u32[]{:S(2)}) collective-permute-start(bf16[384,1536]{1,0:T(8,128)(2,1)S(1)} %get-tuple-element.237), channel_id=1, source_target_pairs={{0,2},{2,0},{4,6},{6,4},{8,10},{10,8},{12,14},{14,12},{16,18},{18,... | collective-permute-start | bytes 3538952 | tf_op jit(solution)/shard_map/ppermute | solution.py:750
  163.2 13.7 %collective-permute-start.27 = (bf16[512,1536]{1,0:T(8,128)(2,1)}, bf16[512,1536]{1,0:T(8,128)(2,1)S(1)}, u32[]{:S(2)}, u32[]{:S(2)}) collective-permute-start(bf16[512,1536]{1,0:T(8,128)(2,1)} %get-tuple-element.249), channel_id=1, source_target_pairs={{0,1},{1,0},{2,3},{3,2},{4,5},{5,4},{6,7},{7,6},{8,9},{9,8},{10,11... | collective-permute-start | bytes 4718600 | tf_op jit(solution)/shard_map/ppermute | solution.py:819
  163.3 17.2 %collective-permute-start.28 = (bf16[768,512]{1,0:T(8,128)(2,1)S(1)}, bf16[768,512]{1,0:T(8,128)(2,1)S(1)}, u32[]{:S(2)}, u32[]{:S(2)}) collective-permute-start(bf16[768,512]{1,0:T(8,128)(2,1)S(1)} %get-tuple-element.251.refs_4_), channel_id=1, source_target_pairs={{0,1},{1,0},{2,3},{3,2},{4,5},{5,4},{6,7},{7,6},{8,9},{9,8},{10,11... | collective-permute-start | bytes 2359304 | tf_op jit(solution)/shard_map/ppermute | solution.py:819
  166.8 8.6 %collective-permute-start.26 = (bf16[96,1536]{1,0:T(8,128)(2,1)S(1)}, bf16[96,1536]{1,0:T(8,128)(2,1)S(1)}, u32[]{:S(2)}, u32[]{:S(2)}) collective-permute-start(bf16[96,1536]{1,0:T(8,128)(2,1)S(1)} %add_convert_fusion.10), channel_id=1, source_target_pairs={{0,8},{2,10},{4,12},{6,14},{8,0},{10,2},{12,4},{14,6},{16,24},{18,... | collective-permute-start | bytes 884744 | tf_op jit(solution)/shard_map/ppermute | solution.py:750
  173.3 7.1 %collective-permute-start.29 = (bf16[3,512,384]{2,1,0:T(8,128)(2,1)S(1)}, bf16[3,512,384]{2,1,0:T(8,128)(2,1)S(1)}, u32[]{:S(2)}, u32[]{:S(2)}) collective-permute-start(bf16[3,512,384]{2,1,0:T(8,128)(2,1)S(1)} %get-tuple-element.252.joint_far), channel_id=1, source_target_pairs={{0,1},{1,0},{2,3},{3,2},{4,5},{5,4},{6,7},{7,6},{8,9},{9,8},{10,11... | collective-permute-start | bytes 3538952 | tf_op jit(solution)/shard_map/ppermute | solution.py:819
  180.4 28.6 %collective-permute-start.32 = (bf16[384,1536]{1,0:T(8,128)(2,1)S(1)}, bf16[384,1536]{1,0:T(8,128)(2,1)S(1)}, u32[]{:S(2)}, u32[]{:S(2)}) collective-permute-start(bf16[384,1536]{1,0:T(8,128)(2,1)S(1)} %get-tuple-element.270), channel_id=1, source_target_pairs={{0,2},{2,0},{4,6},{6,4},{8,10},{10,8},{12,14},{14,12},{16,18},{18,... | collective-permute-start | bytes 3538952 | tf_op jit(solution)/shard_map/ppermute | solution.py:750
  181.0 14.9 %collective-permute-start.30 = (bf16[192,1536]{1,0:T(8,128)(2,1)S(1)}, bf16[192,1536]{1,0:T(8,128)(2,1)S(1)}, u32[]{:S(2)}, u32[]{:S(2)}) collective-permute-start(bf16[192,1536]{1,0:T(8,128)(2,1)S(1)} %add_convert_fusion.3), channel_id=1, source_target_pairs={{0,4},{2,6},{4,0},{6,2},{8,12},{10,14},{12,8},{14,10},{16,20},{18,... | collective-permute-start | bytes 1769480 | tf_op jit(solution)/shard_map/ppermute | solution.py:750
  181.4 14.4 %collective-permute-start.31 = (bf16[48,3072]{1,0:T(8,128)(2,1)S(1)}, bf16[48,3072]{1,0:T(8,128)(2,1)S(1)}, u32[]{:S(2)}, u32[]{:S(2)}) collective-permute-start(bf16[48,3072]{1,0:T(8,128)(2,1)S(1)} %pad_maximum_fusion), channel_id=1, source_target_pairs={{0,16},{2,18},{4,20},{6,22},{8,24},{10,26},{12,28},{14,30},{16,0},... | collective-permute-start | bytes 884744 | tf_op jit(solution)/shard_map/ppermute | solution.py:750
  195.9 26.8 %collective-permute-start.33 = (bf16[384,1536]{1,0:T(8,128)(2,1)S(1)}, bf16[384,1536]{1,0:T(8,128)(2,1)S(1)}, u32[]{:S(2)}, u32[]{:S(2)}) collective-permute-start(bf16[384,1536]{1,0:T(8,128)(2,1)S(1)} %get-tuple-element.278), channel_id=1, source_target_pairs={{0,4},{2,6},{4,0},{6,2},{8,12},{10,14},{12,8},{14,10},{16,20},{18,... | collective-permute-start | bytes 3538952 | tf_op jit(solution)/shard_map/ppermute | solution.py:750
  198.5 13.6 %collective-permute-start.37 = (bf16[96,1536]{1,0:T(8,128)(2,1)S(1)}, bf16[96,1536]{1,0:T(8,128)(2,1)S(1)}, u32[]{:S(2)}, u32[]{:S(2)}) collective-permute-start(bf16[96,1536]{1,0:T(8,128)(2,1)S(1)} %add_convert_fusion.9), channel_id=1, source_target_pairs={{0,8},{2,10},{4,12},{6,14},{8,0},{10,2},{12,4},{14,6},{16,24},{18,... | collective-permute-start | bytes 884744 | tf_op jit(solution)/shard_map/ppermute | solution.py:750
  209.1 14.8 %collective-permute-start.34 = (bf16[192,1536]{1,0:T(8,128)(2,1)S(1)}, bf16[192,1536]{1,0:T(8,128)(2,1)S(1)}, u32[]{:S(2)}, u32[]{:S(2)}) collective-permute-start(bf16[192,1536]{1,0:T(8,128)(2,1)S(1)} %add_convert_fusion.1), channel_id=1, source_target_pairs={{0,8},{2,10},{4,12},{6,14},{8,0},{10,2},{12,4},{14,6},{16,24},{18,... | collective-permute-start | bytes 1769480 | tf_op jit(solution)/shard_map/ppermute | solution.py:750
  210.6 13.4 %collective-permute-start.36 = (bf16[192,1536]{1,0:T(8,128)(2,1)S(1)}, bf16[192,1536]{1,0:T(8,128)(2,1)S(1)}, u32[]{:S(2)}, u32[]{:S(2)}) collective-permute-start(bf16[192,1536]{1,0:T(8,128)(2,1)S(1)} %add_convert_fusion.2), channel_id=1, source_target_pairs={{0,2},{2,0},{4,6},{6,4},{8,10},{10,8},{12,14},{14,12},{16,18},{18,... | collective-permute-start | bytes 1769480 | tf_op jit(solution)/shard_map/ppermute | solution.py:750
  212.1 10.6 %collective-permute-start.35 = (f32[18,768]{1,0:T(8,128)S(1)}, f32[18,768]{1,0:T(8,128)S(1)}, u32[]{:S(2)}, u32[]{:S(2)}) collective-permute-start(f32[18,768]{1,0:T(8,128)S(1)} %get-tuple-element.281), channel_id=1, source_target_pairs={{0,1},{1,0},{2,3},{3,2},{4,5},{5,4},{6,7},{7,6},{8,9},{9,8},{10,11... | collective-permute-start | bytes 165896 | tf_op jit(solution)/shard_map/ppermute | solution.py:819
  224.0 19.9 %collective-permute-start.40 = (f32[18,768]{1,0:T(8,128)S(1)}, f32[18,768]{1,0:T(8,128)S(1)}, u32[]{:S(2)}, u32[]{:S(2)}) collective-permute-start(f32[18,768]{1,0:T(8,128)S(1)} %add.170), channel_id=1, source_target_pairs={{0,2},{2,0},{4,6},{6,4},{8,10},{10,8},{12,14},{14,12},{16,18},{18,... | collective-permute-start | bytes 165896 | tf_op jit(solution)/shard_map/ppermute | solution.py:797
  225.6 18.4 %collective-permute-start.41 = (f32[18,768]{1,0:T(8,128)S(1)}, f32[18,768]{1,0:T(8,128)S(1)}, u32[]{:S(2)}, u32[]{:S(2)}) collective-permute-start(f32[18,768]{1,0:T(8,128)S(1)} %add.170), channel_id=1, source_target_pairs={{0,4},{2,6},{4,0},{6,2},{8,12},{10,14},{12,8},{14,10},{16,20},{18,... | collective-permute-start | bytes 165896 | tf_op jit(solution)/shard_map/ppermute | solution.py:797
  226.0 17.9 %collective-permute-start.42 = (f32[18,768]{1,0:T(8,128)S(1)}, f32[18,768]{1,0:T(8,128)S(1)}, u32[]{:S(2)}, u32[]{:S(2)}) collective-permute-start(f32[18,768]{1,0:T(8,128)S(1)} %add.170), channel_id=1, source_target_pairs={{0,6},{2,4},{4,2},{6,0},{8,14},{10,12},{12,10},{14,8},{16,22},{18,... | collective-permute-start | bytes 165896 | tf_op jit(solution)/shard_map/ppermute | solution.py:797
  227.7 16.0 %collective-permute-start.38 = (bf16[192,1536]{1,0:T(8,128)(2,1)S(1)}, bf16[192,1536]{1,0:T(8,128)(2,1)S(1)}, u32[]{:S(2)}, u32[]{:S(2)}) collective-permute-start(bf16[192,1536]{1,0:T(8,128)(2,1)S(1)} %add_convert_fusion), channel_id=1, source_target_pairs={{0,2},{2,0},{4,6},{6,4},{8,10},{10,8},{12,14},{14,12},{16,18},{18,... | collective-permute-start | bytes 1769480 | tf_op jit(solution)/shard_map/ppermute | solution.py:750
  229.4 14.3 %collective-permute-start.39 = (bf16[96,1536]{1,0:T(8,128)(2,1)S(1)}, bf16[96,1536]{1,0:T(8,128)(2,1)S(1)}, u32[]{:S(2)}, u32[]{:S(2)}) collective-permute-start(bf16[96,1536]{1,0:T(8,128)(2,1)S(1)} %add_convert_fusion.8), channel_id=1, source_target_pairs={{0,16},{2,18},{4,20},{6,22},{8,24},{10,26},{12,28},{14,30},{16,0},... | collective-permute-start | bytes 884744 | tf_op jit(solution)/shard_map/ppermute | solution.py:750
  244.0 12.8 %collective-permute-start.43 = (bf16[96,1536]{1,0:T(8,128)(2,1)S(1)}, bf16[96,1536]{1,0:T(8,128)(2,1)S(1)}, u32[]{:S(2)}, u32[]{:S(2)}) collective-permute-start(bf16[96,1536]{1,0:T(8,128)(2,1)S(1)} %add_convert_fusion.7), channel_id=1, source_target_pairs={{0,8},{2,10},{4,12},{6,14},{8,0},{10,2},{12,4},{14,6},{16,24},{18,... | collective-permute-start | bytes 884744 | tf_op jit(solution)/shard_map/ppermute | solution.py:750
  244.7 12.1 %collective-permute-start.46 = (bf16[96,1536]{1,0:T(8,128)(2,1)S(1)}, bf16[96,1536]{1,0:T(8,128)(2,1)S(1)}, u32[]{:S(2)}, u32[]{:S(2)}) collective-permute-start(bf16[96,1536]{1,0:T(8,128)(2,1)S(1)} %add_convert_fusion.6), channel_id=1, source_target_pairs={{0,4},{2,6},{4,0},{6,2},{8,12},{10,14},{12,8},{14,10},{16,20},{18,... | collective-permute-start | bytes 884744 | tf_op jit(solution)/shard_map/ppermute | solution.py:750
  245.2 11.6 %collective-permute-start.44 = (bf16[48,1536]{1,0:T(8,128)(2,1)S(1)}, bf16[48,1536]{1,0:T(8,128)(2,1)S(1)}, u32[]{:S(2)}, u32[]{:S(2)}) collective-permute-start(bf16[48,1536]{1,0:T(8,128)(2,1)S(1)} %add_convert_fusion.14), channel_id=1, source_target_pairs={{0,4},{2,6},{4,0},{6,2},{8,12},{10,14},{12,8},{14,10},{16,20},{18,... | collective-permute-start | bytes 442376 | tf_op jit(solution)/shard_map/ppermute | solution.py:750
  246.7 10.1 %collective-permute-start.45 = (bf16[48,1536]{1,0:T(8,128)(2,1)S(1)}, bf16[48,1536]{1,0:T(8,128)(2,1)S(1)}, u32[]{:S(2)}, u32[]{:S(2)}) collective-permute-start(bf16[48,1536]{1,0:T(8,128)(2,1)S(1)} %add_convert_fusion.15), channel_id=1, source_target_pairs={{0,16},{2,18},{4,20},{6,22},{8,24},{10,26},{12,28},{14,30},{16,0},... | collective-permute-start | bytes 442376 | tf_op jit(solution)/shard_map/ppermute | solution.py:750
  250.1 6.7 %collective-permute-start.47 = (f32[18,768]{1,0:T(8,128)S(1)}, f32[18,768]{1,0:T(8,128)S(1)}, u32[]{:S(2)}, u32[]{:S(2)}) collective-permute-start(f32[18,768]{1,0:T(8,128)S(1)} %add_add_fusion), channel_id=1, source_target_pairs={{0,8},{2,10},{4,12},{6,14},{8,0},{10,2},{12,4},{14,6},{16,24},{18,... | collective-permute-start | bytes 165896 | tf_op jit(solution)/shard_map/ppermute | solution.py:797
  257.8 18.2 %collective-permute-start.50 = (bf16[48,1536]{1,0:T(8,128)(2,1)S(1)}, bf16[48,1536]{1,0:T(8,128)(2,1)S(1)}, u32[]{:S(2)}, u32[]{:S(2)}) collective-permute-start(bf16[48,1536]{1,0:T(8,128)(2,1)S(1)} %add_convert_fusion.12), channel_id=1, source_target_pairs={{0,16},{2,18},{4,20},{6,22},{8,24},{10,26},{12,28},{14,30},{16,0},... | collective-permute-start | bytes 442376 | tf_op jit(solution)/shard_map/ppermute | solution.py:750
  260.7 15.3 %collective-permute-start.49 = (bf16[48,1536]{1,0:T(8,128)(2,1)S(1)}, bf16[48,1536]{1,0:T(8,128)(2,1)S(1)}, u32[]{:S(2)}, u32[]{:S(2)}) collective-permute-start(bf16[48,1536]{1,0:T(8,128)(2,1)S(1)} %add_convert_fusion.13), channel_id=1, source_target_pairs={{0,16},{2,18},{4,20},{6,22},{8,24},{10,26},{12,28},{14,30},{16,0},... | collective-permute-start | bytes 442376 | tf_op jit(solution)/shard_map/ppermute | solution.py:750
  261.0 15.0 %collective-permute-start.48 = (f32[18,768]{1,0:T(8,128)S(1)}, f32[18,768]{1,0:T(8,128)S(1)}, u32[]{:S(2)}, u32[]{:S(2)}) collective-permute-start(f32[18,768]{1,0:T(8,128)S(1)} %add.184), channel_id=1, source_target_pairs={{0,16},{2,18},{4,20},{6,22},{8,24},{10,26},{12,28},{14,30},{16,0},... | collective-permute-start | bytes 165896 | tf_op jit(solution)/shard_map/ppermute | solution.py:797
  (34 other events, 296.1 us)

commit v4 on v3

--- a/solution.py
+++ b/solution.py
@@ -15,6 +15,7 @@
 BF16 = jnp.bfloat16
 F32 = jnp.float32
 CHUNK = 16
+BAND = 64
 
 
 def dot(left, right):
@@ -83,10 +84,10 @@
 def by_rows(rows, body, unroll=1):
     def step(index, carry):
         for part in range(unroll):
-            body(pl.multiple_of((index * unroll + part) * CHUNK, CHUNK))
+            body(pl.multiple_of((index * unroll + part) * BAND, BAND))
         return carry
 
-    lax.fori_loop(0, rows // (CHUNK * unroll), step, 0)
+    lax.fori_loop(0, rows // (BAND * unroll), step, 0)
 
 
 def moments(values):
@@ -119,12 +120,12 @@
 
 def prep_kernel(images, cotangent, gain, bias, order, normed, normed_t, cotangent_t, wide_cotangent):
     def rows(start):
-        here = pl.ds(start, CHUNK)
+        here = pl.ds(start, BAND)
         values = images[here, :].astype(F32)
         normed[here, :] = normalized(values, gain[0, 0:1, :], bias[0, 0:1, :]).astype(BF16)
         wide_cotangent[here, :] = cotangent[here, :].astype(F32)
 
-    by_rows(images.shape[0], rows, 4)
+    by_rows(images.shape[0], rows, 1)
     by_blocks(normed_t, order, lambda: normed[...], dot_nt)
     by_blocks(cotangent_t, order, lambda: cotangent[...], dot_nt)
 
@@ -276,12 +277,12 @@
     total[...] = dot(jnp.concatenate([att_own[...], att_far[...]], axis=1), w_out[...])
 
     def enter(start):
-        here = pl.ds(start, CHUNK)
+        here = pl.ds(start, BAND)
         value = stream[here, :].astype(F32) + (total[here, :] + out_bias[layer, 0:1, :])
         mid[here, :] = value
         normed[here, :] = normalized(value, gain[layer, 1:2, :], bias[layer, 1:2, :]).astype(BF16)
 
-    by_rows(tokens, enter, 4)
+    by_rows(tokens, enter, 1)
     up_in[0].wait()
     by_blocks(pre.at[0], normed, lambda: w_up[0], dot)
     by_blocks(normed_t, order, lambda: normed[...], dot_nt)
@@ -321,7 +322,7 @@
     by_blocks(total, hid.at[units - 1], lambda: w_down[units - 1], dot, add=True)
 
     def leave(start):
-        here = pl.ds(start, CHUNK)
+        here = pl.ds(start, BAND)
         value = mid[here, :] + (total[here, :] + out_bias[layer, 1:2, :])
         stream_out[here, :] = value
         if not last_layer:
@@ -329,7 +330,7 @@
                 value, gain[layer + 1, 0:1, :], bias[layer + 1, 0:1, :]
             ).astype(BF16)
 
-    by_rows(tokens, leave, 4)
+    by_rows(tokens, leave, 1)
     if last_layer:
         index = lax.broadcasted_iota(jnp.int32, (slots, 1), 0)
         for image in range(tokens // slots):
@@ -399,7 +400,7 @@
     partial[...] = jnp.zeros_like(partial)
 
     def enter(start):
-        here = pl.ds(start, CHUNK)
+        here = pl.ds(start, BAND)
         value = grad_in[here, :].astype(F32)
         low[here, :] = value.astype(BF16)
         partial[0] += fold_rows(value)
@@ -464,7 +465,7 @@
     by_blocks(total, pre.at[units - 1], lambda: w_up[units - 1], dot_nt, add=True)
 
     def leave(start):
-        here = pl.ds(start, CHUNK)
+        here = pl.ds(start, BAND)
         normed_grad = total[here, :]
         through, gain_term = norm_backward(mid[here, :], normed_grad, gain[layer, 1:2, :])
         value = grad_in[here, :].astype(F32) + through
@@ -474,7 +475,7 @@
         partial[2] += fold_rows(gain_term)
         partial[3] += fold_rows(normed_grad)
 
-    by_rows(tokens, leave, 2)
+    by_rows(tokens, leave, 1)
     sums[...] = jnp.sum(partial[...], axis=1)
     by_blocks(mid_t, order, lambda: low[...], dot_nt)
     for copy in out_in:
@@ -562,7 +563,7 @@
     total[...] += dot_nt(left, right)
 
     def rows(start):
-        here = pl.ds(start, CHUNK)
+        here = pl.ds(start, BAND)
         normed_grad = total[here, :]
         through, gain_term = norm_backward(
             stream[here, :].astype(F32), normed_grad, gain[layer, 0:1, :]
@@ -576,7 +577,7 @@
 
     @pl.when(member == 2)
     def _():
-        by_rows(stream.shape[0], rows, 2)
+        by_rows(stream.shape[0], rows, 1)
         sums[...] = jnp.sum(partial[...], axis=1)
         if with_low:
             by_blocks(low_t, order, lambda: low[...], dot_nt)
@@ -1194,12 +1195,14 @@
     last = gate(last, [], [rest_0, up_0, vector], [down_0.outgoing], [rest_1])
     last = gate(last, holds=[rest_0, up_0])
     last = gate(last, [rest_0, up_0, down_0, rest_1], [vector])
-    last = gate(last, [], [rest_0, up_0, down_0, rest_1, vector])
-    last = gate(last, [], [rest_0, rest_1])
+    last = gate(last, holds=[rest_0, rest_1])
+    late_0 = DpSum.joined([rest_0, rest_1])
+    last = gate(last, [late_0], [up_0, down_0, vector])
+    last = gate(last, [], [late_0])
     last = gate(last, [], [vector])
     while vector.flying():
         vector.turn()
-    running = [late_1, rest_1, down_0, up_0, rest_0]
+    running = [late_1, late_0, down_0, up_0]
     while any(unit.incoming is not None for unit in running):
         last = gate(last, [], [unit for unit in running if unit.incoming is not None][:4])
 
@@ -1217,7 +1220,7 @@
 
     (down_grad,) = finish(down_0.members[0], late_1.members[1], [(1, block, ff_half)])
     (up_grad,) = finish(up_0.members[0], late_1.members[0], [(1, block, ff_half)])
-    qkv_grad, out_grad = finish(rest_0.members[0], rest_1.members[0], [(3, block, half), (1, block, half)])
+    qkv_grad, out_grad = finish(late_0.members[0], late_0.members[1], [(3, block, half), (1, block, half)])
     total, qkv_grad = lax.optimization_barrier((vector.mine, qkv_grad))
     gain_grads, shift_grads, outb_grads, qv_grads, upb_grads = call(
         functools.partial(unpack_kernel, LAYERS),

time: 278 us -> 273 us (0.982)
  waiting for transfers between devices: 54.7 us -> 64.6 us
  Pallas kernels: 159 us -> 151 us
  starting transfers between devices: 47.3 us -> 43.9 us
  other arithmetic: 8.34 us -> 5.55 us
    ppermute x23 -> x22, waiting for transfers between devices: 31.4 us -> 40.3 us  [start(): self.incoming = lax.ppermute(self.outgoing, 'dp', flip(self.order.pop(0)))]
    pallas_call x24, Pallas kernels: 159 us -> 151 us  [call(): pl.pallas_call(body, name=name, grid=grid, in_specs=in_specs, out_specs=o...]
    convert_element_type x18 -> x17, other arithmetic: 7.99 us -> 5.18 us  [halve(): sum((part[rows:].astype(F32) for part in parts)).astype(BF16)]
    ppermute x23 -> x22, starting transfers between devices: 35 us -> 33.5 us  [start(): self.incoming = lax.ppermute(self.outgoing, 'dp', flip(self.order.pop(0)))]
  transfers between devices with their start and end apart: 51 -> 50, of which waited for: 15 -> 15; matrix products, arithmetic and copies ran while one was open for 4% -> 3% of each run, Pallas kernels for 43% -> 41%
where the time goes in v4:
time: 273 us; the launch traced here: 272 us
  Pallas kernels  151 us (55%)
  waiting for transfers between devices  64.6 us (24%)
  starting transfers between devices  43.9 us (16%)
  local copies, waits for them, and re-layouts  5.91 us (2%)
  other arithmetic  5.55 us (2%)
    pallas_call x24, Pallas kernels, call(): pl.pallas_call(body, name=name, grid=grid, in_specs=in_specs, out_specs=o...  151 us
    ppermute x22, waiting for transfers between devices, start(): self.incoming = lax.ppermute(self.outgoing, 'dp', flip(self.order.pop(0)))  40.3 us
    ppermute x22, starting transfers between devices, start(): self.incoming = lax.ppermute(self.outgoing, 'dp', flip(self.order.pop(0)))  33.5 us
    ppermute x5, waiting for transfers between devices, turn(): lax.ppermute(self.mine, 'dp', [(index, index ^ mask) for index in range(s...  14.6 us
    ppermute x23, waiting for transfers between devices, swap(): return lax.ppermute(values, 'tensor', [(0, 1), (1, 0)])  9.78 us
    ppermute x23, starting transfers between devices, swap(): return lax.ppermute(values, 'tensor', [(0, 1), (1, 0)])  5.69 us
  transfers between devices with their start and end apart: 50, of which 15 were waited for; matrix products, arithmetic and copies ran while one was open for 3% of the time, Pallas kernels for 41%

profile of v4, /device:TPU:0, one launch (start us, length us, event | category | flops | bytes accessed | tf_op | source)
XLA Modules:
  0.0 272.2 jit_solution(11883713821160763487)
XLA Ops:
  2.9 4.1 %prep.1 = (bf16[512,768]{1,0:T(8,128)(2,1)S(1)}, bf16[768,512]{1,0:T(8,128)(2,1)S(1)}, bf16[768,512]{1,0:T(8,128)(2,1)S(1)}, f32[512,768]{1,0:T(8,128)S(1)}) custom-call(bf16[512,768]{1,0:T(8,128)(2,1)S(1)} %bitcast.13, bf16[512,768]{1,0:T(8,128)(2,1)S(1)} %bitcast.16, f32[2,2,768]{2,1,0:T(2,128)S(1)} %copy-done.17, f32[2,2,768]{2,1,0:T(2,128)S(1)} %copy-done.18, ...), custom_call_target="tpu_custom_call" | custom-call | flops 18874368 | bytes 104832 | tf_op jit(solution)/shard_map/prep/pallas_call | solution.py:51
  8.4 9.7 %attend.2 = (bf16[3,512,384]{2,1,0:T(8,128)(2,1)S(1)}, bf16[3,512,384]{2,1,0:T(8,128)(2,1)S(1)}, bf16[512,384]{1,0:T(8,128)(2,1)S(1)}, bf16[512,384]{1,0:T(8,128...) custom-call(s32[1]{0:T(128)} %constant.14.clone.1.which, s32[4]{0:T(128)S(1)} %copy-done.22, ...), custom_call_target="tpu_custom_call" | custom-call | flops 34603008 | bytes 172608 | tf_op jit(solution)/shard_map/attend/pallas_call | solution.py:51
  18.1 6.0 %collective-permute-done.5.down_far = bf16[2,1536,768]{2,1,0:T(8,128)(2,1)} collective-permute-done((bf16[2,1536,768]{2,1,0:T(8,128)(2,1)}, bf16[2,1536,768]{2,1,0:T(8,128)(2,1)}, u32[]{:S(2)}, u32[]{:S(2)}) %collective-permute-start.5) | collective-permute-done | bytes 4718624 | tf_op jit(solution)/shard_map/ppermute | solution.py:820
  24.1 17.7 %feed.2 = (f32[512,768]{1,0:T(8,128)S(1)}, bf16[768,512]{1,0:T(8,128)(2,1)S(1)}, bf16[512,1536]{1,0:T(8,128)(2,1)}, bf16[512,1536]{1,0:T(8,128)(2,1)}, bf16[512,...) custom-call(s32[4]{0:T(128)S(1)} %copy-done.22, ...), custom_call_target="tpu_custom_call" | custom-call | flops 94371840 | bytes 560064 | tf_op jit(solution)/shard_map/feed/pallas_call | solution.py:51
  44.2 9.7 %attend.3 = (bf16[3,512,384]{2,1,0:T(8,128)(2,1)S(1)}, bf16[3,512,384]{2,1,0:T(8,128)(2,1)S(1)}, bf16[512,384]{1,0:T(8,128)(2,1)S(1)}, bf16[512,384]{1,0:T(8,128...) custom-call(s32[1]{0:T(128)} %constant.36.clone.1.which, s32[4]{0:T(128)S(1)} %copy-done.22, ...), custom_call_target="tpu_custom_call" | custom-call | flops 34603008 | bytes 172608 | tf_op jit(solution)/shard_map/attend/pallas_call | solution.py:51
  53.9 16.6 %feed.3 = (f32[512,768]{1,0:T(8,128)S(1)}, bf16[768,512]{1,0:T(8,128)(2,1)S(1)}, bf16[512,1536]{1,0:T(8,128)(2,1)}, bf16[512,1536]{1,0:T(8,128)(2,1)}, bf16[512,...) custom-call(s32[4]{0:T(128)S(1)} %copy-done.22, ...), custom_call_target="tpu_custom_call" | custom-call | flops 94371840 | bytes 547872 | tf_op jit(solution)/shard_map/feed/pallas_call | solution.py:51
  70.8 3.5 %collective-permute-done.12.refs_3_ = bf16[512,1536]{1,0:T(8,128)(2,1)S(1)} collective-permute-done((bf16[512,1536]{1,0:T(8,128)(2,1)}, bf16[512,1536]{1,0:T(8,128)(2,1)S(1)}, u32[]{:S(2)}, u32[]{:S(2)}) %collective-permute-start.12) | collective-permute-done | bytes 1572896 | tf_op jit(solution)/shard_map/ppermute | solution.py:820
  75.4 4.3 %down_grad.2 = (bf16[384,1536]{1,0:T(8,128)(2,1)S(1)}, bf16[384,1536]{1,0:T(8,128)(2,1)S(1)}) custom-call(bf16[768,512]{1,0:T(8,128)(2,1)S(1)} %copy-done.11, bf16[768,512]{1,0:T(8,128)(2,1)S(1)} %copy-done.15, bf16[512,1536]{1,0:T(8,128)(2,1)} %get-tuple-element.184.refs_2_, bf16[512,1536]{1,0:T(8,128)(2,1)S(1)} %collective-permute-done.12.refs_3_), custom_call_target="tpu_custom_call" | custom-call | flops 37748736 | bytes 110592 | tf_op jit(solution)/shard_map/down_grad/pallas_call | solution.py:51
  79.7 2.7 collective-permute-start.13
  82.4 15.9 %feed_back.2 = (bf16[512,1536]{1,0:T(8,128)(2,1)}, bf16[512,1536]{1,0:T(8,128)(2,1)}, f32[2,768]{1,0:T(2,128)S(1)}, f32[2,768]{1,0:T(2,128)S(1)}, f32[512,768]{1...) custom-call(s32[1]{0:T(128)} %constant.36.clone.1.which, ...), custom_call_target="tpu_custom_call" | custom-call | flops 94371840 | bytes 547392 | tf_op jit(solution)/shard_map/feed_back/pallas_call | solution.py:51
  98.9 4.8 %attend_back.4 = (bf16[3,512,384]{2,1,0:T(8,128)(2,1)S(1)}, f32[1,768]{1,0:T(1,128)S(1)}) custom-call(s32[4]{0:T(128)S(1)} %copy-done.22, bf16[3,512,384]{2,1,0:T(8,128)(2,1)S(1)} %get-tuple-element.192.joint, f32[12,1,256]{2,1,0:T(1,128)S(1)} %get-tuple-element.193.lse, bf16[512,384]{1,0:T(8,128)(2,1)S(1)} %get-tuple-element.194.grad_att), custom_call_target="tpu_custom_call" | custom-call | flops 7864320 | bytes 43248 | tf_op jit(solution)/shard_map/attend_back/pallas_call | solution.py:51
  103.7 5.2 %collective-permute-done.13 = bf16[384,1536]{1,0:T(8,128)(2,1)S(1)} collective-permute-done((bf16[384,1536]{1,0:T(8,128)(2,1)S(1)}, bf16[384,1536]{1,0:T(8,128)(2,1)S(1)}, u32[]{:S(2)}, u32[]{:S(2)}) %collective-permute-start.13) | collective-permute-done | bytes 1179680 | tf_op jit(solution)/shard_map/ppermute | solution.py:751
  109.1 1.8 collective-permute-start.16
  111.4 3.3 %up_grad.2 = (bf16[384,1536]{1,0:T(8,128)(2,1)S(1)}, bf16[384,1536]{1,0:T(8,128)(2,1)S(1)}) custom-call(bf16[768,512]{1,0:T(8,128)(2,1)S(1)} %copy-done.13, bf16[768,512]{1,0:T(8,128)(2,1)S(1)} %collective-permute-done.11.refs_1_, bf16[512,1536]{1,0:T(8,128)(2,1)S(1)} %copy-done.7, bf16[512,1536]{1,0:T(8,128)(2,1)S(1)} %collective-permute-done.14.refs_3_), custom_call_target="tpu_custom_call" | custom-call | flops 37748736 | bytes 110592 | tf_op jit(solution)/shard_map/up_grad/pallas_call | solution.py:51
  114.8 1.6 collective-permute-start.21
  116.8 4.8 %attend_back.5 = (bf16[3,512,384]{2,1,0:T(8,128)(2,1)S(1)}, f32[1,768]{1,0:T(1,128)S(1)}) custom-call(s32[4]{0:T(128)S(1)} %copy-done.22, bf16[3,512,384]{2,1,0:T(8,128)(2,1)S(1)} %get-tuple-element.204.joint, f32[12,1,256]{2,1,0:T(1,128)S(1)} %get-tuple-element.205.lse, bf16[512,384]{1,0:T(8,128)(2,1)S(1)} %get-tuple-element.206.grad_att), custom_call_target="tpu_custom_call" | custom-call | flops 7864320 | bytes 43248 | tf_op jit(solution)/shard_map/attend_back/pallas_call | solution.py:51
  121.6 7.8 %entry_back.2 = (f32[512,768]{1,0:T(8,128)S(1)}, f32[2,768]{1,0:T(2,128)S(1)}, bf16[768,512]{1,0:T(8,128)(2,1)S(1)}) custom-call(bf16[3,512,384]{2,1,0:T(8,128)(2,1)S(1)} %get-tuple-element.216.joint_own.refs_2_, bf16[3,512,384]{2,1,0:T(8,128)(2,1)S(1)} %get-tuple-element.210.joint_far, bf16[2,3,768,384]{3,2,1,0:T(8,128)(2,1)} %bitcast.20, ...), custom_call_target="tpu_custom_call" | custom-call | flops 28311552 | bytes 252192 | tf_op jit(solution)/shard_map/entry_back/pallas_call | solution.py:51
  129.8 1.6 collective-permute-start.22
  131.5 4.2 %qkv_out_grad.2 = (bf16[384,1536]{1,0:T(8,128)(2,1)S(1)}, bf16[384,1536]{1,0:T(8,128)(2,1)S(1)}) custom-call(bf16[768,512]{1,0:T(8,128)(2,1)S(1)} %copy-done.9, bf16[768,512]{1,0:T(8,128)(2,1)S(1)} %collective-permute-done.15.refs_1_, bf16[3,512,384]{2,1,0:T(8,128)(2,1)S(1)} %get-tuple-element.216.joint_own.refs_2_, ...), custom_call_target="tpu_custom_call" | custom-call | flops 37748736 | bytes 135168 | tf_op jit(solution)/shard_map/qkv_out_grad/pallas_call | solution.py:51
  136.2 3.3 %down_grad.3 = (bf16[384,1536]{1,0:T(8,128)(2,1)S(1)}, bf16[384,1536]{1,0:T(8,128)(2,1)S(1)}) custom-call(bf16[768,512]{1,0:T(8,128)(2,1)S(1)} %get-tuple-element.219.refs_0_, bf16[768,512]{1,0:T(8,128)(2,1)S(1)} %collective-permute-done.20.refs_1_, bf16[512,1536]{1,0:T(8,128)(2,1)S(1)} %copy-done.5, bf16[512,1536]{1,0:T(8,128)(2,1)S(1)} %collective-permute-done.10.refs_3_), custom_call_target="tpu_custom_call" | custom-call | flops 37748736 | bytes 110592 | tf_op jit(solution)/shard_map/down_grad/pallas_call | solution.py:51
  139.7 3.0 %collective-permute-done.21 = bf16[384,1536]{1,0:T(8,128)(2,1)S(1)} collective-permute-done((bf16[384,1536]{1,0:T(8,128)(2,1)S(1)}, bf16[384,1536]{1,0:T(8,128)(2,1)S(1)}, u32[]{:S(2)}, u32[]{:S(2)}) %collective-permute-start.21) | collective-permute-done | bytes 1179680 | tf_op jit(solution)/shard_map/ppermute | solution.py:751
  143.2 1.7 collective-permute-start.25
  144.9 16.2 %feed_back.3 = (bf16[512,1536]{1,0:T(8,128)(2,1)}, bf16[512,1536]{1,0:T(8,128)(2,1)}, f32[2,768]{1,0:T(2,128)S(1)}, f32[2,768]{1,0:T(2,128)S(1)}, f32[512,768]{1...) custom-call(s32[1]{0:T(128)} %constant.14.clone.1.which, ...), custom_call_target="tpu_custom_call" | custom-call | flops 94371840 | bytes 547392 | tf_op jit(solution)/shard_map/feed_back/pallas_call | solution.py:51
  161.7 2.8 %collective-permute-done.24 = bf16[384,1536]{1,0:T(8,128)(2,1)S(1)} collective-permute-done((bf16[384,1536]{1,0:T(8,128)(2,1)S(1)}, bf16[384,1536]{1,0:T(8,128)(2,1)S(1)}, u32[]{:S(2)}, u32[]{:S(2)}) %collective-permute-start.24) | collective-permute-done | bytes 1179680 | tf_op jit(solution)/shard_map/ppermute | solution.py:751
  164.6 1.6 collective-permute-start.26
  166.4 4.8 %attend_back.6 = (bf16[3,512,384]{2,1,0:T(8,128)(2,1)S(1)}, f32[1,768]{1,0:T(1,128)S(1)}) custom-call(s32[4]{0:T(128)S(1)} %copy-done.22, bf16[3,512,384]{2,1,0:T(8,128)(2,1)S(1)} %get-tuple-element.238.joint, f32[12,1,256]{2,1,0:T(1,128)S(1)} %get-tuple-element.239.lse, bf16[512,384]{1,0:T(8,128)(2,1)S(1)} %get-tuple-element.240.grad_att), custom_call_target="tpu_custom_call" | custom-call | flops 7864320 | bytes 43248 | tf_op jit(solution)/shard_map/attend_back/pallas_call | solution.py:51
  171.2 2.1 collective-permute-done.26
  175.1 3.3 %up_grad.3 = (bf16[384,1536]{1,0:T(8,128)(2,1)S(1)}, bf16[384,1536]{1,0:T(8,128)(2,1)S(1)}) custom-call(bf16[768,512]{1,0:T(8,128)(2,1)S(1)} %get-tuple-element.175.refs_0_, bf16[768,512]{1,0:T(8,128)(2,1)S(1)} %collective-permute-done.9.refs_1_, bf16[512,1536]{1,0:T(8,128)(2,1)S(1)} %copy-done.6, bf16[512,1536]{1,0:T(8,128)(2,1)S(1)} %collective-permute-done.27.refs_3_), custom_call_target="tpu_custom_call" | custom-call | flops 37748736 | bytes 110592 | tf_op jit(solution)/shard_map/up_grad/pallas_call | solution.py:51
  179.4 2.6 collective-permute-start.31
  182.2 4.8 %attend_back.7 = (bf16[3,512,384]{2,1,0:T(8,128)(2,1)S(1)}, f32[1,768]{1,0:T(1,128)S(1)}) custom-call(s32[4]{0:T(128)S(1)} %copy-done.22, bf16[3,512,384]{2,1,0:T(8,128)(2,1)S(1)} %get-tuple-element.253.joint, f32[12,1,256]{2,1,0:T(1,128)S(1)} %get-tuple-element.254.lse, bf16[512,384]{1,0:T(8,128)(2,1)S(1)} %get-tuple-element.255.grad_att), custom_call_target="tpu_custom_call" | custom-call | flops 7864320 | bytes 43248 | tf_op jit(solution)/shard_map/attend_back/pallas_call | solution.py:51
  187.0 4.2 %qkv_out_grad.3 = (bf16[384,1536]{1,0:T(8,128)(2,1)S(1)}, bf16[384,1536]{1,0:T(8,128)(2,1)S(1)}) custom-call(bf16[768,512]{1,0:T(8,128)(2,1)S(1)} %get-tuple-element.174.refs_0_, bf16[768,512]{1,0:T(8,128)(2,1)S(1)} %collective-permute-done.7.refs_1_, bf16[3,512,384]{2,1,0:T(8,128)(2,1)S(1)} %get-tuple-element.256.refs_2_.joint_own, ...), custom_call_target="tpu_custom_call" | custom-call | flops 37748736 | bytes 135168 | tf_op jit(solution)/shard_map/qkv_out_grad/pallas_call | solution.py:51
  191.3 2.8 %collective-permute-done.31 = bf16[48,3072]{1,0:T(8,128)(2,1)S(1)} collective-permute-done((bf16[48,3072]{1,0:T(8,128)(2,1)S(1)}, bf16[48,3072]{1,0:T(8,128)(2,1)S(1)}, u32[]{:S(2)}, u32[]{:S(2)}) %collective-permute-start.31) | collective-permute-done | bytes 294944 | tf_op jit(solution)/shard_map/ppermute | solution.py:751
  194.1 1.3 collective-permute-start.33
  197.3 7.7 %entry_back.3 = (f32[512,768]{1,0:T(8,128)}, f32[2,768]{1,0:T(2,128)S(1)}) custom-call(bf16[3,512,384]{2,1,0:T(8,128)(2,1)S(1)} %get-tuple-element.256.refs_2_.joint_own, bf16[3,512,384]{2,1,0:T(8,128)(2,1)S(1)} %get-tuple-element.251.joint_far, bf16[2,3,768,384]{3,2,1,0:T(8,128)(2,1)} %bitcast.21, bf16[2,3,768,384]{3,2,1,0:T(8,128)(2,1)} %collective-permute-done.weight_far, ...), custom_call_target="tpu_custom_call" | custom-call | flops 28311552 | bytes 227616 | tf_op jit(solution)/shard_map/entry_back/pallas_call | solution.py:51
  205.4 1.6 collective-permute-start.34
  209.2 11.8 %collective-permute-done.33 = bf16[384,1536]{1,0:T(8,128)(2,1)S(1)} collective-permute-done((bf16[384,1536]{1,0:T(8,128)(2,1)S(1)}, bf16[384,1536]{1,0:T(8,128)(2,1)S(1)}, u32[]{:S(2)}, u32[]{:S(2)}) %collective-permute-start.33) | collective-permute-done | bytes 1179680 | tf_op jit(solution)/shard_map/ppermute | solution.py:751
  221.0 1.3 collective-permute-start.40
  222.4 1.5 collective-permute-start.41
  224.7 1.4 collective-permute-start.38
  226.2 2.7 collective-permute-start.39
  229.0 10.8 %collective-permute-done.39 = bf16[96,1536]{1,0:T(8,128)(2,1)S(1)} collective-permute-done((bf16[96,1536]{1,0:T(8,128)(2,1)S(1)}, bf16[96,1536]{1,0:T(8,128)(2,1)S(1)}, u32[]{:S(2)}, u32[]{:S(2)}) %collective-permute-start.39) | collective-permute-done | bytes 294944 | tf_op jit(solution)/shard_map/ppermute | solution.py:751
  240.0 1.6 collective-permute-start.43
  241.6 1.4 collective-permute-start.44
  245.7 3.4 %collective-permute-start.46 = (bf16[48,1536]{1,0:T(8,128)(2,1)S(1)}, bf16[48,1536]{1,0:T(8,128)(2,1)S(1)}, u32[]{:S(2)}, u32[]{:S(2)}) collective-permute-start(bf16[48,1536]{1,0:T(8,128)(2,1)S(1)} %add_convert_fusion.15), channel_id=1, source_target_pairs={{0,16},{2,18},{4,20},{6,22},{8,24},{10,26},{12,28},{14,30},{16,0},... | collective-permute-start | bytes 442376 | tf_op jit(solution)/shard_map/ppermute | solution.py:751
  249.3 1.4 collective-permute-done.44
  250.8 2.9 %collective-permute-done.47 = f32[18,768]{1,0:T(8,128)S(1)} collective-permute-done((f32[18,768]{1,0:T(8,128)S(1)}, f32[18,768]{1,0:T(8,128)S(1)}, u32[]{:S(2)}, u32[]{:S(2)}) %collective-permute-start.47) | collective-permute-done | bytes 55328 | tf_op jit(solution)/shard_map/ppermute | solution.py:798
  253.8 2.0 collective-permute-start.49
  259.0 11.6 %collective-permute-done.48 = f32[18,768]{1,0:T(8,128)S(1)} collective-permute-done((f32[18,768]{1,0:T(8,128)S(1)}, f32[18,768]{1,0:T(8,128)S(1)}, u32[]{:S(2)}, u32[]{:S(2)}) %collective-permute-start.48) | collective-permute-done | bytes 55328 | tf_op jit(solution)/shard_map/ppermute | solution.py:798
  (193 shorter events, 27.7 us)
Async XLA Ops:
  0.7 6.7 %collective-permute-start = (bf16[2,3,768,384]{3,2,1,0:T(8,128)(2,1)}, bf16[2,3,768,384]{3,2,1,0:T(8,128)(2,1)}, u32[]{:S(2)}, u32[]{:S(2)}) collective-permute-start(bf16[2,3,768,384]{3,2,1,0:T(8,128)(2,1)} %bitcast.17), channel_id=1, source_target_pairs={{0,1},{1,0},{2,3},{3,2},{4,5},{5,4},{6,7},{7,6},{8,9},{9,8},{10,11... | collective-permute-start | bytes 10616840 | tf_op jit(solution)/shard_map/ppermute | solution.py:820
  1.2 5.9 %collective-permute-start.1 = (f32[2,2,384]{2,1,0:T(2,128)}, f32[2,2,384]{2,1,0:T(2,128)S(1)}, u32[]{:S(2)}, u32[]{:S(2)}) collective-permute-start(f32[2,2,384]{2,1,0:T(2,128)} %bias_own.3), channel_id=1, source_target_pairs={{0,1},{1,0},{2,3},{3,2},{4,5},{5,4},{6,7},{7,6},{8,9},{9,8},{10,11... | collective-permute-start | bytes 18440 | tf_op jit(solution)/shard_map/ppermute | solution.py:820
  7.4 10.7 %collective-permute-start.3 = (bf16[2,768,1536]{2,1,0:T(8,128)(2,1)}, bf16[2,768,1536]{2,1,0:T(8,128)(2,1)}, u32[]{:S(2)}, u32[]{:S(2)}) collective-permute-start(bf16[2,768,1536]{2,1,0:T(8,128)(2,1)} %up_own.7), channel_id=1, source_target_pairs={{0,1},{1,0},{2,3},{3,2},{4,5},{5,4},{6,7},{7,6},{8,9},{9,8},{10,11... | collective-permute-start | bytes 14155784 | tf_op jit(solution)/shard_map/ppermute | solution.py:820
  7.8 16.3 %collective-permute-start.5 = (bf16[2,1536,768]{2,1,0:T(8,128)(2,1)}, bf16[2,1536,768]{2,1,0:T(8,128)(2,1)}, u32[]{:S(2)}, u32[]{:S(2)}) collective-permute-start(bf16[2,1536,768]{2,1,0:T(8,128)(2,1)} %down_own.7), channel_id=1, source_target_pairs={{0,1},{1,0},{2,3},{3,2},{4,5},{5,4},{6,7},{7,6},{8,9},{9,8},{10,11... | collective-permute-start | bytes 14155784 | tf_op jit(solution)/shard_map/ppermute | solution.py:820
  7.9 10.2 %collective-permute-start.2 = (bf16[2,384,768]{2,1,0:T(8,128)(2,1)S(1)}, bf16[2,384,768]{2,1,0:T(8,128)(2,1)S(1)}, u32[]{:S(2)}, u32[]{:S(2)}) collective-permute-start(bf16[2,384,768]{2,1,0:T(8,128)(2,1)S(1)} %copy-done.26), channel_id=1, source_target_pairs={{0,1},{1,0},{2,3},{3,2},{4,5},{5,4},{6,7},{7,6},{8,9},{9,8},{10,11... | collective-permute-start | bytes 3538952 | tf_op jit(solution)/shard_map/ppermute | solution.py:820
  8.3 9.8 %collective-permute-start.4 = (f32[2,1536]{1,0:T(2,128)S(1)}, f32[2,1536]{1,0:T(2,128)S(1)}, u32[]{:S(2)}, u32[]{:S(2)}) collective-permute-start(f32[2,1536]{1,0:T(2,128)S(1)} %copy-done.21), channel_id=1, source_target_pairs={{0,1},{1,0},{2,3},{3,2},{4,5},{5,4},{6,7},{7,6},{8,9},{9,8},{10,11... | collective-permute-start | bytes 36872 | tf_op jit(solution)/shard_map/ppermute | solution.py:820
  42.8 11.1 %collective-permute-start.10 = (bf16[512,1536]{1,0:T(8,128)(2,1)}, bf16[512,1536]{1,0:T(8,128)(2,1)S(1)}, u32[]{:S(2)}, u32[]{:S(2)}) collective-permute-start(bf16[512,1536]{1,0:T(8,128)(2,1)} %get-tuple-element.176), channel_id=1, source_target_pairs={{0,1},{1,0},{2,3},{3,2},{4,5},{5,4},{6,7},{7,6},{8,9},{9,8},{10,11... | collective-permute-start | bytes 4718600 | tf_op jit(solution)/shard_map/ppermute | solution.py:820
  43.2 10.7 %collective-permute-start.6 = (bf16[768,512]{1,0:T(8,128)(2,1)S(1)}, bf16[768,512]{1,0:T(8,128)(2,1)S(1)}, u32[]{:S(2)}, u32[]{:S(2)}) collective-permute-start(bf16[768,512]{1,0:T(8,128)(2,1)S(1)} %get-tuple-element.173.refs_0_), channel_id=1, source_target_pairs={{0,1},{1,0},{2,3},{3,2},{4,5},{5,4},{6,7},{7,6},{8,9},{9,8},{10,11... | collective-permute-start | bytes 2359304 | tf_op jit(solution)/shard_map/ppermute | solution.py:820
  43.3 10.6 %collective-permute-start.7 = (bf16[768,512]{1,0:T(8,128)(2,1)S(1)}, bf16[768,512]{1,0:T(8,128)(2,1)S(1)}, u32[]{:S(2)}, u32[]{:S(2)}) collective-permute-start(bf16[768,512]{1,0:T(8,128)(2,1)S(1)} %get-tuple-element.174.refs_0_), channel_id=1, source_target_pairs={{0,1},{1,0},{2,3},{3,2},{4,5},{5,4},{6,7},{7,6},{8,9},{9,8},{10,11... | collective-permute-start | bytes 2359304 | tf_op jit(solution)/shard_map/ppermute | solution.py:820
  43.7 10.2 %collective-permute-start.9 = (bf16[768,512]{1,0:T(8,128)(2,1)S(1)}, bf16[768,512]{1,0:T(8,128)(2,1)S(1)}, u32[]{:S(2)}, u32[]{:S(2)}) collective-permute-start(bf16[768,512]{1,0:T(8,128)(2,1)S(1)} %get-tuple-element.175.refs_0_), channel_id=1, source_target_pairs={{0,1},{1,0},{2,3},{3,2},{4,5},{5,4},{6,7},{7,6},{8,9},{9,8},{10,11... | collective-permute-start | bytes 2359304 | tf_op jit(solution)/shard_map/ppermute | solution.py:820
  43.8 10.1 %collective-permute-start.8 = (bf16[512,384]{1,0:T(8,128)(2,1)S(1)}, bf16[512,384]{1,0:T(8,128)(2,1)S(1)}, u32[]{:S(2)}, u32[]{:S(2)}) collective-permute-start(bf16[512,384]{1,0:T(8,128)(2,1)S(1)} %get-tuple-element.165.att_far), channel_id=1, source_target_pairs={{0,1},{1,0},{2,3},{3,2},{4,5},{5,4},{6,7},{7,6},{8,9},{9,8},{10,11... | collective-permute-start | bytes 1179656 | tf_op jit(solution)/shard_map/ppermute | solution.py:820
  79.7 29.2 %collective-permute-start.13 = (bf16[384,1536]{1,0:T(8,128)(2,1)S(1)}, bf16[384,1536]{1,0:T(8,128)(2,1)S(1)}, u32[]{:S(2)}, u32[]{:S(2)}) collective-permute-start(bf16[384,1536]{1,0:T(8,128)(2,1)S(1)} %get-tuple-element.191), channel_id=1, source_target_pairs={{0,2},{2,0},{4,6},{6,4},{8,10},{10,8},{12,14},{14,12},{16,18},{18,... | collective-permute-start | bytes 3538952 | tf_op jit(solution)/shard_map/ppermute | solution.py:751
  98.3 13.2 %collective-permute-start.14 = (bf16[512,1536]{1,0:T(8,128)(2,1)}, bf16[512,1536]{1,0:T(8,128)(2,1)S(1)}, u32[]{:S(2)}, u32[]{:S(2)}) collective-permute-start(bf16[512,1536]{1,0:T(8,128)(2,1)} %get-tuple-element.200), channel_id=1, source_target_pairs={{0,1},{1,0},{2,3},{3,2},{4,5},{5,4},{6,7},{7,6},{8,9},{9,8},{10,11... | collective-permute-start | bytes 4718600 | tf_op jit(solution)/shard_map/ppermute | solution.py:820
  98.4 13.0 %collective-permute-start.11 = (bf16[768,512]{1,0:T(8,128)(2,1)S(1)}, bf16[768,512]{1,0:T(8,128)(2,1)S(1)}, u32[]{:S(2)}, u32[]{:S(2)}) collective-permute-start(bf16[768,512]{1,0:T(8,128)(2,1)S(1)} %get-tuple-element.180.refs_0_), channel_id=1, source_target_pairs={{0,1},{1,0},{2,3},{3,2},{4,5},{5,4},{6,7},{7,6},{8,9},{9,8},{10,11... | collective-permute-start | bytes 2359304 | tf_op jit(solution)/shard_map/ppermute | solution.py:820
  109.1 20.4 %collective-permute-start.16 = (bf16[192,1536]{1,0:T(8,128)(2,1)S(1)}, bf16[192,1536]{1,0:T(8,128)(2,1)S(1)}, u32[]{:S(2)}, u32[]{:S(2)}) collective-permute-start(bf16[192,1536]{1,0:T(8,128)(2,1)S(1)} %add_convert_fusion.5), channel_id=1, source_target_pairs={{0,4},{2,6},{4,0},{6,2},{8,12},{10,14},{12,8},{14,10},{16,20},{18,... | collective-permute-start | bytes 1769480 | tf_op jit(solution)/shard_map/ppermute | solution.py:751
  110.9 5.4 %collective-permute-start.19 = (bf16[512,384]{1,0:T(8,128)(2,1)S(1)}, bf16[512,384]{1,0:T(8,128)(2,1)S(1)}, u32[]{:S(2)}, u32[]{:S(2)}) collective-permute-start(bf16[512,384]{1,0:T(8,128)(2,1)S(1)} %get-tuple-element.172.att_far), channel_id=1, source_target_pairs={{0,1},{1,0},{2,3},{3,2},{4,5},{5,4},{6,7},{7,6},{8,9},{9,8},{10,11... | collective-permute-start | bytes 1179656 | tf_op jit(solution)/shard_map/ppermute | solution.py:820
  110.9 20.5 %collective-permute-start.17 = (bf16[3,512,384]{2,1,0:T(8,128)(2,1)S(1)}, bf16[3,512,384]{2,1,0:T(8,128)(2,1)S(1)}, u32[]{:S(2)}, u32[]{:S(2)}) collective-permute-start(bf16[3,512,384]{2,1,0:T(8,128)(2,1)S(1)} %get-tuple-element.210.joint_far), channel_id=1, source_target_pairs={{0,1},{1,0},{2,3},{3,2},{4,5},{5,4},{6,7},{7,6},{8,9},{9,8},{10,11... | collective-permute-start | bytes 3538952 | tf_op jit(solution)/shard_map/ppermute | solution.py:820
  114.8 28.0 %collective-permute-start.21 = (bf16[384,1536]{1,0:T(8,128)(2,1)S(1)}, bf16[384,1536]{1,0:T(8,128)(2,1)S(1)}, u32[]{:S(2)}, u32[]{:S(2)}) collective-permute-start(bf16[384,1536]{1,0:T(8,128)(2,1)S(1)} %get-tuple-element.223), channel_id=1, source_target_pairs={{0,2},{2,0},{4,6},{6,4},{8,10},{10,8},{12,14},{14,12},{16,18},{18,... | collective-permute-start | bytes 3538952 | tf_op jit(solution)/shard_map/ppermute | solution.py:751
  116.3 13.5 %collective-permute-start.15 = (bf16[768,512]{1,0:T(8,128)(2,1)S(1)}, bf16[768,512]{1,0:T(8,128)(2,1)S(1)}, u32[]{:S(2)}, u32[]{:S(2)}) collective-permute-start(bf16[768,512]{1,0:T(8,128)(2,1)S(1)} %copy-done.9), channel_id=1, source_target_pairs={{0,1},{1,0},{2,3},{3,2},{4,5},{5,4},{6,7},{7,6},{8,9},{9,8},{10,11... | collective-permute-start | bytes 2359304 | tf_op jit(solution)/shard_map/ppermute | solution.py:820
  116.3 15.1 %collective-permute-start.18 = (bf16[768,512]{1,0:T(8,128)(2,1)S(1)}, bf16[768,512]{1,0:T(8,128)(2,1)S(1)}, u32[]{:S(2)}, u32[]{:S(2)}) collective-permute-start(bf16[768,512]{1,0:T(8,128)(2,1)S(1)} %get-tuple-element.217.refs_4_), channel_id=1, source_target_pairs={{0,1},{1,0},{2,3},{3,2},{4,5},{5,4},{6,7},{7,6},{8,9},{9,8},{10,11... | collective-permute-start | bytes 2359304 | tf_op jit(solution)/shard_map/ppermute | solution.py:820
  129.5 6.7 %collective-permute-start.20 = (bf16[768,512]{1,0:T(8,128)(2,1)S(1)}, bf16[768,512]{1,0:T(8,128)(2,1)S(1)}, u32[]{:S(2)}, u32[]{:S(2)}) collective-permute-start(bf16[768,512]{1,0:T(8,128)(2,1)S(1)} %get-tuple-element.219.refs_0_), channel_id=1, source_target_pairs={{0,1},{1,0},{2,3},{3,2},{4,5},{5,4},{6,7},{7,6},{8,9},{9,8},{10,11... | collective-permute-start | bytes 2359304 | tf_op jit(solution)/shard_map/ppermute | solution.py:820
  129.8 9.9 %collective-permute-start.22 = (bf16[96,1536]{1,0:T(8,128)(2,1)S(1)}, bf16[96,1536]{1,0:T(8,128)(2,1)S(1)}, u32[]{:S(2)}, u32[]{:S(2)}) collective-permute-start(bf16[96,1536]{1,0:T(8,128)(2,1)S(1)} %add_convert_fusion.11), channel_id=1, source_target_pairs={{0,8},{2,10},{4,12},{6,14},{8,0},{10,2},{12,4},{14,6},{16,24},{18,... | collective-permute-start | bytes 884744 | tf_op jit(solution)/shard_map/ppermute | solution.py:751
  135.7 28.8 %collective-permute-start.24 = (bf16[384,1536]{1,0:T(8,128)(2,1)S(1)}, bf16[384,1536]{1,0:T(8,128)(2,1)S(1)}, u32[]{:S(2)}, u32[]{:S(2)}) collective-permute-start(bf16[384,1536]{1,0:T(8,128)(2,1)S(1)} %get-tuple-element.226), channel_id=1, source_target_pairs={{0,8},{2,10},{4,12},{6,14},{8,0},{10,2},{12,4},{14,6},{16,24},{18,... | collective-permute-start | bytes 3538952 | tf_op jit(solution)/shard_map/ppermute | solution.py:751
  142.9 21.6 %collective-permute-start.23 = (bf16[192,1536]{1,0:T(8,128)(2,1)S(1)}, bf16[192,1536]{1,0:T(8,128)(2,1)S(1)}, u32[]{:S(2)}, u32[]{:S(2)}) collective-permute-start(bf16[192,1536]{1,0:T(8,128)(2,1)S(1)} %add_convert_fusion.4), channel_id=1, source_target_pairs={{0,4},{2,6},{4,0},{6,2},{8,12},{10,14},{12,8},{14,10},{16,20},{18,... | collective-permute-start | bytes 1769480 | tf_op jit(solution)/shard_map/ppermute | solution.py:751
  143.2 30.2 %collective-permute-start.25 = (bf16[384,1536]{1,0:T(8,128)(2,1)S(1)}, bf16[384,1536]{1,0:T(8,128)(2,1)}, u32[]{:S(2)}, u32[]{:S(2)}) collective-permute-start(bf16[384,1536]{1,0:T(8,128)(2,1)S(1)} %get-tuple-element.236), channel_id=1, source_target_pairs={{0,2},{2,0},{4,6},{6,4},{8,10},{10,8},{12,14},{14,12},{16,18},{18,... | collective-permute-start | bytes 3538952 | tf_op jit(solution)/shard_map/ppermute | solution.py:751
  161.1 13.7 %collective-permute-start.27 = (bf16[512,1536]{1,0:T(8,128)(2,1)}, bf16[512,1536]{1,0:T(8,128)(2,1)S(1)}, u32[]{:S(2)}, u32[]{:S(2)}) collective-permute-start(bf16[512,1536]{1,0:T(8,128)(2,1)} %get-tuple-element.248), channel_id=1, source_target_pairs={{0,1},{1,0},{2,3},{3,2},{4,5},{5,4},{6,7},{7,6},{8,9},{9,8},{10,11... | collective-permute-start | bytes 4718600 | tf_op jit(solution)/shard_map/ppermute | solution.py:820
  161.2 17.1 %collective-permute-start.28 = (bf16[768,512]{1,0:T(8,128)(2,1)S(1)}, bf16[768,512]{1,0:T(8,128)(2,1)S(1)}, u32[]{:S(2)}, u32[]{:S(2)}) collective-permute-start(bf16[768,512]{1,0:T(8,128)(2,1)S(1)} %get-tuple-element.250.refs_4_), channel_id=1, source_target_pairs={{0,1},{1,0},{2,3},{3,2},{4,5},{5,4},{6,7},{7,6},{8,9},{9,8},{10,11... | collective-permute-start | bytes 2359304 | tf_op jit(solution)/shard_map/ppermute | solution.py:820
  164.6 8.7 %collective-permute-start.26 = (bf16[96,1536]{1,0:T(8,128)(2,1)S(1)}, bf16[96,1536]{1,0:T(8,128)(2,1)S(1)}, u32[]{:S(2)}, u32[]{:S(2)}) collective-permute-start(bf16[96,1536]{1,0:T(8,128)(2,1)S(1)} %add_convert_fusion.10), channel_id=1, source_target_pairs={{0,8},{2,10},{4,12},{6,14},{8,0},{10,2},{12,4},{14,6},{16,24},{18,... | collective-permute-start | bytes 884744 | tf_op jit(solution)/shard_map/ppermute | solution.py:751
  171.2 7.2 %collective-permute-start.29 = (bf16[3,512,384]{2,1,0:T(8,128)(2,1)S(1)}, bf16[3,512,384]{2,1,0:T(8,128)(2,1)S(1)}, u32[]{:S(2)}, u32[]{:S(2)}) collective-permute-start(bf16[3,512,384]{2,1,0:T(8,128)(2,1)S(1)} %get-tuple-element.251.joint_far), channel_id=1, source_target_pairs={{0,1},{1,0},{2,3},{3,2},{4,5},{5,4},{6,7},{7,6},{8,9},{9,8},{10,11... | collective-permute-start | bytes 3538952 | tf_op jit(solution)/shard_map/ppermute | solution.py:820
  178.4 26.8 %collective-permute-start.32 = (bf16[384,1536]{1,0:T(8,128)(2,1)S(1)}, bf16[384,1536]{1,0:T(8,128)(2,1)S(1)}, u32[]{:S(2)}, u32[]{:S(2)}) collective-permute-start(bf16[384,1536]{1,0:T(8,128)(2,1)S(1)} %get-tuple-element.269), channel_id=1, source_target_pairs={{0,2},{2,0},{4,6},{6,4},{8,10},{10,8},{12,14},{14,12},{16,18},{18,... | collective-permute-start | bytes 3538952 | tf_op jit(solution)/shard_map/ppermute | solution.py:751
  178.9 15.1 %collective-permute-start.30 = (bf16[192,1536]{1,0:T(8,128)(2,1)S(1)}, bf16[192,1536]{1,0:T(8,128)(2,1)S(1)}, u32[]{:S(2)}, u32[]{:S(2)}) collective-permute-start(bf16[192,1536]{1,0:T(8,128)(2,1)S(1)} %add_convert_fusion.3), channel_id=1, source_target_pairs={{0,4},{2,6},{4,0},{6,2},{8,12},{10,14},{12,8},{14,10},{16,20},{18,... | collective-permute-start | bytes 1769480 | tf_op jit(solution)/shard_map/ppermute | solution.py:751
  179.4 14.7 %collective-permute-start.31 = (bf16[48,3072]{1,0:T(8,128)(2,1)S(1)}, bf16[48,3072]{1,0:T(8,128)(2,1)S(1)}, u32[]{:S(2)}, u32[]{:S(2)}) collective-permute-start(bf16[48,3072]{1,0:T(8,128)(2,1)S(1)} %pad_maximum_fusion), channel_id=1, source_target_pairs={{0,16},{2,18},{4,20},{6,22},{8,24},{10,26},{12,28},{14,30},{16,0},... | collective-permute-start | bytes 884744 | tf_op jit(solution)/shard_map/ppermute | solution.py:751
  194.1 26.9 %collective-permute-start.33 = (bf16[384,1536]{1,0:T(8,128)(2,1)S(1)}, bf16[384,1536]{1,0:T(8,128)(2,1)S(1)}, u32[]{:S(2)}, u32[]{:S(2)}) collective-permute-start(bf16[384,1536]{1,0:T(8,128)(2,1)S(1)} %get-tuple-element.277), channel_id=1, source_target_pairs={{0,4},{2,6},{4,0},{6,2},{8,12},{10,14},{12,8},{14,10},{16,20},{18,... | collective-permute-start | bytes 3538952 | tf_op jit(solution)/shard_map/ppermute | solution.py:751
  196.5 11.6 %collective-permute-start.37 = (bf16[96,1536]{1,0:T(8,128)(2,1)S(1)}, bf16[96,1536]{1,0:T(8,128)(2,1)S(1)}, u32[]{:S(2)}, u32[]{:S(2)}) collective-permute-start(bf16[96,1536]{1,0:T(8,128)(2,1)S(1)} %add_convert_fusion.9), channel_id=1, source_target_pairs={{0,8},{2,10},{4,12},{6,14},{8,0},{10,2},{12,4},{14,6},{16,24},{18,... | collective-permute-start | bytes 884744 | tf_op jit(solution)/shard_map/ppermute | solution.py:751
  205.4 15.6 %collective-permute-start.34 = (bf16[192,1536]{1,0:T(8,128)(2,1)S(1)}, bf16[192,1536]{1,0:T(8,128)(2,1)S(1)}, u32[]{:S(2)}, u32[]{:S(2)}) collective-permute-start(bf16[192,1536]{1,0:T(8,128)(2,1)S(1)} %add_convert_fusion.1), channel_id=1, source_target_pairs={{0,8},{2,10},{4,12},{6,14},{8,0},{10,2},{12,4},{14,6},{16,24},{18,... | collective-permute-start | bytes 1769480 | tf_op jit(solution)/shard_map/ppermute | solution.py:751
  207.0 14.0 %collective-permute-start.36 = (bf16[192,1536]{1,0:T(8,128)(2,1)S(1)}, bf16[192,1536]{1,0:T(8,128)(2,1)S(1)}, u32[]{:S(2)}, u32[]{:S(2)}) collective-permute-start(bf16[192,1536]{1,0:T(8,128)(2,1)S(1)} %add_convert_fusion.2), channel_id=1, source_target_pairs={{0,2},{2,0},{4,6},{6,4},{8,10},{10,8},{12,14},{14,12},{16,18},{18,... | collective-permute-start | bytes 1769480 | tf_op jit(solution)/shard_map/ppermute | solution.py:751
  208.1 12.8 %collective-permute-start.35 = (f32[18,768]{1,0:T(8,128)S(1)}, f32[18,768]{1,0:T(8,128)S(1)}, u32[]{:S(2)}, u32[]{:S(2)}) collective-permute-start(f32[18,768]{1,0:T(8,128)S(1)} %get-tuple-element.280), channel_id=1, source_target_pairs={{0,1},{1,0},{2,3},{3,2},{4,5},{5,4},{6,7},{7,6},{8,9},{9,8},{10,11... | collective-permute-start | bytes 165896 | tf_op jit(solution)/shard_map/ppermute | solution.py:820
  221.0 18.9 %collective-permute-start.40 = (f32[18,768]{1,0:T(8,128)S(1)}, f32[18,768]{1,0:T(8,128)S(1)}, u32[]{:S(2)}, u32[]{:S(2)}) collective-permute-start(f32[18,768]{1,0:T(8,128)S(1)} %add.170), channel_id=1, source_target_pairs={{0,2},{2,0},{4,6},{6,4},{8,10},{10,8},{12,14},{14,12},{16,18},{18,... | collective-permute-start | bytes 165896 | tf_op jit(solution)/shard_map/ppermute | solution.py:798
  222.4 17.6 %collective-permute-start.41 = (f32[18,768]{1,0:T(8,128)S(1)}, f32[18,768]{1,0:T(8,128)S(1)}, u32[]{:S(2)}, u32[]{:S(2)}) collective-permute-start(f32[18,768]{1,0:T(8,128)S(1)} %add.170), channel_id=1, source_target_pairs={{0,4},{2,6},{4,0},{6,2},{8,12},{10,14},{12,8},{14,10},{16,20},{18,... | collective-permute-start | bytes 165896 | tf_op jit(solution)/shard_map/ppermute | solution.py:798
  223.9 16.1 %collective-permute-start.42 = (f32[18,768]{1,0:T(8,128)S(1)}, f32[18,768]{1,0:T(8,128)S(1)}, u32[]{:S(2)}, u32[]{:S(2)}) collective-permute-start(f32[18,768]{1,0:T(8,128)S(1)} %add.170), channel_id=1, source_target_pairs={{0,6},{2,4},{4,2},{6,0},{8,14},{10,12},{12,10},{14,8},{16,22},{18,... | collective-permute-start | bytes 165896 | tf_op jit(solution)/shard_map/ppermute | solution.py:798
  224.7 15.0 %collective-permute-start.38 = (bf16[192,1536]{1,0:T(8,128)(2,1)S(1)}, bf16[192,1536]{1,0:T(8,128)(2,1)S(1)}, u32[]{:S(2)}, u32[]{:S(2)}) collective-permute-start(bf16[192,1536]{1,0:T(8,128)(2,1)S(1)} %add_convert_fusion), channel_id=1, source_target_pairs={{0,2},{2,0},{4,6},{6,4},{8,10},{10,8},{12,14},{14,12},{16,18},{18,... | collective-permute-start | bytes 1769480 | tf_op jit(solution)/shard_map/ppermute | solution.py:751
  226.2 13.6 %collective-permute-start.39 = (bf16[96,1536]{1,0:T(8,128)(2,1)S(1)}, bf16[96,1536]{1,0:T(8,128)(2,1)S(1)}, u32[]{:S(2)}, u32[]{:S(2)}) collective-permute-start(bf16[96,1536]{1,0:T(8,128)(2,1)S(1)} %add_convert_fusion.8), channel_id=1, source_target_pairs={{0,16},{2,18},{4,20},{6,22},{8,24},{10,26},{12,28},{14,30},{16,0},... | collective-permute-start | bytes 884744 | tf_op jit(solution)/shard_map/ppermute | solution.py:751
  240.0 9.3 %collective-permute-start.43 = (bf16[96,1536]{1,0:T(8,128)(2,1)S(1)}, bf16[96,1536]{1,0:T(8,128)(2,1)S(1)}, u32[]{:S(2)}, u32[]{:S(2)}) collective-permute-start(bf16[96,1536]{1,0:T(8,128)(2,1)S(1)} %add_convert_fusion.7), channel_id=1, source_target_pairs={{0,8},{2,10},{4,12},{6,14},{8,0},{10,2},{12,4},{14,6},{16,24},{18,... | collective-permute-start | bytes 884744 | tf_op jit(solution)/shard_map/ppermute | solution.py:751
  241.6 9.1 %collective-permute-start.44 = (bf16[96,1536]{1,0:T(8,128)(2,1)S(1)}, bf16[96,1536]{1,0:T(8,128)(2,1)S(1)}, u32[]{:S(2)}, u32[]{:S(2)}) collective-permute-start(bf16[96,1536]{1,0:T(8,128)(2,1)S(1)} %add_convert_fusion.6), channel_id=1, source_target_pairs={{0,4},{2,6},{4,0},{6,2},{8,12},{10,14},{12,8},{14,10},{16,20},{18,... | collective-permute-start | bytes 884744 | tf_op jit(solution)/shard_map/ppermute | solution.py:751
  245.0 8.7 %collective-permute-start.45 = (bf16[48,1536]{1,0:T(8,128)(2,1)S(1)}, bf16[48,1536]{1,0:T(8,128)(2,1)S(1)}, u32[]{:S(2)}, u32[]{:S(2)}) collective-permute-start(bf16[48,1536]{1,0:T(8,128)(2,1)S(1)} %add_convert_fusion.14), channel_id=1, source_target_pairs={{0,4},{2,6},{4,0},{6,2},{8,12},{10,14},{12,8},{14,10},{16,20},{18,... | collective-permute-start | bytes 442376 | tf_op jit(solution)/shard_map/ppermute | solution.py:751
  245.7 8.0 %collective-permute-start.46 = (bf16[48,1536]{1,0:T(8,128)(2,1)S(1)}, bf16[48,1536]{1,0:T(8,128)(2,1)S(1)}, u32[]{:S(2)}, u32[]{:S(2)}) collective-permute-start(bf16[48,1536]{1,0:T(8,128)(2,1)S(1)} %add_convert_fusion.15), channel_id=1, source_target_pairs={{0,16},{2,18},{4,20},{6,22},{8,24},{10,26},{12,28},{14,30},{16,0},... | collective-permute-start | bytes 442376 | tf_op jit(solution)/shard_map/ppermute | solution.py:751
  253.8 16.9 %collective-permute-start.49 = (bf16[48,3072]{1,0:T(8,128)(2,1)S(1)}, bf16[48,3072]{1,0:T(8,128)(2,1)S(1)}, u32[]{:S(2)}, u32[]{:S(2)}) collective-permute-start(bf16[48,3072]{1,0:T(8,128)(2,1)S(1)} %pad_maximum_fusion.1), channel_id=1, source_target_pairs={{0,16},{2,18},{4,20},{6,22},{8,24},{10,26},{12,28},{14,30},{16,0},... | collective-permute-start | bytes 884744 | tf_op jit(solution)/shard_map/ppermute | solution.py:751
  255.7 14.9 %collective-permute-start.48 = (f32[18,768]{1,0:T(8,128)S(1)}, f32[18,768]{1,0:T(8,128)S(1)}, u32[]{:S(2)}, u32[]{:S(2)}) collective-permute-start(f32[18,768]{1,0:T(8,128)S(1)} %add.190), channel_id=1, source_target_pairs={{0,16},{2,18},{4,20},{6,22},{8,24},{10,26},{12,28},{14,30},{16,0},... | collective-permute-start | bytes 165896 | tf_op jit(solution)/shard_map/ppermute | solution.py:798
  (35 other events, 304.8 us)

commit v5 on v4

--- a/solution.py
+++ b/solution.py
@@ -903,7 +903,7 @@
             [whole()] * 6,
             [pltpu.VMEM((2, 3, width, half), BF16), pltpu.SemaphoreType.DMA((2, 3))],
             flops=12 * tokens * width * half + 8 * tokens * slots * half,
-            limit=44,
+            limit=32,
         )
         return results[0::2], results[1::2]
 

time: 273 us -> 270 us (0.989)
  no operation moved by 1% of the time
where the time goes in v5:
time: 270 us
  Pallas kernels  151 us (56%)
  waiting for transfers between devices  64.4 us (24%)
  starting transfers between devices  44.1 us (16%)
  other arithmetic  5.38 us (2%)
  local copies, waits for them, and re-layouts  3.79 us (1%)
    pallas_call x24, Pallas kernels, call(): pl.pallas_call(body, name=name, grid=grid, in_specs=in_specs, out_specs=o...  151 us
    ppermute x22, waiting for transfers between devices, start(): self.incoming = lax.ppermute(self.outgoing, 'dp', flip(self.order.pop(0)))  40.2 us
    ppermute x22, starting transfers between devices, start(): self.incoming = lax.ppermute(self.outgoing, 'dp', flip(self.order.pop(0)))  33.6 us
    ppermute x5, waiting for transfers between devices, turn(): lax.ppermute(self.mine, 'dp', [(index, index ^ mask) for index in range(s...  14.5 us
    ppermute x23, waiting for transfers between devices, swap(): return lax.ppermute(values, 'tensor', [(0, 1), (1, 0)])  9.81 us
    ppermute x23, starting transfers between devices, swap(): return lax.ppermute(values, 'tensor', [(0, 1), (1, 0)])  5.73 us
  transfers between devices with their start and end apart: 50, of which 15 were waited for; matrix products, arithmetic and copies ran while one was open for 3% of the time, Pallas kernels for 41%

profile of v5, /device:TPU:0, one launch (start us, length us, event | category | flops | bytes accessed | tf_op | source)
XLA Modules:
  0.0 269.9 jit_solution(12733391786020797702)
XLA Ops:
  2.9 4.1 %prep.1 = (bf16[512,768]{1,0:T(8,128)(2,1)S(1)}, bf16[768,512]{1,0:T(8,128)(2,1)S(1)}, bf16[768,512]{1,0:T(8,128)(2,1)S(1)}, f32[512,768]{1,0:T(8,128)S(1)}) custom-call(bf16[512,768]{1,0:T(8,128)(2,1)S(1)} %bitcast.13, bf16[512,768]{1,0:T(8,128)(2,1)S(1)} %bitcast.16, f32[2,2,768]{2,1,0:T(2,128)S(1)} %copy-done.9, f32[2,2,768]{2,1,0:T(2,128)S(1)} %copy-done.10, ...), custom_call_target="tpu_custom_call" | custom-call | flops 18874368 | bytes 104832 | tf_op jit(solution)/shard_map/prep/pallas_call | solution.py:51
  8.4 9.7 %attend.2 = (bf16[3,512,384]{2,1,0:T(8,128)(2,1)S(1)}, bf16[3,512,384]{2,1,0:T(8,128)(2,1)S(1)}, bf16[512,384]{1,0:T(8,128)(2,1)S(1)}, bf16[512,384]{1,0:T(8,128...) custom-call(s32[1]{0:T(128)} %constant.14.clone.1.which, s32[4]{0:T(128)S(1)} %copy-done.13, ...), custom_call_target="tpu_custom_call" | custom-call | flops 34603008 | bytes 172608 | tf_op jit(solution)/shard_map/attend/pallas_call | solution.py:51
  18.1 6.0 %collective-permute-done.5.down_far = bf16[2,1536,768]{2,1,0:T(8,128)(2,1)} collective-permute-done((bf16[2,1536,768]{2,1,0:T(8,128)(2,1)}, bf16[2,1536,768]{2,1,0:T(8,128)(2,1)}, u32[]{:S(2)}, u32[]{:S(2)}) %collective-permute-start.5) | collective-permute-done | bytes 4718624 | tf_op jit(solution)/shard_map/ppermute | solution.py:820
  24.1 17.7 %feed.2 = (f32[512,768]{1,0:T(8,128)S(1)}, bf16[768,512]{1,0:T(8,128)(2,1)S(1)}, bf16[512,1536]{1,0:T(8,128)(2,1)}, bf16[512,1536]{1,0:T(8,128)(2,1)}, bf16[512,...) custom-call(s32[4]{0:T(128)S(1)} %copy-done.13, ...), custom_call_target="tpu_custom_call" | custom-call | flops 94371840 | bytes 560064 | tf_op jit(solution)/shard_map/feed/pallas_call | solution.py:51
  43.3 9.7 %attend.3 = (bf16[3,512,384]{2,1,0:T(8,128)(2,1)S(1)}, bf16[3,512,384]{2,1,0:T(8,128)(2,1)S(1)}, bf16[512,384]{1,0:T(8,128)(2,1)S(1)}, bf16[512,384]{1,0:T(8,128...) custom-call(s32[1]{0:T(128)} %constant.36.clone.1.which, s32[4]{0:T(128)S(1)} %copy-done.13, ...), custom_call_target="tpu_custom_call" | custom-call | flops 34603008 | bytes 172608 | tf_op jit(solution)/shard_map/attend/pallas_call | solution.py:51
  53.0 16.6 %feed.3 = (f32[512,768]{1,0:T(8,128)S(1)}, bf16[768,512]{1,0:T(8,128)(2,1)S(1)}, bf16[512,1536]{1,0:T(8,128)(2,1)}, bf16[512,1536]{1,0:T(8,128)(2,1)}, bf16[512,...) custom-call(s32[4]{0:T(128)S(1)} %copy-done.13, ...), custom_call_target="tpu_custom_call" | custom-call | flops 94371840 | bytes 547872 | tf_op jit(solution)/shard_map/feed/pallas_call | solution.py:51
  69.8 3.5 %collective-permute-done.12.refs_3_ = bf16[512,1536]{1,0:T(8,128)(2,1)S(1)} collective-permute-done((bf16[512,1536]{1,0:T(8,128)(2,1)}, bf16[512,1536]{1,0:T(8,128)(2,1)S(1)}, u32[]{:S(2)}, u32[]{:S(2)}) %collective-permute-start.12) | collective-permute-done | bytes 1572896 | tf_op jit(solution)/shard_map/ppermute | solution.py:820
  73.3 4.3 %down_grad.2 = (bf16[384,1536]{1,0:T(8,128)(2,1)S(1)}, bf16[384,1536]{1,0:T(8,128)(2,1)S(1)}) custom-call(bf16[768,512]{1,0:T(8,128)(2,1)S(1)} %get-tuple-element.173.refs_0_, bf16[768,512]{1,0:T(8,128)(2,1)S(1)} %collective-permute-done.6.refs_1_, bf16[512,1536]{1,0:T(8,128)(2,1)} %get-tuple-element.184.refs_2_, ...), custom_call_target="tpu_custom_call" | custom-call | flops 37748736 | bytes 110592 | tf_op jit(solution)/shard_map/down_grad/pallas_call | solution.py:51
  77.6 2.7 %collective-permute-start.13 = (bf16[384,1536]{1,0:T(8,128)(2,1)S(1)}, bf16[384,1536]{1,0:T(8,128)(2,1)S(1)}, u32[]{:S(2)}, u32[]{:S(2)}) collective-permute-start(bf16[384,1536]{1,0:T(8,128)(2,1)S(1)} %get-tuple-element.191), channel_id=1, source_target_pairs={{0,2},{2,0},{4,6},{6,4},{8,10},{10,8},{12,14},{14,12},{16,18},{18,... | collective-permute-start | bytes 3538952 | tf_op jit(solution)/shard_map/ppermute | solution.py:751
  80.3 15.9 %feed_back.2 = (bf16[512,1536]{1,0:T(8,128)(2,1)}, bf16[512,1536]{1,0:T(8,128)(2,1)}, f32[2,768]{1,0:T(2,128)S(1)}, f32[2,768]{1,0:T(2,128)S(1)}, f32[512,768]{1...) custom-call(s32[1]{0:T(128)} %constant.36.clone.1.which, ...), custom_call_target="tpu_custom_call" | custom-call | flops 94371840 | bytes 547392 | tf_op jit(solution)/shard_map/feed_back/pallas_call | solution.py:51
  96.8 4.8 %attend_back.4 = (bf16[3,512,384]{2,1,0:T(8,128)(2,1)S(1)}, f32[1,768]{1,0:T(1,128)S(1)}) custom-call(s32[4]{0:T(128)S(1)} %copy-done.13, bf16[3,512,384]{2,1,0:T(8,128)(2,1)S(1)} %get-tuple-element.192.joint, f32[12,1,256]{2,1,0:T(1,128)S(1)} %get-tuple-element.193.lse, bf16[512,384]{1,0:T(8,128)(2,1)S(1)} %get-tuple-element.194.grad_att), custom_call_target="tpu_custom_call" | custom-call | flops 7864320 | bytes 43248 | tf_op jit(solution)/shard_map/attend_back/pallas_call | solution.py:51
  101.6 5.2 %collective-permute-done.13 = bf16[384,1536]{1,0:T(8,128)(2,1)S(1)} collective-permute-done((bf16[384,1536]{1,0:T(8,128)(2,1)S(1)}, bf16[384,1536]{1,0:T(8,128)(2,1)S(1)}, u32[]{:S(2)}, u32[]{:S(2)}) %collective-permute-start.13) | collective-permute-done | bytes 1179680 | tf_op jit(solution)/shard_map/ppermute | solution.py:751
  107.0 1.8 collective-permute-start.16
  109.3 3.3 %up_grad.2 = (bf16[384,1536]{1,0:T(8,128)(2,1)S(1)}, bf16[384,1536]{1,0:T(8,128)(2,1)S(1)}) custom-call(bf16[768,512]{1,0:T(8,128)(2,1)S(1)} %get-tuple-element.180.refs_0_, bf16[768,512]{1,0:T(8,128)(2,1)S(1)} %collective-permute-done.11.refs_1_, bf16[512,1536]{1,0:T(8,128)(2,1)S(1)} %copy-done.7, bf16[512,1536]{1,0:T(8,128)(2,1)S(1)} %collective-permute-done.14.refs_3_), custom_call_target="tpu_custom_call" | custom-call | flops 37748736 | bytes 110592 | tf_op jit(solution)/shard_map/up_grad/pallas_call | solution.py:51
  112.6 1.6 collective-permute-start.21
  114.7 4.7 %attend_back.5 = (bf16[3,512,384]{2,1,0:T(8,128)(2,1)S(1)}, f32[1,768]{1,0:T(1,128)S(1)}) custom-call(s32[4]{0:T(128)S(1)} %copy-done.13, bf16[3,512,384]{2,1,0:T(8,128)(2,1)S(1)} %get-tuple-element.204.joint, f32[12,1,256]{2,1,0:T(1,128)S(1)} %get-tuple-element.205.lse, bf16[512,384]{1,0:T(8,128)(2,1)S(1)} %get-tuple-element.206.grad_att), custom_call_target="tpu_custom_call" | custom-call | flops 7864320 | bytes 43248 | tf_op jit(solution)/shard_map/attend_back/pallas_call | solution.py:51
  119.5 7.9 %entry_back.2 = (f32[512,768]{1,0:T(8,128)S(1)}, f32[2,768]{1,0:T(2,128)S(1)}, bf16[768,512]{1,0:T(8,128)(2,1)S(1)}) custom-call(bf16[3,512,384]{2,1,0:T(8,128)(2,1)S(1)} %get-tuple-element.216.joint_own.refs_2_, bf16[3,512,384]{2,1,0:T(8,128)(2,1)S(1)} %get-tuple-element.210.joint_far, bf16[2,3,768,384]{3,2,1,0:T(8,128)(2,1)} %bitcast.20, ...), custom_call_target="tpu_custom_call" | custom-call | flops 28311552 | bytes 252192 | tf_op jit(solution)/shard_map/entry_back/pallas_call | solution.py:51
  127.6 1.6 collective-permute-start.22
  129.3 4.2 %qkv_out_grad.2 = (bf16[384,1536]{1,0:T(8,128)(2,1)S(1)}, bf16[384,1536]{1,0:T(8,128)(2,1)S(1)}) custom-call(bf16[768,512]{1,0:T(8,128)(2,1)S(1)} %get-tuple-element.213.refs_0_, bf16[768,512]{1,0:T(8,128)(2,1)S(1)} %collective-permute-done.15.refs_1_, bf16[3,512,384]{2,1,0:T(8,128)(2,1)S(1)} %get-tuple-element.216.joint_own.refs_2_, ...), custom_call_target="tpu_custom_call" | custom-call | flops 37748736 | bytes 135168 | tf_op jit(solution)/shard_map/qkv_out_grad/pallas_call | solution.py:51
  134.1 3.3 %down_grad.3 = (bf16[384,1536]{1,0:T(8,128)(2,1)S(1)}, bf16[384,1536]{1,0:T(8,128)(2,1)S(1)}) custom-call(bf16[768,512]{1,0:T(8,128)(2,1)S(1)} %get-tuple-element.219.refs_0_, bf16[768,512]{1,0:T(8,128)(2,1)S(1)} %collective-permute-done.20.refs_1_, bf16[512,1536]{1,0:T(8,128)(2,1)S(1)} %copy-done.5, bf16[512,1536]{1,0:T(8,128)(2,1)S(1)} %collective-permute-done.10.refs_3_), custom_call_target="tpu_custom_call" | custom-call | flops 37748736 | bytes 110592 | tf_op jit(solution)/shard_map/down_grad/pallas_call | solution.py:51
  137.5 3.1 %collective-permute-done.21 = bf16[384,1536]{1,0:T(8,128)(2,1)S(1)} collective-permute-done((bf16[384,1536]{1,0:T(8,128)(2,1)S(1)}, bf16[384,1536]{1,0:T(8,128)(2,1)S(1)}, u32[]{:S(2)}, u32[]{:S(2)}) %collective-permute-start.21) | collective-permute-done | bytes 1179680 | tf_op jit(solution)/shard_map/ppermute | solution.py:751
  141.1 1.7 collective-permute-start.25
  142.8 16.2 %feed_back.3 = (bf16[512,1536]{1,0:T(8,128)(2,1)}, bf16[512,1536]{1,0:T(8,128)(2,1)}, f32[2,768]{1,0:T(2,128)S(1)}, f32[2,768]{1,0:T(2,128)S(1)}, f32[512,768]{1...) custom-call(s32[1]{0:T(128)} %constant.14.clone.1.which, ...), custom_call_target="tpu_custom_call" | custom-call | flops 94371840 | bytes 547392 | tf_op jit(solution)/shard_map/feed_back/pallas_call | solution.py:51
  159.6 2.7 %collective-permute-done.24 = bf16[384,1536]{1,0:T(8,128)(2,1)S(1)} collective-permute-done((bf16[384,1536]{1,0:T(8,128)(2,1)S(1)}, bf16[384,1536]{1,0:T(8,128)(2,1)S(1)}, u32[]{:S(2)}, u32[]{:S(2)}) %collective-permute-start.24) | collective-permute-done | bytes 1179680 | tf_op jit(solution)/shard_map/ppermute | solution.py:751
  162.5 1.6 collective-permute-start.26
  164.2 4.8 %attend_back.6 = (bf16[3,512,384]{2,1,0:T(8,128)(2,1)S(1)}, f32[1,768]{1,0:T(1,128)S(1)}) custom-call(s32[4]{0:T(128)S(1)} %copy-done.13, bf16[3,512,384]{2,1,0:T(8,128)(2,1)S(1)} %get-tuple-element.238.joint, f32[12,1,256]{2,1,0:T(1,128)S(1)} %get-tuple-element.239.lse, bf16[512,384]{1,0:T(8,128)(2,1)S(1)} %get-tuple-element.240.grad_att), custom_call_target="tpu_custom_call" | custom-call | flops 7864320 | bytes 43248 | tf_op jit(solution)/shard_map/attend_back/pallas_call | solution.py:51
  169.1 2.1 collective-permute-done.26
  171.3 1.3 add_convert_fusion.3
  172.9 3.3 %up_grad.3 = (bf16[384,1536]{1,0:T(8,128)(2,1)S(1)}, bf16[384,1536]{1,0:T(8,128)(2,1)S(1)}) custom-call(bf16[768,512]{1,0:T(8,128)(2,1)S(1)} %get-tuple-element.175.refs_0_, bf16[768,512]{1,0:T(8,128)(2,1)S(1)} %collective-permute-done.9.refs_1_, bf16[512,1536]{1,0:T(8,128)(2,1)S(1)} %copy-done.6, bf16[512,1536]{1,0:T(8,128)(2,1)S(1)} %collective-permute-done.27.refs_3_), custom_call_target="tpu_custom_call" | custom-call | flops 37748736 | bytes 110592 | tf_op jit(solution)/shard_map/up_grad/pallas_call | solution.py:51
  177.3 2.7 collective-permute-start.31
  180.1 4.8 %attend_back.7 = (bf16[3,512,384]{2,1,0:T(8,128)(2,1)S(1)}, f32[1,768]{1,0:T(1,128)S(1)}) custom-call(s32[4]{0:T(128)S(1)} %copy-done.13, bf16[3,512,384]{2,1,0:T(8,128)(2,1)S(1)} %get-tuple-element.253.joint, f32[12,1,256]{2,1,0:T(1,128)S(1)} %get-tuple-element.254.lse, bf16[512,384]{1,0:T(8,128)(2,1)S(1)} %get-tuple-element.255.grad_att), custom_call_target="tpu_custom_call" | custom-call | flops 7864320 | bytes 43248 | tf_op jit(solution)/shard_map/attend_back/pallas_call | solution.py:51
  184.8 4.2 %qkv_out_grad.3 = (bf16[384,1536]{1,0:T(8,128)(2,1)S(1)}, bf16[384,1536]{1,0:T(8,128)(2,1)S(1)}) custom-call(bf16[768,512]{1,0:T(8,128)(2,1)S(1)} %get-tuple-element.174.refs_0_, bf16[768,512]{1,0:T(8,128)(2,1)S(1)} %collective-permute-done.7.refs_1_, bf16[3,512,384]{2,1,0:T(8,128)(2,1)S(1)} %get-tuple-element.256.refs_2_.joint_own, ...), custom_call_target="tpu_custom_call" | custom-call | flops 37748736 | bytes 135168 | tf_op jit(solution)/shard_map/qkv_out_grad/pallas_call | solution.py:51
  189.1 2.9 %collective-permute-done.31 = bf16[48,3072]{1,0:T(8,128)(2,1)S(1)} collective-permute-done((bf16[48,3072]{1,0:T(8,128)(2,1)S(1)}, bf16[48,3072]{1,0:T(8,128)(2,1)S(1)}, u32[]{:S(2)}, u32[]{:S(2)}) %collective-permute-start.31) | collective-permute-done | bytes 294944 | tf_op jit(solution)/shard_map/ppermute | solution.py:751
  191.9 1.4 collective-permute-start.33
  195.1 7.8 %entry_back.3 = (f32[512,768]{1,0:T(8,128)}, f32[2,768]{1,0:T(2,128)S(1)}) custom-call(bf16[3,512,384]{2,1,0:T(8,128)(2,1)S(1)} %get-tuple-element.256.refs_2_.joint_own, bf16[3,512,384]{2,1,0:T(8,128)(2,1)S(1)} %get-tuple-element.251.joint_far, bf16[2,3,768,384]{3,2,1,0:T(8,128)(2,1)} %bitcast.21, bf16[2,3,768,384]{3,2,1,0:T(8,128)(2,1)} %collective-permute-done.weight_far, ...), custom_call_target="tpu_custom_call" | custom-call | flops 28311552 | bytes 227616 | tf_op jit(solution)/shard_map/entry_back/pallas_call | solution.py:51
  203.1 1.6 collective-permute-start.34
  207.0 11.8 %collective-permute-done.33 = bf16[384,1536]{1,0:T(8,128)(2,1)S(1)} collective-permute-done((bf16[384,1536]{1,0:T(8,128)(2,1)S(1)}, bf16[384,1536]{1,0:T(8,128)(2,1)S(1)}, u32[]{:S(2)}, u32[]{:S(2)}) %collective-permute-start.33) | collective-permute-done | bytes 1179680 | tf_op jit(solution)/shard_map/ppermute | solution.py:751
  218.8 1.3 collective-permute-start.40
  220.2 1.5 collective-permute-start.41
  222.5 1.3 collective-permute-start.38
  224.0 2.7 collective-permute-start.39
  226.7 10.8 %collective-permute-done.39 = bf16[96,1536]{1,0:T(8,128)(2,1)S(1)} collective-permute-done((bf16[96,1536]{1,0:T(8,128)(2,1)S(1)}, bf16[96,1536]{1,0:T(8,128)(2,1)S(1)}, u32[]{:S(2)}, u32[]{:S(2)}) %collective-permute-start.39) | collective-permute-done | bytes 294944 | tf_op jit(solution)/shard_map/ppermute | solution.py:751
  237.8 1.7 collective-permute-start.43
  239.4 1.4 collective-permute-start.44
  243.6 3.4 %collective-permute-start.46 = (bf16[48,1536]{1,0:T(8,128)(2,1)S(1)}, bf16[48,1536]{1,0:T(8,128)(2,1)S(1)}, u32[]{:S(2)}, u32[]{:S(2)}) collective-permute-start(bf16[48,1536]{1,0:T(8,128)(2,1)S(1)} %add_convert_fusion.15), channel_id=1, source_target_pairs={{0,16},{2,18},{4,20},{6,22},{8,24},{10,26},{12,28},{14,30},{16,0},... | collective-permute-start | bytes 442376 | tf_op jit(solution)/shard_map/ppermute | solution.py:751
  248.6 2.9 %collective-permute-done.47 = f32[18,768]{1,0:T(8,128)S(1)} collective-permute-done((f32[18,768]{1,0:T(8,128)S(1)}, f32[18,768]{1,0:T(8,128)S(1)}, u32[]{:S(2)}, u32[]{:S(2)}) %collective-permute-start.47) | collective-permute-done | bytes 55328 | tf_op jit(solution)/shard_map/ppermute | solution.py:798
  251.5 2.0 collective-permute-start.49
  256.8 11.5 %collective-permute-done.48 = f32[18,768]{1,0:T(8,128)S(1)} collective-permute-done((f32[18,768]{1,0:T(8,128)S(1)}, f32[18,768]{1,0:T(8,128)S(1)}, u32[]{:S(2)}, u32[]{:S(2)}) %collective-permute-start.48) | collective-permute-done | bytes 55328 | tf_op jit(solution)/shard_map/ppermute | solution.py:798
  (171 shorter events, 25.4 us)
Async XLA Ops:
  0.7 6.7 %collective-permute-start = (bf16[2,3,768,384]{3,2,1,0:T(8,128)(2,1)}, bf16[2,3,768,384]{3,2,1,0:T(8,128)(2,1)}, u32[]{:S(2)}, u32[]{:S(2)}) collective-permute-start(bf16[2,3,768,384]{3,2,1,0:T(8,128)(2,1)} %bitcast.17), channel_id=1, source_target_pairs={{0,1},{1,0},{2,3},{3,2},{4,5},{5,4},{6,7},{7,6},{8,9},{9,8},{10,11... | collective-permute-start | bytes 10616840 | tf_op jit(solution)/shard_map/ppermute | solution.py:820
  1.2 5.9 %collective-permute-start.1 = (f32[2,2,384]{2,1,0:T(2,128)}, f32[2,2,384]{2,1,0:T(2,128)S(1)}, u32[]{:S(2)}, u32[]{:S(2)}) collective-permute-start(f32[2,2,384]{2,1,0:T(2,128)} %bias_own.3), channel_id=1, source_target_pairs={{0,1},{1,0},{2,3},{3,2},{4,5},{5,4},{6,7},{7,6},{8,9},{9,8},{10,11... | collective-permute-start | bytes 18440 | tf_op jit(solution)/shard_map/ppermute | solution.py:820
  7.4 10.7 %collective-permute-start.3 = (bf16[2,768,1536]{2,1,0:T(8,128)(2,1)}, bf16[2,768,1536]{2,1,0:T(8,128)(2,1)}, u32[]{:S(2)}, u32[]{:S(2)}) collective-permute-start(bf16[2,768,1536]{2,1,0:T(8,128)(2,1)} %up_own.7), channel_id=1, source_target_pairs={{0,1},{1,0},{2,3},{3,2},{4,5},{5,4},{6,7},{7,6},{8,9},{9,8},{10,11... | collective-permute-start | bytes 14155784 | tf_op jit(solution)/shard_map/ppermute | solution.py:820
  7.8 16.3 %collective-permute-start.5 = (bf16[2,1536,768]{2,1,0:T(8,128)(2,1)}, bf16[2,1536,768]{2,1,0:T(8,128)(2,1)}, u32[]{:S(2)}, u32[]{:S(2)}) collective-permute-start(bf16[2,1536,768]{2,1,0:T(8,128)(2,1)} %down_own.7), channel_id=1, source_target_pairs={{0,1},{1,0},{2,3},{3,2},{4,5},{5,4},{6,7},{7,6},{8,9},{9,8},{10,11... | collective-permute-start | bytes 14155784 | tf_op jit(solution)/shard_map/ppermute | solution.py:820
  7.9 10.2 %collective-permute-start.2 = (bf16[2,384,768]{2,1,0:T(8,128)(2,1)S(1)}, bf16[2,384,768]{2,1,0:T(8,128)(2,1)S(1)}, u32[]{:S(2)}, u32[]{:S(2)}) collective-permute-start(bf16[2,384,768]{2,1,0:T(8,128)(2,1)S(1)} %copy-done.15), channel_id=1, source_target_pairs={{0,1},{1,0},{2,3},{3,2},{4,5},{5,4},{6,7},{7,6},{8,9},{9,8},{10,11... | collective-permute-start | bytes 3538952 | tf_op jit(solution)/shard_map/ppermute | solution.py:820
  8.3 9.8 %collective-permute-start.4 = (f32[2,1536]{1,0:T(2,128)S(1)}, f32[2,1536]{1,0:T(2,128)S(1)}, u32[]{:S(2)}, u32[]{:S(2)}) collective-permute-start(f32[2,1536]{1,0:T(2,128)S(1)} %copy-done.12), channel_id=1, source_target_pairs={{0,1},{1,0},{2,3},{3,2},{4,5},{5,4},{6,7},{7,6},{8,9},{9,8},{10,11... | collective-permute-start | bytes 36872 | tf_op jit(solution)/shard_map/ppermute | solution.py:820
  41.8 11.2 %collective-permute-start.10 = (bf16[512,1536]{1,0:T(8,128)(2,1)}, bf16[512,1536]{1,0:T(8,128)(2,1)S(1)}, u32[]{:S(2)}, u32[]{:S(2)}) collective-permute-start(bf16[512,1536]{1,0:T(8,128)(2,1)} %get-tuple-element.176), channel_id=1, source_target_pairs={{0,1},{1,0},{2,3},{3,2},{4,5},{5,4},{6,7},{7,6},{8,9},{9,8},{10,11... | collective-permute-start | bytes 4718600 | tf_op jit(solution)/shard_map/ppermute | solution.py:820
  42.3 10.7 %collective-permute-start.6 = (bf16[768,512]{1,0:T(8,128)(2,1)S(1)}, bf16[768,512]{1,0:T(8,128)(2,1)S(1)}, u32[]{:S(2)}, u32[]{:S(2)}) collective-permute-start(bf16[768,512]{1,0:T(8,128)(2,1)S(1)} %get-tuple-element.173.refs_0_), channel_id=1, source_target_pairs={{0,1},{1,0},{2,3},{3,2},{4,5},{5,4},{6,7},{7,6},{8,9},{9,8},{10,11... | collective-permute-start | bytes 2359304 | tf_op jit(solution)/shard_map/ppermute | solution.py:820
  42.4 10.6 %collective-permute-start.7 = (bf16[768,512]{1,0:T(8,128)(2,1)S(1)}, bf16[768,512]{1,0:T(8,128)(2,1)S(1)}, u32[]{:S(2)}, u32[]{:S(2)}) collective-permute-start(bf16[768,512]{1,0:T(8,128)(2,1)S(1)} %get-tuple-element.174.refs_0_), channel_id=1, source_target_pairs={{0,1},{1,0},{2,3},{3,2},{4,5},{5,4},{6,7},{7,6},{8,9},{9,8},{10,11... | collective-permute-start | bytes 2359304 | tf_op jit(solution)/shard_map/ppermute | solution.py:820
  42.8 10.2 %collective-permute-start.9 = (bf16[768,512]{1,0:T(8,128)(2,1)S(1)}, bf16[768,512]{1,0:T(8,128)(2,1)S(1)}, u32[]{:S(2)}, u32[]{:S(2)}) collective-permute-start(bf16[768,512]{1,0:T(8,128)(2,1)S(1)} %get-tuple-element.175.refs_0_), channel_id=1, source_target_pairs={{0,1},{1,0},{2,3},{3,2},{4,5},{5,4},{6,7},{7,6},{8,9},{9,8},{10,11... | collective-permute-start | bytes 2359304 | tf_op jit(solution)/shard_map/ppermute | solution.py:820
  42.9 10.1 %collective-permute-start.8 = (bf16[512,384]{1,0:T(8,128)(2,1)S(1)}, bf16[512,384]{1,0:T(8,128)(2,1)S(1)}, u32[]{:S(2)}, u32[]{:S(2)}) collective-permute-start(bf16[512,384]{1,0:T(8,128)(2,1)S(1)} %get-tuple-element.165.att_far), channel_id=1, source_target_pairs={{0,1},{1,0},{2,3},{3,2},{4,5},{5,4},{6,7},{7,6},{8,9},{9,8},{10,11... | collective-permute-start | bytes 1179656 | tf_op jit(solution)/shard_map/ppermute | solution.py:820
  77.6 29.2 %collective-permute-start.13 = (bf16[384,1536]{1,0:T(8,128)(2,1)S(1)}, bf16[384,1536]{1,0:T(8,128)(2,1)S(1)}, u32[]{:S(2)}, u32[]{:S(2)}) collective-permute-start(bf16[384,1536]{1,0:T(8,128)(2,1)S(1)} %get-tuple-element.191), channel_id=1, source_target_pairs={{0,2},{2,0},{4,6},{6,4},{8,10},{10,8},{12,14},{14,12},{16,18},{18,... | collective-permute-start | bytes 3538952 | tf_op jit(solution)/shard_map/ppermute | solution.py:751
  96.2 13.1 %collective-permute-start.14 = (bf16[512,1536]{1,0:T(8,128)(2,1)}, bf16[512,1536]{1,0:T(8,128)(2,1)S(1)}, u32[]{:S(2)}, u32[]{:S(2)}) collective-permute-start(bf16[512,1536]{1,0:T(8,128)(2,1)} %get-tuple-element.200), channel_id=1, source_target_pairs={{0,1},{1,0},{2,3},{3,2},{4,5},{5,4},{6,7},{7,6},{8,9},{9,8},{10,11... | collective-permute-start | bytes 4718600 | tf_op jit(solution)/shard_map/ppermute | solution.py:820
  96.4 13.0 %collective-permute-start.11 = (bf16[768,512]{1,0:T(8,128)(2,1)S(1)}, bf16[768,512]{1,0:T(8,128)(2,1)S(1)}, u32[]{:S(2)}, u32[]{:S(2)}) collective-permute-start(bf16[768,512]{1,0:T(8,128)(2,1)S(1)} %get-tuple-element.180.refs_0_), channel_id=1, source_target_pairs={{0,1},{1,0},{2,3},{3,2},{4,5},{5,4},{6,7},{7,6},{8,9},{9,8},{10,11... | collective-permute-start | bytes 2359304 | tf_op jit(solution)/shard_map/ppermute | solution.py:820
  107.0 20.4 %collective-permute-start.16 = (bf16[192,1536]{1,0:T(8,128)(2,1)S(1)}, bf16[192,1536]{1,0:T(8,128)(2,1)S(1)}, u32[]{:S(2)}, u32[]{:S(2)}) collective-permute-start(bf16[192,1536]{1,0:T(8,128)(2,1)S(1)} %add_convert_fusion.5), channel_id=1, source_target_pairs={{0,4},{2,6},{4,0},{6,2},{8,12},{10,14},{12,8},{14,10},{16,20},{18,... | collective-permute-start | bytes 1769480 | tf_op jit(solution)/shard_map/ppermute | solution.py:751
  108.8 5.4 %collective-permute-start.19 = (bf16[512,384]{1,0:T(8,128)(2,1)S(1)}, bf16[512,384]{1,0:T(8,128)(2,1)S(1)}, u32[]{:S(2)}, u32[]{:S(2)}) collective-permute-start(bf16[512,384]{1,0:T(8,128)(2,1)S(1)} %get-tuple-element.172.att_far), channel_id=1, source_target_pairs={{0,1},{1,0},{2,3},{3,2},{4,5},{5,4},{6,7},{7,6},{8,9},{9,8},{10,11... | collective-permute-start | bytes 1179656 | tf_op jit(solution)/shard_map/ppermute | solution.py:820
  108.8 20.5 %collective-permute-start.17 = (bf16[3,512,384]{2,1,0:T(8,128)(2,1)S(1)}, bf16[3,512,384]{2,1,0:T(8,128)(2,1)S(1)}, u32[]{:S(2)}, u32[]{:S(2)}) collective-permute-start(bf16[3,512,384]{2,1,0:T(8,128)(2,1)S(1)} %get-tuple-element.210.joint_far), channel_id=1, source_target_pairs={{0,1},{1,0},{2,3},{3,2},{4,5},{5,4},{6,7},{7,6},{8,9},{9,8},{10,11... | collective-permute-start | bytes 3538952 | tf_op jit(solution)/shard_map/ppermute | solution.py:820
  112.6 28.0 %collective-permute-start.21 = (bf16[384,1536]{1,0:T(8,128)(2,1)S(1)}, bf16[384,1536]{1,0:T(8,128)(2,1)S(1)}, u32[]{:S(2)}, u32[]{:S(2)}) collective-permute-start(bf16[384,1536]{1,0:T(8,128)(2,1)S(1)} %get-tuple-element.223), channel_id=1, source_target_pairs={{0,2},{2,0},{4,6},{6,4},{8,10},{10,8},{12,14},{14,12},{16,18},{18,... | collective-permute-start | bytes 3538952 | tf_op jit(solution)/shard_map/ppermute | solution.py:751
  114.2 13.4 %collective-permute-start.15 = (bf16[768,512]{1,0:T(8,128)(2,1)S(1)}, bf16[768,512]{1,0:T(8,128)(2,1)S(1)}, u32[]{:S(2)}, u32[]{:S(2)}) collective-permute-start(bf16[768,512]{1,0:T(8,128)(2,1)S(1)} %get-tuple-element.213.refs_0_), channel_id=1, source_target_pairs={{0,1},{1,0},{2,3},{3,2},{4,5},{5,4},{6,7},{7,6},{8,9},{9,8},{10,11... | collective-permute-start | bytes 2359304 | tf_op jit(solution)/shard_map/ppermute | solution.py:820
  114.2 15.1 %collective-permute-start.18 = (bf16[768,512]{1,0:T(8,128)(2,1)S(1)}, bf16[768,512]{1,0:T(8,128)(2,1)S(1)}, u32[]{:S(2)}, u32[]{:S(2)}) collective-permute-start(bf16[768,512]{1,0:T(8,128)(2,1)S(1)} %get-tuple-element.217.refs_4_), channel_id=1, source_target_pairs={{0,1},{1,0},{2,3},{3,2},{4,5},{5,4},{6,7},{7,6},{8,9},{9,8},{10,11... | collective-permute-start | bytes 2359304 | tf_op jit(solution)/shard_map/ppermute | solution.py:820
  127.4 6.7 %collective-permute-start.20 = (bf16[768,512]{1,0:T(8,128)(2,1)S(1)}, bf16[768,512]{1,0:T(8,128)(2,1)S(1)}, u32[]{:S(2)}, u32[]{:S(2)}) collective-permute-start(bf16[768,512]{1,0:T(8,128)(2,1)S(1)} %get-tuple-element.219.refs_0_), channel_id=1, source_target_pairs={{0,1},{1,0},{2,3},{3,2},{4,5},{5,4},{6,7},{7,6},{8,9},{9,8},{10,11... | collective-permute-start | bytes 2359304 | tf_op jit(solution)/shard_map/ppermute | solution.py:820
  127.6 9.9 %collective-permute-start.22 = (bf16[96,1536]{1,0:T(8,128)(2,1)S(1)}, bf16[96,1536]{1,0:T(8,128)(2,1)S(1)}, u32[]{:S(2)}, u32[]{:S(2)}) collective-permute-start(bf16[96,1536]{1,0:T(8,128)(2,1)S(1)} %add_convert_fusion.11), channel_id=1, source_target_pairs={{0,8},{2,10},{4,12},{6,14},{8,0},{10,2},{12,4},{14,6},{16,24},{18,... | collective-permute-start | bytes 884744 | tf_op jit(solution)/shard_map/ppermute | solution.py:751
  133.5 28.8 %collective-permute-start.24 = (bf16[384,1536]{1,0:T(8,128)(2,1)S(1)}, bf16[384,1536]{1,0:T(8,128)(2,1)S(1)}, u32[]{:S(2)}, u32[]{:S(2)}) collective-permute-start(bf16[384,1536]{1,0:T(8,128)(2,1)S(1)} %get-tuple-element.226), channel_id=1, source_target_pairs={{0,8},{2,10},{4,12},{6,14},{8,0},{10,2},{12,4},{14,6},{16,24},{18,... | collective-permute-start | bytes 3538952 | tf_op jit(solution)/shard_map/ppermute | solution.py:751
  140.7 21.6 %collective-permute-start.23 = (bf16[192,1536]{1,0:T(8,128)(2,1)S(1)}, bf16[192,1536]{1,0:T(8,128)(2,1)S(1)}, u32[]{:S(2)}, u32[]{:S(2)}) collective-permute-start(bf16[192,1536]{1,0:T(8,128)(2,1)S(1)} %add_convert_fusion.4), channel_id=1, source_target_pairs={{0,4},{2,6},{4,0},{6,2},{8,12},{10,14},{12,8},{14,10},{16,20},{18,... | collective-permute-start | bytes 1769480 | tf_op jit(solution)/shard_map/ppermute | solution.py:751
  141.1 30.1 %collective-permute-start.25 = (bf16[384,1536]{1,0:T(8,128)(2,1)S(1)}, bf16[384,1536]{1,0:T(8,128)(2,1)}, u32[]{:S(2)}, u32[]{:S(2)}) collective-permute-start(bf16[384,1536]{1,0:T(8,128)(2,1)S(1)} %get-tuple-element.236), channel_id=1, source_target_pairs={{0,2},{2,0},{4,6},{6,4},{8,10},{10,8},{12,14},{14,12},{16,18},{18,... | collective-permute-start | bytes 3538952 | tf_op jit(solution)/shard_map/ppermute | solution.py:751
  159.0 13.6 %collective-permute-start.27 = (bf16[512,1536]{1,0:T(8,128)(2,1)}, bf16[512,1536]{1,0:T(8,128)(2,1)S(1)}, u32[]{:S(2)}, u32[]{:S(2)}) collective-permute-start(bf16[512,1536]{1,0:T(8,128)(2,1)} %get-tuple-element.248), channel_id=1, source_target_pairs={{0,1},{1,0},{2,3},{3,2},{4,5},{5,4},{6,7},{7,6},{8,9},{9,8},{10,11... | collective-permute-start | bytes 4718600 | tf_op jit(solution)/shard_map/ppermute | solution.py:820
  159.1 17.1 %collective-permute-start.28 = (bf16[768,512]{1,0:T(8,128)(2,1)S(1)}, bf16[768,512]{1,0:T(8,128)(2,1)S(1)}, u32[]{:S(2)}, u32[]{:S(2)}) collective-permute-start(bf16[768,512]{1,0:T(8,128)(2,1)S(1)} %get-tuple-element.250.refs_4_), channel_id=1, source_target_pairs={{0,1},{1,0},{2,3},{3,2},{4,5},{5,4},{6,7},{7,6},{8,9},{9,8},{10,11... | collective-permute-start | bytes 2359304 | tf_op jit(solution)/shard_map/ppermute | solution.py:820
  162.5 8.7 %collective-permute-start.26 = (bf16[96,1536]{1,0:T(8,128)(2,1)S(1)}, bf16[96,1536]{1,0:T(8,128)(2,1)S(1)}, u32[]{:S(2)}, u32[]{:S(2)}) collective-permute-start(bf16[96,1536]{1,0:T(8,128)(2,1)S(1)} %add_convert_fusion.10), channel_id=1, source_target_pairs={{0,8},{2,10},{4,12},{6,14},{8,0},{10,2},{12,4},{14,6},{16,24},{18,... | collective-permute-start | bytes 884744 | tf_op jit(solution)/shard_map/ppermute | solution.py:751
  169.0 7.2 %collective-permute-start.29 = (bf16[3,512,384]{2,1,0:T(8,128)(2,1)S(1)}, bf16[3,512,384]{2,1,0:T(8,128)(2,1)S(1)}, u32[]{:S(2)}, u32[]{:S(2)}) collective-permute-start(bf16[3,512,384]{2,1,0:T(8,128)(2,1)S(1)} %get-tuple-element.251.joint_far), channel_id=1, source_target_pairs={{0,1},{1,0},{2,3},{3,2},{4,5},{5,4},{6,7},{7,6},{8,9},{9,8},{10,11... | collective-permute-start | bytes 3538952 | tf_op jit(solution)/shard_map/ppermute | solution.py:820
  176.2 26.8 %collective-permute-start.32 = (bf16[384,1536]{1,0:T(8,128)(2,1)S(1)}, bf16[384,1536]{1,0:T(8,128)(2,1)S(1)}, u32[]{:S(2)}, u32[]{:S(2)}) collective-permute-start(bf16[384,1536]{1,0:T(8,128)(2,1)S(1)} %get-tuple-element.269), channel_id=1, source_target_pairs={{0,2},{2,0},{4,6},{6,4},{8,10},{10,8},{12,14},{14,12},{16,18},{18,... | collective-permute-start | bytes 3538952 | tf_op jit(solution)/shard_map/ppermute | solution.py:751
  176.8 15.1 %collective-permute-start.30 = (bf16[192,1536]{1,0:T(8,128)(2,1)S(1)}, bf16[192,1536]{1,0:T(8,128)(2,1)S(1)}, u32[]{:S(2)}, u32[]{:S(2)}) collective-permute-start(bf16[192,1536]{1,0:T(8,128)(2,1)S(1)} %add_convert_fusion.3), channel_id=1, source_target_pairs={{0,4},{2,6},{4,0},{6,2},{8,12},{10,14},{12,8},{14,10},{16,20},{18,... | collective-permute-start | bytes 1769480 | tf_op jit(solution)/shard_map/ppermute | solution.py:751
  177.3 14.7 %collective-permute-start.31 = (bf16[48,3072]{1,0:T(8,128)(2,1)S(1)}, bf16[48,3072]{1,0:T(8,128)(2,1)S(1)}, u32[]{:S(2)}, u32[]{:S(2)}) collective-permute-start(bf16[48,3072]{1,0:T(8,128)(2,1)S(1)} %pad_maximum_fusion), channel_id=1, source_target_pairs={{0,16},{2,18},{4,20},{6,22},{8,24},{10,26},{12,28},{14,30},{16,0},... | collective-permute-start | bytes 884744 | tf_op jit(solution)/shard_map/ppermute | solution.py:751
  191.9 26.8 %collective-permute-start.33 = (bf16[384,1536]{1,0:T(8,128)(2,1)S(1)}, bf16[384,1536]{1,0:T(8,128)(2,1)S(1)}, u32[]{:S(2)}, u32[]{:S(2)}) collective-permute-start(bf16[384,1536]{1,0:T(8,128)(2,1)S(1)} %get-tuple-element.277), channel_id=1, source_target_pairs={{0,4},{2,6},{4,0},{6,2},{8,12},{10,14},{12,8},{14,10},{16,20},{18,... | collective-permute-start | bytes 3538952 | tf_op jit(solution)/shard_map/ppermute | solution.py:751
  194.4 11.5 %collective-permute-start.37 = (bf16[96,1536]{1,0:T(8,128)(2,1)S(1)}, bf16[96,1536]{1,0:T(8,128)(2,1)S(1)}, u32[]{:S(2)}, u32[]{:S(2)}) collective-permute-start(bf16[96,1536]{1,0:T(8,128)(2,1)S(1)} %add_convert_fusion.9), channel_id=1, source_target_pairs={{0,8},{2,10},{4,12},{6,14},{8,0},{10,2},{12,4},{14,6},{16,24},{18,... | collective-permute-start | bytes 884744 | tf_op jit(solution)/shard_map/ppermute | solution.py:751
  203.1 15.6 %collective-permute-start.34 = (bf16[192,1536]{1,0:T(8,128)(2,1)S(1)}, bf16[192,1536]{1,0:T(8,128)(2,1)S(1)}, u32[]{:S(2)}, u32[]{:S(2)}) collective-permute-start(bf16[192,1536]{1,0:T(8,128)(2,1)S(1)} %add_convert_fusion.1), channel_id=1, source_target_pairs={{0,8},{2,10},{4,12},{6,14},{8,0},{10,2},{12,4},{14,6},{16,24},{18,... | collective-permute-start | bytes 1769480 | tf_op jit(solution)/shard_map/ppermute | solution.py:751
  204.8 14.0 %collective-permute-start.36 = (bf16[192,1536]{1,0:T(8,128)(2,1)S(1)}, bf16[192,1536]{1,0:T(8,128)(2,1)S(1)}, u32[]{:S(2)}, u32[]{:S(2)}) collective-permute-start(bf16[192,1536]{1,0:T(8,128)(2,1)S(1)} %add_convert_fusion.2), channel_id=1, source_target_pairs={{0,2},{2,0},{4,6},{6,4},{8,10},{10,8},{12,14},{14,12},{16,18},{18,... | collective-permute-start | bytes 1769480 | tf_op jit(solution)/shard_map/ppermute | solution.py:751
  205.9 12.9 %collective-permute-start.35 = (f32[18,768]{1,0:T(8,128)S(1)}, f32[18,768]{1,0:T(8,128)S(1)}, u32[]{:S(2)}, u32[]{:S(2)}) collective-permute-start(f32[18,768]{1,0:T(8,128)S(1)} %get-tuple-element.280), channel_id=1, source_target_pairs={{0,1},{1,0},{2,3},{3,2},{4,5},{5,4},{6,7},{7,6},{8,9},{9,8},{10,11... | collective-permute-start | bytes 165896 | tf_op jit(solution)/shard_map/ppermute | solution.py:820
  218.8 18.9 %collective-permute-start.40 = (f32[18,768]{1,0:T(8,128)S(1)}, f32[18,768]{1,0:T(8,128)S(1)}, u32[]{:S(2)}, u32[]{:S(2)}) collective-permute-start(f32[18,768]{1,0:T(8,128)S(1)} %add.170), channel_id=1, source_target_pairs={{0,2},{2,0},{4,6},{6,4},{8,10},{10,8},{12,14},{14,12},{16,18},{18,... | collective-permute-start | bytes 165896 | tf_op jit(solution)/shard_map/ppermute | solution.py:798
  220.2 17.6 %collective-permute-start.41 = (f32[18,768]{1,0:T(8,128)S(1)}, f32[18,768]{1,0:T(8,128)S(1)}, u32[]{:S(2)}, u32[]{:S(2)}) collective-permute-start(f32[18,768]{1,0:T(8,128)S(1)} %add.170), channel_id=1, source_target_pairs={{0,4},{2,6},{4,0},{6,2},{8,12},{10,14},{12,8},{14,10},{16,20},{18,... | collective-permute-start | bytes 165896 | tf_op jit(solution)/shard_map/ppermute | solution.py:798
  221.7 16.1 %collective-permute-start.42 = (f32[18,768]{1,0:T(8,128)S(1)}, f32[18,768]{1,0:T(8,128)S(1)}, u32[]{:S(2)}, u32[]{:S(2)}) collective-permute-start(f32[18,768]{1,0:T(8,128)S(1)} %add.170), channel_id=1, source_target_pairs={{0,6},{2,4},{4,2},{6,0},{8,14},{10,12},{12,10},{14,8},{16,22},{18,... | collective-permute-start | bytes 165896 | tf_op jit(solution)/shard_map/ppermute | solution.py:798
  222.5 15.0 %collective-permute-start.38 = (bf16[192,1536]{1,0:T(8,128)(2,1)S(1)}, bf16[192,1536]{1,0:T(8,128)(2,1)S(1)}, u32[]{:S(2)}, u32[]{:S(2)}) collective-permute-start(bf16[192,1536]{1,0:T(8,128)(2,1)S(1)} %add_convert_fusion), channel_id=1, source_target_pairs={{0,2},{2,0},{4,6},{6,4},{8,10},{10,8},{12,14},{14,12},{16,18},{18,... | collective-permute-start | bytes 1769480 | tf_op jit(solution)/shard_map/ppermute | solution.py:751
  224.0 13.6 %collective-permute-start.39 = (bf16[96,1536]{1,0:T(8,128)(2,1)S(1)}, bf16[96,1536]{1,0:T(8,128)(2,1)S(1)}, u32[]{:S(2)}, u32[]{:S(2)}) collective-permute-start(bf16[96,1536]{1,0:T(8,128)(2,1)S(1)} %add_convert_fusion.8), channel_id=1, source_target_pairs={{0,16},{2,18},{4,20},{6,22},{8,24},{10,26},{12,28},{14,30},{16,0},... | collective-permute-start | bytes 884744 | tf_op jit(solution)/shard_map/ppermute | solution.py:751
  237.8 9.4 %collective-permute-start.43 = (bf16[96,1536]{1,0:T(8,128)(2,1)S(1)}, bf16[96,1536]{1,0:T(8,128)(2,1)S(1)}, u32[]{:S(2)}, u32[]{:S(2)}) collective-permute-start(bf16[96,1536]{1,0:T(8,128)(2,1)S(1)} %add_convert_fusion.7), channel_id=1, source_target_pairs={{0,8},{2,10},{4,12},{6,14},{8,0},{10,2},{12,4},{14,6},{16,24},{18,... | collective-permute-start | bytes 884744 | tf_op jit(solution)/shard_map/ppermute | solution.py:751
  239.4 9.0 %collective-permute-start.44 = (bf16[96,1536]{1,0:T(8,128)(2,1)S(1)}, bf16[96,1536]{1,0:T(8,128)(2,1)S(1)}, u32[]{:S(2)}, u32[]{:S(2)}) collective-permute-start(bf16[96,1536]{1,0:T(8,128)(2,1)S(1)} %add_convert_fusion.6), channel_id=1, source_target_pairs={{0,4},{2,6},{4,0},{6,2},{8,12},{10,14},{12,8},{14,10},{16,20},{18,... | collective-permute-start | bytes 884744 | tf_op jit(solution)/shard_map/ppermute | solution.py:751
  242.9 8.6 %collective-permute-start.45 = (bf16[48,1536]{1,0:T(8,128)(2,1)S(1)}, bf16[48,1536]{1,0:T(8,128)(2,1)S(1)}, u32[]{:S(2)}, u32[]{:S(2)}) collective-permute-start(bf16[48,1536]{1,0:T(8,128)(2,1)S(1)} %add_convert_fusion.14), channel_id=1, source_target_pairs={{0,4},{2,6},{4,0},{6,2},{8,12},{10,14},{12,8},{14,10},{16,20},{18,... | collective-permute-start | bytes 442376 | tf_op jit(solution)/shard_map/ppermute | solution.py:751
  243.6 7.9 %collective-permute-start.46 = (bf16[48,1536]{1,0:T(8,128)(2,1)S(1)}, bf16[48,1536]{1,0:T(8,128)(2,1)S(1)}, u32[]{:S(2)}, u32[]{:S(2)}) collective-permute-start(bf16[48,1536]{1,0:T(8,128)(2,1)S(1)} %add_convert_fusion.15), channel_id=1, source_target_pairs={{0,16},{2,18},{4,20},{6,22},{8,24},{10,26},{12,28},{14,30},{16,0},... | collective-permute-start | bytes 442376 | tf_op jit(solution)/shard_map/ppermute | solution.py:751
  251.5 16.8 %collective-permute-start.49 = (bf16[48,3072]{1,0:T(8,128)(2,1)S(1)}, bf16[48,3072]{1,0:T(8,128)(2,1)S(1)}, u32[]{:S(2)}, u32[]{:S(2)}) collective-permute-start(bf16[48,3072]{1,0:T(8,128)(2,1)S(1)} %pad_maximum_fusion.1), channel_id=1, source_target_pairs={{0,16},{2,18},{4,20},{6,22},{8,24},{10,26},{12,28},{14,30},{16,0},... | collective-permute-start | bytes 884744 | tf_op jit(solution)/shard_map/ppermute | solution.py:751
  253.5 14.8 %collective-permute-start.48 = (f32[18,768]{1,0:T(8,128)S(1)}, f32[18,768]{1,0:T(8,128)S(1)}, u32[]{:S(2)}, u32[]{:S(2)}) collective-permute-start(f32[18,768]{1,0:T(8,128)S(1)} %add.190), channel_id=1, source_target_pairs={{0,16},{2,18},{4,20},{6,22},{8,24},{10,26},{12,28},{14,30},{16,0},... | collective-permute-start | bytes 165896 | tf_op jit(solution)/shard_map/ppermute | solution.py:798
  (24 other events, 142.7 us)

commit v6 on v5

--- a/solution.py
+++ b/solution.py
@@ -903,7 +903,7 @@
             [whole()] * 6,
             [pltpu.VMEM((2, 3, width, half), BF16), pltpu.SemaphoreType.DMA((2, 3))],
             flops=12 * tokens * width * half + 8 * tokens * slots * half,
-            limit=32,
+            limit=26,
         )
         return results[0::2], results[1::2]
 

time: 270 us -> 271 us (level)
  transfers between devices with their start and end apart: 50 -> 50, of which waited for: 15 -> 18; matrix products, arithmetic and copies ran while one was open for 3% -> 2% of each run, Pallas kernels for 41% -> 41%
where the time goes in v6:
time: 271 us
  Pallas kernels  151 us (56%)
  waiting for transfers between devices  65.6 us (24%)
  starting transfers between devices  44.1 us (16%)
  other arithmetic  5.39 us (2%)
  local copies, waits for them, and re-layouts  3.56 us (1%)
    pallas_call x24, Pallas kernels, call(): pl.pallas_call(body, name=name, grid=grid, in_specs=in_specs, out_specs=o...  151 us
    ppermute x22, waiting for transfers between devices, start(): self.incoming = lax.ppermute(self.outgoing, 'dp', flip(self.order.pop(0)))  41.1 us
    ppermute x22, starting transfers between devices, start(): self.incoming = lax.ppermute(self.outgoing, 'dp', flip(self.order.pop(0)))  34.4 us
    ppermute x5, waiting for transfers between devices, turn(): lax.ppermute(self.mine, 'dp', [(index, index ^ mask) for index in range(s...  14.6 us
    ppermute x23, waiting for transfers between devices, swap(): return lax.ppermute(values, 'tensor', [(0, 1), (1, 0)])  9.85 us
    ppermute x23, starting transfers between devices, swap(): return lax.ppermute(values, 'tensor', [(0, 1), (1, 0)])  5.65 us
  transfers between devices with their start and end apart: 50, of which 18 were waited for; matrix products, arithmetic and copies ran while one was open for 2% of the time, Pallas kernels for 41%

profile of v6, /device:TPU:0, one launch (start us, length us, event | category | flops | bytes accessed | tf_op | source)
XLA Modules:
  0.0 270.9 jit_solution(10167682180585424373)
XLA Ops:
  2.9 4.1 %prep.1 = (bf16[512,768]{1,0:T(8,128)(2,1)S(1)}, bf16[768,512]{1,0:T(8,128)(2,1)S(1)}, bf16[768,512]{1,0:T(8,128)(2,1)S(1)}, f32[512,768]{1,0:T(8,128)S(1)}) custom-call(bf16[512,768]{1,0:T(8,128)(2,1)S(1)} %bitcast.13, bf16[512,768]{1,0:T(8,128)(2,1)S(1)} %bitcast.16, f32[2,2,768]{2,1,0:T(2,128)S(1)} %copy-done.9, f32[2,2,768]{2,1,0:T(2,128)S(1)} %copy-done.10, ...), custom_call_target="tpu_custom_call" | custom-call | flops 18874368 | bytes 104832 | tf_op jit(solution)/shard_map/prep/pallas_call | solution.py:51
  8.4 9.7 %attend.2 = (bf16[3,512,384]{2,1,0:T(8,128)(2,1)S(1)}, bf16[3,512,384]{2,1,0:T(8,128)(2,1)S(1)}, bf16[512,384]{1,0:T(8,128)(2,1)S(1)}, bf16[512,384]{1,0:T(8,128...) custom-call(s32[1]{0:T(128)} %constant.14.clone.1.which, s32[4]{0:T(128)S(1)} %copy-done.13, ...), custom_call_target="tpu_custom_call" | custom-call | flops 34603008 | bytes 172608 | tf_op jit(solution)/shard_map/attend/pallas_call | solution.py:51
  18.1 3.7 %collective-permute-done.4.up_bias_far = f32[2,1536]{1,0:T(2,128)S(1)} collective-permute-done((f32[2,1536]{1,0:T(2,128)S(1)}, f32[2,1536]{1,0:T(2,128)S(1)}, u32[]{:S(2)}, u32[]{:S(2)}) %collective-permute-start.4) | collective-permute-done | bytes 12320 | tf_op jit(solution)/shard_map/ppermute | solution.py:820
  22.6 1.5 collective-permute-done.5.down_far
  24.8 17.7 %feed.2 = (f32[512,768]{1,0:T(8,128)S(1)}, bf16[768,512]{1,0:T(8,128)(2,1)S(1)}, bf16[512,1536]{1,0:T(8,128)(2,1)}, bf16[512,1536]{1,0:T(8,128)(2,1)}, bf16[512,...) custom-call(s32[4]{0:T(128)S(1)} %copy-done.13, ...), custom_call_target="tpu_custom_call" | custom-call | flops 94371840 | bytes 560064 | tf_op jit(solution)/shard_map/feed/pallas_call | solution.py:51
  44.0 9.7 %attend.3 = (bf16[3,512,384]{2,1,0:T(8,128)(2,1)S(1)}, bf16[3,512,384]{2,1,0:T(8,128)(2,1)S(1)}, bf16[512,384]{1,0:T(8,128)(2,1)S(1)}, bf16[512,384]{1,0:T(8,128...) custom-call(s32[1]{0:T(128)} %constant.36.clone.1.which, s32[4]{0:T(128)S(1)} %copy-done.13, ...), custom_call_target="tpu_custom_call" | custom-call | flops 34603008 | bytes 172608 | tf_op jit(solution)/shard_map/attend/pallas_call | solution.py:51
  53.7 16.6 %feed.3 = (f32[512,768]{1,0:T(8,128)S(1)}, bf16[768,512]{1,0:T(8,128)(2,1)S(1)}, bf16[512,1536]{1,0:T(8,128)(2,1)}, bf16[512,1536]{1,0:T(8,128)(2,1)}, bf16[512,...) custom-call(s32[4]{0:T(128)S(1)} %copy-done.13, ...), custom_call_target="tpu_custom_call" | custom-call | flops 94371840 | bytes 547872 | tf_op jit(solution)/shard_map/feed/pallas_call | solution.py:51
  70.5 3.5 %collective-permute-done.12.refs_3_ = bf16[512,1536]{1,0:T(8,128)(2,1)S(1)} collective-permute-done((bf16[512,1536]{1,0:T(8,128)(2,1)}, bf16[512,1536]{1,0:T(8,128)(2,1)S(1)}, u32[]{:S(2)}, u32[]{:S(2)}) %collective-permute-start.12) | collective-permute-done | bytes 1572896 | tf_op jit(solution)/shard_map/ppermute | solution.py:820
  74.0 4.3 %down_grad.2 = (bf16[384,1536]{1,0:T(8,128)(2,1)S(1)}, bf16[384,1536]{1,0:T(8,128)(2,1)S(1)}) custom-call(bf16[768,512]{1,0:T(8,128)(2,1)S(1)} %get-tuple-element.173.refs_0_, bf16[768,512]{1,0:T(8,128)(2,1)S(1)} %collective-permute-done.6.refs_1_, bf16[512,1536]{1,0:T(8,128)(2,1)} %get-tuple-element.184.refs_2_, ...), custom_call_target="tpu_custom_call" | custom-call | flops 37748736 | bytes 110592 | tf_op jit(solution)/shard_map/down_grad/pallas_call | solution.py:51
  78.3 2.7 collective-permute-start.13
  81.0 15.9 %feed_back.2 = (bf16[512,1536]{1,0:T(8,128)(2,1)}, bf16[512,1536]{1,0:T(8,128)(2,1)}, f32[2,768]{1,0:T(2,128)S(1)}, f32[2,768]{1,0:T(2,128)S(1)}, f32[512,768]{1...) custom-call(s32[1]{0:T(128)} %constant.36.clone.1.which, ...), custom_call_target="tpu_custom_call" | custom-call | flops 94371840 | bytes 547392 | tf_op jit(solution)/shard_map/feed_back/pallas_call | solution.py:51
  97.4 4.8 %attend_back.4 = (bf16[3,512,384]{2,1,0:T(8,128)(2,1)S(1)}, f32[1,768]{1,0:T(1,128)S(1)}) custom-call(s32[4]{0:T(128)S(1)} %copy-done.13, bf16[3,512,384]{2,1,0:T(8,128)(2,1)S(1)} %get-tuple-element.192.joint, f32[12,1,256]{2,1,0:T(1,128)S(1)} %get-tuple-element.193.lse, bf16[512,384]{1,0:T(8,128)(2,1)S(1)} %get-tuple-element.194.grad_att), custom_call_target="tpu_custom_call" | custom-call | flops 7864320 | bytes 43248 | tf_op jit(solution)/shard_map/attend_back/pallas_call | solution.py:51
  102.3 5.2 %collective-permute-done.13 = bf16[384,1536]{1,0:T(8,128)(2,1)S(1)} collective-permute-done((bf16[384,1536]{1,0:T(8,128)(2,1)S(1)}, bf16[384,1536]{1,0:T(8,128)(2,1)S(1)}, u32[]{:S(2)}, u32[]{:S(2)}) %collective-permute-start.13) | collective-permute-done | bytes 1179680 | tf_op jit(solution)/shard_map/ppermute | solution.py:751
  107.6 1.8 collective-permute-start.16
  110.0 3.3 %up_grad.2 = (bf16[384,1536]{1,0:T(8,128)(2,1)S(1)}, bf16[384,1536]{1,0:T(8,128)(2,1)S(1)}) custom-call(bf16[768,512]{1,0:T(8,128)(2,1)S(1)} %get-tuple-element.180.refs_0_, bf16[768,512]{1,0:T(8,128)(2,1)S(1)} %collective-permute-done.11.refs_1_, bf16[512,1536]{1,0:T(8,128)(2,1)S(1)} %copy-done.7, bf16[512,1536]{1,0:T(8,128)(2,1)S(1)} %collective-permute-done.14.refs_3_), custom_call_target="tpu_custom_call" | custom-call | flops 37748736 | bytes 110592 | tf_op jit(solution)/shard_map/up_grad/pallas_call | solution.py:51
  113.3 1.6 collective-permute-start.21
  115.4 4.8 %attend_back.5 = (bf16[3,512,384]{2,1,0:T(8,128)(2,1)S(1)}, f32[1,768]{1,0:T(1,128)S(1)}) custom-call(s32[4]{0:T(128)S(1)} %copy-done.13, bf16[3,512,384]{2,1,0:T(8,128)(2,1)S(1)} %get-tuple-element.204.joint, f32[12,1,256]{2,1,0:T(1,128)S(1)} %get-tuple-element.205.lse, bf16[512,384]{1,0:T(8,128)(2,1)S(1)} %get-tuple-element.206.grad_att), custom_call_target="tpu_custom_call" | custom-call | flops 7864320 | bytes 43248 | tf_op jit(solution)/shard_map/attend_back/pallas_call | solution.py:51
  120.2 7.9 %entry_back.2 = (f32[512,768]{1,0:T(8,128)S(1)}, f32[2,768]{1,0:T(2,128)S(1)}, bf16[768,512]{1,0:T(8,128)(2,1)S(1)}) custom-call(bf16[3,512,384]{2,1,0:T(8,128)(2,1)S(1)} %get-tuple-element.216.joint_own.refs_2_, bf16[3,512,384]{2,1,0:T(8,128)(2,1)S(1)} %get-tuple-element.210.joint_far, bf16[2,3,768,384]{3,2,1,0:T(8,128)(2,1)} %bitcast.20, ...), custom_call_target="tpu_custom_call" | custom-call | flops 28311552 | bytes 252192 | tf_op jit(solution)/shard_map/entry_back/pallas_call | solution.py:51
  128.3 1.6 collective-permute-start.22
  129.9 4.2 %qkv_out_grad.2 = (bf16[384,1536]{1,0:T(8,128)(2,1)S(1)}, bf16[384,1536]{1,0:T(8,128)(2,1)S(1)}) custom-call(bf16[768,512]{1,0:T(8,128)(2,1)S(1)} %get-tuple-element.213.refs_0_, bf16[768,512]{1,0:T(8,128)(2,1)S(1)} %collective-permute-done.15.refs_1_, bf16[3,512,384]{2,1,0:T(8,128)(2,1)S(1)} %get-tuple-element.216.joint_own.refs_2_, ...), custom_call_target="tpu_custom_call" | custom-call | flops 37748736 | bytes 135168 | tf_op jit(solution)/shard_map/qkv_out_grad/pallas_call | solution.py:51
  134.7 3.3 %down_grad.3 = (bf16[384,1536]{1,0:T(8,128)(2,1)S(1)}, bf16[384,1536]{1,0:T(8,128)(2,1)S(1)}) custom-call(bf16[768,512]{1,0:T(8,128)(2,1)S(1)} %get-tuple-element.219.refs_0_, bf16[768,512]{1,0:T(8,128)(2,1)S(1)} %collective-permute-done.20.refs_1_, bf16[512,1536]{1,0:T(8,128)(2,1)S(1)} %copy-done.5, bf16[512,1536]{1,0:T(8,128)(2,1)S(1)} %collective-permute-done.10.refs_3_), custom_call_target="tpu_custom_call" | custom-call | flops 37748736 | bytes 110592 | tf_op jit(solution)/shard_map/down_grad/pallas_call | solution.py:51
  138.2 3.1 %collective-permute-done.21 = bf16[384,1536]{1,0:T(8,128)(2,1)S(1)} collective-permute-done((bf16[384,1536]{1,0:T(8,128)(2,1)S(1)}, bf16[384,1536]{1,0:T(8,128)(2,1)S(1)}, u32[]{:S(2)}, u32[]{:S(2)}) %collective-permute-start.21) | collective-permute-done | bytes 1179680 | tf_op jit(solution)/shard_map/ppermute | solution.py:751
  141.7 1.7 collective-permute-start.25
  143.5 16.2 %feed_back.3 = (bf16[512,1536]{1,0:T(8,128)(2,1)}, bf16[512,1536]{1,0:T(8,128)(2,1)}, f32[2,768]{1,0:T(2,128)S(1)}, f32[2,768]{1,0:T(2,128)S(1)}, f32[512,768]{1...) custom-call(s32[1]{0:T(128)} %constant.14.clone.1.which, ...), custom_call_target="tpu_custom_call" | custom-call | flops 94371840 | bytes 547392 | tf_op jit(solution)/shard_map/feed_back/pallas_call | solution.py:51
  160.3 2.8 %collective-permute-done.24 = bf16[384,1536]{1,0:T(8,128)(2,1)S(1)} collective-permute-done((bf16[384,1536]{1,0:T(8,128)(2,1)S(1)}, bf16[384,1536]{1,0:T(8,128)(2,1)S(1)}, u32[]{:S(2)}, u32[]{:S(2)}) %collective-permute-start.24) | collective-permute-done | bytes 1179680 | tf_op jit(solution)/shard_map/ppermute | solution.py:751
  163.2 1.6 collective-permute-start.26
  164.9 4.8 %attend_back.6 = (bf16[3,512,384]{2,1,0:T(8,128)(2,1)S(1)}, f32[1,768]{1,0:T(1,128)S(1)}) custom-call(s32[4]{0:T(128)S(1)} %copy-done.13, bf16[3,512,384]{2,1,0:T(8,128)(2,1)S(1)} %get-tuple-element.238.joint, f32[12,1,256]{2,1,0:T(1,128)S(1)} %get-tuple-element.239.lse, bf16[512,384]{1,0:T(8,128)(2,1)S(1)} %get-tuple-element.240.grad_att), custom_call_target="tpu_custom_call" | custom-call | flops 7864320 | bytes 43248 | tf_op jit(solution)/shard_map/attend_back/pallas_call | solution.py:51
  169.8 2.2 collective-permute-done.26
  173.6 3.3 %up_grad.3 = (bf16[384,1536]{1,0:T(8,128)(2,1)S(1)}, bf16[384,1536]{1,0:T(8,128)(2,1)S(1)}) custom-call(bf16[768,512]{1,0:T(8,128)(2,1)S(1)} %get-tuple-element.175.refs_0_, bf16[768,512]{1,0:T(8,128)(2,1)S(1)} %collective-permute-done.9.refs_1_, bf16[512,1536]{1,0:T(8,128)(2,1)S(1)} %copy-done.6, bf16[512,1536]{1,0:T(8,128)(2,1)S(1)} %collective-permute-done.27.refs_3_), custom_call_target="tpu_custom_call" | custom-call | flops 37748736 | bytes 110592 | tf_op jit(solution)/shard_map/up_grad/pallas_call | solution.py:51
  178.0 2.7 collective-permute-start.31
  180.8 4.8 %attend_back.7 = (bf16[3,512,384]{2,1,0:T(8,128)(2,1)S(1)}, f32[1,768]{1,0:T(1,128)S(1)}) custom-call(s32[4]{0:T(128)S(1)} %copy-done.13, bf16[3,512,384]{2,1,0:T(8,128)(2,1)S(1)} %get-tuple-element.253.joint, f32[12,1,256]{2,1,0:T(1,128)S(1)} %get-tuple-element.254.lse, bf16[512,384]{1,0:T(8,128)(2,1)S(1)} %get-tuple-element.255.grad_att), custom_call_target="tpu_custom_call" | custom-call | flops 7864320 | bytes 43248 | tf_op jit(solution)/shard_map/attend_back/pallas_call | solution.py:51
  185.6 4.2 %qkv_out_grad.3 = (bf16[384,1536]{1,0:T(8,128)(2,1)S(1)}, bf16[384,1536]{1,0:T(8,128)(2,1)S(1)}) custom-call(bf16[768,512]{1,0:T(8,128)(2,1)S(1)} %get-tuple-element.174.refs_0_, bf16[768,512]{1,0:T(8,128)(2,1)S(1)} %collective-permute-done.7.refs_1_, bf16[3,512,384]{2,1,0:T(8,128)(2,1)S(1)} %get-tuple-element.256.refs_2_.joint_own, ...), custom_call_target="tpu_custom_call" | custom-call | flops 37748736 | bytes 135168 | tf_op jit(solution)/shard_map/qkv_out_grad/pallas_call | solution.py:51
  189.8 2.8 %collective-permute-done.31 = bf16[48,3072]{1,0:T(8,128)(2,1)S(1)} collective-permute-done((bf16[48,3072]{1,0:T(8,128)(2,1)S(1)}, bf16[48,3072]{1,0:T(8,128)(2,1)S(1)}, u32[]{:S(2)}, u32[]{:S(2)}) %collective-permute-start.31) | collective-permute-done | bytes 294944 | tf_op jit(solution)/shard_map/ppermute | solution.py:751
  192.6 1.5 collective-permute-start.33
  195.9 7.7 %entry_back.3 = (f32[512,768]{1,0:T(8,128)}, f32[2,768]{1,0:T(2,128)S(1)}) custom-call(bf16[3,512,384]{2,1,0:T(8,128)(2,1)S(1)} %get-tuple-element.256.refs_2_.joint_own, bf16[3,512,384]{2,1,0:T(8,128)(2,1)S(1)} %get-tuple-element.251.joint_far, bf16[2,3,768,384]{3,2,1,0:T(8,128)(2,1)} %bitcast.21, bf16[2,3,768,384]{3,2,1,0:T(8,128)(2,1)} %collective-permute-done.weight_far, ...), custom_call_target="tpu_custom_call" | custom-call | flops 28311552 | bytes 227616 | tf_op jit(solution)/shard_map/entry_back/pallas_call | solution.py:51
  204.0 1.6 collective-permute-start.34
  207.8 11.6 %collective-permute-done.33 = bf16[384,1536]{1,0:T(8,128)(2,1)S(1)} collective-permute-done((bf16[384,1536]{1,0:T(8,128)(2,1)S(1)}, bf16[384,1536]{1,0:T(8,128)(2,1)S(1)}, u32[]{:S(2)}, u32[]{:S(2)}) %collective-permute-start.33) | collective-permute-done | bytes 1179680 | tf_op jit(solution)/shard_map/ppermute | solution.py:751
  219.4 1.6 collective-permute-start.40
  221.0 1.5 collective-permute-start.41
  223.1 1.6 collective-permute-start.38
  224.8 2.7 collective-permute-start.39
  227.6 10.8 %collective-permute-done.39 = bf16[96,1536]{1,0:T(8,128)(2,1)S(1)} collective-permute-done((bf16[96,1536]{1,0:T(8,128)(2,1)S(1)}, bf16[96,1536]{1,0:T(8,128)(2,1)S(1)}, u32[]{:S(2)}, u32[]{:S(2)}) %collective-permute-start.39) | collective-permute-done | bytes 294944 | tf_op jit(solution)/shard_map/ppermute | solution.py:751
  238.6 1.5 collective-permute-start.43
  240.1 1.5 collective-permute-start.44
  243.4 3.4 %collective-permute-start.46 = (bf16[48,1536]{1,0:T(8,128)(2,1)S(1)}, bf16[48,1536]{1,0:T(8,128)(2,1)S(1)}, u32[]{:S(2)}, u32[]{:S(2)}) collective-permute-start(bf16[48,1536]{1,0:T(8,128)(2,1)S(1)} %add_convert_fusion.15), channel_id=1, source_target_pairs={{0,16},{2,18},{4,20},{6,22},{8,24},{10,26},{12,28},{14,30},{16,0},... | collective-permute-start | bytes 442376 | tf_op jit(solution)/shard_map/ppermute | solution.py:751
  249.5 2.3 collective-permute-done.47
  251.7 2.7 collective-permute-start.49
  256.9 12.4 %collective-permute-done.48 = f32[18,768]{1,0:T(8,128)S(1)} collective-permute-done((f32[18,768]{1,0:T(8,128)S(1)}, f32[18,768]{1,0:T(8,128)S(1)}, u32[]{:S(2)}, u32[]{:S(2)}) %collective-permute-start.48) | collective-permute-done | bytes 55328 | tf_op jit(solution)/shard_map/ppermute | solution.py:798
  (175 shorter events, 27.3 us)
Async XLA Ops:
  0.7 6.7 %collective-permute-start = (bf16[2,3,768,384]{3,2,1,0:T(8,128)(2,1)}, bf16[2,3,768,384]{3,2,1,0:T(8,128)(2,1)}, u32[]{:S(2)}, u32[]{:S(2)}) collective-permute-start(bf16[2,3,768,384]{3,2,1,0:T(8,128)(2,1)} %bitcast.17), channel_id=1, source_target_pairs={{0,1},{1,0},{2,3},{3,2},{4,5},{5,4},{6,7},{7,6},{8,9},{9,8},{10,11... | collective-permute-start | bytes 10616840 | tf_op jit(solution)/shard_map/ppermute | solution.py:820
  1.2 5.9 %collective-permute-start.1 = (f32[2,2,384]{2,1,0:T(2,128)}, f32[2,2,384]{2,1,0:T(2,128)S(1)}, u32[]{:S(2)}, u32[]{:S(2)}) collective-permute-start(f32[2,2,384]{2,1,0:T(2,128)} %bias_own.3), channel_id=1, source_target_pairs={{0,1},{1,0},{2,3},{3,2},{4,5},{5,4},{6,7},{7,6},{8,9},{9,8},{10,11... | collective-permute-start | bytes 18440 | tf_op jit(solution)/shard_map/ppermute | solution.py:820
  7.4 15.2 %collective-permute-start.3 = (bf16[2,768,1536]{2,1,0:T(8,128)(2,1)}, bf16[2,768,1536]{2,1,0:T(8,128)(2,1)S(1)}, u32[]{:S(2)}, u32[]{:S(2)}) collective-permute-start(bf16[2,768,1536]{2,1,0:T(8,128)(2,1)} %up_own.7), channel_id=1, source_target_pairs={{0,1},{1,0},{2,3},{3,2},{4,5},{5,4},{6,7},{7,6},{8,9},{9,8},{10,11... | collective-permute-start | bytes 14155784 | tf_op jit(solution)/shard_map/ppermute | solution.py:820
  7.8 16.3 %collective-permute-start.5 = (bf16[2,1536,768]{2,1,0:T(8,128)(2,1)}, bf16[2,1536,768]{2,1,0:T(8,128)(2,1)}, u32[]{:S(2)}, u32[]{:S(2)}) collective-permute-start(bf16[2,1536,768]{2,1,0:T(8,128)(2,1)} %down_own.7), channel_id=1, source_target_pairs={{0,1},{1,0},{2,3},{3,2},{4,5},{5,4},{6,7},{7,6},{8,9},{9,8},{10,11... | collective-permute-start | bytes 14155784 | tf_op jit(solution)/shard_map/ppermute | solution.py:820
  7.9 13.9 %collective-permute-start.2 = (bf16[2,384,768]{2,1,0:T(8,128)(2,1)S(1)}, bf16[2,384,768]{2,1,0:T(8,128)(2,1)S(1)}, u32[]{:S(2)}, u32[]{:S(2)}) collective-permute-start(bf16[2,384,768]{2,1,0:T(8,128)(2,1)S(1)} %copy-done.16), channel_id=1, source_target_pairs={{0,1},{1,0},{2,3},{3,2},{4,5},{5,4},{6,7},{7,6},{8,9},{9,8},{10,11... | collective-permute-start | bytes 3538952 | tf_op jit(solution)/shard_map/ppermute | solution.py:820
  8.3 13.5 %collective-permute-start.4 = (f32[2,1536]{1,0:T(2,128)S(1)}, f32[2,1536]{1,0:T(2,128)S(1)}, u32[]{:S(2)}, u32[]{:S(2)}) collective-permute-start(f32[2,1536]{1,0:T(2,128)S(1)} %copy-done.12), channel_id=1, source_target_pairs={{0,1},{1,0},{2,3},{3,2},{4,5},{5,4},{6,7},{7,6},{8,9},{9,8},{10,11... | collective-permute-start | bytes 36872 | tf_op jit(solution)/shard_map/ppermute | solution.py:820
  42.5 11.2 %collective-permute-start.10 = (bf16[512,1536]{1,0:T(8,128)(2,1)}, bf16[512,1536]{1,0:T(8,128)(2,1)S(1)}, u32[]{:S(2)}, u32[]{:S(2)}) collective-permute-start(bf16[512,1536]{1,0:T(8,128)(2,1)} %get-tuple-element.176), channel_id=1, source_target_pairs={{0,1},{1,0},{2,3},{3,2},{4,5},{5,4},{6,7},{7,6},{8,9},{9,8},{10,11... | collective-permute-start | bytes 4718600 | tf_op jit(solution)/shard_map/ppermute | solution.py:820
  42.9 10.7 %collective-permute-start.6 = (bf16[768,512]{1,0:T(8,128)(2,1)S(1)}, bf16[768,512]{1,0:T(8,128)(2,1)S(1)}, u32[]{:S(2)}, u32[]{:S(2)}) collective-permute-start(bf16[768,512]{1,0:T(8,128)(2,1)S(1)} %get-tuple-element.173.refs_0_), channel_id=1, source_target_pairs={{0,1},{1,0},{2,3},{3,2},{4,5},{5,4},{6,7},{7,6},{8,9},{9,8},{10,11... | collective-permute-start | bytes 2359304 | tf_op jit(solution)/shard_map/ppermute | solution.py:820
  43.1 10.6 %collective-permute-start.7 = (bf16[768,512]{1,0:T(8,128)(2,1)S(1)}, bf16[768,512]{1,0:T(8,128)(2,1)S(1)}, u32[]{:S(2)}, u32[]{:S(2)}) collective-permute-start(bf16[768,512]{1,0:T(8,128)(2,1)S(1)} %get-tuple-element.174.refs_0_), channel_id=1, source_target_pairs={{0,1},{1,0},{2,3},{3,2},{4,5},{5,4},{6,7},{7,6},{8,9},{9,8},{10,11... | collective-permute-start | bytes 2359304 | tf_op jit(solution)/shard_map/ppermute | solution.py:820
  43.4 10.2 %collective-permute-start.9 = (bf16[768,512]{1,0:T(8,128)(2,1)S(1)}, bf16[768,512]{1,0:T(8,128)(2,1)S(1)}, u32[]{:S(2)}, u32[]{:S(2)}) collective-permute-start(bf16[768,512]{1,0:T(8,128)(2,1)S(1)} %get-tuple-element.175.refs_0_), channel_id=1, source_target_pairs={{0,1},{1,0},{2,3},{3,2},{4,5},{5,4},{6,7},{7,6},{8,9},{9,8},{10,11... | collective-permute-start | bytes 2359304 | tf_op jit(solution)/shard_map/ppermute | solution.py:820
  43.6 10.1 %collective-permute-start.8 = (bf16[512,384]{1,0:T(8,128)(2,1)S(1)}, bf16[512,384]{1,0:T(8,128)(2,1)S(1)}, u32[]{:S(2)}, u32[]{:S(2)}) collective-permute-start(bf16[512,384]{1,0:T(8,128)(2,1)S(1)} %get-tuple-element.165.att_far), channel_id=1, source_target_pairs={{0,1},{1,0},{2,3},{3,2},{4,5},{5,4},{6,7},{7,6},{8,9},{9,8},{10,11... | collective-permute-start | bytes 1179656 | tf_op jit(solution)/shard_map/ppermute | solution.py:820
  78.3 29.2 %collective-permute-start.13 = (bf16[384,1536]{1,0:T(8,128)(2,1)S(1)}, bf16[384,1536]{1,0:T(8,128)(2,1)S(1)}, u32[]{:S(2)}, u32[]{:S(2)}) collective-permute-start(bf16[384,1536]{1,0:T(8,128)(2,1)S(1)} %get-tuple-element.191), channel_id=1, source_target_pairs={{0,2},{2,0},{4,6},{6,4},{8,10},{10,8},{12,14},{14,12},{16,18},{18,... | collective-permute-start | bytes 3538952 | tf_op jit(solution)/shard_map/ppermute | solution.py:751
  96.9 13.1 %collective-permute-start.14 = (bf16[512,1536]{1,0:T(8,128)(2,1)}, bf16[512,1536]{1,0:T(8,128)(2,1)S(1)}, u32[]{:S(2)}, u32[]{:S(2)}) collective-permute-start(bf16[512,1536]{1,0:T(8,128)(2,1)} %get-tuple-element.200), channel_id=1, source_target_pairs={{0,1},{1,0},{2,3},{3,2},{4,5},{5,4},{6,7},{7,6},{8,9},{9,8},{10,11... | collective-permute-start | bytes 4718600 | tf_op jit(solution)/shard_map/ppermute | solution.py:820
  97.0 12.9 %collective-permute-start.11 = (bf16[768,512]{1,0:T(8,128)(2,1)S(1)}, bf16[768,512]{1,0:T(8,128)(2,1)S(1)}, u32[]{:S(2)}, u32[]{:S(2)}) collective-permute-start(bf16[768,512]{1,0:T(8,128)(2,1)S(1)} %get-tuple-element.180.refs_0_), channel_id=1, source_target_pairs={{0,1},{1,0},{2,3},{3,2},{4,5},{5,4},{6,7},{7,6},{8,9},{9,8},{10,11... | collective-permute-start | bytes 2359304 | tf_op jit(solution)/shard_map/ppermute | solution.py:820
  107.6 20.4 %collective-permute-start.16 = (bf16[192,1536]{1,0:T(8,128)(2,1)S(1)}, bf16[192,1536]{1,0:T(8,128)(2,1)S(1)}, u32[]{:S(2)}, u32[]{:S(2)}) collective-permute-start(bf16[192,1536]{1,0:T(8,128)(2,1)S(1)} %add_convert_fusion.5), channel_id=1, source_target_pairs={{0,4},{2,6},{4,0},{6,2},{8,12},{10,14},{12,8},{14,10},{16,20},{18,... | collective-permute-start | bytes 1769480 | tf_op jit(solution)/shard_map/ppermute | solution.py:751
  109.4 5.4 %collective-permute-start.19 = (bf16[512,384]{1,0:T(8,128)(2,1)S(1)}, bf16[512,384]{1,0:T(8,128)(2,1)S(1)}, u32[]{:S(2)}, u32[]{:S(2)}) collective-permute-start(bf16[512,384]{1,0:T(8,128)(2,1)S(1)} %get-tuple-element.172.att_far), channel_id=1, source_target_pairs={{0,1},{1,0},{2,3},{3,2},{4,5},{5,4},{6,7},{7,6},{8,9},{9,8},{10,11... | collective-permute-start | bytes 1179656 | tf_op jit(solution)/shard_map/ppermute | solution.py:820
  109.5 20.5 %collective-permute-start.17 = (bf16[3,512,384]{2,1,0:T(8,128)(2,1)S(1)}, bf16[3,512,384]{2,1,0:T(8,128)(2,1)S(1)}, u32[]{:S(2)}, u32[]{:S(2)}) collective-permute-start(bf16[3,512,384]{2,1,0:T(8,128)(2,1)S(1)} %get-tuple-element.210.joint_far), channel_id=1, source_target_pairs={{0,1},{1,0},{2,3},{3,2},{4,5},{5,4},{6,7},{7,6},{8,9},{9,8},{10,11... | collective-permute-start | bytes 3538952 | tf_op jit(solution)/shard_map/ppermute | solution.py:820
  113.3 28.0 %collective-permute-start.21 = (bf16[384,1536]{1,0:T(8,128)(2,1)S(1)}, bf16[384,1536]{1,0:T(8,128)(2,1)S(1)}, u32[]{:S(2)}, u32[]{:S(2)}) collective-permute-start(bf16[384,1536]{1,0:T(8,128)(2,1)S(1)} %get-tuple-element.223), channel_id=1, source_target_pairs={{0,2},{2,0},{4,6},{6,4},{8,10},{10,8},{12,14},{14,12},{16,18},{18,... | collective-permute-start | bytes 3538952 | tf_op jit(solution)/shard_map/ppermute | solution.py:751
  114.8 13.4 %collective-permute-start.15 = (bf16[768,512]{1,0:T(8,128)(2,1)S(1)}, bf16[768,512]{1,0:T(8,128)(2,1)S(1)}, u32[]{:S(2)}, u32[]{:S(2)}) collective-permute-start(bf16[768,512]{1,0:T(8,128)(2,1)S(1)} %get-tuple-element.213.refs_0_), channel_id=1, source_target_pairs={{0,1},{1,0},{2,3},{3,2},{4,5},{5,4},{6,7},{7,6},{8,9},{9,8},{10,11... | collective-permute-start | bytes 2359304 | tf_op jit(solution)/shard_map/ppermute | solution.py:820
  114.9 15.1 %collective-permute-start.18 = (bf16[768,512]{1,0:T(8,128)(2,1)S(1)}, bf16[768,512]{1,0:T(8,128)(2,1)S(1)}, u32[]{:S(2)}, u32[]{:S(2)}) collective-permute-start(bf16[768,512]{1,0:T(8,128)(2,1)S(1)} %get-tuple-element.217.refs_4_), channel_id=1, source_target_pairs={{0,1},{1,0},{2,3},{3,2},{4,5},{5,4},{6,7},{7,6},{8,9},{9,8},{10,11... | collective-permute-start | bytes 2359304 | tf_op jit(solution)/shard_map/ppermute | solution.py:820
  128.1 6.6 %collective-permute-start.20 = (bf16[768,512]{1,0:T(8,128)(2,1)S(1)}, bf16[768,512]{1,0:T(8,128)(2,1)S(1)}, u32[]{:S(2)}, u32[]{:S(2)}) collective-permute-start(bf16[768,512]{1,0:T(8,128)(2,1)S(1)} %get-tuple-element.219.refs_0_), channel_id=1, source_target_pairs={{0,1},{1,0},{2,3},{3,2},{4,5},{5,4},{6,7},{7,6},{8,9},{9,8},{10,11... | collective-permute-start | bytes 2359304 | tf_op jit(solution)/shard_map/ppermute | solution.py:820
  128.3 9.9 %collective-permute-start.22 = (bf16[96,1536]{1,0:T(8,128)(2,1)S(1)}, bf16[96,1536]{1,0:T(8,128)(2,1)S(1)}, u32[]{:S(2)}, u32[]{:S(2)}) collective-permute-start(bf16[96,1536]{1,0:T(8,128)(2,1)S(1)} %add_convert_fusion.11), channel_id=1, source_target_pairs={{0,8},{2,10},{4,12},{6,14},{8,0},{10,2},{12,4},{14,6},{16,24},{18,... | collective-permute-start | bytes 884744 | tf_op jit(solution)/shard_map/ppermute | solution.py:751
  134.2 28.8 %collective-permute-start.24 = (bf16[384,1536]{1,0:T(8,128)(2,1)S(1)}, bf16[384,1536]{1,0:T(8,128)(2,1)S(1)}, u32[]{:S(2)}, u32[]{:S(2)}) collective-permute-start(bf16[384,1536]{1,0:T(8,128)(2,1)S(1)} %get-tuple-element.226), channel_id=1, source_target_pairs={{0,8},{2,10},{4,12},{6,14},{8,0},{10,2},{12,4},{14,6},{16,24},{18,... | collective-permute-start | bytes 3538952 | tf_op jit(solution)/shard_map/ppermute | solution.py:751
  141.4 21.7 %collective-permute-start.23 = (bf16[192,1536]{1,0:T(8,128)(2,1)S(1)}, bf16[192,1536]{1,0:T(8,128)(2,1)S(1)}, u32[]{:S(2)}, u32[]{:S(2)}) collective-permute-start(bf16[192,1536]{1,0:T(8,128)(2,1)S(1)} %add_convert_fusion.4), channel_id=1, source_target_pairs={{0,4},{2,6},{4,0},{6,2},{8,12},{10,14},{12,8},{14,10},{16,20},{18,... | collective-permute-start | bytes 1769480 | tf_op jit(solution)/shard_map/ppermute | solution.py:751
  141.7 30.2 %collective-permute-start.25 = (bf16[384,1536]{1,0:T(8,128)(2,1)S(1)}, bf16[384,1536]{1,0:T(8,128)(2,1)}, u32[]{:S(2)}, u32[]{:S(2)}) collective-permute-start(bf16[384,1536]{1,0:T(8,128)(2,1)S(1)} %get-tuple-element.236), channel_id=1, source_target_pairs={{0,2},{2,0},{4,6},{6,4},{8,10},{10,8},{12,14},{14,12},{16,18},{18,... | collective-permute-start | bytes 3538952 | tf_op jit(solution)/shard_map/ppermute | solution.py:751
  159.7 13.7 %collective-permute-start.27 = (bf16[512,1536]{1,0:T(8,128)(2,1)}, bf16[512,1536]{1,0:T(8,128)(2,1)S(1)}, u32[]{:S(2)}, u32[]{:S(2)}) collective-permute-start(bf16[512,1536]{1,0:T(8,128)(2,1)} %get-tuple-element.248), channel_id=1, source_target_pairs={{0,1},{1,0},{2,3},{3,2},{4,5},{5,4},{6,7},{7,6},{8,9},{9,8},{10,11... | collective-permute-start | bytes 4718600 | tf_op jit(solution)/shard_map/ppermute | solution.py:820
  159.8 17.2 %collective-permute-start.28 = (bf16[768,512]{1,0:T(8,128)(2,1)S(1)}, bf16[768,512]{1,0:T(8,128)(2,1)S(1)}, u32[]{:S(2)}, u32[]{:S(2)}) collective-permute-start(bf16[768,512]{1,0:T(8,128)(2,1)S(1)} %get-tuple-element.250.refs_4_), channel_id=1, source_target_pairs={{0,1},{1,0},{2,3},{3,2},{4,5},{5,4},{6,7},{7,6},{8,9},{9,8},{10,11... | collective-permute-start | bytes 2359304 | tf_op jit(solution)/shard_map/ppermute | solution.py:820
  163.2 8.8 %collective-permute-start.26 = (bf16[96,1536]{1,0:T(8,128)(2,1)S(1)}, bf16[96,1536]{1,0:T(8,128)(2,1)S(1)}, u32[]{:S(2)}, u32[]{:S(2)}) collective-permute-start(bf16[96,1536]{1,0:T(8,128)(2,1)S(1)} %add_convert_fusion.10), channel_id=1, source_target_pairs={{0,8},{2,10},{4,12},{6,14},{8,0},{10,2},{12,4},{14,6},{16,24},{18,... | collective-permute-start | bytes 884744 | tf_op jit(solution)/shard_map/ppermute | solution.py:751
  169.7 7.3 %collective-permute-start.29 = (bf16[3,512,384]{2,1,0:T(8,128)(2,1)S(1)}, bf16[3,512,384]{2,1,0:T(8,128)(2,1)S(1)}, u32[]{:S(2)}, u32[]{:S(2)}) collective-permute-start(bf16[3,512,384]{2,1,0:T(8,128)(2,1)S(1)} %get-tuple-element.251.joint_far), channel_id=1, source_target_pairs={{0,1},{1,0},{2,3},{3,2},{4,5},{5,4},{6,7},{7,6},{8,9},{9,8},{10,11... | collective-permute-start | bytes 3538952 | tf_op jit(solution)/shard_map/ppermute | solution.py:820
  177.0 26.9 %collective-permute-start.32 = (bf16[384,1536]{1,0:T(8,128)(2,1)S(1)}, bf16[384,1536]{1,0:T(8,128)(2,1)S(1)}, u32[]{:S(2)}, u32[]{:S(2)}) collective-permute-start(bf16[384,1536]{1,0:T(8,128)(2,1)S(1)} %get-tuple-element.269), channel_id=1, source_target_pairs={{0,2},{2,0},{4,6},{6,4},{8,10},{10,8},{12,14},{14,12},{16,18},{18,... | collective-permute-start | bytes 3538952 | tf_op jit(solution)/shard_map/ppermute | solution.py:751
  177.5 15.1 %collective-permute-start.30 = (bf16[192,1536]{1,0:T(8,128)(2,1)S(1)}, bf16[192,1536]{1,0:T(8,128)(2,1)S(1)}, u32[]{:S(2)}, u32[]{:S(2)}) collective-permute-start(bf16[192,1536]{1,0:T(8,128)(2,1)S(1)} %add_convert_fusion.3), channel_id=1, source_target_pairs={{0,4},{2,6},{4,0},{6,2},{8,12},{10,14},{12,8},{14,10},{16,20},{18,... | collective-permute-start | bytes 1769480 | tf_op jit(solution)/shard_map/ppermute | solution.py:751
  178.0 14.6 %collective-permute-start.31 = (bf16[48,3072]{1,0:T(8,128)(2,1)S(1)}, bf16[48,3072]{1,0:T(8,128)(2,1)S(1)}, u32[]{:S(2)}, u32[]{:S(2)}) collective-permute-start(bf16[48,3072]{1,0:T(8,128)(2,1)S(1)} %pad_maximum_fusion), channel_id=1, source_target_pairs={{0,16},{2,18},{4,20},{6,22},{8,24},{10,26},{12,28},{14,30},{16,0},... | collective-permute-start | bytes 884744 | tf_op jit(solution)/shard_map/ppermute | solution.py:751
  192.6 26.8 %collective-permute-start.33 = (bf16[384,1536]{1,0:T(8,128)(2,1)S(1)}, bf16[384,1536]{1,0:T(8,128)(2,1)S(1)}, u32[]{:S(2)}, u32[]{:S(2)}) collective-permute-start(bf16[384,1536]{1,0:T(8,128)(2,1)S(1)} %get-tuple-element.277), channel_id=1, source_target_pairs={{0,4},{2,6},{4,0},{6,2},{8,12},{10,14},{12,8},{14,10},{16,20},{18,... | collective-permute-start | bytes 3538952 | tf_op jit(solution)/shard_map/ppermute | solution.py:751
  195.2 11.6 %collective-permute-start.37 = (bf16[96,1536]{1,0:T(8,128)(2,1)S(1)}, bf16[96,1536]{1,0:T(8,128)(2,1)S(1)}, u32[]{:S(2)}, u32[]{:S(2)}) collective-permute-start(bf16[96,1536]{1,0:T(8,128)(2,1)S(1)} %add_convert_fusion.9), channel_id=1, source_target_pairs={{0,8},{2,10},{4,12},{6,14},{8,0},{10,2},{12,4},{14,6},{16,24},{18,... | collective-permute-start | bytes 884744 | tf_op jit(solution)/shard_map/ppermute | solution.py:751
  204.0 15.4 %collective-permute-start.34 = (bf16[192,1536]{1,0:T(8,128)(2,1)S(1)}, bf16[192,1536]{1,0:T(8,128)(2,1)S(1)}, u32[]{:S(2)}, u32[]{:S(2)}) collective-permute-start(bf16[192,1536]{1,0:T(8,128)(2,1)S(1)} %add_convert_fusion.1), channel_id=1, source_target_pairs={{0,8},{2,10},{4,12},{6,14},{8,0},{10,2},{12,4},{14,6},{16,24},{18,... | collective-permute-start | bytes 1769480 | tf_op jit(solution)/shard_map/ppermute | solution.py:751
  205.6 13.8 %collective-permute-start.36 = (bf16[192,1536]{1,0:T(8,128)(2,1)S(1)}, bf16[192,1536]{1,0:T(8,128)(2,1)S(1)}, u32[]{:S(2)}, u32[]{:S(2)}) collective-permute-start(bf16[192,1536]{1,0:T(8,128)(2,1)S(1)} %add_convert_fusion.2), channel_id=1, source_target_pairs={{0,2},{2,0},{4,6},{6,4},{8,10},{10,8},{12,14},{14,12},{16,18},{18,... | collective-permute-start | bytes 1769480 | tf_op jit(solution)/shard_map/ppermute | solution.py:751
  206.8 12.7 %collective-permute-start.35 = (f32[18,768]{1,0:T(8,128)S(1)}, f32[18,768]{1,0:T(8,128)S(1)}, u32[]{:S(2)}, u32[]{:S(2)}) collective-permute-start(f32[18,768]{1,0:T(8,128)S(1)} %get-tuple-element.280), channel_id=1, source_target_pairs={{0,1},{1,0},{2,3},{3,2},{4,5},{5,4},{6,7},{7,6},{8,9},{9,8},{10,11... | collective-permute-start | bytes 165896 | tf_op jit(solution)/shard_map/ppermute | solution.py:820
  219.4 19.2 %collective-permute-start.40 = (f32[18,768]{1,0:T(8,128)S(1)}, f32[18,768]{1,0:T(8,128)S(1)}, u32[]{:S(2)}, u32[]{:S(2)}) collective-permute-start(f32[18,768]{1,0:T(8,128)S(1)} %add.170), channel_id=1, source_target_pairs={{0,2},{2,0},{4,6},{6,4},{8,10},{10,8},{12,14},{14,12},{16,18},{18,... | collective-permute-start | bytes 165896 | tf_op jit(solution)/shard_map/ppermute | solution.py:798
  221.0 17.6 %collective-permute-start.41 = (f32[18,768]{1,0:T(8,128)S(1)}, f32[18,768]{1,0:T(8,128)S(1)}, u32[]{:S(2)}, u32[]{:S(2)}) collective-permute-start(f32[18,768]{1,0:T(8,128)S(1)} %add.170), channel_id=1, source_target_pairs={{0,4},{2,6},{4,0},{6,2},{8,12},{10,14},{12,8},{14,10},{16,20},{18,... | collective-permute-start | bytes 165896 | tf_op jit(solution)/shard_map/ppermute | solution.py:798
  222.5 16.1 %collective-permute-start.42 = (f32[18,768]{1,0:T(8,128)S(1)}, f32[18,768]{1,0:T(8,128)S(1)}, u32[]{:S(2)}, u32[]{:S(2)}) collective-permute-start(f32[18,768]{1,0:T(8,128)S(1)} %add.170), channel_id=1, source_target_pairs={{0,6},{2,4},{4,2},{6,0},{8,14},{10,12},{12,10},{14,8},{16,22},{18,... | collective-permute-start | bytes 165896 | tf_op jit(solution)/shard_map/ppermute | solution.py:798
  223.1 15.3 %collective-permute-start.38 = (bf16[192,1536]{1,0:T(8,128)(2,1)S(1)}, bf16[192,1536]{1,0:T(8,128)(2,1)S(1)}, u32[]{:S(2)}, u32[]{:S(2)}) collective-permute-start(bf16[192,1536]{1,0:T(8,128)(2,1)S(1)} %add_convert_fusion), channel_id=1, source_target_pairs={{0,2},{2,0},{4,6},{6,4},{8,10},{10,8},{12,14},{14,12},{16,18},{18,... | collective-permute-start | bytes 1769480 | tf_op jit(solution)/shard_map/ppermute | solution.py:751
  224.8 13.6 %collective-permute-start.39 = (bf16[96,1536]{1,0:T(8,128)(2,1)S(1)}, bf16[96,1536]{1,0:T(8,128)(2,1)S(1)}, u32[]{:S(2)}, u32[]{:S(2)}) collective-permute-start(bf16[96,1536]{1,0:T(8,128)(2,1)S(1)} %add_convert_fusion.8), channel_id=1, source_target_pairs={{0,16},{2,18},{4,20},{6,22},{8,24},{10,26},{12,28},{14,30},{16,0},... | collective-permute-start | bytes 884744 | tf_op jit(solution)/shard_map/ppermute | solution.py:751
  238.6 9.6 %collective-permute-start.43 = (bf16[96,1536]{1,0:T(8,128)(2,1)S(1)}, bf16[96,1536]{1,0:T(8,128)(2,1)S(1)}, u32[]{:S(2)}, u32[]{:S(2)}) collective-permute-start(bf16[96,1536]{1,0:T(8,128)(2,1)S(1)} %add_convert_fusion.7), channel_id=1, source_target_pairs={{0,8},{2,10},{4,12},{6,14},{8,0},{10,2},{12,4},{14,6},{16,24},{18,... | collective-permute-start | bytes 884744 | tf_op jit(solution)/shard_map/ppermute | solution.py:751
  240.1 9.1 %collective-permute-start.44 = (bf16[96,1536]{1,0:T(8,128)(2,1)S(1)}, bf16[96,1536]{1,0:T(8,128)(2,1)S(1)}, u32[]{:S(2)}, u32[]{:S(2)}) collective-permute-start(bf16[96,1536]{1,0:T(8,128)(2,1)S(1)} %add_convert_fusion.6), channel_id=1, source_target_pairs={{0,4},{2,6},{4,0},{6,2},{8,12},{10,14},{12,8},{14,10},{16,20},{18,... | collective-permute-start | bytes 884744 | tf_op jit(solution)/shard_map/ppermute | solution.py:751
  242.8 8.9 %collective-permute-start.45 = (bf16[48,1536]{1,0:T(8,128)(2,1)S(1)}, bf16[48,1536]{1,0:T(8,128)(2,1)S(1)}, u32[]{:S(2)}, u32[]{:S(2)}) collective-permute-start(bf16[48,1536]{1,0:T(8,128)(2,1)S(1)} %add_convert_fusion.14), channel_id=1, source_target_pairs={{0,4},{2,6},{4,0},{6,2},{8,12},{10,14},{12,8},{14,10},{16,20},{18,... | collective-permute-start | bytes 442376 | tf_op jit(solution)/shard_map/ppermute | solution.py:751
  243.4 8.3 %collective-permute-start.46 = (bf16[48,1536]{1,0:T(8,128)(2,1)S(1)}, bf16[48,1536]{1,0:T(8,128)(2,1)S(1)}, u32[]{:S(2)}, u32[]{:S(2)}) collective-permute-start(bf16[48,1536]{1,0:T(8,128)(2,1)S(1)} %add_convert_fusion.15), channel_id=1, source_target_pairs={{0,16},{2,18},{4,20},{6,22},{8,24},{10,26},{12,28},{14,30},{16,0},... | collective-permute-start | bytes 442376 | tf_op jit(solution)/shard_map/ppermute | solution.py:751
  251.7 17.6 %collective-permute-start.49 = (bf16[48,3072]{1,0:T(8,128)(2,1)S(1)}, bf16[48,3072]{1,0:T(8,128)(2,1)S(1)}, u32[]{:S(2)}, u32[]{:S(2)}) collective-permute-start(bf16[48,3072]{1,0:T(8,128)(2,1)S(1)} %pad_maximum_fusion.1), channel_id=1, source_target_pairs={{0,16},{2,18},{4,20},{6,22},{8,24},{10,26},{12,28},{14,30},{16,0},... | collective-permute-start | bytes 884744 | tf_op jit(solution)/shard_map/ppermute | solution.py:751
  254.4 14.9 %collective-permute-start.48 = (f32[18,768]{1,0:T(8,128)S(1)}, f32[18,768]{1,0:T(8,128)S(1)}, u32[]{:S(2)}, u32[]{:S(2)}) collective-permute-start(f32[18,768]{1,0:T(8,128)S(1)} %add.190), channel_id=1, source_target_pairs={{0,16},{2,18},{4,20},{6,22},{8,24},{10,26},{12,28},{14,30},{16,0},... | collective-permute-start | bytes 165896 | tf_op jit(solution)/shard_map/ppermute | solution.py:798
  (26 other events, 143.0 us)
